TPU v7x, 256 devices: a whole 4x4x8 slice. The times are simulated.
256 devices in a mesh: dp: 16 (over y_lo, x, core), seq: 16 (over z, y_hi).
Axes of the slice: x: 4, y: 4 (y_hi: 2, y_lo: 2; y = y_hi * 2 + y_lo), z: 8, core: 2. Of those that a mesh axis runs over, the one named last changes fastest.
Arguments:
- student_in: bfloat16 [32768, 3584], P(('dp', 'seq')), may hold values from -24 to 24
- weight: bfloat16 [3584, 512], P(('dp', 'seq')), may hold values from -0.09375 to 0.09375
- queries: bfloat16 [32768, 512], P(('dp', 'seq')), may hold values from -8 to 8, as said below
- keys: bfloat16 [32768, 128], P(('dp', 'seq')), may hold values from -8 to 8
- values: bfloat16 [32768, 128], P(('dp', 'seq')), may hold values from -6 to 6
- lengths: int32 [16, 4], P('dp'), may hold values from 1 to 1536, 2048 in all within a row
- assignment: int32 [16, 16], P('dp'), may hold values from 0 to 15, each once within a row
Outputs:
- attention: bfloat16 [32768, 512], P(('dp', 'seq'))
- weight_grad: float32 [3584, 512], P(('dp', 'seq'))
Inputs may be any that keep to these rules, and one draw needn't show every extreme that they name: `queries`: entries of head 0 and of keys may reach the ends of this range. Each row holds the lengths of 4 rollouts of one sequence, summing to 2048, the longest exactly 1536. `assignment`: each row is a permutation of the 16 rollout blocks of one sequence.
All inputs are finite; a program needn't handle non-finite values.
Results may differ from a plain program's by a relative error of at most 0.012.
Values may be sent and summed in bfloat16 or wider, within the bound.
No kernel may reach another device: no remote copies, remote signals or barrier semaphores. Data moves between devices by JAX's collectives and lax.ppermute only.
A program may use at most 64 MiB of HBM per device.

v0:
```python
import math

import jax
import jax.numpy as jnp
from jax import lax
from jax.sharding import PartitionSpec as P

HD = 128
HQ = 4
BLK = 128


EPSILON = 1e-06
NEGATIVE = -1e30


def side_by_side(arrays, axis, dim, along):
    both = jnp.concatenate(arrays, axis=along)
    whole, at, gathered = (lax.all_gather(both, axis, axis=dim, tiled=True), 0, [])
    for a in arrays:
        gathered.append(lax.slice_in_dim(whole, at, at + a.shape[along], axis=along))
        at += a.shape[along]
    return tuple(gathered)


def laid_out(tiles, dim):
    tiles = jnp.moveaxis(tiles, 0, dim)
    dims = tiles.shape
    return tiles.reshape(*dims[:dim], dims[dim] * dims[dim + 1], *dims[dim + 2 :])


def from_everyone(x, axis):
    copies = jnp.broadcast_to(x, (lax.axis_size(axis), *x.shape))
    return lax.all_to_all(copies, axis, split_axis=0, concat_axis=0, tiled=True)


def collect(x, axis, dim):
    return laid_out(from_everyone(x, axis), dim)


def in_blocks(x, dim, length):
    before, after = (x.shape[:dim], x.shape[dim + 1 :])
    return jnp.moveaxis(x.reshape(*before, length, -1, *after), dim, 0)


def sum_at_owner(x, axis, dim):
    tiles = in_blocks(x, dim, lax.axis_size(axis))
    arrived = lax.all_to_all(tiles, axis, split_axis=0, concat_axis=0, tiled=True)
    return arrived.astype(jnp.float32).sum(axis=0)


def locate(assign_row, doc_ends, first_slot, count):
    slot_ids = first_slot + jnp.arange(count, dtype=jnp.int32)
    block_ids = slot_ids // BLK
    block_table = jnp.arange(assign_row.shape[0], dtype=jnp.int32)
    placed = jnp.sum(
        jnp.where(block_ids[:, None] == block_table[None, :], assign_row[None, :], 0), axis=1
    )
    position = placed * BLK + slot_ids % BLK
    document = jnp.sum((position[:, None] >= doc_ends[None, :]).astype(jnp.int32), axis=1)
    return (position, document)


def absorb_block(state, key_block, value_block, query_heads, allowed):
    run_max, run_total, run_acc = state
    scores = jnp.einsum(
        "qhd,kd->hqk", query_heads, key_block, preferred_element_type=jnp.float32
    ) * HD ** (-0.5)
    masked = jnp.where(allowed[None], scores, NEGATIVE)
    new_max = jnp.maximum(run_max, jnp.max(masked, axis=-1))
    fading = jnp.exp(run_max - new_max)
    exp_terms = jnp.where(allowed[None], jnp.exp(masked - new_max[:, :, None]), 0.0)
    new_total = run_total * fading + jnp.sum(exp_terms, axis=-1)
    mixture = jnp.einsum(
        "hqk,kd->qhd",
        exp_terms.astype(jnp.bfloat16),
        value_block,
        preferred_element_type=jnp.float32,
    )
    new_acc = run_acc * fading.T[:, :, None] + mixture
    return (new_max, new_total, new_acc)


def local(student_in, weight, queries, keys, values, lengths, assignment):
    rows = queries.shape[0]
    assign_row = assignment[0]
    doc_ends = jnp.cumsum(lengths[0])
    query_pos, query_doc = locate(assign_row, doc_ends, lax.axis_index("seq") * rows, rows)
    query_heads = queries.reshape(rows, HQ, HD)
    start_state = (
        jnp.full((HQ, rows), NEGATIVE, jnp.float32),
        jnp.zeros((HQ, rows), jnp.float32),
        jnp.zeros((rows, HQ, HD), jnp.float32),
    )
    key_piece, value_piece = side_by_side((keys, values), "seq", 0, 1)
    count = key_piece.shape[0]
    step_rows = math.gcd(count, 512)
    steps_count = count // step_rows
    key_pos, key_doc = locate(assign_row, doc_ends, jnp.int32(0), count)

    def one_step(running, slabs):
        key_block, value_block, key_position, key_document = slabs
        allowed = (query_doc[:, None] == key_document[None, :]) & (
            query_pos[:, None] >= key_position[None, :]
        )
        updated = absorb_block(running, key_block, value_block, query_heads, allowed)
        return (updated, None)

    slabs = (
        key_piece.reshape(steps_count, step_rows, HD),
        value_piece.reshape(steps_count, step_rows, HD),
        key_pos.reshape(steps_count, step_rows),
        key_doc.reshape(steps_count, step_rows),
    )
    result, _ = lax.scan(one_step, start_state, slabs)
    final_max, final_total, final_acc = result
    attention = (final_acc / final_total.T[:, :, None]).reshape(rows, HQ * HD).astype(jnp.bfloat16)
    as_float = student_in.astype(jnp.float32)
    normed = (
        as_float * lax.rsqrt(jnp.mean(as_float * as_float, axis=1, keepdims=True) + EPSILON)
    ).astype(jnp.bfloat16)
    group_rows = collect(weight, "seq", 0)
    columns = normed
    predicted = jnp.dot(
        columns,
        lax.all_gather(group_rows, "dp", axis=0, tiled=True),
        preferred_element_type=jnp.float32,
    )
    dp_count = lax.axis_size("dp")
    seq_count = lax.axis_size("seq")
    token_total = rows * dp_count * seq_count
    scaled = ((predicted - attention.astype(jnp.float32)) * token_total ** (-0.5)).astype(
        jnp.bfloat16
    )
    columns = normed
    outer_rows = lax.psum_scatter(
        lax.dot_general(
            columns, scaled, (((0,), (0,)), ((), ())), preferred_element_type=jnp.float32
        ).astype(jnp.bfloat16),
        "dp",
        scatter_dimension=0,
        tiled=True,
    )
    weight_grad = sum_at_owner(outer_rows, "seq", 0)
    return (attention, weight_grad)


def solution(mesh):
    placed = (
        P(("dp", "seq"), None),
        P(("dp", "seq"), None),
        P(("dp", "seq"), None),
        P(("dp", "seq"), None),
        P(("dp", "seq"), None),
        P("dp", None),
        P("dp", None),
    )
    return jax.shard_map(
        local,
        mesh=mesh,
        in_specs=placed,
        out_specs=(P(("dp", "seq"), None), P(("dp", "seq"), None)),
        check_vma=False,
    )
```

profile of v0, /device:TPU:32, one launch (start us, length us, event | category | flops | bytes accessed | tf_op | source)
XLA Modules:
  0.0 233.2 jit_solution(15278113678716373417)
XLA Ops:
  7.2 0.0 all-gather.3.cloned.1.call-start
  7.2 1.4 pad_maximum_fusion
  8.6 0.0 all-gather.3.cloned.1.call-update
  8.6 1.4 broadcast_in_dim.82
  10.1 11.2 %all-to-all-start = ((bf16[16,14,512]{2,1,0:T(8,128)(2,1)}), bf16[16,14,512]{2,1,0:T(8,128)(2,1)S(1)}, u32[]{:S(2)}, u32[]{:S(2)}) async-start(bf16[16,14,512]{2,1,0:T(8,128)(2,1)} %broadcast_in_dim.82), calls=%async_computation | async-start | bytes 524288 | tf_op jit(solution)/shard_map/all_to_all | solution.py:34
  21.3 0.0 all-gather.5.cloned.1.call-start
  21.4 0.8 reduce-window.8
  22.2 0.7 select_reduce_fusion.1
  22.9 0.8 select_reduce_fusion
  23.7 0.1 convert_reduce_fusion.1
  23.8 0.1 convert_reduce_fusion.2
  23.9 1.0 copy.17
  25.0 0.1 copy.18
  25.1 1.5 fusion.18
  26.6 6.8 %all-to-all-done = bf16[16,14,512]{2,1,0:T(8,128)(2,1)S(1)} async-done(((bf16[16,14,512]{2,1,0:T(8,128)(2,1)}), bf16[16,14,512]{2,1,0:T(8,128)(2,1)S(1)}, u32[]{:S(2)}, u32[]{:S(2)}) %all-to-all-start) | async-done | bytes 229408 | tf_op jit(solution)/shard_map/all_to_all | solution.py:34
  33.4 0.8 reshape.189
  34.2 0.0 all-gather.5.cloned.1.call-update
  34.2 0.0 reduce-scatter.2.cloned.1.call-start
  34.3 57.6 %all-gather.3.cloned.1.call-done = bf16[2048,256]{1,0:T(8,128)(2,1)} async-done(((bf16[128,256]{1,0:T(8,128)(2,1)}), bf16[2048,256]{1,0:T(8,128)(2,1)}) %all-gather.3.cloned.1.call-update) | async-done | bytes 1048592 | tf_op jit(solution)/shard_map/all_gather | solution.py:19
  91.8 1.3 fusion.41
  93.1 0.0 copy-start
  93.1 4.8 %while.15 = (s32[]{:T(128)}, f32[4,128]{1,0:T(4,128)S(1)}, f32[4,128]{1,0:T(4,128)S(1)}, f32[128,4,128]{0,2,1:T(8,128)S(1)}, s32[128]{0:T(128)S(1)}, /*index=5*/...) while((s32[]{:T(128)}, f32[4,128]{1,0:T(4,128)S(1)}, ...), condition=%wide.region_8.9_spmd.clone, body=%wide.region_5.8_spmd.clone.sunk | while | flops 136973312 | bytes 4371613 | solution.py:115
  93.1 0.2 compare_and_fusion.2
  93.4 0.3 fusion.55
  93.7 0.2 fusion.57
  93.9 0.4 fusion.59
  94.3 0.2 compare_and_fusion.2
  94.6 0.3 fusion.55
  94.9 0.2 fusion.57
  95.1 0.4 fusion.59
  95.5 0.2 compare_and_fusion.2
  95.7 0.3 fusion.55
  96.1 0.2 fusion.57
  96.3 0.4 fusion.59
  96.7 0.2 compare_and_fusion.2
  96.9 0.3 fusion.55
  97.3 0.2 fusion.57
  97.5 0.4 fusion.59
  97.9 0.1 copy.22
  98.1 0.0 copy-start.1
  98.1 32.2 %all-gather.5.cloned.1.call-done = bf16[3584,512]{1,0:T(8,128)(2,1)} async-done(((bf16[224,512]{1,0:T(8,128)(2,1)}), bf16[3584,512]{1,0:T(8,128)(2,1)}) %all-gather.5.cloned.1.call-update) | async-done | bytes 3670032 | tf_op jit(solution)/shard_map/all_gather | solution.py:126
  130.3 0.0 copy-done
  130.3 5.7 %convolution_convert_fusion = bf16[3584,512]{1,0:T(8,128)(2,1)} fusion(bf16[3584,512]{1,0:T(8,128)(2,1)} %all-gather.5.cloned.1.call-done, bf16[128,3584]{1,0:T(8,128)(2,1)S(1)} %copy-done, f32[128]{0:T(128)S(1)} %add_rsqrt_fusion, bf16[128,512]{1,0:T(8,128)(2,1)S(1)} %copy.22), kind=kOutput, calls=%fused_computation.27 | convolution fusion | flops 944373760 | bytes 8389120 | tf_op jit(solution)/shard_map/dot_general | solution.py:137
  135.9 0.0 copy-done.1
  135.9 0.0 reduce-scatter.2.cloned.1.call-update
  135.9 68.7 %reduce-scatter.2.cloned.1.call-done = bf16[224,512]{1,0:T(8,128)(2,1)} async-done(((bf16[3584,512]{1,0:T(8,128)(2,1)}), bf16[224,512]{1,0:T(8,128)(2,1)}) %reduce-scatter.2.cloned.1.call-update) | async-done | bytes 229392 | tf_op jit(solution)/shard_map/reduce_scatter | solution.py:136
  204.7 1.0 reshape.190
  205.7 20.3 %all_to_all.10 = bf16[16,14,512]{2,1,0:T(8,128)(2,1)S(1)} all-to-all(bf16[16,14,512]{2,1,0:T(8,128)(2,1)S(1)} %reshape.190), channel_id=1, replica_groups=mesh['dp'=16,'seq'=16] {'seq'}, dimensions={0} | all-to-all | bytes 458752 | tf_op jit(solution)/shard_map/all_to_all | solution.py:48
  226.0 0.7 convert_reduce_fusion
  (28 shorter events, 0.3 us)
Async XLA Ops:
  7.2 84.7 %all-gather.3.cloned.1.call-start = ((), (), s32[]{:S(2)}) async-start(), calls=%async_computation.3 | async-start | bytes 1114112 | tf_op jit(solution)/shard_map/all_gather | solution.py:19
  10.1 23.3 %all-to-all-start = ((bf16[16,14,512]{2,1,0:T(8,128)(2,1)}), bf16[16,14,512]{2,1,0:T(8,128)(2,1)S(1)}, u32[]{:S(2)}, u32[]{:S(2)}) async-start(bf16[16,14,512]{2,1,0:T(8,128)(2,1)} %broadcast_in_dim.82), calls=%async_computation | async-start | bytes 524288 | tf_op jit(solution)/shard_map/all_to_all | solution.py:34
  21.3 109.0 %all-gather.5.cloned.1.call-start = ((), (), s32[]{:S(2)}) async-start(), calls=%async_computation.4 | async-start | bytes 3899392 | tf_op jit(solution)/shard_map/all_gather | solution.py:126
  34.2 170.5 %reduce-scatter.2.cloned.1.call-start = ((), (), s32[]{:S(2)}) async-start(), calls=%async_computation.5 | async-start | bytes 3899392 | tf_op jit(solution)/shard_map/reduce_scatter | solution.py:136
  93.1 37.2 %copy-start = (bf16[128,3584]{1,0:T(8,128)(2,1)S(1)}, bf16[128,3584]{1,0:T(8,128)(2,1)}, u32[]{:S(2)}) copy-start(bf16[128,3584]{1,0:T(8,128)(2,1)} %param.9) | copy-start | bytes 2752516
  98.1 37.9 %copy-start.1 = (bf16[128,512]{1,0:T(8,128)(2,1)}, bf16[128,512]{1,0:T(8,128)(2,1)S(1)}, u32[]{:S(2)}) copy-start(bf16[128,512]{1,0:T(8,128)(2,1)S(1)} %copy.22) | copy-start | bytes 393220
Sparse Core Ops, SparseCore 0:
  11.2 80.6 all-gather.2
  93.7 36.5 all-gather.4
  136.1 68.5 reduce-scatter.1
where the time goes:
time: 234 us; the launch traced here: 233 us
  waiting for transfers between devices  165 us (71%)
  blocking collectives  20.3 us (9%)
  between operations  13.8 us (6%)
  starting transfers between devices  11.3 us (5%)
  matrix products  8.4 us (4%)
  other arithmetic  7.87 us (3%)
  local copies, waits for them, and re-layouts  5.83 us (2%)
    reduce_scatter x1, waiting for transfers between devices, local(): lax.psum_scatter(lax.dot_general(columns, scaled, (((0,), (0,)), ((), ())...  68.7 us
    all_gather x1, waiting for transfers between devices, side_by_side(): lax.all_gather(both, axis, axis=dim, tiled=True)  57.6 us
    all_gather x1, waiting for transfers between devices, local(): lax.all_gather(group_rows, 'dp', axis=0, tiled=True)  32.2 us
    all_to_all x1, blocking collectives, sum_at_owner(): lax.all_to_all(tiles, axis, split_axis=0, concat_axis=0, tiled=True)  20.3 us
    all_to_all x1, starting transfers between devices, from_everyone(): return lax.all_to_all(copies, axis, split_axis=0, concat_axis=0, tiled=True)  11.2 us
    all_to_all x1, waiting for transfers between devices, from_everyone(): return lax.all_to_all(copies, axis, split_axis=0, concat_axis=0, tiled=True)  6.84 us
    dot_general x1, matrix products, local(): lax.dot_general(columns, scaled, (((0,), (0,)), ((), ())), preferred_elem...  5.66 us
  transfers between devices with their start and end apart: 4, of which 4 were waited for; matrix products, arithmetic and copies ran while one was open for 6% of the time, Pallas kernels for 0%

commit v1 on v0

v1 whole, which is shorter than its diff:
```python
import math

import jax
import jax.numpy as jnp
from jax import lax
from jax.sharding import Mesh, PartitionSpec as P

HD = 128
HQ = 4
BLK = 128
DS = 3584
COLS = HQ * HD
HALF = COLS // 2
TOKENS_ALL = 32768

EPSILON = 1e-06
NEGATIVE = -1e30

AXES = ("ylo", "x", "core", "z", "yhi")
SIZES = (2, 4, 2, 8, 2)
SEQ = ("z", "yhi")
WIDE = ("ylo", "x")
SWAP = ((0, 1), (1, 0))


def locate(assign_row, doc_ends, first_slot, count):
    slot_ids = first_slot + jnp.arange(count, dtype=jnp.int32)
    block_ids = slot_ids // BLK
    block_table = jnp.arange(assign_row.shape[0], dtype=jnp.int32)
    placed = jnp.sum(
        jnp.where(block_ids[:, None] == block_table[None, :], assign_row[None, :], 0), axis=1
    )
    position = placed * BLK + slot_ids % BLK
    document = jnp.sum((position[:, None] >= doc_ends[None, :]).astype(jnp.int32), axis=1)
    return (position, document)


def absorb_block(state, key_block, value_block, query_heads, allowed):
    run_max, run_total, run_acc = state
    scores = jnp.einsum(
        "qhd,kd->hqk", query_heads, key_block, preferred_element_type=jnp.float32
    ) * HD ** (-0.5)
    masked = jnp.where(allowed[None], scores, NEGATIVE)
    new_max = jnp.maximum(run_max, jnp.max(masked, axis=-1))
    fading = jnp.exp(run_max - new_max)
    exp_terms = jnp.where(allowed[None], jnp.exp(masked - new_max[:, :, None]), 0.0)
    new_total = run_total * fading + jnp.sum(exp_terms, axis=-1)
    mixture = jnp.einsum(
        "hqk,kd->qhd",
        exp_terms.astype(jnp.bfloat16),
        value_block,
        preferred_element_type=jnp.float32,
    )
    new_acc = run_acc * fading.T[:, :, None] + mixture
    return (new_max, new_total, new_acc)


def attend(queries, key_piece, value_piece, lengths, assignment):
    rows = queries.shape[0]
    assign_row = assignment[0]
    doc_ends = jnp.cumsum(lengths[0])
    query_pos, query_doc = locate(assign_row, doc_ends, lax.axis_index(SEQ) * rows, rows)
    query_heads = queries.reshape(rows, HQ, HD)
    start_state = (
        jnp.full((HQ, rows), NEGATIVE, jnp.float32),
        jnp.zeros((HQ, rows), jnp.float32),
        jnp.zeros((rows, HQ, HD), jnp.float32),
    )
    count = key_piece.shape[0]
    step_rows = math.gcd(count, 512)
    steps_count = count // step_rows
    key_pos, key_doc = locate(assign_row, doc_ends, jnp.int32(0), count)

    def one_step(running, slabs):
        key_block, value_block, key_position, key_document = slabs
        allowed = (query_doc[:, None] == key_document[None, :]) & (
            query_pos[:, None] >= key_position[None, :]
        )
        return (absorb_block(running, key_block, value_block, query_heads, allowed), None)

    slabs = (
        key_piece.reshape(steps_count, step_rows, HD),
        value_piece.reshape(steps_count, step_rows, HD),
        key_pos.reshape(steps_count, step_rows),
        key_doc.reshape(steps_count, step_rows),
    )
    result, _ = lax.scan(one_step, start_state, slabs)
    _, final_total, final_acc = result
    return (final_acc / final_total.T[:, :, None]).reshape(rows, COLS).astype(jnp.bfloat16)


def to_everyone(x, axes):
    size = math.prod(SIZES[AXES.index(a)] for a in axes)
    copies = jnp.broadcast_to(x, (size, *x.shape))
    return lax.all_to_all(copies, axes, split_axis=0, concat_axis=0, tiled=True)


def halves(x, core):
    low, high = x[:, :HALF], x[:, HALF:]
    return jnp.where(core == 0, low, high), jnp.where(core == 0, high, low)


def local(student_in, weight, queries, keys, values, lengths, assignment):
    rows = queries.shape[0]
    core = lax.axis_index("core")
    wrows = weight.shape[0]

    w_mine, w_other = halves(weight, core)
    w_got = lax.ppermute(w_other, "core", SWAP)
    w_first = jnp.where(core == 0, w_mine, w_got)
    w_second = jnp.where(core == 0, w_got, w_mine)
    kv = jnp.concatenate([keys, values], axis=1)
    pad = jnp.zeros((16 - wrows, HALF), jnp.bfloat16)
    packed = jnp.concatenate([kv, w_first, pad, w_second, pad], axis=0)
    arrived = to_everyone(packed, SEQ)

    as_float = student_in.astype(jnp.float32)
    normed = (
        as_float * lax.rsqrt(jnp.mean(as_float * as_float, axis=1, keepdims=True) + EPSILON)
    ).astype(jnp.bfloat16)
    both = jnp.concatenate([normed, lax.ppermute(normed, "core", SWAP)], axis=0)

    w_near = jnp.concatenate(
        [
            arrived[:, rows : rows + wrows].reshape(-1, HALF),
            arrived[:, rows + 16 : rows + 16 + wrows].reshape(-1, HALF),
        ],
        axis=0,
    )
    w_all = to_everyone(w_near, WIDE).reshape(DS, HALF)

    key_piece = arrived[:, :rows, :HD].reshape(-1, HD)
    value_piece = arrived[:, :rows, HD:].reshape(-1, HD)
    attention = attend(queries, key_piece, value_piece, lengths, assignment)
    a_mine, a_other = halves(attention, core)
    attended = jnp.concatenate([a_mine, lax.ppermute(a_other, "core", SWAP)], axis=0)

    predicted = jnp.dot(both, w_all, preferred_element_type=jnp.float32)
    scaled = ((predicted - attended.astype(jnp.float32)) * TOKENS_ALL ** (-0.5)).astype(
        jnp.bfloat16
    )
    part = lax.dot_general(
        both, scaled, (((0,), (0,)), ((), ())), preferred_element_type=jnp.float32
    ).astype(jnp.bfloat16)
    wide = lax.all_to_all(
        part.reshape(8, -1, HALF), WIDE, split_axis=0, concat_axis=0, tiled=True
    )
    near = wide.astype(jnp.float32).sum(axis=0).astype(jnp.bfloat16).reshape(32, wrows, HALF)
    last = lax.all_to_all(near, ("core", *SEQ), split_axis=0, concat_axis=0, tiled=True)
    summed = last.reshape(2, 16, wrows, HALF).astype(jnp.float32).sum(axis=1)
    weight_grad = jnp.concatenate([summed[0], summed[1]], axis=1)
    return (attention, weight_grad)


def solution(mesh):
    mesh = Mesh(mesh.devices.reshape(SIZES), AXES)
    token = P(AXES, None)
    row = P(("ylo", "x", "core"), None)
    return jax.shard_map(
        local,
        mesh=mesh,
        in_specs=(token, token, token, token, token, row, row),
        out_specs=(token, token),
        check_vma=False,
    )
```

time: 234 us -> 136 us (0.58)
  waiting for transfers between devices: 165 us -> 49.5 us
  blocking collectives: 20.3 us -> 48.5 us
  between operations: 13.8 us -> 0.83 us
  starting transfers between devices: 11.3 us -> 15.9 us
    all_gather x2 -> x0, waiting for transfers between devices: 89.7 us -> none  [the longest x1 57.6 us: side_by_side(): lax.all_gather(both, axis, axis=dim, tiled=True)]
    reduce_scatter x1 -> x0, waiting for transfers between devices: 68.7 us -> none  [local(): lax.psum_scatter(lax.dot_general(columns, scaled, (((0,), (0,)), ((), ())...]
    all_to_all x1 -> x2, waiting for transfers between devices: 6.84 us -> 48.3 us  [to_everyone(): return lax.all_to_all(copies, axes, split_axis=0, concat_axis=0, tiled=True)]
    all_to_all x1 -> x2, blocking collectives: 20.3 us -> 48.5 us  [the longest x1 27.7 us: local(): lax.all_to_all(part.reshape(8, -1, HALF), WIDE, split_axis=0, concat_axis...]
    all_to_all x1 -> x2, starting transfers between devices: 11.2 us -> 15.8 us  [to_everyone(): return lax.all_to_all(copies, axes, split_axis=0, concat_axis=0, tiled=True)]
  transfers between devices with their start and end apart: 4 -> 5, of which waited for: 4 -> 3; matrix products, arithmetic and copies ran while one was open for 6% -> 8% of each run, Pallas kernels for 0% -> 0%
where the time goes in v1:
time: 136 us; the launch traced here: 135 us
  waiting for transfers between devices  49.5 us (36%)
  blocking collectives  48.5 us (36%)
  starting transfers between devices  15.9 us (12%)
  matrix products  8.72 us (6%)
  other arithmetic  8.22 us (6%)
  local copies, waits for them, and re-layouts  3.5 us (3%)
    all_to_all x2, waiting for transfers between devices, to_everyone(): return lax.all_to_all(copies, axes, split_axis=0, concat_axis=0, tiled=True)  48.3 us
    all_to_all x1, blocking collectives, local(): lax.all_to_all(part.reshape(8, -1, HALF), WIDE, split_axis=0, concat_axis...  27.7 us
    all_to_all x1, blocking collectives, local(): lax.all_to_all(near, ('core', *SEQ), split_axis=0, concat_axis=0, tiled=T...  20.8 us
    all_to_all x2, starting transfers between devices, to_everyone(): return lax.all_to_all(copies, axes, split_axis=0, concat_axis=0, tiled=True)  15.8 us
    dot_general x1, matrix products, local(): lax.dot_general(both, scaled, (((0,), (0,)), ((), ())), preferred_element...  6.02 us
  transfers between devices with their start and end apart: 5, of which 3 were waited for; matrix products, arithmetic and copies ran while one was open for 8% of the time, Pallas kernels for 0%

profile of v1, /device:TPU:32, one launch (start us, length us, event | category | flops | bytes accessed | tf_op | source)
XLA Modules:
  0.0 135.4 jit_solution(14202016126133903333)
XLA Ops:
  0.6 0.7 broadcast_select_fusion.4
  1.4 0.0 collective-permute-start
  1.4 1.4 %fusion.18 = f32[128]{0:T(128)S(1)} fusion(bf16[128,3584]{1,0:T(8,128)(2,1)} %param.9), kind=kLoop, calls=%fused_computation.30 | loop fusion | flops 1376128 | bytes 918016 | tf_op jit(solution)/shard_map/reduce_sum | solution.py:119
  2.8 0.8 pad_maximum_fusion.12
  3.6 0.0 collective-permute-done
  3.6 0.7 broadcast_select_fusion.2
  4.4 0.0 copy-start
  4.4 1.2 broadcast_in_dim.89
  5.6 0.0 copy-start.4
  5.6 0.0 copy-start.3
  5.6 0.0 copy-start.2
  5.6 11.3 %all-to-all-start = ((bf16[16,160,256]{2,1,0:T(8,128)(2,1)}), bf16[16,160,256]{2,1,0:T(8,128)(2,1)S(1)}, u32[]{:S(2)}, u32[]{:S(2)}) async-start(bf16[16,160,256]{2,1,0:T(8,128)(2,1)} %broadcast_in_dim.89), calls=%async_computation | async-start | bytes 2621440 | tf_op jit(solution)/shard_map/all_to_all | solution.py:95
  16.9 0.0 copy-done
  16.9 1.1 fusion.19
  18.1 0.0 collective-permute-start.1
  18.1 0.0 copy-done.4
  18.1 0.2 reduce-window.8
  18.3 0.0 copy-done.3
  18.3 0.1 select_reduce_fusion
  18.4 0.1 convert_reduce_fusion.1
  18.5 0.0 copy-done.2
  18.5 0.1 copy.17
  18.6 0.1 copy.18
  18.8 0.1 select_reduce_fusion.1
  18.9 0.1 convert_reduce_fusion.2
  19.0 30.9 %all-to-all-done = bf16[16,160,256]{2,1,0:T(8,128)(2,1)S(1)} async-done(((bf16[16,160,256]{2,1,0:T(8,128)(2,1)}), bf16[16,160,256]{2,1,0:T(8,128)(2,1)S(1)}, u32[]{:S(2)}, u32[]{:S(2)}) %all-to-all-start) | async-done | bytes 1310752 | tf_op jit(solution)/shard_map/all_to_all | solution.py:95
  50.1 1.3 broadcast_in_dim.90
  51.5 4.4 %all-to-all-start.1 = ((bf16[8,448,256]{2,1,0:T(8,128)(2,1)}), bf16[8,448,256]{2,1,0:T(8,128)(2,1)}, u32[]{:S(2)}, u32[]{:S(2)}) async-start(bf16[8,448,256]{2,1,0:T(8,128)(2,1)} %broadcast_in_dim.90), calls=%async_computation.1 | async-start | bytes 3670016 | tf_op jit(solution)/shard_map/all_to_all | solution.py:95
  55.9 0.3 fusion.45
  56.2 4.7 %while.15 = (s32[]{:T(128)}, f32[4,128]{1,0:T(4,128)S(1)}, f32[4,128]{1,0:T(4,128)S(1)}, f32[128,4,128]{0,2,1:T(8,128)S(1)}, s32[128]{0:T(128)S(1)}, /*index=5*/...) while((s32[]{:T(128)}, f32[4,128]{1,0:T(4,128)S(1)}, ...), condition=%wide.region_8.9_spmd.clone, body=%wide.region_5.8_spmd.clone.sunk | while | flops 136973312 | bytes 4371605 | solution.py:87
  56.2 0.2 compare_and_fusion.2
  56.4 0.3 fusion.59
  56.7 0.4 fusion.63
  57.1 0.2 fusion.61
  57.4 0.2 compare_and_fusion.2
  57.6 0.3 fusion.59
  57.9 0.4 fusion.63
  58.3 0.2 fusion.61
  58.6 0.2 compare_and_fusion.2
  58.8 0.3 fusion.59
  59.1 0.4 fusion.63
  59.5 0.2 fusion.61
  59.8 0.2 compare_and_fusion.2
  60.0 0.3 fusion.59
  60.3 0.4 fusion.63
  60.7 0.2 fusion.61
  61.0 0.1 copy.22
  61.1 0.0 copy-start.1
  61.1 0.1 collective-permute-start.2
  61.2 0.0 collective-permute-done.1
  61.2 1.2 collective-permute-done.2
  62.5 17.3 %all-to-all-done.1 = bf16[8,448,256]{2,1,0:T(8,128)(2,1)} async-done(((bf16[8,448,256]{2,1,0:T(8,128)(2,1)}), bf16[8,448,256]{2,1,0:T(8,128)(2,1)}, u32[]{:S(2)}, u32[]{:S(2)}) %all-to-all-start.1) | async-done | bytes 1835040 | tf_op jit(solution)/shard_map/all_to_all | solution.py:95
  79.8 6.0 %convolution_convert_fusion = bf16[3584,256]{1,0:T(8,128)(2,1)} fusion(bf16[128,3584]{1,0:T(8,128)(2,1)} %collective-permute-done.1, bf16[128,3584]{1,0:T(8,128)(2,1)} %fusion.19, bf16[3584,256]{1,0:T(8,128)(2,1)} %bitcast.8, bf16[128,256]{1,0:T(8,128)(2,1)S(1)} %collective-permute-done.2, bf16[128,256]{1,0:T(8,128)(2,1)S(1)} %get-tuple-element.152), kind=kOutput, calls=%fused_computation.27 | convolution fusion | flops 948240384 | bytes 5636096 | tf_op jit(solution)/shard_map/dot_general | solution.py:142
  85.8 0.0 copy-done.1
  85.8 27.7 %all_to_all.20 = bf16[8,448,256]{2,1,0:T(8,128)(2,1)S(1)} all-to-all(bf16[8,448,256]{2,1,0:T(8,128)(2,1)} %bitcast.58), channel_id=1, replica_groups=mesh['ylo'=2,'x'=4,'core'=2,'z'=8,'yhi'=2] {'ylo','x'}, dimensions={0} | all-to-all | bytes 3670016 | tf_op jit(solution)/shard_map/all_to_all | solution.py:145
  113.5 0.3 reduce_sum.80
  113.9 0.1 reshape.197
  113.9 20.8 %all_to_all.21 = bf16[32,14,256]{2,1,0:T(8,128)(2,1)S(1)} all-to-all(bf16[32,14,256]{2,1,0:T(8,128)(2,1)S(1)} %reshape.197), channel_id=1, replica_groups=mesh['ylo'=2,'x'=4,'core'=2,'z'=8,'yhi'=2] {'core','z','yhi'}, dimensions={0} | all-to-all | bytes 458752 | tf_op jit(solution)/shard_map/all_to_all | solution.py:149
  134.8 0.6 pad_maximum_fusion.13
  (37 shorter events, 0.5 us)
Async XLA Ops:
  1.4 2.2 %collective-permute-start = (bf16[14,256]{1,0:T(8,128)(2,1)S(1)}, bf16[14,256]{1,0:T(8,128)(2,1)S(1)}, u32[]{:S(2)}, u32[]{:S(2)}) collective-permute-start(bf16[14,256]{1,0:T(8,128)(2,1)S(1)} %broadcast_select_fusion.4), channel_id=1, source_target_pairs={{0,16},{16,0},{1,17},{17,1},{2,18},{18,2},{3,19},{19,3},{4,20},{20... | collective-permute-start | bytes 21512 | tf_op jit(solution)/shard_map/ppermute | solution.py:109
  4.4 12.6 %copy-start = (bf16[128,3584]{1,0:T(8,128)(2,1)S(1)}, bf16[128,3584]{1,0:T(8,128)(2,1)}, u32[]{:S(2)}) copy-start(bf16[128,3584]{1,0:T(8,128)(2,1)} %param.9) | copy-start | bytes 2752516
  5.6 12.5 %copy-start.4 = (s32[1,4]{1,0:T(1,128)S(1)}, s32[1,4]{1,0:T(1,128)}, u32[]{:S(2)}) copy-start(s32[1,4]{1,0:T(1,128)} %param.14) | copy-start | bytes 52
  5.6 12.7 %copy-start.3 = (s32[1,16]{1,0:T(1,128)S(1)}, s32[1,16]{1,0:T(1,128)}, u32[]{:S(2)}) copy-start(s32[1,16]{1,0:T(1,128)} %param.15) | copy-start | bytes 196
  5.6 12.9 %copy-start.2 = (bf16[128,512]{1,0:T(8,128)(2,1)S(1)}, bf16[128,512]{1,0:T(8,128)(2,1)}, u32[]{:S(2)}) copy-start(bf16[128,512]{1,0:T(8,128)(2,1)} %param.11) | copy-start | bytes 393220
  5.6 44.4 %all-to-all-start = ((bf16[16,160,256]{2,1,0:T(8,128)(2,1)}), bf16[16,160,256]{2,1,0:T(8,128)(2,1)S(1)}, u32[]{:S(2)}, u32[]{:S(2)}) async-start(bf16[16,160,256]{2,1,0:T(8,128)(2,1)} %broadcast_in_dim.89), calls=%async_computation | async-start | bytes 2621440 | tf_op jit(solution)/shard_map/all_to_all | solution.py:95
  18.1 43.1 %collective-permute-start.1 = (bf16[128,3584]{1,0:T(8,128)(2,1)}, bf16[128,3584]{1,0:T(8,128)(2,1)}, u32[]{:S(2)}, u32[]{:S(2)}) collective-permute-start(bf16[128,3584]{1,0:T(8,128)(2,1)} %fusion.19), channel_id=1, source_target_pairs={{0,16},{16,0},{1,17},{17,1},{2,18},{18,2},{3,19},{19,3},{4,20},{20... | collective-permute-start | bytes 2752520 | tf_op jit(solution)/shard_map/ppermute | solution.py:121
  51.5 28.3 %all-to-all-start.1 = ((bf16[8,448,256]{2,1,0:T(8,128)(2,1)}), bf16[8,448,256]{2,1,0:T(8,128)(2,1)}, u32[]{:S(2)}, u32[]{:S(2)}) async-start(bf16[8,448,256]{2,1,0:T(8,128)(2,1)} %broadcast_in_dim.90), calls=%async_computation.1 | async-start | bytes 3670016 | tf_op jit(solution)/shard_map/all_to_all | solution.py:95
  61.1 24.7 %copy-start.1 = (bf16[128,512]{1,0:T(8,128)(2,1)}, bf16[128,512]{1,0:T(8,128)(2,1)S(1)}, u32[]{:S(2)}) copy-start(bf16[128,512]{1,0:T(8,128)(2,1)S(1)} %copy.22) | copy-start | bytes 393220
  61.1 1.3 collective-permute-start.2

commit v2 on v1

v2 whole, which is shorter than its diff:
```python
import math

import jax
import jax.numpy as jnp
from jax import lax
from jax.sharding import Mesh, PartitionSpec as P

HD = 128
HQ = 4
BLK = 128
DS = 3584
COLS = HQ * HD
HALF = COLS // 2
TOKENS_ALL = 32768

EPSILON = 1e-06
NEGATIVE = -1e30

AXES = ("ylo", "x", "core", "z", "yhi")
SIZES = (2, 4, 2, 8, 2)
SEQ = ("z", "yhi")
SWAP = ((0, 1), (1, 0))


def locate(assign_row, doc_ends, block_ids):
    block_table = jnp.arange(assign_row.shape[0], dtype=jnp.int32)
    placed = jnp.sum(
        jnp.where(block_ids[:, None] == block_table[None, :], assign_row[None, :], 0), axis=1
    )
    position = (placed[:, None] * BLK + jnp.arange(BLK, dtype=jnp.int32)[None, :]).reshape(-1)
    document = jnp.sum((position[:, None] >= doc_ends[None, :]).astype(jnp.int32), axis=1)
    return (position, document)


def absorb_block(state, key_block, value_block, query_heads, allowed):
    run_max, run_total, run_acc = state
    scores = jnp.einsum(
        "qhd,kd->hqk", query_heads, key_block, preferred_element_type=jnp.float32
    ) * HD ** (-0.5)
    masked = jnp.where(allowed[None], scores, NEGATIVE)
    new_max = jnp.maximum(run_max, jnp.max(masked, axis=-1))
    fading = jnp.exp(run_max - new_max)
    exp_terms = jnp.where(allowed[None], jnp.exp(masked - new_max[:, :, None]), 0.0)
    new_total = run_total * fading + jnp.sum(exp_terms, axis=-1)
    mixture = jnp.einsum(
        "hqk,kd->qhd",
        exp_terms.astype(jnp.bfloat16),
        value_block,
        preferred_element_type=jnp.float32,
    )
    new_acc = run_acc * fading.T[:, :, None] + mixture
    return (new_max, new_total, new_acc)


def attend(queries, key_piece, value_piece, block_ids, lengths, assignment):
    rows = queries.shape[0]
    assign_row = assignment[0]
    doc_ends = jnp.cumsum(lengths[0])
    query_pos, query_doc = locate(assign_row, doc_ends, lax.axis_index(SEQ)[None])
    query_heads = queries.reshape(rows, HQ, HD)
    start_state = (
        jnp.full((HQ, rows), NEGATIVE, jnp.float32),
        jnp.zeros((HQ, rows), jnp.float32),
        jnp.zeros((rows, HQ, HD), jnp.float32),
    )
    count = key_piece.shape[0]
    step_rows = math.gcd(count, 512)
    steps_count = count // step_rows
    key_pos, key_doc = locate(assign_row, doc_ends, block_ids)

    def one_step(running, slabs):
        key_block, value_block, key_position, key_document = slabs
        allowed = (query_doc[:, None] == key_document[None, :]) & (
            query_pos[:, None] >= key_position[None, :]
        )
        return (absorb_block(running, key_block, value_block, query_heads, allowed), None)

    slabs = (
        key_piece.reshape(steps_count, step_rows, HD),
        value_piece.reshape(steps_count, step_rows, HD),
        key_pos.reshape(steps_count, step_rows),
        key_doc.reshape(steps_count, step_rows),
    )
    result, _ = lax.scan(one_step, start_state, slabs)
    _, final_total, final_acc = result
    return (final_acc / final_total.T[:, :, None]).reshape(rows, COLS).astype(jnp.bfloat16)


def to_everyone(x, axes):
    size = math.prod(SIZES[AXES.index(a)] for a in axes)
    copies = jnp.broadcast_to(x, (size, *x.shape))
    return lax.all_to_all(copies, axes, split_axis=0, concat_axis=0, tiled=True)


def halves(x, which):
    half = x.shape[1] // 2
    low, high = x[:, :half], x[:, half:]
    return jnp.where(which == 0, low, high), jnp.where(which == 0, high, low)


def from_z(x, distance):
    return lax.ppermute(x, "z", [((i + distance) % 8, i) for i in range(8)])


def local(student_in, weight, queries, keys, values, lengths, assignment):
    rows = queries.shape[0]
    core = lax.axis_index("core")
    ylo = lax.axis_index("ylo")
    wrows = weight.shape[0]

    w_mine, w_other = halves(weight, core)
    w_got = lax.ppermute(w_other, "core", SWAP)
    kv = jnp.concatenate([keys, values], axis=1)
    kv_pair = jnp.concatenate([kv, lax.ppermute(kv, "yhi", SWAP)], axis=0)

    w_first = jnp.where(core == 0, w_mine, w_got)
    w_second = jnp.where(core == 0, w_got, w_mine)
    pad = jnp.zeros((16 - wrows, HALF), jnp.bfloat16)
    arrived = to_everyone(jnp.concatenate([w_first, pad, w_second, pad], axis=0), SEQ)

    as_float = student_in.astype(jnp.float32)
    normed = (
        as_float * lax.rsqrt(jnp.mean(as_float * as_float, axis=1, keepdims=True) + EPSILON)
    ).astype(jnp.bfloat16)
    n_keep, n_send = halves(normed, ylo)
    n_pair = jnp.concatenate([n_keep, lax.ppermute(n_send, "ylo", SWAP)], axis=0)
    n_all = jnp.concatenate([n_pair, lax.ppermute(n_pair, "core", SWAP)], axis=0)

    w_near = jnp.concatenate(
        [
            arrived[:, :wrows].reshape(-1, HALF),
            arrived[:, 16 : 16 + wrows].reshape(-1, HALF),
        ],
        axis=0,
    )
    w_near, n_all = lax.optimization_barrier((w_near, n_all))
    w_all = to_everyone(w_near, ("x",)).reshape(DS // 2, HALF)

    got = {d: from_z(kv_pair, d) for d in (3, -3, 2, -2, 1, -1)}
    got[0] = kv_pair
    got[4] = from_z(got[3], 1)
    order = sorted(got)
    pieces = lax.optimization_barrier(([got[d] for d in order], w_near))[0]
    kv_all = jnp.concatenate(pieces, axis=0)
    zs = (lax.axis_index("z") + jnp.array(order, jnp.int32)) % 8
    yhi = lax.axis_index("yhi")
    block_ids = (zs[:, None] * 2 + jnp.stack([yhi, 1 - yhi])[None, :]).reshape(-1)

    attention = attend(queries, kv_all[:, :HD], kv_all[:, HD:], block_ids, lengths, assignment)
    a_mine, a_other = halves(attention, core)
    a_got = lax.ppermute(a_other, "core", SWAP)

    partial = jnp.dot(n_all, w_all, preferred_element_type=jnp.float32)
    partial = partial.reshape(2, 2, rows, HALF)
    mine = partial[:, 0] - jnp.stack([a_mine, a_got]).astype(jnp.float32)
    theirs = partial[:, 1]
    back = lax.ppermute(jnp.stack([mine, theirs], axis=1).astype(jnp.bfloat16), "ylo", SWAP)
    back = back.astype(jnp.float32)
    diff = jnp.stack([mine + back[:, 1], theirs + back[:, 0]], axis=1)
    scaled = (diff * TOKENS_ALL ** (-0.5)).astype(jnp.bfloat16).reshape(4 * rows, HALF)
    part = lax.dot_general(
        n_all, scaled, (((0,), (0,)), ((), ())), preferred_element_type=jnp.float32
    ).astype(jnp.bfloat16)
    part = jnp.pad(part.reshape(-1, wrows, HALF), ((0, 0), (0, 16 - wrows), (0, 0)))
    last = lax.all_to_all(part, ("x", "core", *SEQ), split_axis=0, concat_axis=0, tiled=True)
    summed = last.reshape(4, 2, 16, 16, HALF).astype(jnp.float32).sum(axis=(0, 2))
    weight_grad = jnp.concatenate([summed[0, :wrows], summed[1, :wrows]], axis=1)
    return (attention, weight_grad)


def solution(mesh):
    mesh = Mesh(mesh.devices.reshape(SIZES), AXES)
    token = P(AXES, None)
    row = P(("ylo", "x", "core"), None)
    return jax.shard_map(
        local,
        mesh=mesh,
        in_specs=(token, token, token, token, token, row, row),
        out_specs=(token, token),
        check_vma=False,
    )
```

time: 136 us -> 132 us (0.971)
  the two profiles are of different devices: /device:TPU:32 before, /device:TPU:1 now
where the time goes in v2:
time: 132 us
  blocking collectives  45.5 us (34%)
  starting transfers between devices  33.3 us (25%)
  waiting for transfers between devices  17.6 us (13%)
  local copies, waits for them, and re-layouts  14.4 us (11%)
  other arithmetic  13.3 us (10%)
  matrix products  5.56 us (4%)
  between operations  1.69 us (1%)
    all_to_all x1, blocking collectives, local(): lax.all_to_all(part, ('x', 'core', *SEQ), split_axis=0, concat_axis=0, ti...  45.5 us
    all_to_all x2, starting transfers between devices, to_everyone(): return lax.all_to_all(copies, axes, split_axis=0, concat_axis=0, tiled=True)  12.4 us
    ppermute x7, waiting for transfers between devices, from_z(): return lax.ppermute(x, 'z', [((i + distance) % 8, i) for i in range(8)])  11.7 us
    ppermute x7, starting transfers between devices, from_z(): return lax.ppermute(x, 'z', [((i + distance) % 8, i) for i in range(8)])  11.6 us
    unnamed x33, local copies, waits for them, and re-layouts  5.3 us
    ppermute x1, waiting for transfers between devices, local(): lax.ppermute(jnp.stack([mine, theirs], axis=1).astype(jnp.bfloat16), 'ylo...  5.05 us
    ppermute x1, starting transfers between devices, local(): w_got = lax.ppermute(w_other, 'core', SWAP)  3.24 us
    dynamic_slice x4, local copies, waits for them, and re-layouts, attend(): result, _ = lax.scan(one_step, start_state, slabs)  2.83 us
  transfers between devices with their start and end apart: 15, of which 7 were waited for; matrix products, arithmetic and copies ran while one was open for 19% of the time, Pallas kernels for 0%

profile of v2, /device:TPU:1, one launch (start us, length us, event | category | flops | bytes accessed | tf_op | source)
XLA Modules:
  0.0 131.5 jit_solution(17420417350684662746)
XLA Ops:
  0.6 0.7 broadcast_select_fusion.5
  1.4 3.2 %collective-permute-start.8 = (bf16[14,256]{1,0:T(8,128)(2,1)S(1)}, bf16[14,256]{1,0:T(8,128)(2,1)S(1)}, u32[]{:S(2)}, u32[]{:S(2)}) collective-permute-start(bf16[14,256]{1,0:T(8,128)(2,1)S(1)} %broadcast_select_fusion.5), channel_id=1, source_target_pairs={{0,16},{16,0},{1,17},{17,1},{2,18},{18,2},{3,19},{19,3},{4,20},{20... | collective-permute-start | bytes 21512 | tf_op jit(solution)/shard_map/ppermute | solution.py:112
  4.6 1.4 %fusion.20 = f32[128]{0:T(128)S(1)} fusion(bf16[128,3584]{1,0:T(8,128)(2,1)} %param.10), kind=kLoop, calls=%fused_computation.33 | loop fusion | flops 1376128 | bytes 918016 | tf_op jit(solution)/shard_map/reduce_sum | solution.py:123
  6.1 1.4 %fusion.21 = bf16[128,3584]{1,0:T(8,128)(2,1)S(1)} fusion(bf16[128,3584]{1,0:T(8,128)(2,1)} %param.10, f32[128]{0:T(128)S(1)} %add_rsqrt_fusion), kind=kLoop, calls=%fused_computation.34 | loop fusion | flops 1376256 | bytes 1835520 | tf_op jit(solution)/shard_map/convert_element_type | solution.py:124
  7.8 0.6 constant_dynamic-update-slice_fusion.1
  8.4 0.6 constant_dynamic-update-slice_fusion
  9.0 2.2 %collective-permute-start = (bf16[128,256]{1,0:T(8,128)(2,1)}, bf16[128,256]{1,0:T(8,128)(2,1)}, u32[]{:S(2)}, u32[]{:S(2)}) collective-permute-start(bf16[128,256]{1,0:T(8,128)(2,1)} %constant_dynamic-update-slice_fusion), channel_id=1, source_target_pairs={{0,1},{1,0},{2,3},{3,2},{4,5},{5,4},{6,7},{7,6},{8,9},{9,8},{10,11... | collective-permute-start | bytes 196616 | tf_op jit(solution)/shard_map/ppermute | solution.py:114
  11.9 0.7 broadcast_bitcast_fusion
  12.7 0.6 fusion.26
  13.3 0.6 iota_bitcast_fusion
  14.6 0.7 broadcast_in_dim.81
  15.4 8.4 %all-to-all-start = ((bf16[16,32,256]{2,1,0:T(8,128)(2,1)}), bf16[16,32,256]{2,1,0:T(8,128)(2,1)S(1)}, u32[]{:S(2)}, u32[]{:S(2)}) async-start(bf16[16,32,256]{2,1,0:T(8,128)(2,1)} %broadcast_in_dim.81), calls=%async_computation | async-start | bytes 524288 | tf_op jit(solution)/shard_map/all_to_all | solution.py:92
  23.8 0.9 collective-permute-start.10
  24.7 0.5 iota_add_fusion
  25.6 1.3 bitcast_add_fusion
  26.9 1.3 convert_reduce_fusion.2
  28.1 0.9 pad_maximum_fusion.4
  29.0 4.7 %collective-permute-start.6 = (bf16[256,256]{1,0:T(8,128)(2,1)S(1)}, bf16[256,256]{1,0:T(8,128)(2,1)}, u32[]{:S(2)}, u32[]{:S(2)}) collective-permute-start(bf16[256,256]{1,0:T(8,128)(2,1)S(1)} %pad_maximum_fusion.4), channel_id=1, source_target_pairs={{6,0},{8,2},{10,4},{12,6},{14,8},{0,10},{2,12},{4,14},{7,1},{9,3},... | collective-permute-start | bytes 393224 | tf_op jit(solution)/shard_map/ppermute | solution.py:102
  33.7 2.4 %collective-permute-start.2 = (bf16[256,256]{1,0:T(8,128)(2,1)S(1)}, bf16[256,256]{1,0:T(8,128)(2,1)}, u32[]{:S(2)}, u32[]{:S(2)}) collective-permute-start(bf16[256,256]{1,0:T(8,128)(2,1)S(1)} %pad_maximum_fusion.4), channel_id=1, source_target_pairs={{12,0},{14,2},{0,4},{2,6},{4,8},{6,10},{8,12},{10,14},{13,1},{15,3... | collective-permute-start | bytes 393224 | tf_op jit(solution)/shard_map/ppermute | solution.py:102
  36.1 1.2 collective-permute-start.3
  37.3 0.7 fusion.29
  38.0 0.9 reshape.244
  38.9 0.9 reshape.245
  39.9 2.5 %collective-permute-done.6 = bf16[256,256]{1,0:T(8,128)(2,1)} collective-permute-done((bf16[256,256]{1,0:T(8,128)(2,1)S(1)}, bf16[256,256]{1,0:T(8,128)(2,1)}, u32[]{:S(2)}, u32[]{:S(2)}) %collective-permute-start.6) | collective-permute-done | bytes 131104 | tf_op jit(solution)/shard_map/ppermute | solution.py:102
  42.4 2.6 %collective-permute-start.4 = (bf16[256,256]{1,0:T(8,128)(2,1)S(1)}, bf16[256,256]{1,0:T(8,128)(2,1)S(1)}, u32[]{:S(2)}, u32[]{:S(2)}) collective-permute-start(bf16[256,256]{1,0:T(8,128)(2,1)S(1)} %pad_maximum_fusion.4), channel_id=1, source_target_pairs={{2,0},{4,2},{6,4},{8,6},{10,8},{12,10},{14,12},{0,14},{3,1},{5,3},... | collective-permute-start | bytes 393224 | tf_op jit(solution)/shard_map/ppermute | solution.py:102
  45.0 3.3 %collective-permute-done.1 = bf16[256,256]{1,0:T(8,128)(2,1)} collective-permute-done((bf16[256,256]{1,0:T(8,128)(2,1)S(1)}, bf16[256,256]{1,0:T(8,128)(2,1)}, u32[]{:S(2)}, u32[]{:S(2)}) %collective-permute-start.1) | collective-permute-done | bytes 131104 | tf_op jit(solution)/shard_map/ppermute | solution.py:102
  48.4 0.7 collective-permute-start.7
  49.1 1.4 %pad_maximum_fusion = bf16[512,1792]{1,0:T(8,128)(2,1)} fusion(bf16[256,1792]{1,0:T(8,128)(2,1)S(1)} %collective-permute-done.10, bf16[128,1792]{1,0:T(8,128)(2,1)S(1)} %collective-permute-done.9, bf16[128,1792]{1,0:T(8,128)(2,1)S(1)} %get-tuple-element.175), kind=kLoop, calls=%fused_computation.35 | loop fusion | flops 5505024 | bytes 3670016 | tf_op jit(solution)/shard_map/concatenate | solution.py:127
  50.4 3.5 %collective-permute-done.3 = bf16[256,256]{1,0:T(8,128)(2,1)} collective-permute-done((bf16[256,256]{1,0:T(8,128)(2,1)S(1)}, bf16[256,256]{1,0:T(8,128)(2,1)}, u32[]{:S(2)}, u32[]{:S(2)}) %collective-permute-start.3) | collective-permute-done | bytes 131104 | tf_op jit(solution)/shard_map/ppermute | solution.py:102
  53.9 1.6 %collective-permute-done.5 = bf16[256,256]{1,0:T(8,128)(2,1)S(1)} collective-permute-done((bf16[256,256]{1,0:T(8,128)(2,1)S(1)}, bf16[256,256]{1,0:T(8,128)(2,1)S(1)}, u32[]{:S(2)}, u32[]{:S(2)}) %collective-permute-start.5) | collective-permute-done | bytes 131104 | tf_op jit(solution)/shard_map/ppermute | solution.py:102
  55.5 0.8 collective-permute-done.7
  56.3 0.9 constant_dynamic-update-slice_fusion.9
  57.2 0.9 constant_dynamic-update-slice_fusion.8
  58.1 0.9 constant_dynamic-update-slice_fusion.7
  59.1 0.9 constant_dynamic-update-slice_fusion.3
  60.1 1.0 broadcast_in_dim.82
  61.1 4.0 %all-to-all-start.1 = ((bf16[4,448,256]{2,1,0:T(8,128)(2,1)}), bf16[4,448,256]{2,1,0:T(8,128)(2,1)S(1)}, u32[]{:S(2)}, u32[]{:S(2)}) async-start(bf16[4,448,256]{2,1,0:T(8,128)(2,1)} %broadcast_in_dim.82), calls=%async_computation.1 | async-start | bytes 1835008 | tf_op jit(solution)/shard_map/all_to_all | solution.py:92
  65.1 7.6 %while.15 = (s32[]{:T(128)}, f32[4,128]{1,0:T(4,128)S(1)}, f32[4,128]{1,0:T(4,128)S(1)}, f32[128,4,128]{0,2,1:T(8,128)S(1)}, s32[128]{0:T(128)S(1)}, /*index=5*/...) while((s32[]{:T(128)}, f32[4,128]{1,0:T(4,128)S(1)}, ...), condition=%wide.region_9.10_spmd.clone, body=%wide.region_6.9_spmd.clone.sunk | while | flops 136973440 | bytes 4372121 | solution.py:84
  65.1 0.7 constant_dynamic-slice_fusion.3
  66.1 0.3 fusion.47
  66.4 0.4 fusion.51
  66.8 0.2 fusion.49
  67.0 0.7 constant_dynamic-slice_fusion.3
  67.7 0.2 compare_and_fusion.2
  67.9 0.3 fusion.47
  68.3 0.4 fusion.51
  68.7 0.2 fusion.49
  68.9 0.7 constant_dynamic-slice_fusion.3
  69.8 0.3 fusion.47
  70.2 0.4 fusion.51
  70.6 0.2 fusion.49
  70.8 0.7 constant_dynamic-slice_fusion.3
  71.7 0.3 fusion.47
  72.1 0.4 fusion.51
  72.4 0.2 fusion.49
  72.9 2.5 %collective-permute-start.11 = (bf16[128,256]{1,0:T(8,128)(2,1)S(1)}, bf16[128,256]{1,0:T(8,128)(2,1)S(1)}, u32[]{:S(2)}, u32[]{:S(2)}) collective-permute-start(bf16[128,256]{1,0:T(8,128)(2,1)S(1)} %get-tuple-element.180), channel_id=1, source_target_pairs={{0,16},{16,0},{1,17},{17,1},{2,18},{18,2},{3,19},{19,3},{4,20},{20... | collective-permute-start | bytes 196616 | tf_op jit(solution)/shard_map/ppermute | solution.py:151
  75.4 0.8 all-to-all-done.1
  76.2 2.1 %fusion.30 = f32[2,2,128,256]{3,2,1,0:T(8,128)S(1)} fusion(bf16[2,2,128,1792]{3,2,1,0:T(8,128)(2,1)} %bitcast.83, bf16[1792,256,1,1]{1,0,3,2:T(8,128)(2,1)S(1)} %bitcast.84), kind=kOutput, calls=%fused_computation.94 | convolution fusion | flops 469762048 | bytes 3276800 | tf_op jit(solution)/shard_map/dot_general | solution.py:153
  78.4 0.4 collective-permute-start.12
  78.9 5.1 %collective-permute-done.12 = bf16[2,2,128,256]{3,2,1,0:T(8,128)(2,1)S(1)} collective-permute-done((bf16[2,2,128,256]{3,2,1,0:T(8,128)(2,1)S(1)}, bf16[2,2,128,256]{3,2,1,0:T(8,128)(2,1)S(1)}, u32[]{:S(2)}, u32[]{:S(2)}) %collective-permute-start.12) | collective-permute-done | bytes 262176 | tf_op jit(solution)/shard_map/ppermute | solution.py:157
  84.1 0.7 convolution_convert_fusion
  84.8 0.3 reshape.250
  85.2 45.5 %all_to_all.15 = bf16[128,16,256]{2,1,0:T(8,128)(2,1)S(1)} all-to-all(bf16[128,16,256]{2,1,0:T(8,128)(2,1)S(1)} %pad.4), channel_id=1, replica_groups=mesh['ylo'=2,'x'=4,'core'=2,'z'=8,'yhi'=2] {'x','core','z','yhi'}, dimensions={0} | all-to-all | bytes 2097152 | tf_op jit(solution)/shard_map/all_to_all | solution.py:165
  130.9 0.6 pad_maximum_fusion.6
  (92 shorter events, 3.0 us)
Async XLA Ops:
  1.4 13.2 %collective-permute-start.8 = (bf16[14,256]{1,0:T(8,128)(2,1)S(1)}, bf16[14,256]{1,0:T(8,128)(2,1)S(1)}, u32[]{:S(2)}, u32[]{:S(2)}) collective-permute-start(bf16[14,256]{1,0:T(8,128)(2,1)S(1)} %broadcast_select_fusion.5), channel_id=1, source_target_pairs={{0,16},{16,0},{1,17},{17,1},{2,18},{18,2},{3,19},{19,3},{4,20},{20... | collective-permute-start | bytes 21512 | tf_op jit(solution)/shard_map/ppermute | solution.py:112
  6.1 1.7 %copy-start.4 = (bf16[128,128]{1,0:T(8,128)(2,1)S(1)}, bf16[128,128]{1,0:T(8,128)(2,1)}, u32[]{:S(2)}) copy-start(bf16[128,128]{1,0:T(8,128)(2,1)} %param.13) | copy-start | bytes 98308
  6.1 2.3 %copy-start.5 = (bf16[128,128]{1,0:T(8,128)(2,1)S(1)}, bf16[128,128]{1,0:T(8,128)(2,1)}, u32[]{:S(2)}) copy-start(bf16[128,128]{1,0:T(8,128)(2,1)} %param.14) | copy-start | bytes 98308
  6.1 5.2 %copy-start.10 = (s32[8]{0:T(128)S(1)}, s32[8]{0:T(128)}, u32[]{:S(2)}) copy-start(s32[8]{0:T(128)} %constant.80.clone) | copy-start | bytes 100
  6.1 5.3 %copy-start.9 = (s32[1,16]{1,0:T(1,128)S(1)}, s32[1,16]{1,0:T(1,128)}, u32[]{:S(2)}) copy-start(s32[1,16]{1,0:T(1,128)} %param.16) | copy-start | bytes 196
  6.1 5.6 %copy-start.8 = (s32[1,4]{1,0:T(1,128)S(1)}, s32[1,4]{1,0:T(1,128)}, u32[]{:S(2)}) copy-start(s32[1,4]{1,0:T(1,128)} %param.15) | copy-start | bytes 52
  6.1 8.5 %copy-start.3 = (bf16[14,512]{1,0:T(8,128)(2,1)S(1)}, bf16[14,512]{1,0:T(8,128)(2,1)}, u32[]{:S(2)}) copy-start(bf16[14,512]{1,0:T(8,128)(2,1)} %param.11) | copy-start | bytes 43012
  7.6 17.7 %copy-start.2 = (bf16[128,512]{1,0:T(8,128)(2,1)S(1)}, bf16[128,512]{1,0:T(8,128)(2,1)}, u32[]{:S(2)}) copy-start(bf16[128,512]{1,0:T(8,128)(2,1)} %param.12) | copy-start | bytes 393220
  7.6 16.1 %collective-permute-start.9 = (bf16[128,1792]{1,0:T(8,128)(2,1)S(1)}, bf16[128,1792]{1,0:T(8,128)(2,1)S(1)}, u32[]{:S(2)}, u32[]{:S(2)}) collective-permute-start(bf16[128,1792]{1,0:T(8,128)(2,1)S(1)} %get-tuple-element.176), channel_id=1, source_target_pairs={{0,128},{128,0},{1,129},{129,1},{2,130},{130,2},{3,131},{131,3},{4... | collective-permute-start | bytes 1376264 | tf_op jit(solution)/shard_map/ppermute | solution.py:126
  9.0 19.1 %collective-permute-start = (bf16[128,256]{1,0:T(8,128)(2,1)}, bf16[128,256]{1,0:T(8,128)(2,1)}, u32[]{:S(2)}, u32[]{:S(2)}) collective-permute-start(bf16[128,256]{1,0:T(8,128)(2,1)} %constant_dynamic-update-slice_fusion), channel_id=1, source_target_pairs={{0,1},{1,0},{2,3},{3,2},{4,5},{5,4},{6,7},{7,6},{8,9},{9,8},{10,11... | collective-permute-start | bytes 196616 | tf_op jit(solution)/shard_map/ppermute | solution.py:114
  11.9 2.6 %copy-start.7 = (s32[4,1]{0,1:T(1,128)}, s32[4,1]{0,1:T(1,128)S(1)}, u32[]{:S(2)}) copy-start(s32[4,1]{0,1:T(1,128)S(1)} %reduce-window.8) | copy-start | bytes 52
  15.4 21.9 %all-to-all-start = ((bf16[16,32,256]{2,1,0:T(8,128)(2,1)}), bf16[16,32,256]{2,1,0:T(8,128)(2,1)S(1)}, u32[]{:S(2)}, u32[]{:S(2)}) async-start(bf16[16,32,256]{2,1,0:T(8,128)(2,1)} %broadcast_in_dim.81), calls=%async_computation | async-start | bytes 524288 | tf_op jit(solution)/shard_map/all_to_all | solution.py:92
  23.8 24.6 %collective-permute-start.10 = (bf16[256,1792]{1,0:T(8,128)(2,1)S(1)}, bf16[256,1792]{1,0:T(8,128)(2,1)S(1)}, u32[]{:S(2)}, u32[]{:S(2)}) collective-permute-start(bf16[256,1792]{1,0:T(8,128)(2,1)S(1)} %pad_maximum_fusion.1), channel_id=1, source_target_pairs={{0,16},{16,0},{1,17},{17,1},{2,18},{18,2},{3,19},{19,3},{4,20},{20... | collective-permute-start | bytes 2752520 | tf_op jit(solution)/shard_map/ppermute | solution.py:127
  29.0 13.4 %collective-permute-start.6 = (bf16[256,256]{1,0:T(8,128)(2,1)S(1)}, bf16[256,256]{1,0:T(8,128)(2,1)}, u32[]{:S(2)}, u32[]{:S(2)}) collective-permute-start(bf16[256,256]{1,0:T(8,128)(2,1)S(1)} %pad_maximum_fusion.4), channel_id=1, source_target_pairs={{6,0},{8,2},{10,4},{12,6},{14,8},{0,10},{2,12},{4,14},{7,1},{9,3},... | collective-permute-start | bytes 393224 | tf_op jit(solution)/shard_map/ppermute | solution.py:102
  33.7 14.6 %collective-permute-start.1 = (bf16[256,256]{1,0:T(8,128)(2,1)S(1)}, bf16[256,256]{1,0:T(8,128)(2,1)}, u32[]{:S(2)}, u32[]{:S(2)}) collective-permute-start(bf16[256,256]{1,0:T(8,128)(2,1)S(1)} %pad_maximum_fusion.4), channel_id=1, source_target_pairs={{10,0},{12,2},{14,4},{0,6},{2,8},{4,10},{6,12},{8,14},{11,1},{13,3... | collective-permute-start | bytes 393224 | tf_op jit(solution)/shard_map/ppermute | solution.py:102
  33.7 16.7 %collective-permute-start.2 = (bf16[256,256]{1,0:T(8,128)(2,1)S(1)}, bf16[256,256]{1,0:T(8,128)(2,1)}, u32[]{:S(2)}, u32[]{:S(2)}) collective-permute-start(bf16[256,256]{1,0:T(8,128)(2,1)S(1)} %pad_maximum_fusion.4), channel_id=1, source_target_pairs={{12,0},{14,2},{0,4},{2,6},{4,8},{6,10},{8,12},{10,14},{13,1},{15,3... | collective-permute-start | bytes 393224 | tf_op jit(solution)/shard_map/ppermute | solution.py:102
  36.1 17.8 %collective-permute-start.3 = (bf16[256,256]{1,0:T(8,128)(2,1)S(1)}, bf16[256,256]{1,0:T(8,128)(2,1)}, u32[]{:S(2)}, u32[]{:S(2)}) collective-permute-start(bf16[256,256]{1,0:T(8,128)(2,1)S(1)} %pad_maximum_fusion.4), channel_id=1, source_target_pairs={{14,0},{0,2},{2,4},{4,6},{6,8},{8,10},{10,12},{12,14},{15,1},{1,3}... | collective-permute-start | bytes 393224 | tf_op jit(solution)/shard_map/ppermute | solution.py:102
  42.4 11.5 %collective-permute-start.4 = (bf16[256,256]{1,0:T(8,128)(2,1)S(1)}, bf16[256,256]{1,0:T(8,128)(2,1)S(1)}, u32[]{:S(2)}, u32[]{:S(2)}) collective-permute-start(bf16[256,256]{1,0:T(8,128)(2,1)S(1)} %pad_maximum_fusion.4), channel_id=1, source_target_pairs={{2,0},{4,2},{6,4},{8,6},{10,8},{12,10},{14,12},{0,14},{3,1},{5,3},... | collective-permute-start | bytes 393224 | tf_op jit(solution)/shard_map/ppermute | solution.py:102
  48.4 7.1 %collective-permute-start.5 = (bf16[256,256]{1,0:T(8,128)(2,1)S(1)}, bf16[256,256]{1,0:T(8,128)(2,1)S(1)}, u32[]{:S(2)}, u32[]{:S(2)}) collective-permute-start(bf16[256,256]{1,0:T(8,128)(2,1)S(1)} %pad_maximum_fusion.4), channel_id=1, source_target_pairs={{4,0},{6,2},{8,4},{10,6},{12,8},{14,10},{0,12},{2,14},{5,1},{7,3},... | collective-permute-start | bytes 393224 | tf_op jit(solution)/shard_map/ppermute | solution.py:102
  48.4 7.9 %collective-permute-start.7 = (bf16[256,256]{1,0:T(8,128)(2,1)}, bf16[256,256]{1,0:T(8,128)(2,1)S(1)}, u32[]{:S(2)}, u32[]{:S(2)}) collective-permute-start(bf16[256,256]{1,0:T(8,128)(2,1)} %collective-permute-done.6), channel_id=1, source_target_pairs={{2,0},{4,2},{6,4},{8,6},{10,8},{12,10},{14,12},{0,14},{3,1},{5,3},... | collective-permute-start | bytes 393224 | tf_op jit(solution)/shard_map/ppermute | solution.py:102
  60.1 5.0 %copy-start.6 = (s32[128]{0:T(128)S(1)}, s32[128]{0:T(128)}, u32[]{:S(2)}) copy-start(s32[128]{0:T(128)} %convert_reduce_fusion.2) | copy-start | bytes 1540
  61.1 15.1 %all-to-all-start.1 = ((bf16[4,448,256]{2,1,0:T(8,128)(2,1)}), bf16[4,448,256]{2,1,0:T(8,128)(2,1)S(1)}, u32[]{:S(2)}, u32[]{:S(2)}) async-start(bf16[4,448,256]{2,1,0:T(8,128)(2,1)} %broadcast_in_dim.82), calls=%async_computation.1 | async-start | bytes 1835008 | tf_op jit(solution)/shard_map/all_to_all | solution.py:92
  72.8 5.5 %copy-start.1 = (bf16[128,512]{1,0:T(8,128)(2,1)}, bf16[128,512]{1,0:T(8,128)(2,1)S(1)}, u32[]{:S(2)}) copy-start(bf16[128,512]{1,0:T(8,128)(2,1)S(1)} %copy.24) | copy-start | bytes 393220
  72.9 5.5 %collective-permute-start.11 = (bf16[128,256]{1,0:T(8,128)(2,1)S(1)}, bf16[128,256]{1,0:T(8,128)(2,1)S(1)}, u32[]{:S(2)}, u32[]{:S(2)}) collective-permute-start(bf16[128,256]{1,0:T(8,128)(2,1)S(1)} %get-tuple-element.180), channel_id=1, source_target_pairs={{0,16},{16,0},{1,17},{17,1},{2,18},{18,2},{3,19},{19,3},{4,20},{20... | collective-permute-start | bytes 196616 | tf_op jit(solution)/shard_map/ppermute | solution.py:151
  78.4 5.7 %copy-start = (bf16[512,1792]{1,0:T(8,128)(2,1)S(1)}, bf16[512,1792]{1,0:T(8,128)(2,1)}, u32[]{:S(2)}) copy-start(bf16[512,1792]{1,0:T(8,128)(2,1)} %pad_maximum_fusion) | copy-start | bytes 5505028
  78.4 5.5 %collective-permute-start.12 = (bf16[2,2,128,256]{3,2,1,0:T(8,128)(2,1)S(1)}, bf16[2,2,128,256]{3,2,1,0:T(8,128)(2,1)S(1)}, u32[]{:S(2)}, u32[]{:S(2)}) collective-permute-start(bf16[2,2,128,256]{3,2,1,0:T(8,128)(2,1)S(1)} %pad_maximum_fusion.2), channel_id=1, source_target_pairs={{0,128},{128,0},{1,129},{129,1},{2,130},{130,2},{3,131},{131,3},{4... | collective-permute-start | bytes 786440 | tf_op jit(solution)/shard_map/ppermute | solution.py:157

commit v3 on v2

v3 whole, which is shorter than its diff:
```python
import math

import jax
import jax.numpy as jnp
from jax import lax
from jax.experimental import pallas as pl
from jax.experimental.pallas import tpu as pltpu
from jax.sharding import Mesh, PartitionSpec as P

HD = 128
HQ = 4
BLK = 128
DS = 3584
COLS = HQ * HD
HALF = COLS // 2
TOKENS_ALL = 32768

EPSILON = 1e-06
NEGATIVE = -1e30
LOG2E = math.log2(math.e)

AXES = ("ylo", "x", "core", "z", "yhi")
SIZES = (2, 4, 2, 8, 2)
SEQ = ("z", "yhi")
SWAP = ((0, 1), (1, 0))


def attend_kernel(where_ref, assign_ref, length_ref, q_ref, kv_ref, out_ref, mine_ref, other_ref, s_ref):
    z, yhi, core = where_ref[0], where_ref[1], where_ref[2]
    rows = q_ref.shape[0]
    count = kv_ref.shape[0]
    chunk = 512
    per = chunk // BLK
    own = assign_ref[0, 2 * z + yhi] * BLK
    first = length_ref[0, 0]
    second = first + length_ref[0, 1]
    third = second + length_ref[0, 2]
    q_pos = own + lax.broadcasted_iota(jnp.int32, (rows, 1), 0)
    q_start = jnp.where(
        q_pos >= third,
        third,
        jnp.where(q_pos >= second, second, jnp.where(q_pos >= first, first, 0)),
    )
    q_all = jnp.concatenate([q_ref[:, h * HD : (h + 1) * HD] for h in range(HQ)], axis=0)
    lane = lax.broadcasted_iota(jnp.int32, (1, BLK), 1)
    top = None
    for c in range(count // chunk):
        k_pos = []
        for b in range(c * per, (c + 1) * per):
            slot = b // 2 * 2 + (yhi if b % 2 == 0 else 1 - yhi)
            k_pos.append(assign_ref[0, slot] * BLK + lane)
        k_pos = jnp.concatenate(k_pos, axis=1)
        bias = jnp.where((k_pos >= q_start) & (k_pos <= q_pos), 0.0, NEGATIVE)
        scores = lax.dot_general(
            q_all,
            kv_ref[c * chunk : (c + 1) * chunk, :HD],
            (((1,), (1,)), ((), ())),
            preferred_element_type=jnp.float32,
        )
        scores = scores.reshape(HQ, rows, chunk) * (HD ** (-0.5) * LOG2E) + bias[None]
        scores = scores.reshape(HQ * rows, chunk)
        s_ref[:, c * chunk : (c + 1) * chunk] = scores
        best = jnp.max(scores, axis=1, keepdims=True)
        top = best if top is None else jnp.maximum(top, best)
    total = jnp.zeros((HQ * rows, 1), jnp.float32)
    mixture = jnp.zeros((HQ * rows, HD), jnp.float32)
    for c in range(count // chunk):
        terms = jnp.exp2(s_ref[:, c * chunk : (c + 1) * chunk] - top)
        total = total + jnp.sum(terms, axis=1, keepdims=True)
        mixture = mixture + jnp.dot(
            terms.astype(jnp.bfloat16),
            kv_ref[c * chunk : (c + 1) * chunk, HD:],
            preferred_element_type=jnp.float32,
        )
    result = (mixture / total).astype(jnp.bfloat16)
    for h in range(HQ):
        head = result[h * rows : (h + 1) * rows]
        out_ref[:, h * HD : (h + 1) * HD] = head
        at = h % (HQ // 2) * HD

        @pl.when(core == h // (HQ // 2))
        def _():
            mine_ref[:, at : at + HD] = head

        @pl.when(core != h // (HQ // 2))
        def _():
            other_ref[:, at : at + HD] = head


def attend(queries, kv_all, lengths, assignment):
    rows = queries.shape[0]
    count = kv_all.shape[0]
    here = jnp.stack([lax.axis_index("z"), lax.axis_index("yhi"), lax.axis_index("core")])
    smem = pl.BlockSpec(memory_space=pltpu.SMEM)
    vmem = pl.BlockSpec(memory_space=pltpu.VMEM)
    half = jax.ShapeDtypeStruct((rows, HALF), jnp.bfloat16)
    return pl.pallas_call(
        attend_kernel,
        out_shape=(jax.ShapeDtypeStruct((rows, COLS), jnp.bfloat16), half, half),
        in_specs=[smem, smem, smem, vmem, vmem],
        out_specs=(vmem, vmem, vmem),
        scratch_shapes=[pltpu.VMEM((HQ * rows, count), jnp.float32)],
        compiler_params=pltpu.CompilerParams(vmem_limit_bytes=24 << 20),
        name="attend",
    )(here.astype(jnp.int32), assignment, lengths, queries, kv_all)


def to_everyone(x, axes):
    size = math.prod(SIZES[AXES.index(a)] for a in axes)
    copies = jnp.broadcast_to(x, (size, *x.shape))
    return lax.all_to_all(copies, axes, split_axis=0, concat_axis=0, tiled=True)


def halves(x, which):
    half = x.shape[1] // 2
    low, high = x[:, :half], x[:, half:]
    return jnp.where(which == 0, low, high), jnp.where(which == 0, high, low)


def local(student_in, weight, queries, keys, values, lengths, assignment):
    rows = queries.shape[0]
    core = lax.axis_index("core")
    ylo = lax.axis_index("ylo")
    wrows = weight.shape[0]

    w_mine, w_other = halves(weight, core)
    w_got = lax.ppermute(w_other, "core", SWAP)
    kv = jnp.concatenate([keys, values], axis=1)
    kv_pair = jnp.concatenate([kv, lax.ppermute(kv, "yhi", SWAP)], axis=0)
    kv_all = lax.all_gather(kv_pair, "z", axis=0, tiled=True)

    w_first = jnp.where(core == 0, w_mine, w_got)
    w_second = jnp.where(core == 0, w_got, w_mine)
    pad = jnp.zeros((16 - wrows, HALF), jnp.bfloat16)
    arrived = to_everyone(jnp.concatenate([w_first, pad, w_second, pad], axis=0), SEQ)

    as_float = student_in.astype(jnp.float32)
    normed = (
        as_float * lax.rsqrt(jnp.mean(as_float * as_float, axis=1, keepdims=True) + EPSILON)
    ).astype(jnp.bfloat16)
    n_keep, n_send = halves(normed, ylo)
    n_pair = jnp.concatenate([n_keep, lax.ppermute(n_send, "ylo", SWAP)], axis=0)
    n_all = jnp.concatenate([n_pair, lax.ppermute(n_pair, "core", SWAP)], axis=0)

    w_near = jnp.concatenate(
        [
            arrived[:, :wrows].reshape(-1, HALF),
            arrived[:, 16 : 16 + wrows].reshape(-1, HALF),
        ],
        axis=0,
    )
    w_near, n_all = lax.optimization_barrier((w_near, n_all))
    w_all = to_everyone(w_near, ("x",)).reshape(DS // 2, HALF)

    attention, a_mine, a_other = attend(queries, kv_all, lengths, assignment)
    a_got = lax.ppermute(a_other, "core", SWAP)

    partial = jnp.dot(n_all, w_all, preferred_element_type=jnp.float32)
    partial = partial.reshape(2, 2, rows, HALF)
    mine = partial[:, 0] - jnp.stack([a_mine, a_got]).astype(jnp.float32)
    theirs = partial[:, 1]
    back = lax.ppermute(jnp.stack([mine, theirs], axis=1).astype(jnp.bfloat16), "ylo", SWAP)
    back = back.astype(jnp.float32)
    diff = jnp.stack([mine + back[:, 1], theirs + back[:, 0]], axis=1)
    scaled = (diff * TOKENS_ALL ** (-0.5)).astype(jnp.bfloat16).reshape(4 * rows, HALF)
    part = lax.dot_general(
        n_all, scaled, (((0,), (0,)), ((), ())), preferred_element_type=jnp.float32
    ).astype(jnp.bfloat16)
    wide = lax.all_to_all(
        part.reshape(4, -1, HALF), "x", split_axis=0, concat_axis=0, tiled=True
    )
    near = wide.astype(jnp.float32).sum(axis=0).astype(jnp.bfloat16).reshape(-1, wrows, HALF)
    near = jnp.pad(near, ((0, 0), (0, 16 - wrows), (0, 0)))
    last = lax.all_to_all(near, ("core", *SEQ), split_axis=0, concat_axis=0, tiled=True)
    summed = last.reshape(2, 16, 16, HALF).astype(jnp.float32).sum(axis=1)
    weight_grad = jnp.concatenate([summed[0, :wrows], summed[1, :wrows]], axis=1)
    return (attention, weight_grad)


def solution(mesh):
    mesh = Mesh(mesh.devices.reshape(SIZES), AXES)
    token = P(AXES, None)
    row = P(("ylo", "x", "core"), None)
    return jax.shard_map(
        local,
        mesh=mesh,
        in_specs=(token, token, token, token, token, row, row),
        out_specs=(token, token),
        check_vma=False,
    )
```

time: 132 us -> 133 us (level)
  the two profiles are of different devices: /device:TPU:1 before, /device:TPU:32 now
where the time goes in v3:
time: 133 us; the launch traced here: 132 us
  blocking collectives  60.8 us (46%)
  waiting for transfers between devices  30.3 us (23%)
  between operations  14.3 us (11%)
  starting transfers between devices  10.8 us (8%)
  other arithmetic  6.9 us (5%)
  Pallas kernels  3.94 us (3%)
  local copies, waits for them, and re-layouts  2.51 us (2%)
  matrix products  2.51 us (2%)
    all_to_all x1, blocking collectives, to_everyone(): return lax.all_to_all(copies, axes, split_axis=0, concat_axis=0, tiled=True)  21.8 us
    all_to_all x1, blocking collectives, local(): lax.all_to_all(near, ('core', *SEQ), split_axis=0, concat_axis=0, tiled=T...  21.3 us
    all_to_all x1, blocking collectives, local(): lax.all_to_all(part.reshape(4, -1, HALF), 'x', split_axis=0, concat_axis=...  17.7 us
    ppermute x1, waiting for transfers between devices, local(): kv_pair = jnp.concatenate([kv, lax.ppermute(kv, 'yhi', SWAP)], axis=0)  12.2 us
    all_gather x1, waiting for transfers between devices, local(): kv_all = lax.all_gather(kv_pair, 'z', axis=0, tiled=True)  10.9 us
    ppermute x1, waiting for transfers between devices, local(): lax.ppermute(jnp.stack([mine, theirs], axis=1).astype(jnp.bfloat16), 'ylo...  7.16 us
    all_to_all x1, starting transfers between devices, to_everyone(): return lax.all_to_all(copies, axes, split_axis=0, concat_axis=0, tiled=True)  4.34 us
    pallas_call x1, Pallas kernels, attend(): pl.pallas_call(attend_kernel, out_shape=(jax.ShapeDtypeStruct((rows, COLS...  3.94 us
  transfers between devices with their start and end apart: 8, of which 3 were waited for; matrix products, arithmetic and copies ran while one was open for 6% of the time, Pallas kernels for 3%

profile of v3, /device:TPU:32, one launch (start us, length us, event | category | flops | bytes accessed | tf_op | source)
XLA Modules:
  0.0 132.0 jit_solution(14734688219435236821)
XLA Ops:
  7.2 0.0 all-gather.2.cloned.1.call-start
  7.2 0.7 broadcast_select_fusion.4
  7.9 0.0 collective-permute-start.1
  7.9 1.4 %fusion = f32[128]{0:T(128)S(1)} fusion(bf16[128,3584]{1,0:T(8,128)(2,1)} %param.7), kind=kLoop, calls=%fused_computation.3 | loop fusion | flops 1376128 | bytes 918016 | tf_op jit(solution)/shard_map/reduce_sum | solution.py:139
  9.4 0.0 copy-start.5
  9.4 0.0 copy-start.6
  9.4 0.0 copy-start.4
  9.4 1.4 %fusion.1 = bf16[128,3584]{1,0:T(8,128)(2,1)S(1)} fusion(bf16[128,3584]{1,0:T(8,128)(2,1)} %param.7, f32[128]{0:T(128)S(1)} %add_rsqrt_fusion), kind=kLoop, calls=%fused_computation.4 | loop fusion | flops 1376256 | bytes 1835520 | tf_op jit(solution)/shard_map/convert_element_type | solution.py:140
  10.8 0.1 broadcast_select_fusion.1
  10.9 1.7 %collective-permute-start.2 = (bf16[128,1792]{1,0:T(8,128)(2,1)S(1)}, bf16[128,1792]{1,0:T(8,128)(2,1)S(1)}, u32[]{:S(2)}, u32[]{:S(2)}) collective-permute-start(bf16[128,1792]{1,0:T(8,128)(2,1)S(1)} %get-tuple-element.15), channel_id=1, source_target_pairs={{0,128},{128,0},{1,129},{129,1},{2,130},{130,2},{3,131},{131,3},{4... | collective-permute-start | bytes 1376264 | tf_op jit(solution)/shard_map/ppermute | solution.py:142
  12.6 0.0 copy-done.5
  12.6 0.0 copy-done.6
  12.6 3.0 %collective-permute-start = (bf16[128,256]{1,0:T(8,128)(2,1)S(1)}, bf16[128,256]{1,0:T(8,128)(2,1)S(1)}, u32[]{:S(2)}, u32[]{:S(2)}) collective-permute-start(bf16[128,256]{1,0:T(8,128)(2,1)S(1)} %constant_dynamic-update-slice_fusion), channel_id=1, source_target_pairs={{0,1},{1,0},{2,3},{3,2},{4,5},{5,4},{6,7},{7,6},{8,9},{9,8},{10,11... | collective-permute-start | bytes 196616 | tf_op jit(solution)/shard_map/ppermute | solution.py:129
  15.6 0.0 collective-permute-done.1
  15.6 0.0 copy-done.4
  15.6 12.2 %collective-permute-done = bf16[128,256]{1,0:T(8,128)(2,1)S(1)} collective-permute-done((bf16[128,256]{1,0:T(8,128)(2,1)S(1)}, bf16[128,256]{1,0:T(8,128)(2,1)S(1)}, u32[]{:S(2)}, u32[]{:S(2)}) %collective-permute-start) | collective-permute-done | bytes 65568 | tf_op jit(solution)/shard_map/ppermute | solution.py:129
  27.8 0.7 pad_maximum_fusion.4
  28.5 0.0 all-gather.2.cloned.1.call-update
  28.5 0.0 collective-permute-done.2
  28.5 0.1 pad_maximum_fusion.1
  28.6 0.1 collective-permute-start.3
  28.7 21.8 %all_to_all.20 = bf16[16,32,256]{2,1,0:T(8,128)(2,1)S(1)} all-to-all(bf16[16,32,256]{2,1,0:T(8,128)(2,1)S(1)} %broadcast_in_dim.11), channel_id=1, replica_groups=mesh['ylo'=2,'x'=4,'core'=2,'z'=8,'yhi'=2] {'z','yhi'}, dimensions={0} | all-to-all | bytes 524288 | tf_op jit(solution)/shard_map/all_to_all | solution.py:111
  50.7 0.0 collective-permute-done.3
  50.7 1.3 pad_maximum_fusion
  52.0 0.0 copy-start.1
  52.0 0.0 copy-start.2
  52.0 0.0 copy-start.3
  52.0 1.0 broadcast_in_dim.12
  53.0 4.3 %all-to-all-start.1 = ((bf16[4,448,256]{2,1,0:T(8,128)(2,1)}), bf16[4,448,256]{2,1,0:T(8,128)(2,1)}, u32[]{:S(2)}, u32[]{:S(2)}) async-start(bf16[4,448,256]{2,1,0:T(8,128)(2,1)} %broadcast_in_dim.12), calls=%async_computation.1 | async-start | bytes 1835008 | tf_op jit(solution)/shard_map/all_to_all | solution.py:111
  57.4 0.1 pad_add_fusion.where_ref
  57.5 10.9 %all-gather.2.cloned.1.call-done.kv_ref = bf16[2048,256]{1,0:T(8,128)(2,1)} async-done(((bf16[256,256]{1,0:T(8,128)(2,1)}), bf16[2048,256]{1,0:T(8,128)(2,1)}) %all-gather.2.cloned.1.call-update) | async-done | bytes 1048592 | tf_op jit(solution)/shard_map/all_gather | solution.py:130
  68.4 0.0 copy-done.1
  68.4 0.0 copy-done.2
  68.4 0.0 copy-done.3
  68.4 0.0 copy-start
  68.4 1.2 copy-done
  69.6 3.9 %attend.1 = (bf16[128,512]{1,0:T(8,128)(2,1)}, bf16[128,256]{1,0:T(8,128)(2,1)S(1)}, bf16[128,256]{1,0:T(8,128)(2,1)S(1)}) custom-call(s32[3]{0:T(128)S(1)} %pad_add_fusion.where_ref, s32[1,16]{1,0:T(1,128)S(1)} %copy-done.2, s32[1,4]{1,0:T(1,128)S(1)} %copy-done.3, bf16[128,512]{1,0:T(8,128)(2,1)S(1)} %copy-done.1, bf16[2048,256]{1,0:T(8,128)(2,1)S(1)} %copy-done), custom_call_target="tpu_custom_call" | custom-call | tf_op jit(solution)/shard_map/attend/pallas_call | solution.py:97
  73.6 0.0 collective-permute-start.4
  73.6 0.0 all-to-all-done.1
  73.6 1.8 %fusion.5 = f32[2,2,128,256]{3,2,1,0:T(8,128)S(1)} fusion(bf16[2,2,128,1792]{3,2,1,0:T(8,128)(2,1)S(1)} %bitcast.26, bf16[1792,256,1,1]{1,0,3,2:T(8,128)(2,1)} %bitcast.6), kind=kOutput, calls=%fused_computation.34 | convolution fusion | flops 469762048 | bytes 3276800 | tf_op jit(solution)/shard_map/dot_general | solution.py:158
  75.4 0.0 collective-permute-done.4
  75.5 1.6 %collective-permute-start.5 = (bf16[2,2,128,256]{3,2,1,0:T(8,128)(2,1)S(1)}, bf16[2,2,128,256]{3,2,1,0:T(8,128)(2,1)S(1)}, u32[]{:S(2)}, u32[]{:S(2)}) collective-permute-start(bf16[2,2,128,256]{3,2,1,0:T(8,128)(2,1)S(1)} %pad_maximum_fusion.2), channel_id=1, source_target_pairs={{0,128},{128,0},{1,129},{129,1},{2,130},{130,2},{3,131},{131,3},{4... | collective-permute-start | bytes 786440 | tf_op jit(solution)/shard_map/ppermute | solution.py:162
  77.2 7.2 %collective-permute-done.5 = bf16[2,2,128,256]{3,2,1,0:T(8,128)(2,1)S(1)} collective-permute-done((bf16[2,2,128,256]{3,2,1,0:T(8,128)(2,1)S(1)}, bf16[2,2,128,256]{3,2,1,0:T(8,128)(2,1)S(1)}, u32[]{:S(2)}, u32[]{:S(2)}) %collective-permute-start.5) | collective-permute-done | bytes 262176 | tf_op jit(solution)/shard_map/ppermute | solution.py:162
  84.4 0.1 slice_add_fusion.1
  84.5 0.7 convolution_convert_fusion
  85.2 17.7 %all_to_all.21 = bf16[4,448,256]{2,1,0:T(8,128)(2,1)S(1)} all-to-all(bf16[4,448,256]{2,1,0:T(8,128)(2,1)S(1)} %bitcast.27), channel_id=1, replica_groups=mesh['ylo'=2,'x'=4,'core'=2,'z'=8,'yhi'=2] {'x'}, dimensions={0} | all-to-all | bytes 1835008 | tf_op jit(solution)/shard_map/all_to_all | solution.py:169
  102.9 0.2 reduce_sum.31
  103.1 0.1 reshape.76
  103.2 21.3 %all_to_all.22 = bf16[32,16,256]{2,1,0:T(8,128)(2,1)S(1)} all-to-all(bf16[32,16,256]{2,1,0:T(8,128)(2,1)S(1)} %pad.4), channel_id=1, replica_groups=mesh['ylo'=2,'x'=4,'core'=2,'z'=8,'yhi'=2] {'core','z','yhi'}, dimensions={0} | all-to-all | bytes 524288 | tf_op jit(solution)/shard_map/all_to_all | solution.py:174
  124.6 0.6 pad_maximum_fusion.6
  (19 shorter events, 0.4 us)
Async XLA Ops:
  7.2 61.2 %all-gather.2.cloned.1.call-start = ((), (), s32[]{:S(2)}) async-start(), calls=%async_computation.4 | async-start | bytes 1179648 | tf_op jit(solution)/shard_map/all_gather | solution.py:130
  7.9 7.7 %collective-permute-start.1 = (bf16[14,256]{1,0:T(8,128)(2,1)S(1)}, bf16[14,256]{1,0:T(8,128)(2,1)S(1)}, u32[]{:S(2)}, u32[]{:S(2)}) collective-permute-start(bf16[14,256]{1,0:T(8,128)(2,1)S(1)} %broadcast_select_fusion.4), channel_id=1, source_target_pairs={{0,16},{16,0},{1,17},{17,1},{2,18},{18,2},{3,19},{19,3},{4,20},{20... | collective-permute-start | bytes 21512 | tf_op jit(solution)/shard_map/ppermute | solution.py:127
  9.4 3.2 %copy-start.5 = (bf16[128,128]{1,0:T(8,128)(2,1)S(1)}, bf16[128,128]{1,0:T(8,128)(2,1)}, u32[]{:S(2)}) copy-start(bf16[128,128]{1,0:T(8,128)(2,1)} %param.10) | copy-start | bytes 98308
  9.4 3.2 %copy-start.6 = (bf16[128,128]{1,0:T(8,128)(2,1)S(1)}, bf16[128,128]{1,0:T(8,128)(2,1)}, u32[]{:S(2)}) copy-start(bf16[128,128]{1,0:T(8,128)(2,1)} %param.11) | copy-start | bytes 98308
  9.4 6.2 %copy-start.4 = (bf16[14,512]{1,0:T(8,128)(2,1)S(1)}, bf16[14,512]{1,0:T(8,128)(2,1)}, u32[]{:S(2)}) copy-start(bf16[14,512]{1,0:T(8,128)(2,1)} %param.8) | copy-start | bytes 43012
  10.9 17.6 %collective-permute-start.2 = (bf16[128,1792]{1,0:T(8,128)(2,1)S(1)}, bf16[128,1792]{1,0:T(8,128)(2,1)S(1)}, u32[]{:S(2)}, u32[]{:S(2)}) collective-permute-start(bf16[128,1792]{1,0:T(8,128)(2,1)S(1)} %get-tuple-element.15), channel_id=1, source_target_pairs={{0,128},{128,0},{1,129},{129,1},{2,130},{130,2},{3,131},{131,3},{4... | collective-permute-start | bytes 1376264 | tf_op jit(solution)/shard_map/ppermute | solution.py:142
  12.6 15.2 %collective-permute-start = (bf16[128,256]{1,0:T(8,128)(2,1)S(1)}, bf16[128,256]{1,0:T(8,128)(2,1)S(1)}, u32[]{:S(2)}, u32[]{:S(2)}) collective-permute-start(bf16[128,256]{1,0:T(8,128)(2,1)S(1)} %constant_dynamic-update-slice_fusion), channel_id=1, source_target_pairs={{0,1},{1,0},{2,3},{3,2},{4,5},{5,4},{6,7},{7,6},{8,9},{9,8},{10,11... | collective-permute-start | bytes 196616 | tf_op jit(solution)/shard_map/ppermute | solution.py:129
  28.6 22.1 %collective-permute-start.3 = (bf16[256,1792]{1,0:T(8,128)(2,1)S(1)}, bf16[256,1792]{1,0:T(8,128)(2,1)}, u32[]{:S(2)}, u32[]{:S(2)}) collective-permute-start(bf16[256,1792]{1,0:T(8,128)(2,1)S(1)} %pad_maximum_fusion.1), channel_id=1, source_target_pairs={{0,16},{16,0},{1,17},{17,1},{2,18},{18,2},{3,19},{19,3},{4,20},{20... | collective-permute-start | bytes 2752520 | tf_op jit(solution)/shard_map/ppermute | solution.py:143
  52.0 16.4 %copy-start.1 = (bf16[128,512]{1,0:T(8,128)(2,1)S(1)}, bf16[128,512]{1,0:T(8,128)(2,1)}, u32[]{:S(2)}) copy-start(bf16[128,512]{1,0:T(8,128)(2,1)} %q_ref.1) | copy-start | bytes 393220
  52.0 16.4 %copy-start.2 = (s32[1,16]{1,0:T(1,128)S(1)}, s32[1,16]{1,0:T(1,128)}, u32[]{:S(2)}) copy-start(s32[1,16]{1,0:T(1,128)} %assign_ref.1) | copy-start | bytes 196
  52.0 16.4 %copy-start.3 = (s32[1,4]{1,0:T(1,128)S(1)}, s32[1,4]{1,0:T(1,128)}, u32[]{:S(2)}) copy-start(s32[1,4]{1,0:T(1,128)} %length_ref.1) | copy-start | bytes 52
  53.0 20.5 %all-to-all-start.1 = ((bf16[4,448,256]{2,1,0:T(8,128)(2,1)}), bf16[4,448,256]{2,1,0:T(8,128)(2,1)}, u32[]{:S(2)}, u32[]{:S(2)}) async-start(bf16[4,448,256]{2,1,0:T(8,128)(2,1)} %broadcast_in_dim.12), calls=%async_computation.1 | async-start | bytes 1835008 | tf_op jit(solution)/shard_map/all_to_all | solution.py:111
  68.4 1.2 copy-start
  73.6 1.9 %collective-permute-start.4 = (bf16[128,256]{1,0:T(8,128)(2,1)S(1)}, bf16[128,256]{1,0:T(8,128)(2,1)S(1)}, u32[]{:S(2)}, u32[]{:S(2)}) collective-permute-start(bf16[128,256]{1,0:T(8,128)(2,1)S(1)} %get-tuple-element.11), channel_id=1, source_target_pairs={{0,16},{16,0},{1,17},{17,1},{2,18},{18,2},{3,19},{19,3},{4,20},{20... | collective-permute-start | bytes 196616 | tf_op jit(solution)/shard_map/ppermute | solution.py:156
  75.5 8.8 %collective-permute-start.5 = (bf16[2,2,128,256]{3,2,1,0:T(8,128)(2,1)S(1)}, bf16[2,2,128,256]{3,2,1,0:T(8,128)(2,1)S(1)}, u32[]{:S(2)}, u32[]{:S(2)}) collective-permute-start(bf16[2,2,128,256]{3,2,1,0:T(8,128)(2,1)S(1)} %pad_maximum_fusion.2), channel_id=1, source_target_pairs={{0,128},{128,0},{1,129},{129,1},{2,130},{130,2},{3,131},{131,3},{4... | collective-permute-start | bytes 786440 | tf_op jit(solution)/shard_map/ppermute | solution.py:162
Sparse Core Ops, SparseCore 0:
  28.6 39.7 all-gather.1

commit v4 on v3

--- a/solution.py
+++ b/solution.py
@@ -10,7 +10,6 @@
 HD = 128
 HQ = 4
 BLK = 128
-DS = 3584
 COLS = HQ * HD
 HALF = COLS // 2
 TOKENS_ALL = 32768
@@ -22,16 +21,15 @@
 AXES = ("ylo", "x", "core", "z", "yhi")
 SIZES = (2, 4, 2, 8, 2)
 SEQ = ("z", "yhi")
-SWAP = ((0, 1), (1, 0))
 
 
 def attend_kernel(where_ref, assign_ref, length_ref, q_ref, kv_ref, out_ref, mine_ref, other_ref, s_ref):
-    z, yhi, core = where_ref[0], where_ref[1], where_ref[2]
+    slot, core = where_ref[0], where_ref[1]
     rows = q_ref.shape[0]
     count = kv_ref.shape[0]
     chunk = 512
     per = chunk // BLK
-    own = assign_ref[0, 2 * z + yhi] * BLK
+    own = assign_ref[0, slot] * BLK
     first = length_ref[0, 0]
     second = first + length_ref[0, 1]
     third = second + length_ref[0, 2]
@@ -47,8 +45,7 @@
     for c in range(count // chunk):
         k_pos = []
         for b in range(c * per, (c + 1) * per):
-            slot = b // 2 * 2 + (yhi if b % 2 == 0 else 1 - yhi)
-            k_pos.append(assign_ref[0, slot] * BLK + lane)
+            k_pos.append(assign_ref[0, b] * BLK + lane)
         k_pos = jnp.concatenate(k_pos, axis=1)
         bias = jnp.where((k_pos >= q_start) & (k_pos <= q_pos), 0.0, NEGATIVE)
         scores = lax.dot_general(
@@ -90,7 +87,7 @@
 def attend(queries, kv_all, lengths, assignment):
     rows = queries.shape[0]
     count = kv_all.shape[0]
-    here = jnp.stack([lax.axis_index("z"), lax.axis_index("yhi"), lax.axis_index("core")])
+    here = jnp.stack([lax.axis_index(SEQ), lax.axis_index("core")])
     smem = pl.BlockSpec(memory_space=pltpu.SMEM)
     vmem = pl.BlockSpec(memory_space=pltpu.VMEM)
     half = jax.ShapeDtypeStruct((rows, HALF), jnp.bfloat16)
@@ -105,16 +102,79 @@
     )(here.astype(jnp.int32), assignment, lengths, queries, kv_all)
 
 
-def to_everyone(x, axes):
-    size = math.prod(SIZES[AXES.index(a)] for a in axes)
-    copies = jnp.broadcast_to(x, (size, *x.shape))
-    return lax.all_to_all(copies, axes, split_axis=0, concat_axis=0, tiled=True)
+DOUBLING = (("z", 4, 3), ("yhi", 1, 0), ("z", 2, 2), ("z", 1, 1))
+
+
+def arrange_kernel(where_ref, blocks_ref, out_ref):
+    slot, core = where_ref[0], where_ref[1]
+    wrows = out_ref.shape[0] // 32
+    for c in range(2):
+        for s in range(16):
+            apart = lax.bitwise_xor(slot, s)
+            at = 0
+            for order, (_, _, bit) in enumerate(DOUBLING):
+                at = at + lax.rem(apart // (1 << bit), 2) * (1 << order)
+            block = blocks_ref[lax.bitwise_xor(core, c), at]
+            first = (c * 16 + s) * wrows
+            out_ref[first : first + wrows, :] = block[:wrows]
+
+
+def arrange(blocks, wrows):
+    here = jnp.stack([lax.axis_index(SEQ), lax.axis_index("core")])
+    vmem = pl.BlockSpec(memory_space=pltpu.VMEM)
+    return pl.pallas_call(
+        arrange_kernel,
+        out_shape=jax.ShapeDtypeStruct((32 * wrows, HALF), jnp.bfloat16),
+        in_specs=[pl.BlockSpec(memory_space=pltpu.SMEM), vmem],
+        out_specs=vmem,
+        name="arrange",
+    )(here.astype(jnp.int32), blocks)
+
+
+def project_kernel(where_ref, n_ref, *refs):
+    *w_refs, own_ref, send_ref, w_all = refs
+    x = where_ref[0]
+    step = w_refs[0].shape[0]
+    for d, w_ref in enumerate(w_refs):
+        at = lax.rem(x + d, len(w_refs)) * step
+        w_all[pl.ds(pl.multiple_of(at, step), step), :] = w_ref[...]
+    rows = n_ref.shape[0] // 4
+    for b in range(4):
+        part = jnp.dot(
+            n_ref[b * rows : (b + 1) * rows, :], w_all[...], preferred_element_type=jnp.float32
+        )
+        own_ref[b * rows : (b + 1) * rows, :] = part
+        t = b ^ 1
+        send_ref[t * rows : (t + 1) * rows, :] = part.astype(jnp.bfloat16)
+
+
+def project(n_all, pieces):
+    here = jnp.stack([lax.axis_index("x")]).astype(jnp.int32)
+    vmem = pl.BlockSpec(memory_space=pltpu.VMEM)
+    shape = (n_all.shape[0], HALF)
+    return pl.pallas_call(
+        project_kernel,
+        out_shape=(
+            jax.ShapeDtypeStruct(shape, jnp.float32),
+            jax.ShapeDtypeStruct(shape, jnp.bfloat16),
+        ),
+        in_specs=[pl.BlockSpec(memory_space=pltpu.SMEM)] + [vmem] * (1 + len(pieces)),
+        out_specs=(vmem, vmem),
+        scratch_shapes=[pltpu.VMEM((n_all.shape[1], HALF), jnp.bfloat16)],
+        compiler_params=pltpu.CompilerParams(vmem_limit_bytes=16 << 20),
+        name="project",
+    )(here, n_all, *pieces)
 
 
 def halves(x, which):
     half = x.shape[1] // 2
     low, high = x[:, :half], x[:, half:]
     return jnp.where(which == 0, low, high), jnp.where(which == 0, high, low)
+
+
+def partner(x, axis, mask):
+    size = SIZES[AXES.index(axis)]
+    return lax.ppermute(x, axis, [(i, i ^ mask) for i in range(size)])
 
 
 def local(student_in, weight, queries, keys, values, lengths, assignment):
@@ -123,46 +183,47 @@
     ylo = lax.axis_index("ylo")
     wrows = weight.shape[0]
 
+    kv = jnp.concatenate([keys, values], axis=1)
+    kv_copies = jnp.broadcast_to(kv, (16, rows, 2 * HD))
+    kv_all = lax.all_to_all(kv_copies, SEQ, split_axis=0, concat_axis=0, tiled=True)
+    kv_all = kv_all.reshape(16 * rows, 2 * HD)
+
     w_mine, w_other = halves(weight, core)
-    w_got = lax.ppermute(w_other, "core", SWAP)
-    kv = jnp.concatenate([keys, values], axis=1)
-    kv_pair = jnp.concatenate([kv, lax.ppermute(kv, "yhi", SWAP)], axis=0)
-    kv_all = lax.all_gather(kv_pair, "z", axis=0, tiled=True)
-
-    w_first = jnp.where(core == 0, w_mine, w_got)
-    w_second = jnp.where(core == 0, w_got, w_mine)
-    pad = jnp.zeros((16 - wrows, HALF), jnp.bfloat16)
-    arrived = to_everyone(jnp.concatenate([w_first, pad, w_second, pad], axis=0), SEQ)
-
+    w_got = partner(w_other, "core", 1)
+    blocks = jnp.pad(jnp.stack([w_mine, w_got])[:, None], ((0, 0), (0, 0), (0, 16 - wrows), (0, 0)))
+    for axis, mask, _ in DOUBLING:
+        blocks = jnp.concatenate([blocks, partner(blocks, axis, mask)], axis=1)
+    w_near = arrange(blocks, wrows)
+    pieces = [w_near]
+    for d in range(1, 4):
+        pieces.append(lax.ppermute(w_near, "x", [((i + d) % 4, i) for i in range(4)]))
+
+    student_in, _, _ = lax.optimization_barrier((student_in, kv_copies, w_got))
     as_float = student_in.astype(jnp.float32)
     normed = (
         as_float * lax.rsqrt(jnp.mean(as_float * as_float, axis=1, keepdims=True) + EPSILON)
     ).astype(jnp.bfloat16)
     n_keep, n_send = halves(normed, ylo)
-    n_pair = jnp.concatenate([n_keep, lax.ppermute(n_send, "ylo", SWAP)], axis=0)
-    n_all = jnp.concatenate([n_pair, lax.ppermute(n_pair, "core", SWAP)], axis=0)
-
-    w_near = jnp.concatenate(
+    n_pair = jnp.concatenate([n_keep, partner(n_send, "ylo", 1)], axis=0)
+    n_all = jnp.concatenate([n_pair, partner(n_pair, "core", 1)], axis=0)
+
+    own, send = project(n_all, pieces)
+    back = partner(send, "ylo", 1)
+
+    kv_all, _ = lax.optimization_barrier((kv_all, w_near))
+    attention, a_mine, a_other = attend(queries, kv_all, lengths, assignment)
+    attended = jnp.concatenate(
         [
-            arrived[:, :wrows].reshape(-1, HALF),
-            arrived[:, 16 : 16 + wrows].reshape(-1, HALF),
+            a_mine,
+            partner(a_mine, "ylo", 1),
+            partner(a_other, "core", 1),
+            lax.ppermute(a_other, ("ylo", "core"), [(i, 3 - i) for i in range(4)]),
         ],
         axis=0,
     )
-    w_near, n_all = lax.optimization_barrier((w_near, n_all))
-    w_all = to_everyone(w_near, ("x",)).reshape(DS // 2, HALF)
-
-    attention, a_mine, a_other = attend(queries, kv_all, lengths, assignment)
-    a_got = lax.ppermute(a_other, "core", SWAP)
-
-    partial = jnp.dot(n_all, w_all, preferred_element_type=jnp.float32)
-    partial = partial.reshape(2, 2, rows, HALF)
-    mine = partial[:, 0] - jnp.stack([a_mine, a_got]).astype(jnp.float32)
-    theirs = partial[:, 1]
-    back = lax.ppermute(jnp.stack([mine, theirs], axis=1).astype(jnp.bfloat16), "ylo", SWAP)
-    back = back.astype(jnp.float32)
-    diff = jnp.stack([mine + back[:, 1], theirs + back[:, 0]], axis=1)
-    scaled = (diff * TOKENS_ALL ** (-0.5)).astype(jnp.bfloat16).reshape(4 * rows, HALF)
+
+    diff = own + back.astype(jnp.float32) - attended.astype(jnp.float32)
+    scaled = (diff * TOKENS_ALL ** (-0.5)).astype(jnp.bfloat16)
     part = lax.dot_general(
         n_all, scaled, (((0,), (0,)), ((), ())), preferred_element_type=jnp.float32
     ).astype(jnp.bfloat16)

time: 133 us -> 127 us (0.955)
  blocking collectives: 60.8 us -> 34.7 us
  starting transfers between devices: 10.8 us -> 28.8 us
  waiting for transfers between devices: 30.3 us -> 45.1 us
  between operations: 14.3 us -> 0.81 us
  Pallas kernels: 3.94 us -> 6.64 us
  other arithmetic: 6.9 us -> 4.78 us
    ppermute x6 -> x14, waiting for transfers between devices: 19.3 us -> 45.1 us  [the longest x10 36 us: partner(): return lax.ppermute(x, axis, [(i, i ^ mask) for i in range(size)])]
    all_to_all x1 -> x0, blocking collectives: 21.8 us -> none  [to_everyone(): return lax.all_to_all(copies, axes, split_axis=0, concat_axis=0, tiled=True)]
    ppermute x6 -> x14, starting transfers between devices: 6.39 us -> 17.9 us  [the longest x10 13.4 us: partner(): return lax.ppermute(x, axis, [(i, i ^ mask) for i in range(size)])]
    all_gather x1 -> x0, waiting for transfers between devices: 10.9 us -> none  [local(): kv_all = lax.all_gather(kv_pair, 'z', axis=0, tiled=True)]
    all_to_all x1, starting transfers between devices: 4.34 us -> 10.9 us  [local(): lax.all_to_all(kv_copies, SEQ, split_axis=0, concat_axis=0, tiled=True)]
    pallas_call x0 -> x2, Pallas kernels: none -> 2.7 us  [the longest x1 1.94 us: arrange(): pl.pallas_call(arrange_kernel, out_shape=jax.ShapeDtypeStruct((32 * wrows...]
    all_to_all x1, blocking collectives: 17.7 us -> 15.4 us  [local(): lax.all_to_all(part.reshape(4, -1, HALF), 'x', split_axis=0, concat_axis=...]
    all_to_all x1, blocking collectives: 21.3 us -> 19.3 us  [local(): lax.all_to_all(near, ('core', *SEQ), split_axis=0, concat_axis=0, tiled=T...]
  transfers between devices with their start and end apart: 8 -> 15, of which waited for: 3 -> 11; matrix products, arithmetic and copies ran while one was open for 6% -> 2% of each run, Pallas kernels for 3% -> 5%
where the time goes in v4:
time: 127 us; the launch traced here: 126 us
  waiting for transfers between devices  45.1 us (36%)
  blocking collectives  34.7 us (27%)
  starting transfers between devices  28.8 us (23%)
  Pallas kernels  6.64 us (5%)
  other arithmetic  4.78 us (4%)
  local copies, waits for them, and re-layouts  2.87 us (2%)
  matrix products  1.92 us (2%)
    ppermute x10, waiting for transfers between devices, partner(): return lax.ppermute(x, axis, [(i, i ^ mask) for i in range(size)])  36 us
    all_to_all x1, blocking collectives, local(): lax.all_to_all(near, ('core', *SEQ), split_axis=0, concat_axis=0, tiled=T...  19.3 us
    all_to_all x1, blocking collectives, local(): lax.all_to_all(part.reshape(4, -1, HALF), 'x', split_axis=0, concat_axis=...  15.4 us
    ppermute x10, starting transfers between devices, partner(): return lax.ppermute(x, axis, [(i, i ^ mask) for i in range(size)])  13.4 us
    all_to_all x1, starting transfers between devices, local(): lax.all_to_all(kv_copies, SEQ, split_axis=0, concat_axis=0, tiled=True)  10.9 us
    ppermute x3, waiting for transfers between devices, local(): lax.ppermute(w_near, 'x', [((i + d) % 4, i) for i in range(4)])  7.4 us
    ppermute x3, starting transfers between devices, local(): lax.ppermute(w_near, 'x', [((i + d) % 4, i) for i in range(4)])  4.44 us
    pallas_call x1, Pallas kernels, attend(): pl.pallas_call(attend_kernel, out_shape=(jax.ShapeDtypeStruct((rows, COLS...  3.93 us
  transfers between devices with their start and end apart: 15, of which 11 were waited for; matrix products, arithmetic and copies ran while one was open for 2% of the time, Pallas kernels for 5%

profile of v4, /device:TPU:32, one launch (start us, length us, event | category | flops | bytes accessed | tf_op | source)
XLA Modules:
  0.0 125.6 jit_solution(1638766935931483296)
XLA Ops:
  0.6 0.0 copy-start.5
  0.6 0.8 select_bitcast_fusion
  1.4 0.0 collective-permute-start
  1.4 0.8 pad_maximum_fusion.3
  2.2 0.4 collective-permute-done
  2.6 1.1 broadcast_in_dim.7
  3.7 0.0 copy-done.5
  3.7 0.3 fusion
  4.0 0.2 fusion.1
  4.2 0.1 broadcast_select_fusion.1
  4.3 1.7 %collective-permute-start.5 = (bf16[128,1792]{1,0:T(8,128)(2,1)S(1)}, bf16[128,1792]{1,0:T(8,128)(2,1)S(1)}, u32[]{:S(2)}, u32[]{:S(2)}) collective-permute-start(bf16[128,1792]{1,0:T(8,128)(2,1)S(1)} %get-tuple-element.17), channel_id=1, source_target_pairs={{0,128},{128,0},{1,129},{129,1},{2,130},{130,2},{3,131},{131,3},{4... | collective-permute-start | bytes 1376264 | tf_op jit(solution)/shard_map/ppermute | solution.py:177
  6.0 10.9 %all-to-all-start = ((bf16[16,128,256]{2,1,0:T(8,128)(2,1)}), bf16[16,128,256]{2,1,0:T(8,128)(2,1)S(1)}, u32[]{:S(2)}, u32[]{:S(2)}) async-start(bf16[16,128,256]{2,1,0:T(8,128)(2,1)} %broadcast_in_dim.7), calls=%async_computation | async-start | bytes 2097152 | tf_op jit(solution)/shard_map/all_to_all | solution.py:188
  16.9 4.6 %collective-permute-start.1 = (bf16[2,1,16,256]{3,2,1,0:T(8,128)(2,1)S(1)}, bf16[2,1,16,256]{3,2,1,0:T(8,128)(2,1)S(1)}, u32[]{:S(2)}, u32[]{:S(2)}) collective-permute-start(bf16[2,1,16,256]{3,2,1,0:T(8,128)(2,1)S(1)} %get-tuple-element.20), channel_id=1, source_target_pairs={{0,8},{2,10},{4,12},{6,14},{8,0},{10,2},{12,4},{14,6},{1,9},{3,11}... | collective-permute-start | bytes 49160 | tf_op jit(solution)/shard_map/ppermute | solution.py:177
  21.5 0.0 collective-permute-done.5
  21.5 1.0 pad_maximum_fusion.1
  22.5 0.0 collective-permute-start.6
  22.5 22.4 %collective-permute-done.1 = bf16[2,1,16,256]{3,2,1,0:T(8,128)(2,1)S(1)} collective-permute-done((bf16[2,1,16,256]{3,2,1,0:T(8,128)(2,1)S(1)}, bf16[2,1,16,256]{3,2,1,0:T(8,128)(2,1)S(1)}, u32[]{:S(2)}, u32[]{:S(2)}) %collective-permute-start.1) | collective-permute-done | bytes 16416 | tf_op jit(solution)/shard_map/ppermute | solution.py:177
  44.9 3.0 %collective-permute-start.2 = (bf16[2,2,16,256]{3,2,1,0:T(8,128)(2,1)S(1)}, bf16[2,2,16,256]{3,2,1,0:T(8,128)(2,1)S(1)}, u32[]{:S(2)}, u32[]{:S(2)}) collective-permute-start(bf16[2,2,16,256]{3,2,1,0:T(8,128)(2,1)S(1)} %pad_maximum_fusion.5), channel_id=1, source_target_pairs={{0,1},{1,0},{2,3},{3,2},{4,5},{5,4},{6,7},{7,6},{8,9},{9,8},{10,11... | collective-permute-start | bytes 98312 | tf_op jit(solution)/shard_map/ppermute | solution.py:177
  47.9 0.6 pad_add_fusion.where_ref
  48.5 1.8 %collective-permute-done.2 = bf16[2,2,16,256]{3,2,1,0:T(8,128)(2,1)S(1)} collective-permute-done((bf16[2,2,16,256]{3,2,1,0:T(8,128)(2,1)S(1)}, bf16[2,2,16,256]{3,2,1,0:T(8,128)(2,1)S(1)}, u32[]{:S(2)}, u32[]{:S(2)}) %collective-permute-start.2) | collective-permute-done | bytes 32800 | tf_op jit(solution)/shard_map/ppermute | solution.py:177
  50.3 0.3 collective-permute-start.3
  50.6 5.5 %collective-permute-done.3 = bf16[2,4,16,256]{3,2,1,0:T(8,128)(2,1)S(1)} collective-permute-done((bf16[2,4,16,256]{3,2,1,0:T(8,128)(2,1)S(1)}, bf16[2,4,16,256]{3,2,1,0:T(8,128)(2,1)S(1)}, u32[]{:S(2)}, u32[]{:S(2)}) %collective-permute-start.3) | collective-permute-done | bytes 65568 | tf_op jit(solution)/shard_map/ppermute | solution.py:177
  56.1 1.6 %collective-permute-start.4 = (bf16[2,8,16,256]{3,2,1,0:T(8,128)(2,1)S(1)}, bf16[2,8,16,256]{3,2,1,0:T(8,128)(2,1)S(1)}, u32[]{:S(2)}, u32[]{:S(2)}) collective-permute-start(bf16[2,8,16,256]{3,2,1,0:T(8,128)(2,1)S(1)} %pad_maximum_fusion.2), channel_id=1, source_target_pairs={{0,2},{2,0},{4,6},{6,4},{8,10},{10,8},{12,14},{14,12},{1,3},{3,1},... | collective-permute-start | bytes 393224 | tf_op jit(solution)/shard_map/ppermute | solution.py:177
  57.7 3.5 %collective-permute-done.4 = bf16[2,8,16,256]{3,2,1,0:T(8,128)(2,1)S(1)} collective-permute-done((bf16[2,8,16,256]{3,2,1,0:T(8,128)(2,1)S(1)}, bf16[2,8,16,256]{3,2,1,0:T(8,128)(2,1)S(1)}, u32[]{:S(2)}, u32[]{:S(2)}) %collective-permute-start.4) | collective-permute-done | bytes 131104 | tf_op jit(solution)/shard_map/ppermute | solution.py:177
  61.2 0.0 copy-start.7
  61.2 0.7 copy-done.7
  61.9 1.9 %arrange.1.refs_0_ = bf16[448,256]{1,0:T(8,128)(2,1)} custom-call(s32[2]{0:T(128)} %pad_add_fusion.where_ref, bf16[2,16,16,256]{3,2,1,0:T(8,128)(2,1)} %copy-done.7), custom_call_target="tpu_custom_call" | custom-call | tf_op jit(solution)/shard_map/arrange/pallas_call | solution.py:125
  63.8 0.0 copy-start
  63.8 2.8 %collective-permute-start.7 = (bf16[448,256]{1,0:T(8,128)(2,1)}, bf16[448,256]{1,0:T(8,128)(2,1)S(1)}, u32[]{:S(2)}, u32[]{:S(2)}) collective-permute-start(bf16[448,256]{1,0:T(8,128)(2,1)} %arrange.1.refs_0_), channel_id=1, source_target_pairs={{32,0},{64,32},{96,64},{0,96},{33,1},{65,33},{97,65},{1,97},{34,2}... | collective-permute-start | bytes 688136 | tf_op jit(solution)/shard_map/ppermute | solution.py:199
  66.6 0.8 collective-permute-start.8
  67.4 0.9 collective-permute-start.9
  68.3 0.0 collective-permute-done.6
  68.3 0.0 copy-start.6
  68.3 0.9 copy-done.6
  69.2 0.1 pad_maximum_fusion.n_ref
  69.3 0.0 copy-start.1
  69.3 0.0 copy-start.2
  69.4 0.0 copy-start.3
  69.4 0.0 copy-start.4
  69.4 3.6 %collective-permute-done.7.refs_1_ = bf16[448,256]{1,0:T(8,128)(2,1)S(1)} collective-permute-done((bf16[448,256]{1,0:T(8,128)(2,1)}, bf16[448,256]{1,0:T(8,128)(2,1)S(1)}, u32[]{:S(2)}, u32[]{:S(2)}) %collective-permute-start.7) | collective-permute-done | bytes 229408 | tf_op jit(solution)/shard_map/ppermute | solution.py:199
  72.9 1.5 %collective-permute-done.8.refs_2_ = bf16[448,256]{1,0:T(8,128)(2,1)S(1)} collective-permute-done((bf16[448,256]{1,0:T(8,128)(2,1)}, bf16[448,256]{1,0:T(8,128)(2,1)S(1)}, u32[]{:S(2)}, u32[]{:S(2)}) %collective-permute-start.8) | collective-permute-done | bytes 229408 | tf_op jit(solution)/shard_map/ppermute | solution.py:199
  74.4 2.4 %collective-permute-done.9.refs_3_ = bf16[448,256]{1,0:T(8,128)(2,1)S(1)} collective-permute-done((bf16[448,256]{1,0:T(8,128)(2,1)}, bf16[448,256]{1,0:T(8,128)(2,1)S(1)}, u32[]{:S(2)}, u32[]{:S(2)}) %collective-permute-start.9) | collective-permute-done | bytes 229408 | tf_op jit(solution)/shard_map/ppermute | solution.py:199
  76.8 0.0 copy-done
  76.8 0.8 project.1
  77.6 0.2 collective-permute-start.10
  77.8 0.0 all-to-all-done
  77.8 0.0 copy-done.1
  77.8 0.0 copy-done.2
  77.8 0.0 copy-done.3
  77.8 0.0 copy-done.4
  77.8 3.9 %attend.1 = (bf16[128,512]{1,0:T(8,128)(2,1)}, bf16[128,256]{1,0:T(8,128)(2,1)S(1)}, bf16[128,256]{1,0:T(8,128)(2,1)S(1)}) custom-call(s32[2]{0:T(128)S(1)} %copy-done.2, s32[1,16]{1,0:T(1,128)S(1)} %copy-done.3, s32[1,4]{1,0:T(1,128)S(1)} %copy-done.4, bf16[128,512]{1,0:T(8,128)(2,1)S(1)} %copy-done.1, bf16[2048,256]{1,0:T(8,128)(2,1)S(1)} %bitcast.17), custom_call_target="tpu_custom_call" | custom-call | tf_op jit(solution)/shard_map/attend/pallas_call | solution.py:94
  81.7 0.0 collective-permute-start.13
  81.8 2.0 %collective-permute-start.12 = (bf16[128,256]{1,0:T(8,128)(2,1)S(1)}, bf16[128,256]{1,0:T(8,128)(2,1)S(1)}, u32[]{:S(2)}, u32[]{:S(2)}) collective-permute-start(bf16[128,256]{1,0:T(8,128)(2,1)S(1)} %get-tuple-element.15), channel_id=1, source_target_pairs={{0,16},{16,0},{1,17},{17,1},{2,18},{18,2},{3,19},{19,3},{4,20},{20... | collective-permute-start | bytes 196616 | tf_op jit(solution)/shard_map/ppermute | solution.py:177
  83.8 0.1 collective-permute-start.11
  83.9 0.1 collective-permute-done.10
  84.0 1.8 %collective-permute-done.13 = bf16[128,256]{1,0:T(8,128)(2,1)S(1)} collective-permute-done((bf16[128,256]{1,0:T(8,128)(2,1)S(1)}, bf16[128,256]{1,0:T(8,128)(2,1)S(1)}, u32[]{:S(2)}, u32[]{:S(2)}) %collective-permute-start.13) | collective-permute-done | bytes 65568 | tf_op jit(solution)/shard_map/ppermute | solution.py:220
  85.8 0.0 collective-permute-done.12
  85.8 2.2 %collective-permute-done.11 = bf16[128,256]{1,0:T(8,128)(2,1)S(1)} collective-permute-done((bf16[128,256]{1,0:T(8,128)(2,1)S(1)}, bf16[128,256]{1,0:T(8,128)(2,1)S(1)}, u32[]{:S(2)}, u32[]{:S(2)}) %collective-permute-start.11) | collective-permute-done | bytes 65568 | tf_op jit(solution)/shard_map/ppermute | solution.py:177
  88.0 1.9 %convolution_convert_fusion = bf16[1792,256]{1,0:T(8,128)(2,1)S(1)} fusion(f32[512,256]{1,0:T(8,128)S(1)} %get-tuple-element.12, bf16[512,256]{1,0:T(8,128)(2,1)S(1)} %collective-permute-done.10, bf16[128,256]{1,0:T(8,128)(2,1)S(1)} %collective-permute-done.13, bf16[128,256]{1,0:T(8,128)(2,1)S(1)} %collective-permute-done.12, ...), kind=kOutput, calls=%fused_computation | convolution fusion | flops 477429760 | bytes 3801088 | tf_op jit(solution)/shard_map/dot_general | solution.py:227
  89.9 15.4 %all_to_all.15 = bf16[4,448,256]{2,1,0:T(8,128)(2,1)S(1)} all-to-all(bf16[4,448,256]{2,1,0:T(8,128)(2,1)S(1)} %bitcast.18), channel_id=1, replica_groups=mesh['ylo'=2,'x'=4,'core'=2,'z'=8,'yhi'=2] {'x'}, dimensions={0} | all-to-all | bytes 1835008 | tf_op jit(solution)/shard_map/all_to_all | solution.py:230
  105.3 0.2 reduce_sum.31
  105.6 0.1 reshape.26
  105.7 19.3 %all_to_all.16 = bf16[32,16,256]{2,1,0:T(8,128)(2,1)S(1)} all-to-all(bf16[32,16,256]{2,1,0:T(8,128)(2,1)S(1)} %pad.9), channel_id=1, replica_groups=mesh['ylo'=2,'x'=4,'core'=2,'z'=8,'yhi'=2] {'core','z','yhi'}, dimensions={0} | all-to-all | bytes 524288 | tf_op jit(solution)/shard_map/all_to_all | solution.py:235
  125.0 0.6 pad_maximum_fusion.6
  (13 shorter events, 0.1 us)
Async XLA Ops:
  0.6 3.1 %copy-start.5 = (bf16[128,3584]{1,0:T(8,128)(2,1)S(1)}, bf16[128,3584]{1,0:T(8,128)(2,1)}, u32[]{:S(2)}) copy-start(bf16[128,3584]{1,0:T(8,128)(2,1)} %param.7) | copy-start | bytes 2752516
  1.4 1.2 collective-permute-start
  4.3 17.2 %collective-permute-start.5 = (bf16[128,1792]{1,0:T(8,128)(2,1)S(1)}, bf16[128,1792]{1,0:T(8,128)(2,1)S(1)}, u32[]{:S(2)}, u32[]{:S(2)}) collective-permute-start(bf16[128,1792]{1,0:T(8,128)(2,1)S(1)} %get-tuple-element.17), channel_id=1, source_target_pairs={{0,128},{128,0},{1,129},{129,1},{2,130},{130,2},{3,131},{131,3},{4... | collective-permute-start | bytes 1376264 | tf_op jit(solution)/shard_map/ppermute | solution.py:177
  6.0 71.8 %all-to-all-start = ((bf16[16,128,256]{2,1,0:T(8,128)(2,1)}), bf16[16,128,256]{2,1,0:T(8,128)(2,1)S(1)}, u32[]{:S(2)}, u32[]{:S(2)}) async-start(bf16[16,128,256]{2,1,0:T(8,128)(2,1)} %broadcast_in_dim.7), calls=%async_computation | async-start | bytes 2097152 | tf_op jit(solution)/shard_map/all_to_all | solution.py:188
  16.9 28.0 %collective-permute-start.1 = (bf16[2,1,16,256]{3,2,1,0:T(8,128)(2,1)S(1)}, bf16[2,1,16,256]{3,2,1,0:T(8,128)(2,1)S(1)}, u32[]{:S(2)}, u32[]{:S(2)}) collective-permute-start(bf16[2,1,16,256]{3,2,1,0:T(8,128)(2,1)S(1)} %get-tuple-element.20), channel_id=1, source_target_pairs={{0,8},{2,10},{4,12},{6,14},{8,0},{10,2},{12,4},{14,6},{1,9},{3,11}... | collective-permute-start | bytes 49160 | tf_op jit(solution)/shard_map/ppermute | solution.py:177
  22.5 45.8 %collective-permute-start.6 = (bf16[256,1792]{1,0:T(8,128)(2,1)}, bf16[256,1792]{1,0:T(8,128)(2,1)S(1)}, u32[]{:S(2)}, u32[]{:S(2)}) collective-permute-start(bf16[256,1792]{1,0:T(8,128)(2,1)} %pad_maximum_fusion.1), channel_id=1, source_target_pairs={{0,16},{16,0},{1,17},{17,1},{2,18},{18,2},{3,19},{19,3},{4,20},{20... | collective-permute-start | bytes 2752520 | tf_op jit(solution)/shard_map/ppermute | solution.py:177
  44.9 5.4 %collective-permute-start.2 = (bf16[2,2,16,256]{3,2,1,0:T(8,128)(2,1)S(1)}, bf16[2,2,16,256]{3,2,1,0:T(8,128)(2,1)S(1)}, u32[]{:S(2)}, u32[]{:S(2)}) collective-permute-start(bf16[2,2,16,256]{3,2,1,0:T(8,128)(2,1)S(1)} %pad_maximum_fusion.5), channel_id=1, source_target_pairs={{0,1},{1,0},{2,3},{3,2},{4,5},{5,4},{6,7},{7,6},{8,9},{9,8},{10,11... | collective-permute-start | bytes 98312 | tf_op jit(solution)/shard_map/ppermute | solution.py:177
  50.3 5.8 %collective-permute-start.3 = (bf16[2,4,16,256]{3,2,1,0:T(8,128)(2,1)S(1)}, bf16[2,4,16,256]{3,2,1,0:T(8,128)(2,1)S(1)}, u32[]{:S(2)}, u32[]{:S(2)}) collective-permute-start(bf16[2,4,16,256]{3,2,1,0:T(8,128)(2,1)S(1)} %pad_maximum_fusion.4), channel_id=1, source_target_pairs={{0,4},{2,6},{4,0},{6,2},{8,12},{10,14},{12,8},{14,10},{1,5},{3,7},... | collective-permute-start | bytes 196616 | tf_op jit(solution)/shard_map/ppermute | solution.py:177
  56.1 5.1 %collective-permute-start.4 = (bf16[2,8,16,256]{3,2,1,0:T(8,128)(2,1)S(1)}, bf16[2,8,16,256]{3,2,1,0:T(8,128)(2,1)S(1)}, u32[]{:S(2)}, u32[]{:S(2)}) collective-permute-start(bf16[2,8,16,256]{3,2,1,0:T(8,128)(2,1)S(1)} %pad_maximum_fusion.2), channel_id=1, source_target_pairs={{0,2},{2,0},{4,6},{6,4},{8,10},{10,8},{12,14},{14,12},{1,3},{3,1},... | collective-permute-start | bytes 393224 | tf_op jit(solution)/shard_map/ppermute | solution.py:177
  61.2 0.7 copy-start.7
  63.8 13.0 %copy-start = (bf16[448,256]{1,0:T(8,128)(2,1)S(1)}, bf16[448,256]{1,0:T(8,128)(2,1)}, u32[]{:S(2)}) copy-start(bf16[448,256]{1,0:T(8,128)(2,1)} %arrange.1.refs_0_) | copy-start | bytes 688132
  63.8 9.1 %collective-permute-start.7 = (bf16[448,256]{1,0:T(8,128)(2,1)}, bf16[448,256]{1,0:T(8,128)(2,1)S(1)}, u32[]{:S(2)}, u32[]{:S(2)}) collective-permute-start(bf16[448,256]{1,0:T(8,128)(2,1)} %arrange.1.refs_0_), channel_id=1, source_target_pairs={{32,0},{64,32},{96,64},{0,96},{33,1},{65,33},{97,65},{1,97},{34,2}... | collective-permute-start | bytes 688136 | tf_op jit(solution)/shard_map/ppermute | solution.py:199
  66.6 7.8 %collective-permute-start.8 = (bf16[448,256]{1,0:T(8,128)(2,1)}, bf16[448,256]{1,0:T(8,128)(2,1)S(1)}, u32[]{:S(2)}, u32[]{:S(2)}) collective-permute-start(bf16[448,256]{1,0:T(8,128)(2,1)} %arrange.1.refs_0_), channel_id=1, source_target_pairs={{64,0},{96,32},{0,64},{32,96},{65,1},{97,33},{1,65},{33,97},{66,2}... | collective-permute-start | bytes 688136 | tf_op jit(solution)/shard_map/ppermute | solution.py:199
  67.4 9.4 %collective-permute-start.9 = (bf16[448,256]{1,0:T(8,128)(2,1)}, bf16[448,256]{1,0:T(8,128)(2,1)S(1)}, u32[]{:S(2)}, u32[]{:S(2)}) collective-permute-start(bf16[448,256]{1,0:T(8,128)(2,1)} %arrange.1.refs_0_), channel_id=1, source_target_pairs={{96,0},{0,32},{32,64},{64,96},{97,1},{1,33},{33,65},{65,97},{98,2}... | collective-permute-start | bytes 688136 | tf_op jit(solution)/shard_map/ppermute | solution.py:199
  68.3 0.9 copy-start.6
  69.3 8.5 %copy-start.1 = (bf16[128,512]{1,0:T(8,128)(2,1)S(1)}, bf16[128,512]{1,0:T(8,128)(2,1)}, u32[]{:S(2)}) copy-start(bf16[128,512]{1,0:T(8,128)(2,1)} %q_ref.1) | copy-start | bytes 393220
  69.3 8.4 %copy-start.2 = (s32[2]{0:T(128)S(1)}, s32[2]{0:T(128)}, u32[]{:S(2)}) copy-start(s32[2]{0:T(128)} %pad_add_fusion.where_ref) | copy-start | bytes 28
  69.4 8.4 %copy-start.3 = (s32[1,16]{1,0:T(1,128)S(1)}, s32[1,16]{1,0:T(1,128)}, u32[]{:S(2)}) copy-start(s32[1,16]{1,0:T(1,128)} %assign_ref.1) | copy-start | bytes 196
  69.4 8.4 %copy-start.4 = (s32[1,4]{1,0:T(1,128)S(1)}, s32[1,4]{1,0:T(1,128)}, u32[]{:S(2)}) copy-start(s32[1,4]{1,0:T(1,128)} %length_ref.1) | copy-start | bytes 52
  77.6 6.5 %collective-permute-start.10 = (bf16[512,256]{1,0:T(8,128)(2,1)S(1)}, bf16[512,256]{1,0:T(8,128)(2,1)S(1)}, u32[]{:S(2)}, u32[]{:S(2)}) collective-permute-start(bf16[512,256]{1,0:T(8,128)(2,1)S(1)} %get-tuple-element.13), channel_id=1, source_target_pairs={{0,128},{128,0},{1,129},{129,1},{2,130},{130,2},{3,131},{131,3},{4... | collective-permute-start | bytes 786440 | tf_op jit(solution)/shard_map/ppermute | solution.py:177
  81.7 4.0 %collective-permute-start.13 = (bf16[128,256]{1,0:T(8,128)(2,1)S(1)}, bf16[128,256]{1,0:T(8,128)(2,1)S(1)}, u32[]{:S(2)}, u32[]{:S(2)}) collective-permute-start(bf16[128,256]{1,0:T(8,128)(2,1)S(1)} %get-tuple-element.15), channel_id=1, source_target_pairs={{0,144},{16,128},{128,16},{144,0},{1,145},{17,129},{129,17},{145,1... | collective-permute-start | bytes 196616 | tf_op jit(solution)/shard_map/ppermute | solution.py:220
  81.8 4.0 %collective-permute-start.12 = (bf16[128,256]{1,0:T(8,128)(2,1)S(1)}, bf16[128,256]{1,0:T(8,128)(2,1)S(1)}, u32[]{:S(2)}, u32[]{:S(2)}) collective-permute-start(bf16[128,256]{1,0:T(8,128)(2,1)S(1)} %get-tuple-element.15), channel_id=1, source_target_pairs={{0,16},{16,0},{1,17},{17,1},{2,18},{18,2},{3,19},{19,3},{4,20},{20... | collective-permute-start | bytes 196616 | tf_op jit(solution)/shard_map/ppermute | solution.py:177
  83.8 4.3 %collective-permute-start.11 = (bf16[128,256]{1,0:T(8,128)(2,1)S(1)}, bf16[128,256]{1,0:T(8,128)(2,1)S(1)}, u32[]{:S(2)}, u32[]{:S(2)}) collective-permute-start(bf16[128,256]{1,0:T(8,128)(2,1)S(1)} %get-tuple-element.14), channel_id=1, source_target_pairs={{0,128},{128,0},{1,129},{129,1},{2,130},{130,2},{3,131},{131,3},{4... | collective-permute-start | bytes 196616 | tf_op jit(solution)/shard_map/ppermute | solution.py:177

commit v5 on v4

v5 whole, which is shorter than its diff:
```python
import math

import jax
import jax.numpy as jnp
from jax import lax
from jax.experimental import pallas as pl
from jax.experimental.pallas import tpu as pltpu
from jax.sharding import Mesh, PartitionSpec as P

HD = 128
HQ = 4
BLK = 128
COLS = HQ * HD
HALF = COLS // 2
TOKENS_ALL = 32768

EPSILON = 1e-06
NEGATIVE = -1e30
LOG2E = math.log2(math.e)

AXES = ("ylo", "x", "core", "z", "yhi")
SIZES = (2, 4, 2, 8, 2)
SEQ = ("z", "yhi")


RING = (0, 1, 2, 3, 4, -3, -2, -1)


def attend_kernel(where_ref, assign_ref, length_ref, q_ref, *refs):
    *kv_refs, out_ref, mine_ref, other_ref, s_ref = refs
    z, yhi, core = where_ref[0], where_ref[1], where_ref[2]
    rows = q_ref.shape[0]
    step = kv_refs[0].shape[0] // 2
    own = assign_ref[0, 2 * z + yhi] * BLK
    first = length_ref[0, 0]
    second = first + length_ref[0, 1]
    third = second + length_ref[0, 2]
    q_pos = own + lax.broadcasted_iota(jnp.int32, (rows, 1), 0)
    q_start = jnp.where(
        q_pos >= third,
        third,
        jnp.where(q_pos >= second, second, jnp.where(q_pos >= first, first, 0)),
    )
    q_all = jnp.concatenate([q_ref[:, h * HD : (h + 1) * HD] for h in range(HQ)], axis=0)
    lane = lax.broadcasted_iota(jnp.int32, (1, BLK), 1)
    chunk = 2 * BLK
    top = None
    for c, (distance, kv_ref) in enumerate(zip(RING, kv_refs)):
        pair = lax.rem(z + distance + 8, 8) * 2
        k_pos = [assign_ref[0, pair + yhi] * BLK + lane, assign_ref[0, pair + 1 - yhi] * BLK + lane]
        k_pos = jnp.concatenate(k_pos, axis=1)
        bias = jnp.where((k_pos >= q_start) & (k_pos <= q_pos), 0.0, NEGATIVE)
        k = jnp.concatenate([kv_ref[:BLK, :HD], kv_ref[step : step + BLK, :HD]], axis=0)
        scores = lax.dot_general(
            q_all, k, (((1,), (1,)), ((), ())), preferred_element_type=jnp.float32
        )
        scores = scores.reshape(HQ, rows, chunk) * (HD ** (-0.5) * LOG2E) + bias[None]
        scores = scores.reshape(HQ * rows, chunk)
        s_ref[:, c * chunk : (c + 1) * chunk] = scores
        best = jnp.max(scores, axis=1, keepdims=True)
        top = best if top is None else jnp.maximum(top, best)
    total = jnp.zeros((HQ * rows, 1), jnp.float32)
    mixture = jnp.zeros((HQ * rows, HD), jnp.float32)
    for c, kv_ref in enumerate(kv_refs):
        terms = jnp.exp2(s_ref[:, c * chunk : (c + 1) * chunk] - top)
        total = total + jnp.sum(terms, axis=1, keepdims=True)
        v = jnp.concatenate([kv_ref[:BLK, HD:], kv_ref[step : step + BLK, HD:]], axis=0)
        mixture = mixture + jnp.dot(
            terms.astype(jnp.bfloat16), v, preferred_element_type=jnp.float32
        )
    result = (mixture / total).astype(jnp.bfloat16)
    for h in range(HQ):
        head = result[h * rows : (h + 1) * rows]
        out_ref[:, h * HD : (h + 1) * HD] = head
        at = h % (HQ // 2) * HD

        @pl.when(core == h // (HQ // 2))
        def _():
            mine_ref[:, at : at + HD] = head

        @pl.when(core != h // (HQ // 2))
        def _():
            other_ref[:, at : at + HD] = head


def attend(here, queries, parts, lengths, assignment):
    rows = queries.shape[0]
    smem = pl.BlockSpec(memory_space=pltpu.SMEM)
    vmem = pl.BlockSpec(memory_space=pltpu.VMEM)
    half = jax.ShapeDtypeStruct((rows, HALF), jnp.bfloat16)
    return pl.pallas_call(
        attend_kernel,
        out_shape=(jax.ShapeDtypeStruct((rows, COLS), jnp.bfloat16), half, half),
        in_specs=[smem, smem, smem, vmem] + [vmem] * len(parts),
        out_specs=(vmem, vmem, vmem),
        scratch_shapes=[pltpu.VMEM((HQ * rows, 16 * BLK), jnp.float32)],
        compiler_params=pltpu.CompilerParams(vmem_limit_bytes=20 << 20),
        name="attend",
    )(here, assignment, lengths, queries, *parts)


def arrange_kernel(where_ref, *refs):
    *parts, out_ref, held = refs
    z, yhi, core = where_ref[0], where_ref[1], where_ref[2]
    wrows = out_ref.shape[0] // 32
    step = parts[0].shape[0] // 2
    for distance, part in zip(RING, parts):
        pair = lax.rem(z + distance + 8, 8) * 2
        for t in range(2):
            slot = pair + (yhi if t == 0 else 1 - yhi)
            for c in range(2):
                first = t * step + BLK + 16 * c
                held[lax.bitwise_xor(core, c), slot] = part[first : first + 16, :]
    for c in range(2):
        for s in range(16):
            first = (c * 16 + s) * wrows
            out_ref[first : first + wrows, :] = held[c, s, :wrows]


def arrange(here, parts, wrows):
    vmem = pl.BlockSpec(memory_space=pltpu.VMEM)
    return pl.pallas_call(
        arrange_kernel,
        out_shape=jax.ShapeDtypeStruct((32 * wrows, HALF), jnp.bfloat16),
        in_specs=[pl.BlockSpec(memory_space=pltpu.SMEM)] + [vmem] * len(parts),
        out_specs=vmem,
        scratch_shapes=[pltpu.VMEM((2, 16, 16, HALF), jnp.bfloat16)],
        compiler_params=pltpu.CompilerParams(vmem_limit_bytes=8 << 20),
        name="arrange",
    )(here, *parts)


def project_kernel(where_ref, n_ref, mine_ref, got_ref, *refs):
    *w_refs, own_ref, send_ref, w_all = refs
    x = where_ref[0]
    step = w_refs[0].shape[0]
    for d, w_ref in enumerate(w_refs):
        at = lax.rem(x + d, len(w_refs)) * step
        w_all[pl.ds(pl.multiple_of(at, step), step), :] = w_ref[...]
    rows = n_ref.shape[0] // 4
    for b in range(4):
        part = jnp.dot(
            n_ref[b * rows : (b + 1) * rows, :], w_all[...], preferred_element_type=jnp.float32
        )
        if b % 2 == 0:
            part = part - (mine_ref, got_ref)[b // 2][...].astype(jnp.float32)
        own_ref[b * rows : (b + 1) * rows, :] = part
        t = b ^ 1
        send_ref[t * rows : (t + 1) * rows, :] = part.astype(jnp.bfloat16)


def project(n_all, pieces, a_mine, a_got):
    here = jnp.stack([lax.axis_index("x")]).astype(jnp.int32)
    vmem = pl.BlockSpec(memory_space=pltpu.VMEM)
    shape = (n_all.shape[0], HALF)
    return pl.pallas_call(
        project_kernel,
        out_shape=(
            jax.ShapeDtypeStruct(shape, jnp.float32),
            jax.ShapeDtypeStruct(shape, jnp.bfloat16),
        ),
        in_specs=[pl.BlockSpec(memory_space=pltpu.SMEM)] + [vmem] * (3 + len(pieces)),
        out_specs=(vmem, vmem),
        scratch_shapes=[pltpu.VMEM((n_all.shape[1], HALF), jnp.bfloat16)],
        compiler_params=pltpu.CompilerParams(vmem_limit_bytes=12 << 20),
        name="project",
    )(here, n_all, a_mine, a_got, *pieces)


def halves(x, which):
    half = x.shape[1] // 2
    low, high = x[:, :half], x[:, half:]
    return jnp.where(which == 0, low, high), jnp.where(which == 0, high, low)


def partner(x, axis, mask):
    size = SIZES[AXES.index(axis)]
    return lax.ppermute(x, axis, [(i, i ^ mask) for i in range(size)])


def from_next(x, axis, distance):
    size = SIZES[AXES.index(axis)]
    return lax.ppermute(x, axis, [((i + distance) % size, i) for i in range(size)])


def local(student_in, weight, queries, keys, values, lengths, assignment):
    rows = queries.shape[0]
    core = lax.axis_index("core")
    ylo = lax.axis_index("ylo")
    wrows = weight.shape[0]

    here = jnp.stack([lax.axis_index("z"), lax.axis_index("yhi"), core]).astype(jnp.int32)
    w_mine, w_other = halves(weight, core)
    w_got = partner(w_other, "core", 1)
    kv = jnp.concatenate([keys, values], axis=1)
    pad = jnp.zeros((16 - wrows, HALF), jnp.bfloat16)
    packed = jnp.concatenate([kv, w_mine, pad, w_got, pad], axis=0)
    packed = jnp.concatenate([packed, partner(packed, "yhi", 1)], axis=0)
    up = down = packed
    held = {0: packed}
    for d in range(1, 5):
        up = from_next(up, "z", 1)
        held[d] = up
        if d < 4:
            down = from_next(down, "z", -1)
            held[-d] = down
    parts = [held[d] for d in RING]
    w_near = arrange(here, parts, wrows)
    pieces = [w_near] + [from_next(w_near, "x", d) for d in range(1, 4)]

    student_in, _ = lax.optimization_barrier((student_in, (held[1], held[-1])))
    as_float = student_in.astype(jnp.float32)
    normed = (
        as_float * lax.rsqrt(jnp.mean(as_float * as_float, axis=1, keepdims=True) + EPSILON)
    ).astype(jnp.bfloat16)
    n_keep, n_send = halves(normed, ylo)
    n_got, _ = lax.optimization_barrier((partner(n_send, "ylo", 1), w_near))
    n_pair = jnp.concatenate([n_keep, n_got], axis=0)
    n_all = jnp.concatenate([n_pair, partner(n_pair, "core", 1)], axis=0)

    parts, _ = lax.optimization_barrier((parts, w_near))
    attention, a_mine, a_other = attend(here, queries, parts, lengths, assignment)

    own, send = project(n_all, pieces, a_mine, partner(a_other, "core", 1))
    diff = own + partner(send, "ylo", 1).astype(jnp.float32)
    scaled = (diff * TOKENS_ALL ** (-0.5)).astype(jnp.bfloat16)
    part = lax.dot_general(
        n_all, scaled, (((0,), (0,)), ((), ())), preferred_element_type=jnp.float32
    ).astype(jnp.bfloat16)
    part = part.reshape(4, -1, HALF)
    x = lax.axis_index("x")
    near = lax.dynamic_index_in_dim(part, x, 0, keepdims=False).astype(jnp.float32)
    for d in range(1, 4):
        away = lax.dynamic_index_in_dim(part, (x - d) % 4, 0, keepdims=False)
        near = near + from_next(away, "x", d).astype(jnp.float32)
    near = near.astype(jnp.bfloat16).reshape(-1, wrows, HALF)
    near = jnp.pad(near, ((0, 0), (0, 16 - wrows), (0, 0)))
    last = lax.all_to_all(near, ("core", *SEQ), split_axis=0, concat_axis=0, tiled=True)
    summed = last.reshape(2, 16, 16, HALF).astype(jnp.float32).sum(axis=1)
    weight_grad = jnp.concatenate([summed[0, :wrows], summed[1, :wrows]], axis=1)
    return (attention, weight_grad)


def solution(mesh):
    mesh = Mesh(mesh.devices.reshape(SIZES), AXES)
    token = P(AXES, None)
    row = P(("ylo", "x", "core"), None)
    return jax.shard_map(
        local,
        mesh=mesh,
        in_specs=(token, token, token, token, token, row, row),
        out_specs=(token, token),
        check_vma=False,
    )
```

time: 127 us -> 105 us (0.83)
  blocking collectives: 34.7 us -> 22.6 us
  starting transfers between devices: 28.8 us -> 24.6 us
  waiting for transfers between devices: 45.1 us -> 43.6 us
  Pallas kernels: 6.64 us -> 5.15 us
    ppermute x10 -> x6, waiting for transfers between devices: 36 us -> 10.9 us  [partner(): return lax.ppermute(x, axis, [(i, i ^ mask) for i in range(size)])]
    ppermute x4 -> x13, waiting for transfers between devices: 9.17 us -> 32.7 us  [from_next(): lax.ppermute(x, axis, [((i + distance) % size, i) for i in range(size)])]
    all_to_all x1 -> x0, blocking collectives: 15.4 us -> none  [local(): lax.all_to_all(part.reshape(4, -1, HALF), 'x', split_axis=0, concat_axis=...]
    ppermute x4 -> x13, starting transfers between devices: 4.45 us -> 18 us  [from_next(): lax.ppermute(x, axis, [((i + distance) % size, i) for i in range(size)])]
    all_to_all x1 -> x0, starting transfers between devices: 10.9 us -> none  [local(): lax.all_to_all(kv_copies, SEQ, split_axis=0, concat_axis=0, tiled=True)]
    ppermute x10 -> x6, starting transfers between devices: 13.4 us -> 6.59 us  [partner(): return lax.ppermute(x, axis, [(i, i ^ mask) for i in range(size)])]
    all_to_all x1, blocking collectives: 19.3 us -> 22.6 us  [local(): lax.all_to_all(near, ('core', *SEQ), split_axis=0, concat_axis=0, tiled=T...]
    another operation x2 -> x1, other arithmetic: 1.42 us -> 0.08 us  [local(): jnp.stack([lax.axis_index('z'), lax.axis_index('yhi'), core])]
  transfers between devices with their start and end apart: 15 -> 19, of which waited for: 11 -> 14; matrix products, arithmetic and copies ran while one was open for 2% -> 2% of each run, Pallas kernels for 5% -> 4%
where the time goes in v5:
time: 105 us; the launch traced here: 104 us
  waiting for transfers between devices  43.6 us (42%)
  starting transfers between devices  24.6 us (23%)
  blocking collectives  22.6 us (22%)
  Pallas kernels  5.15 us (5%)
  other arithmetic  4.51 us (4%)
  local copies, waits for them, and re-layouts  1.82 us (2%)
    ppermute x13, waiting for transfers between devices, from_next(): lax.ppermute(x, axis, [((i + distance) % size, i) for i in range(size)])  32.7 us
    all_to_all x1, blocking collectives, local(): lax.all_to_all(near, ('core', *SEQ), split_axis=0, concat_axis=0, tiled=T...  22.6 us
    ppermute x13, starting transfers between devices, from_next(): lax.ppermute(x, axis, [((i + distance) % size, i) for i in range(size)])  18 us
    ppermute x6, waiting for transfers between devices, partner(): return lax.ppermute(x, axis, [(i, i ^ mask) for i in range(size)])  10.9 us
    ppermute x6, starting transfers between devices, partner(): return lax.ppermute(x, axis, [(i, i ^ mask) for i in range(size)])  6.59 us
    pallas_call x1, Pallas kernels, attend(): pl.pallas_call(attend_kernel, out_shape=(jax.ShapeDtypeStruct((rows, COLS...  3.76 us
  transfers between devices with their start and end apart: 19, of which 14 were waited for; matrix products, arithmetic and copies ran while one was open for 2% of the time, Pallas kernels for 4%

profile of v5, /device:TPU:32, one launch (start us, length us, event | category | flops | bytes accessed | tf_op | source)
XLA Modules:
  0.0 103.8 jit_solution(11726148316862837845)
XLA Ops:
  0.6 0.0 copy-start.3
  0.6 0.8 broadcast_select_fusion.2
  1.4 0.0 collective-permute-start
  1.5 0.8 constant_dynamic-update-slice_fusion.1
  2.2 0.8 constant_dynamic-update-slice_fusion
  3.0 0.0 collective-permute-done
  3.0 0.1 concatenate.21
  3.1 3.3 %collective-permute-start.1 = (bf16[160,256]{1,0:T(8,128)(2,1)S(1)}, bf16[160,256]{1,0:T(8,128)(2,1)S(1)}, u32[]{:S(2)}, u32[]{:S(2)}) collective-permute-start(bf16[160,256]{1,0:T(8,128)(2,1)S(1)} %concatenate.21), channel_id=1, source_target_pairs={{0,1},{1,0},{2,3},{3,2},{4,5},{5,4},{6,7},{7,6},{8,9},{9,8},{10,11... | collective-permute-start | bytes 245768 | tf_op jit(solution)/shard_map/ppermute | solution.py:178
  6.3 3.2 %collective-permute-done.1 = bf16[160,256]{1,0:T(8,128)(2,1)S(1)} collective-permute-done((bf16[160,256]{1,0:T(8,128)(2,1)S(1)}, bf16[160,256]{1,0:T(8,128)(2,1)S(1)}, u32[]{:S(2)}, u32[]{:S(2)}) %collective-permute-start.1) | collective-permute-done | bytes 81952 | tf_op jit(solution)/shard_map/ppermute | solution.py:178
  9.5 1.9 %collective-permute-start.2 = (bf16[320,256]{1,0:T(8,128)(2,1)S(1)}, bf16[320,256]{1,0:T(8,128)(2,1)S(1)}, u32[]{:S(2)}, u32[]{:S(2)}) collective-permute-start(bf16[320,256]{1,0:T(8,128)(2,1)S(1)} %concatenate.22.refs_0_), channel_id=1, source_target_pairs={{2,0},{4,2},{6,4},{8,6},{10,8},{12,10},{14,12},{0,14},{3,1},{5,3},... | collective-permute-start | bytes 491528 | tf_op jit(solution)/shard_map/ppermute | solution.py:183
  11.4 0.2 collective-permute-start.6
  11.6 4.0 %collective-permute-done.2.refs_1_ = bf16[320,256]{1,0:T(8,128)(2,1)S(1)} collective-permute-done((bf16[320,256]{1,0:T(8,128)(2,1)S(1)}, bf16[320,256]{1,0:T(8,128)(2,1)S(1)}, u32[]{:S(2)}, u32[]{:S(2)}) %collective-permute-start.2) | collective-permute-done | bytes 163872 | tf_op jit(solution)/shard_map/ppermute | solution.py:183
  15.6 3.8 %collective-permute-done.6.refs_7_ = bf16[320,256]{1,0:T(8,128)(2,1)S(1)} collective-permute-done((bf16[320,256]{1,0:T(8,128)(2,1)S(1)}, bf16[320,256]{1,0:T(8,128)(2,1)S(1)}, u32[]{:S(2)}, u32[]{:S(2)}) %collective-permute-start.6) | collective-permute-done | bytes 163872 | tf_op jit(solution)/shard_map/ppermute | solution.py:183
  19.4 1.4 %fusion = f32[128]{0:T(128)S(1)} fusion(bf16[128,3584]{1,0:T(8,128)(2,1)} %param.7), kind=kLoop, calls=%fused_computation.3 | loop fusion | flops 1376128 | bytes 918016 | tf_op jit(solution)/shard_map/reduce_sum | solution.py:214
  20.8 0.0 copy-done.3
  20.8 0.2 fusion.1
  21.1 3.0 %collective-permute-start.3 = (bf16[320,256]{1,0:T(8,128)(2,1)S(1)}, bf16[320,256]{1,0:T(8,128)(2,1)S(1)}, u32[]{:S(2)}, u32[]{:S(2)}) collective-permute-start(bf16[320,256]{1,0:T(8,128)(2,1)S(1)} %collective-permute-done.2.refs_1_), channel_id=1, source_target_pairs={{2,0},{4,2},{6,4},{8,6},{10,8},{12,10},{14,12},{0,14},{3,1},{5,3},... | collective-permute-start | bytes 491528 | tf_op jit(solution)/shard_map/ppermute | solution.py:183
  24.1 0.1 broadcast_select_fusion.1
  24.2 0.0 copy-start
  24.2 0.0 copy-start.1
  24.2 0.0 copy-start.2
  24.2 1.7 %collective-permute-start.9 = (bf16[128,1792]{1,0:T(8,128)(2,1)S(1)}, bf16[128,1792]{1,0:T(8,128)(2,1)S(1)}, u32[]{:S(2)}, u32[]{:S(2)}) collective-permute-start(bf16[128,1792]{1,0:T(8,128)(2,1)S(1)} %get-tuple-element.36), channel_id=1, source_target_pairs={{0,128},{128,0},{1,129},{129,1},{2,130},{130,2},{3,131},{131,3},{4... | collective-permute-start | bytes 1376264 | tf_op jit(solution)/shard_map/ppermute | solution.py:178
  25.9 0.0 collective-permute-start.7
  25.9 1.1 %collective-permute-done.3.refs_2_ = bf16[320,256]{1,0:T(8,128)(2,1)S(1)} collective-permute-done((bf16[320,256]{1,0:T(8,128)(2,1)S(1)}, bf16[320,256]{1,0:T(8,128)(2,1)S(1)}, u32[]{:S(2)}, u32[]{:S(2)}) %collective-permute-start.3) | collective-permute-done | bytes 163872 | tf_op jit(solution)/shard_map/ppermute | solution.py:183
  26.9 2.5 %collective-permute-start.4 = (bf16[320,256]{1,0:T(8,128)(2,1)S(1)}, bf16[320,256]{1,0:T(8,128)(2,1)S(1)}, u32[]{:S(2)}, u32[]{:S(2)}) collective-permute-start(bf16[320,256]{1,0:T(8,128)(2,1)S(1)} %collective-permute-done.3.refs_2_), channel_id=1, source_target_pairs={{2,0},{4,2},{6,4},{8,6},{10,8},{12,10},{14,12},{0,14},{3,1},{5,3},... | collective-permute-start | bytes 491528 | tf_op jit(solution)/shard_map/ppermute | solution.py:183
  29.4 2.0 %collective-permute-done.7.refs_6_ = bf16[320,256]{1,0:T(8,128)(2,1)S(1)} collective-permute-done((bf16[320,256]{1,0:T(8,128)(2,1)S(1)}, bf16[320,256]{1,0:T(8,128)(2,1)S(1)}, u32[]{:S(2)}, u32[]{:S(2)}) %collective-permute-start.7) | collective-permute-done | bytes 163872 | tf_op jit(solution)/shard_map/ppermute | solution.py:183
  31.4 0.0 collective-permute-start.8
  31.4 1.7 %collective-permute-done.4.refs_3_ = bf16[320,256]{1,0:T(8,128)(2,1)S(1)} collective-permute-done((bf16[320,256]{1,0:T(8,128)(2,1)S(1)}, bf16[320,256]{1,0:T(8,128)(2,1)S(1)}, u32[]{:S(2)}, u32[]{:S(2)}) %collective-permute-start.4) | collective-permute-done | bytes 163872 | tf_op jit(solution)/shard_map/ppermute | solution.py:183
  33.1 2.5 %collective-permute-start.5 = (bf16[320,256]{1,0:T(8,128)(2,1)S(1)}, bf16[320,256]{1,0:T(8,128)(2,1)S(1)}, u32[]{:S(2)}, u32[]{:S(2)}) collective-permute-start(bf16[320,256]{1,0:T(8,128)(2,1)S(1)} %collective-permute-done.4.refs_3_), channel_id=1, source_target_pairs={{2,0},{4,2},{6,4},{8,6},{10,8},{12,10},{14,12},{0,14},{3,1},{5,3},... | collective-permute-start | bytes 491528 | tf_op jit(solution)/shard_map/ppermute | solution.py:183
  35.6 0.1 pad_add_fusion.where_ref
  35.7 1.1 %collective-permute-done.8.refs_5_ = bf16[320,256]{1,0:T(8,128)(2,1)S(1)} collective-permute-done((bf16[320,256]{1,0:T(8,128)(2,1)S(1)}, bf16[320,256]{1,0:T(8,128)(2,1)S(1)}, u32[]{:S(2)}, u32[]{:S(2)}) %collective-permute-start.8) | collective-permute-done | bytes 163872 | tf_op jit(solution)/shard_map/ppermute | solution.py:183
  36.7 1.7 %collective-permute-done.5.refs_4_ = bf16[320,256]{1,0:T(8,128)(2,1)S(1)} collective-permute-done((bf16[320,256]{1,0:T(8,128)(2,1)S(1)}, bf16[320,256]{1,0:T(8,128)(2,1)S(1)}, u32[]{:S(2)}, u32[]{:S(2)}) %collective-permute-start.5) | collective-permute-done | bytes 163872 | tf_op jit(solution)/shard_map/ppermute | solution.py:183
  38.4 0.6 arrange.1.refs_0_
  39.1 0.0 collective-permute-done.9
  39.1 1.0 pad_maximum_fusion.1
  40.1 0.0 collective-permute-start.10
  40.1 2.8 %collective-permute-start.12 = (bf16[448,256]{1,0:T(8,128)(2,1)S(1)}, bf16[448,256]{1,0:T(8,128)(2,1)S(1)}, u32[]{:S(2)}, u32[]{:S(2)}) collective-permute-start(bf16[448,256]{1,0:T(8,128)(2,1)S(1)} %arrange.1.refs_0_), channel_id=1, source_target_pairs={{32,0},{64,32},{96,64},{0,96},{33,1},{65,33},{97,65},{1,97},{34,2}... | collective-permute-start | bytes 688136 | tf_op jit(solution)/shard_map/ppermute | solution.py:183
  42.8 0.8 collective-permute-start.13
  43.6 0.9 collective-permute-start.14
  44.5 0.0 copy-done
  44.5 0.0 copy-done.1
  44.5 3.8 %attend.1 = (bf16[128,512]{1,0:T(8,128)(2,1)}, bf16[128,256]{1,0:T(8,128)(2,1)S(1)}, bf16[128,256]{1,0:T(8,128)(2,1)S(1)}) custom-call(s32[3]{0:T(128)S(1)} %pad_add_fusion.where_ref, s32[1,16]{1,0:T(1,128)S(1)} %copy-done.1, s32[1,4]{1,0:T(1,128)S(1)} %copy-done.2, bf16[128,512]{1,0:T(8,128)(2,1)S(1)} %copy-done, bf16[320,256]{1,0:T(8,128)(2,1)S(1)} %concatenate.22.refs_0_, ...), custom_call_target="tpu_custom_call" | custom-call | tf_op jit(solution)/shard_map/attend/pallas_call | solution.py:91
  48.3 0.0 collective-permute-start.11
  48.3 0.0 collective-permute-done.10
  48.3 0.1 pad_maximum_fusion.n_ref
  48.4 1.1 %collective-permute-done.11.got_ref = bf16[128,256]{1,0:T(8,128)(2,1)S(1)} collective-permute-done((bf16[128,256]{1,0:T(8,128)(2,1)S(1)}, bf16[128,256]{1,0:T(8,128)(2,1)S(1)}, u32[]{:S(2)}, u32[]{:S(2)}) %collective-permute-start.11) | collective-permute-done | bytes 65568 | tf_op jit(solution)/shard_map/ppermute | solution.py:178
  49.6 3.8 %collective-permute-done.12.refs_1_ = bf16[448,256]{1,0:T(8,128)(2,1)S(1)} collective-permute-done((bf16[448,256]{1,0:T(8,128)(2,1)S(1)}, bf16[448,256]{1,0:T(8,128)(2,1)S(1)}, u32[]{:S(2)}, u32[]{:S(2)}) %collective-permute-start.12) | collective-permute-done | bytes 229408 | tf_op jit(solution)/shard_map/ppermute | solution.py:183
  53.3 0.0 collective-permute-done.13.refs_2_
  53.3 3.7 %collective-permute-done.14.refs_3_ = bf16[448,256]{1,0:T(8,128)(2,1)S(1)} collective-permute-done((bf16[448,256]{1,0:T(8,128)(2,1)S(1)}, bf16[448,256]{1,0:T(8,128)(2,1)S(1)}, u32[]{:S(2)}, u32[]{:S(2)}) %collective-permute-start.14) | collective-permute-done | bytes 229408 | tf_op jit(solution)/shard_map/ppermute | solution.py:183
  57.0 0.8 project.1
  57.8 1.7 %collective-permute-start.15 = (bf16[512,256]{1,0:T(8,128)(2,1)S(1)}, bf16[512,256]{1,0:T(8,128)(2,1)S(1)}, u32[]{:S(2)}, u32[]{:S(2)}) collective-permute-start(bf16[512,256]{1,0:T(8,128)(2,1)S(1)} %get-tuple-element.31), channel_id=1, source_target_pairs={{0,128},{128,0},{1,129},{129,1},{2,130},{130,2},{3,131},{131,3},{4... | collective-permute-start | bytes 786440 | tf_op jit(solution)/shard_map/ppermute | solution.py:178
  59.4 6.6 %collective-permute-done.15 = bf16[512,256]{1,0:T(8,128)(2,1)S(1)} collective-permute-done((bf16[512,256]{1,0:T(8,128)(2,1)S(1)}, bf16[512,256]{1,0:T(8,128)(2,1)S(1)}, u32[]{:S(2)}, u32[]{:S(2)}) %collective-permute-start.15) | collective-permute-done | bytes 262176 | tf_op jit(solution)/shard_map/ppermute | solution.py:178
  66.1 0.7 convolution_convert_fusion
  66.8 0.1 dynamic-slice_bitcast_fusion.2
  66.8 0.1 collective-permute-start.18
  66.9 1.5 %collective-permute-start.17 = (bf16[448,256]{1,0:T(8,128)(2,1)S(1)}, bf16[448,256]{1,0:T(8,128)(2,1)S(1)}, u32[]{:S(2)}, u32[]{:S(2)}) collective-permute-start(bf16[448,256]{1,0:T(8,128)(2,1)S(1)} %get-tuple-element.34), channel_id=1, source_target_pairs={{64,0},{96,32},{0,64},{32,96},{65,1},{97,33},{1,65},{33,97},{66,2}... | collective-permute-start | bytes 688136 | tf_op jit(solution)/shard_map/ppermute | solution.py:183
  68.4 2.0 %collective-permute-start.16 = (bf16[448,256]{1,0:T(8,128)(2,1)S(1)}, bf16[448,256]{1,0:T(8,128)(2,1)S(1)}, u32[]{:S(2)}, u32[]{:S(2)}) collective-permute-start(bf16[448,256]{1,0:T(8,128)(2,1)S(1)} %get-tuple-element.32), channel_id=1, source_target_pairs={{32,0},{64,32},{96,64},{0,96},{33,1},{65,33},{97,65},{1,97},{34,2}... | collective-permute-start | bytes 688136 | tf_op jit(solution)/shard_map/ppermute | solution.py:183
  70.4 9.4 %collective-permute-done.18 = bf16[448,256]{1,0:T(8,128)(2,1)S(1)} collective-permute-done((bf16[448,256]{1,0:T(8,128)(2,1)S(1)}, bf16[448,256]{1,0:T(8,128)(2,1)S(1)}, u32[]{:S(2)}, u32[]{:S(2)}) %collective-permute-start.18) | collective-permute-done | bytes 229408 | tf_op jit(solution)/shard_map/ppermute | solution.py:183
  79.7 0.0 collective-permute-done.17
  79.7 0.6 collective-permute-done.16
  80.3 0.1 fusion.4
  80.5 0.1 reshape.24
  80.6 22.6 %all_to_all.5 = bf16[32,16,256]{2,1,0:T(8,128)(2,1)S(1)} all-to-all(bf16[32,16,256]{2,1,0:T(8,128)(2,1)S(1)} %pad.4), channel_id=1, replica_groups=mesh['ylo'=2,'x'=4,'core'=2,'z'=8,'yhi'=2] {'core','z','yhi'}, dimensions={0} | all-to-all | bytes 524288 | tf_op jit(solution)/shard_map/all_to_all | solution.py:238
  103.2 0.6 pad_maximum_fusion.2
  (7 shorter events, 0.1 us)
Async XLA Ops:
  0.6 20.2 %copy-start.3 = (bf16[128,3584]{1,0:T(8,128)(2,1)S(1)}, bf16[128,3584]{1,0:T(8,128)(2,1)}, u32[]{:S(2)}) copy-start(bf16[128,3584]{1,0:T(8,128)(2,1)} %param.7) | copy-start | bytes 2752516
  1.4 1.5 %collective-permute-start = (bf16[14,256]{1,0:T(8,128)(2,1)S(1)}, bf16[14,256]{1,0:T(8,128)(2,1)S(1)}, u32[]{:S(2)}, u32[]{:S(2)}) collective-permute-start(bf16[14,256]{1,0:T(8,128)(2,1)S(1)} %get-tuple-element.39), channel_id=1, source_target_pairs={{0,16},{16,0},{1,17},{17,1},{2,18},{18,2},{3,19},{19,3},{4,20},{20... | collective-permute-start | bytes 21512 | tf_op jit(solution)/shard_map/ppermute | solution.py:178
  3.1 6.4 %collective-permute-start.1 = (bf16[160,256]{1,0:T(8,128)(2,1)S(1)}, bf16[160,256]{1,0:T(8,128)(2,1)S(1)}, u32[]{:S(2)}, u32[]{:S(2)}) collective-permute-start(bf16[160,256]{1,0:T(8,128)(2,1)S(1)} %concatenate.21), channel_id=1, source_target_pairs={{0,1},{1,0},{2,3},{3,2},{4,5},{5,4},{6,7},{7,6},{8,9},{9,8},{10,11... | collective-permute-start | bytes 245768 | tf_op jit(solution)/shard_map/ppermute | solution.py:178
  9.5 6.1 %collective-permute-start.2 = (bf16[320,256]{1,0:T(8,128)(2,1)S(1)}, bf16[320,256]{1,0:T(8,128)(2,1)S(1)}, u32[]{:S(2)}, u32[]{:S(2)}) collective-permute-start(bf16[320,256]{1,0:T(8,128)(2,1)S(1)} %concatenate.22.refs_0_), channel_id=1, source_target_pairs={{2,0},{4,2},{6,4},{8,6},{10,8},{12,10},{14,12},{0,14},{3,1},{5,3},... | collective-permute-start | bytes 491528 | tf_op jit(solution)/shard_map/ppermute | solution.py:183
  11.4 7.9 %collective-permute-start.6 = (bf16[320,256]{1,0:T(8,128)(2,1)S(1)}, bf16[320,256]{1,0:T(8,128)(2,1)S(1)}, u32[]{:S(2)}, u32[]{:S(2)}) collective-permute-start(bf16[320,256]{1,0:T(8,128)(2,1)S(1)} %concatenate.22.refs_0_), channel_id=1, source_target_pairs={{14,0},{0,2},{2,4},{4,6},{6,8},{8,10},{10,12},{12,14},{15,1},{1,3}... | collective-permute-start | bytes 491528 | tf_op jit(solution)/shard_map/ppermute | solution.py:183
  21.1 5.9 %collective-permute-start.3 = (bf16[320,256]{1,0:T(8,128)(2,1)S(1)}, bf16[320,256]{1,0:T(8,128)(2,1)S(1)}, u32[]{:S(2)}, u32[]{:S(2)}) collective-permute-start(bf16[320,256]{1,0:T(8,128)(2,1)S(1)} %collective-permute-done.2.refs_1_), channel_id=1, source_target_pairs={{2,0},{4,2},{6,4},{8,6},{10,8},{12,10},{14,12},{0,14},{3,1},{5,3},... | collective-permute-start | bytes 491528 | tf_op jit(solution)/shard_map/ppermute | solution.py:183
  24.2 20.4 %copy-start = (bf16[128,512]{1,0:T(8,128)(2,1)S(1)}, bf16[128,512]{1,0:T(8,128)(2,1)}, u32[]{:S(2)}) copy-start(bf16[128,512]{1,0:T(8,128)(2,1)} %q_ref.1) | copy-start | bytes 393220
  24.2 20.4 %copy-start.1 = (s32[1,16]{1,0:T(1,128)S(1)}, s32[1,16]{1,0:T(1,128)}, u32[]{:S(2)}) copy-start(s32[1,16]{1,0:T(1,128)} %assign_ref.1) | copy-start | bytes 196
  24.2 20.4 %copy-start.2 = (s32[1,4]{1,0:T(1,128)S(1)}, s32[1,4]{1,0:T(1,128)}, u32[]{:S(2)}) copy-start(s32[1,4]{1,0:T(1,128)} %length_ref.1) | copy-start | bytes 52
  24.2 14.9 %collective-permute-start.9 = (bf16[128,1792]{1,0:T(8,128)(2,1)S(1)}, bf16[128,1792]{1,0:T(8,128)(2,1)S(1)}, u32[]{:S(2)}, u32[]{:S(2)}) collective-permute-start(bf16[128,1792]{1,0:T(8,128)(2,1)S(1)} %get-tuple-element.36), channel_id=1, source_target_pairs={{0,128},{128,0},{1,129},{129,1},{2,130},{130,2},{3,131},{131,3},{4... | collective-permute-start | bytes 1376264 | tf_op jit(solution)/shard_map/ppermute | solution.py:178
  25.9 5.6 %collective-permute-start.7 = (bf16[320,256]{1,0:T(8,128)(2,1)S(1)}, bf16[320,256]{1,0:T(8,128)(2,1)S(1)}, u32[]{:S(2)}, u32[]{:S(2)}) collective-permute-start(bf16[320,256]{1,0:T(8,128)(2,1)S(1)} %collective-permute-done.6.refs_7_), channel_id=1, source_target_pairs={{14,0},{0,2},{2,4},{4,6},{6,8},{8,10},{10,12},{12,14},{15,1},{1,3}... | collective-permute-start | bytes 491528 | tf_op jit(solution)/shard_map/ppermute | solution.py:183
  26.9 6.2 %collective-permute-start.4 = (bf16[320,256]{1,0:T(8,128)(2,1)S(1)}, bf16[320,256]{1,0:T(8,128)(2,1)S(1)}, u32[]{:S(2)}, u32[]{:S(2)}) collective-permute-start(bf16[320,256]{1,0:T(8,128)(2,1)S(1)} %collective-permute-done.3.refs_2_), channel_id=1, source_target_pairs={{2,0},{4,2},{6,4},{8,6},{10,8},{12,10},{14,12},{0,14},{3,1},{5,3},... | collective-permute-start | bytes 491528 | tf_op jit(solution)/shard_map/ppermute | solution.py:183
  31.4 5.3 %collective-permute-start.8 = (bf16[320,256]{1,0:T(8,128)(2,1)S(1)}, bf16[320,256]{1,0:T(8,128)(2,1)S(1)}, u32[]{:S(2)}, u32[]{:S(2)}) collective-permute-start(bf16[320,256]{1,0:T(8,128)(2,1)S(1)} %collective-permute-done.7.refs_6_), channel_id=1, source_target_pairs={{14,0},{0,2},{2,4},{4,6},{6,8},{8,10},{10,12},{12,14},{15,1},{1,3}... | collective-permute-start | bytes 491528 | tf_op jit(solution)/shard_map/ppermute | solution.py:183
  33.1 5.3 %collective-permute-start.5 = (bf16[320,256]{1,0:T(8,128)(2,1)S(1)}, bf16[320,256]{1,0:T(8,128)(2,1)S(1)}, u32[]{:S(2)}, u32[]{:S(2)}) collective-permute-start(bf16[320,256]{1,0:T(8,128)(2,1)S(1)} %collective-permute-done.4.refs_3_), channel_id=1, source_target_pairs={{2,0},{4,2},{6,4},{8,6},{10,8},{12,10},{14,12},{0,14},{3,1},{5,3},... | collective-permute-start | bytes 491528 | tf_op jit(solution)/shard_map/ppermute | solution.py:183
  40.1 8.2 %collective-permute-start.10 = (bf16[256,1792]{1,0:T(8,128)(2,1)}, bf16[256,1792]{1,0:T(8,128)(2,1)S(1)}, u32[]{:S(2)}, u32[]{:S(2)}) collective-permute-start(bf16[256,1792]{1,0:T(8,128)(2,1)} %pad_maximum_fusion.1), channel_id=1, source_target_pairs={{0,16},{16,0},{1,17},{17,1},{2,18},{18,2},{3,19},{19,3},{4,20},{20... | collective-permute-start | bytes 2752520 | tf_op jit(solution)/shard_map/ppermute | solution.py:178
  40.1 13.2 %collective-permute-start.12 = (bf16[448,256]{1,0:T(8,128)(2,1)S(1)}, bf16[448,256]{1,0:T(8,128)(2,1)S(1)}, u32[]{:S(2)}, u32[]{:S(2)}) collective-permute-start(bf16[448,256]{1,0:T(8,128)(2,1)S(1)} %arrange.1.refs_0_), channel_id=1, source_target_pairs={{32,0},{64,32},{96,64},{0,96},{33,1},{65,33},{97,65},{1,97},{34,2}... | collective-permute-start | bytes 688136 | tf_op jit(solution)/shard_map/ppermute | solution.py:183
  42.8 10.5 %collective-permute-start.13 = (bf16[448,256]{1,0:T(8,128)(2,1)S(1)}, bf16[448,256]{1,0:T(8,128)(2,1)S(1)}, u32[]{:S(2)}, u32[]{:S(2)}) collective-permute-start(bf16[448,256]{1,0:T(8,128)(2,1)S(1)} %arrange.1.refs_0_), channel_id=1, source_target_pairs={{64,0},{96,32},{0,64},{32,96},{65,1},{97,33},{1,65},{33,97},{66,2}... | collective-permute-start | bytes 688136 | tf_op jit(solution)/shard_map/ppermute | solution.py:183
  43.6 13.4 %collective-permute-start.14 = (bf16[448,256]{1,0:T(8,128)(2,1)S(1)}, bf16[448,256]{1,0:T(8,128)(2,1)S(1)}, u32[]{:S(2)}, u32[]{:S(2)}) collective-permute-start(bf16[448,256]{1,0:T(8,128)(2,1)S(1)} %arrange.1.refs_0_), channel_id=1, source_target_pairs={{96,0},{0,32},{32,64},{64,96},{97,1},{1,33},{33,65},{65,97},{98,2}... | collective-permute-start | bytes 688136 | tf_op jit(solution)/shard_map/ppermute | solution.py:183
  48.3 1.3 %collective-permute-start.11 = (bf16[128,256]{1,0:T(8,128)(2,1)S(1)}, bf16[128,256]{1,0:T(8,128)(2,1)S(1)}, u32[]{:S(2)}, u32[]{:S(2)}) collective-permute-start(bf16[128,256]{1,0:T(8,128)(2,1)S(1)} %get-tuple-element.29), channel_id=1, source_target_pairs={{0,16},{16,0},{1,17},{17,1},{2,18},{18,2},{3,19},{19,3},{4,20},{20... | collective-permute-start | bytes 196616 | tf_op jit(solution)/shard_map/ppermute | solution.py:178
  57.8 8.3 %collective-permute-start.15 = (bf16[512,256]{1,0:T(8,128)(2,1)S(1)}, bf16[512,256]{1,0:T(8,128)(2,1)S(1)}, u32[]{:S(2)}, u32[]{:S(2)}) collective-permute-start(bf16[512,256]{1,0:T(8,128)(2,1)S(1)} %get-tuple-element.31), channel_id=1, source_target_pairs={{0,128},{128,0},{1,129},{129,1},{2,130},{130,2},{3,131},{131,3},{4... | collective-permute-start | bytes 786440 | tf_op jit(solution)/shard_map/ppermute | solution.py:178
  66.8 12.9 %collective-permute-start.18 = (bf16[448,256]{1,0:T(8,128)(2,1)S(1)}, bf16[448,256]{1,0:T(8,128)(2,1)S(1)}, u32[]{:S(2)}, u32[]{:S(2)}) collective-permute-start(bf16[448,256]{1,0:T(8,128)(2,1)S(1)} %get-tuple-element.33), channel_id=1, source_target_pairs={{96,0},{0,32},{32,64},{64,96},{97,1},{1,33},{33,65},{65,97},{98,2}... | collective-permute-start | bytes 688136 | tf_op jit(solution)/shard_map/ppermute | solution.py:183
  66.9 12.8 %collective-permute-start.17 = (bf16[448,256]{1,0:T(8,128)(2,1)S(1)}, bf16[448,256]{1,0:T(8,128)(2,1)S(1)}, u32[]{:S(2)}, u32[]{:S(2)}) collective-permute-start(bf16[448,256]{1,0:T(8,128)(2,1)S(1)} %get-tuple-element.34), channel_id=1, source_target_pairs={{64,0},{96,32},{0,64},{32,96},{65,1},{97,33},{1,65},{33,97},{66,2}... | collective-permute-start | bytes 688136 | tf_op jit(solution)/shard_map/ppermute | solution.py:183
  68.4 11.9 %collective-permute-start.16 = (bf16[448,256]{1,0:T(8,128)(2,1)S(1)}, bf16[448,256]{1,0:T(8,128)(2,1)S(1)}, u32[]{:S(2)}, u32[]{:S(2)}) collective-permute-start(bf16[448,256]{1,0:T(8,128)(2,1)S(1)} %get-tuple-element.32), channel_id=1, source_target_pairs={{32,0},{64,32},{96,64},{0,96},{33,1},{65,33},{97,65},{1,97},{34,2}... | collective-permute-start | bytes 688136 | tf_op jit(solution)/shard_map/ppermute | solution.py:183

commit v6 on v5

v6 whole, which is shorter than its diff:
```python
import math

import jax
import jax.numpy as jnp
from jax import lax
from jax.experimental import pallas as pl
from jax.experimental.pallas import tpu as pltpu
from jax.sharding import Mesh, PartitionSpec as P

HD = 128
HQ = 4
BLK = 128
COLS = HQ * HD
HALF = COLS // 2
TOKENS_ALL = 32768
PADDED = 16

EPSILON = 1e-06
NEGATIVE = -1e30
LOG2E = math.log2(math.e)

AXES = ("ylo", "x", "core", "z", "yhi")
SIZES = (2, 4, 2, 8, 2)
SEQ = ("z", "yhi")

NEAR = (0, 1, -1, 2, -2)
FAR = (3, -3, 4)

SMEM = pl.BlockSpec(memory_space=pltpu.SMEM)
VMEM = pl.BlockSpec(memory_space=pltpu.VMEM)


def normalise_kernel(where_ref, student_ref, keep_ref, send_ref, spread_ref, *, wrows):
    core = where_ref[2]
    rows, features = student_ref.shape
    chunk, wide = spread_ref.shape
    target = lax.broadcasted_iota(jnp.int32, (1, wide), 1)
    inside = lax.rem(target, PADDED)
    target = jnp.where(inside < wrows, target // PADDED * wrows + inside, -1)
    source = lax.broadcasted_iota(jnp.int32, (chunk, 1), 0)
    spread_ref[...] = jnp.where(source == target, 1.0, 0.0).astype(jnp.bfloat16)
    as_float = student_ref[...].astype(jnp.float32)
    scale = lax.rsqrt(jnp.mean(as_float * as_float, axis=1, keepdims=True) + EPSILON)
    normed = (as_float * scale).astype(jnp.bfloat16)
    group = 16 * PADDED
    for k in range(features // chunk):
        apart = jnp.dot(
            normed[:, k * chunk : (k + 1) * chunk],
            spread_ref[...],
            preferred_element_type=jnp.float32,
        ).astype(jnp.bfloat16)
        for q in range(wide // group):
            g = k * (wide // group) + q
            at = (g // 2 % 4 * 2 + g // 8) * group
            piece = apart[:, q * group : (q + 1) * group]

            @pl.when(core == g % 2)
            def _():
                keep_ref[:, at : at + group] = piece

            @pl.when(core != g % 2)
            def _():
                send_ref[:, at : at + group] = piece


def normalise(here, student_in, wrows):
    rows, features = student_in.shape
    shape = jax.ShapeDtypeStruct((rows, features // wrows * PADDED // 2), jnp.bfloat16)
    chunk = features // 4

    def body(*refs):
        normalise_kernel(*refs, wrows=wrows)

    return pl.pallas_call(
        body,
        out_shape=(shape, shape),
        in_specs=[SMEM, VMEM],
        out_specs=(VMEM, VMEM),
        scratch_shapes=[pltpu.VMEM((chunk, chunk // wrows * PADDED), jnp.bfloat16)],
        compiler_params=pltpu.CompilerParams(vmem_limit_bytes=16 << 20),
        name="normalise",
    )(here, student_in)


def pack_kernel(kv_ref, kv_other_ref, *refs):
    *w_refs, out_ref = refs
    rows = kv_ref.shape[0]
    wrows, width = w_refs[0].shape
    out_ref[:rows, :] = kv_ref[...]
    out_ref[rows : 2 * rows, :] = kv_other_ref[...]
    for i, w_ref in enumerate(w_refs):
        first = 2 * rows + i * PADDED
        out_ref[first : first + PADDED, :] = jnp.concatenate(
            [w_ref[...], jnp.zeros((PADDED - wrows, width), jnp.bfloat16)], axis=0
        )


def pack(kv, kv_other, w_parts):
    rows = 2 * kv.shape[0] + len(w_parts) * PADDED
    return pl.pallas_call(
        pack_kernel,
        out_shape=jax.ShapeDtypeStruct((rows, kv.shape[1]), jnp.bfloat16),
        in_specs=[VMEM] * (2 + len(w_parts)),
        out_specs=VMEM,
        compiler_params=pltpu.CompilerParams(vmem_limit_bytes=4 << 20),
        name="pack",
    )(kv, kv_other, *w_parts)


def attend_kernel(where_ref, assign_ref, length_ref, q_ref, *refs):
    *kv_refs, out_ref, mine_ref, other_ref, s_ref = refs
    z, yhi, ylo = where_ref[0], where_ref[1], where_ref[3]
    rows = q_ref.shape[0]
    own = assign_ref[0, 2 * z + yhi] * BLK
    first = length_ref[0, 0]
    second = first + length_ref[0, 1]
    third = second + length_ref[0, 2]
    q_pos = own + lax.broadcasted_iota(jnp.int32, (rows, 1), 0)
    q_start = jnp.where(
        q_pos >= third,
        third,
        jnp.where(q_pos >= second, second, jnp.where(q_pos >= first, first, 0)),
    )
    q_all = jnp.concatenate([q_ref[:, h * HD : (h + 1) * HD] for h in range(HQ)], axis=0)
    lane = lax.broadcasted_iota(jnp.int32, (1, BLK), 1)
    chunk = 2 * BLK
    top = None
    for c, (distance, kv_ref) in enumerate(zip(NEAR + FAR, kv_refs)):
        pair = lax.rem(z + distance + 8, 8) * 2
        k_pos = [assign_ref[0, pair + yhi] * BLK + lane, assign_ref[0, pair + 1 - yhi] * BLK + lane]
        k_pos = jnp.concatenate(k_pos, axis=1)
        bias = jnp.where((k_pos >= q_start) & (k_pos <= q_pos), 0.0, NEGATIVE)
        scores = lax.dot_general(
            q_all,
            kv_ref[:chunk, :HD],
            (((1,), (1,)), ((), ())),
            preferred_element_type=jnp.float32,
        )
        scores = scores.reshape(HQ, rows, chunk) * (HD ** (-0.5) * LOG2E) + bias[None]
        scores = scores.reshape(HQ * rows, chunk)
        s_ref[:, c * chunk : (c + 1) * chunk] = scores
        best = jnp.max(scores, axis=1, keepdims=True)
        top = best if top is None else jnp.maximum(top, best)
    total = jnp.zeros((HQ * rows, 1), jnp.float32)
    mixture = jnp.zeros((HQ * rows, HD), jnp.float32)
    for c, kv_ref in enumerate(kv_refs):
        terms = jnp.exp2(s_ref[:, c * chunk : (c + 1) * chunk] - top)
        total = total + jnp.sum(terms, axis=1, keepdims=True)
        mixture = mixture + jnp.dot(
            terms.astype(jnp.bfloat16), kv_ref[:chunk, HD:], preferred_element_type=jnp.float32
        )
    result = (mixture / total).astype(jnp.bfloat16)
    for h in range(HQ):
        head = result[h * rows : (h + 1) * rows]
        out_ref[:, h * HD : (h + 1) * HD] = head
        at = h % (HQ // 2) * HD

        @pl.when(ylo == h // (HQ // 2))
        def _():
            mine_ref[:, at : at + HD] = head

        @pl.when(ylo != h // (HQ // 2))
        def _():
            other_ref[:, at : at + HD] = head


def attend(here, queries, parts, lengths, assignment):
    rows = queries.shape[0]
    half = jax.ShapeDtypeStruct((rows, HALF), jnp.bfloat16)
    return pl.pallas_call(
        attend_kernel,
        out_shape=(jax.ShapeDtypeStruct((rows, COLS), jnp.bfloat16), half, half),
        in_specs=[SMEM, SMEM, SMEM, VMEM] + [VMEM] * len(parts),
        out_specs=(VMEM, VMEM, VMEM),
        scratch_shapes=[pltpu.VMEM((HQ * rows, 16 * BLK), jnp.float32)],
        compiler_params=pltpu.CompilerParams(vmem_limit_bytes=20 << 20),
        name="attend",
    )(here, assignment, lengths, queries, *parts)


def project_kernel(where_ref, n_ref, mine_ref, got_ref, *refs):
    *w_refs, own_ref, send_ref, w_all = refs
    z, yhi, ylo, x = where_ref[0], where_ref[1], where_ref[3], where_ref[4]
    group = 16 * PADDED
    for d in range(4):
        at_x = lax.rem(x + d, 4) * 2
        for batch, w_ref in zip((NEAR, FAR), w_refs[2 * d : 2 * d + 2]):
            for k, distance in enumerate(batch):
                pair = lax.rem(z + distance + 8, 8) * 2
                for t in range(2):
                    slot = pair + (yhi if t == 0 else 1 - yhi)
                    for i in range(2):
                        side = ylo if i == 0 else 1 - ylo
                        at = (at_x + side) * group + slot * PADDED
                        first = (k * 4 + t * 2 + i) * PADDED
                        w_all[pl.ds(pl.multiple_of(at, PADDED), PADDED), :] = w_ref[
                            first : first + PADDED, :
                        ]
    rows = n_ref.shape[0] // 4
    for b in range(4):
        part = jnp.dot(
            n_ref[b * rows : (b + 1) * rows, :], w_all[...], preferred_element_type=jnp.float32
        )
        if b % 2 == 0:
            part = part - (mine_ref, got_ref)[b // 2][...].astype(jnp.float32)
        own_ref[b * rows : (b + 1) * rows, :] = part
        t = b ^ 1
        send_ref[t * rows : (t + 1) * rows, :] = part.astype(jnp.bfloat16)


def project(here, n_all, a_mine, a_got, w_parts):
    shape = (n_all.shape[0], HALF)
    return pl.pallas_call(
        project_kernel,
        out_shape=(
            jax.ShapeDtypeStruct(shape, jnp.float32),
            jax.ShapeDtypeStruct(shape, jnp.bfloat16),
        ),
        in_specs=[SMEM] + [VMEM] * (3 + len(w_parts)),
        out_specs=(VMEM, VMEM),
        scratch_shapes=[pltpu.VMEM((n_all.shape[1], HALF), jnp.bfloat16)],
        compiler_params=pltpu.CompilerParams(vmem_limit_bytes=12 << 20),
        name="project",
    )(here, n_all, a_mine, a_got, *w_parts)


def halves(x, which):
    half = x.shape[1] // 2
    low, high = x[:, :half], x[:, half:]
    return jnp.where(which == 0, low, high), jnp.where(which == 0, high, low)


def partner(x, axis):
    return lax.ppermute(x, axis, [(0, 1), (1, 0)])


def from_next(x, axis, distance):
    size = SIZES[AXES.index(axis)]
    return lax.ppermute(x, axis, [((i + distance) % size, i) for i in range(size)])


def local(student_in, weight, queries, keys, values, lengths, assignment):
    names = ("z", "yhi", "core", "ylo", "x")
    here = jnp.stack([lax.axis_index(a) for a in names]).astype(jnp.int32)
    ylo, x = here[3], here[4]
    wrows = weight.shape[0]

    kv = jnp.concatenate([keys, values], axis=1)
    kv_other = partner(kv, "yhi")
    w_mine, w_other = halves(weight, ylo)
    w_parts = [
        w_mine,
        partner(w_other, "ylo"),
        partner(w_mine, "yhi"),
        lax.ppermute(w_other, ("ylo", "yhi"), [(i, 3 - i) for i in range(4)]),
    ]

    student_in, _ = lax.optimization_barrier((student_in, (kv, w_mine)))
    n_keep, n_send = normalise(here, student_in, wrows)
    n_keep, n_send, kv_other, w_parts = lax.optimization_barrier(
        (n_keep, n_send, kv_other, w_parts)
    )
    packed = pack(kv, kv_other, w_parts)
    n_got = partner(n_send, "core")
    n_got, _ = lax.optimization_barrier((n_got, packed))
    n_pair = jnp.concatenate([n_keep, n_got], axis=0)
    n_all = jnp.concatenate([n_pair, partner(n_pair, "ylo")], axis=0)

    up = down = packed
    held = {0: packed}
    for d in range(1, 5):
        up = from_next(up, "z", 1)
        held[d] = up
        if d < 4:
            down = from_next(down, "z", -1)
            held[-d] = down
    near_rows = jnp.concatenate([held[d][2 * BLK :] for d in NEAR], axis=0)
    far_rows = jnp.concatenate([held[d][2 * BLK :] for d in FAR], axis=0)
    near_got = [from_next(near_rows, "x", d) for d in range(1, 4)]
    far_rows, near_got = lax.optimization_barrier((far_rows, near_got))
    far_got = [from_next(far_rows, "x", d) for d in range(1, 4)]
    w_all = [near_rows, far_rows]
    for pair in zip(near_got, far_got):
        w_all += pair

    parts = [held[d] for d in NEAR + FAR]
    parts, _ = lax.optimization_barrier((parts, far_rows))
    attention, a_mine, a_other = attend(here, queries, parts, lengths, assignment)

    own, send = project(here, n_all, a_mine, partner(a_other, "ylo"), w_all)
    diff = own + partner(send, "core").astype(jnp.float32)
    scaled = (diff * TOKENS_ALL ** (-0.5)).astype(jnp.bfloat16)
    part = lax.dot_general(
        n_all, scaled, (((0,), (0,)), ((), ())), preferred_element_type=jnp.float32
    ).astype(jnp.bfloat16)
    part = part.reshape(4, 32, PADDED, HALF)[:, :, :wrows].reshape(4, 32 * wrows, HALF)
    near = lax.dynamic_index_in_dim(part, x, 0, keepdims=False).astype(jnp.float32)
    for d in range(1, 4):
        away = lax.dynamic_index_in_dim(part, (x - d) % 4, 0, keepdims=False)
        near = near + from_next(away, "x", d).astype(jnp.float32)
    near = near.astype(jnp.bfloat16).reshape(-1, wrows, HALF)
    near = jnp.pad(near, ((0, 0), (0, PADDED - wrows), (0, 0)))
    last = lax.all_to_all(near, ("ylo", *SEQ), split_axis=0, concat_axis=0, tiled=True)
    summed = last.reshape(2, 16, PADDED, HALF).astype(jnp.float32).sum(axis=1)
    weight_grad = jnp.concatenate([summed[0, :wrows], summed[1, :wrows]], axis=1)
    return (attention, weight_grad)


def solution(mesh):
    mesh = Mesh(mesh.devices.reshape(SIZES), AXES)
    token = P(AXES, None)
    row = P(("ylo", "x", "core"), None)
    return jax.shard_map(
        local,
        mesh=mesh,
        in_specs=(token, token, token, token, token, row, row),
        out_specs=(token, token),
        check_vma=False,
    )
```

time: 105 us -> 102 us (0.971)
  waiting for transfers between devices: 43.6 us -> 29.1 us
  starting transfers between devices: 24.6 us -> 35.2 us
  Pallas kernels: 5.15 us -> 8.18 us
  blocking collectives: 22.6 us -> 20.2 us
  local copies, waits for them, and re-layouts: 1.82 us -> 3.92 us
  other arithmetic: 4.51 us -> 3.35 us
    ppermute x13 -> x16, waiting for transfers between devices: 32.7 us -> 24.9 us  [from_next(): lax.ppermute(x, axis, [((i + distance) % size, i) for i in range(size)])]
    ppermute x13 -> x16, starting transfers between devices: 18 us -> 25.5 us  [from_next(): lax.ppermute(x, axis, [((i + distance) % size, i) for i in range(size)])]
    ppermute x6 -> x8, waiting for transfers between devices: 10.9 us -> 4.26 us  [the longest x7 4.26 us: partner(): return lax.ppermute(x, axis, [(0, 1), (1, 0)])]
    ppermute x6 -> x8, starting transfers between devices: 6.59 us -> 9.66 us  [the longest x7 7.48 us: partner(): return lax.ppermute(x, axis, [(0, 1), (1, 0)])]
    all_to_all x1, blocking collectives: 22.6 us -> 20.2 us  [local(): lax.all_to_all(near, ('ylo', *SEQ), split_axis=0, concat_axis=0, tiled=True)]
    pallas_call x1 -> x2, Pallas kernels: 0.63 us -> 2.94 us  [the longest x1 2.93 us: normalise(): pl.pallas_call(body, out_shape=(shape, shape), in_specs=[SMEM, VMEM], out...]
    unnamed x9 -> x19, local copies, waits for them, and re-layouts: 0.79 us -> 2.85 us
    dynamic_slice x0 -> x1, other arithmetic: none -> 1.78 us  [local(): away = lax.dynamic_index_in_dim(part, (x - d) % 4, 0, keepdims=False)]
  transfers between devices with their start and end apart: 19 -> 24, of which waited for: 14 -> 9; matrix products, arithmetic and copies ran while one was open for 2% -> 1% of each run, Pallas kernels for 4% -> 7%
where the time goes in v6:
time: 102 us
  starting transfers between devices  35.2 us (35%)
  waiting for transfers between devices  29.1 us (29%)
  blocking collectives  20.2 us (20%)
  Pallas kernels  8.18 us (8%)
  local copies, waits for them, and re-layouts  3.92 us (4%)
  other arithmetic  3.35 us (3%)
    ppermute x16, starting transfers between devices, from_next(): lax.ppermute(x, axis, [((i + distance) % size, i) for i in range(size)])  25.5 us
    ppermute x16, waiting for transfers between devices, from_next(): lax.ppermute(x, axis, [((i + distance) % size, i) for i in range(size)])  24.9 us
    all_to_all x1, blocking collectives, local(): lax.all_to_all(near, ('ylo', *SEQ), split_axis=0, concat_axis=0, tiled=True)  20.2 us
    ppermute x7, starting transfers between devices, partner(): return lax.ppermute(x, axis, [(0, 1), (1, 0)])  7.48 us
    ppermute x7, waiting for transfers between devices, partner(): return lax.ppermute(x, axis, [(0, 1), (1, 0)])  4.26 us
    pallas_call x1, Pallas kernels, attend(): pl.pallas_call(attend_kernel, out_shape=(jax.ShapeDtypeStruct((rows, COLS...  3.77 us
    pallas_call x1, Pallas kernels, normalise(): pl.pallas_call(body, out_shape=(shape, shape), in_specs=[SMEM, VMEM], out...  2.93 us
    unnamed x19, local copies, waits for them, and re-layouts  2.85 us
  transfers between devices with their start and end apart: 24, of which 9 were waited for; matrix products, arithmetic and copies ran while one was open for 1% of the time, Pallas kernels for 7%

profile of v6, /device:TPU:32, one launch (start us, length us, event | category | flops | bytes accessed | tf_op | source)
XLA Modules:
  0.0 101.8 jit_solution(2017046972209347797)
XLA Ops:
  0.6 0.8 constant_dynamic-update-slice_fusion.1
  1.4 0.8 constant_dynamic-update-slice_fusion.kv_ref
  2.2 3.3 %collective-permute-start = (bf16[128,256]{1,0:T(8,128)(2,1)S(1)}, bf16[128,256]{1,0:T(8,128)(2,1)S(1)}, u32[]{:S(2)}, u32[]{:S(2)}) collective-permute-start(bf16[128,256]{1,0:T(8,128)(2,1)S(1)} %constant_dynamic-update-slice_fusion.kv_ref), channel_id=1, source_target_pairs={{0,1},{1,0},{2,3},{3,2},{4,5},{5,4},{6,7},{7,6},{8,9},{9,8},{10,11... | collective-permute-start | bytes 196616 | tf_op jit(solution)/shard_map/ppermute | solution.py:234
  5.4 0.7 broadcast_select_fusion
  6.2 0.3 collective-permute-start.2
  6.5 1.6 %collective-permute-start.1 = (bf16[14,256]{1,0:T(8,128)(2,1)S(1)}, bf16[14,256]{1,0:T(8,128)(2,1)S(1)}, u32[]{:S(2)}, u32[]{:S(2)}) collective-permute-start(bf16[14,256]{1,0:T(8,128)(2,1)S(1)} %get-tuple-element.64), channel_id=1, source_target_pairs={{0,128},{128,0},{1,129},{129,1},{2,130},{130,2},{3,131},{131,3},{4... | collective-permute-start | bytes 21512 | tf_op jit(solution)/shard_map/ppermute | solution.py:234
  8.1 2.2 %collective-permute-start.3 = (bf16[14,256]{1,0:T(8,128)(2,1)S(1)}, bf16[14,256]{1,0:T(8,128)(2,1)S(1)}, u32[]{:S(2)}, u32[]{:S(2)}) collective-permute-start(bf16[14,256]{1,0:T(8,128)(2,1)S(1)} %get-tuple-element.64), channel_id=1, source_target_pairs={{0,129},{1,128},{128,1},{129,0},{2,131},{3,130},{130,3},{131,2},{4... | collective-permute-start | bytes 21512 | tf_op jit(solution)/shard_map/ppermute | solution.py:255
  10.3 0.1 stack.23.refs_0_.where_ref
  10.3 1.2 %copy-done = bf16[128,3584]{1,0:T(8,128)(2,1)S(1)} copy-done((bf16[128,3584]{1,0:T(8,128)(2,1)S(1)}, bf16[128,3584]{1,0:T(8,128)(2,1)}, u32[]{:S(2)}) %copy-start) | copy-done | bytes 917528
  11.5 2.9 %normalise.1 = (bf16[128,2048]{1,0:T(8,128)(2,1)S(1)}, bf16[128,2048]{1,0:T(8,128)(2,1)S(1)}) custom-call(s32[5]{0:T(128)S(1)} %stack.23.refs_0_.where_ref, bf16[128,3584]{1,0:T(8,128)(2,1)S(1)} %copy-done), custom_call_target="tpu_custom_call" | custom-call | tf_op jit(solution)/shard_map/normalise/pallas_call | solution.py:74
  14.4 0.0 collective-permute-done.2.refs_2_
  14.5 0.0 collective-permute-done.1.refs_1_
  14.5 0.0 collective-permute-done.3.refs_3_
  14.5 0.0 collective-permute-done.kv_other_ref
  14.5 0.1 collective-permute-start.14
  14.6 0.2 collective-permute-start.4
  14.8 1.9 %collective-permute-start.5 = (bf16[320,256]{1,0:T(8,128)(2,1)S(1)}, bf16[320,256]{1,0:T(8,128)(2,1)S(1)}, u32[]{:S(2)}, u32[]{:S(2)}) collective-permute-start(bf16[320,256]{1,0:T(8,128)(2,1)S(1)} %pack.1.refs_0_), channel_id=1, source_target_pairs={{14,0},{0,2},{2,4},{4,6},{6,8},{8,10},{10,12},{12,14},{15,1},{1,3}... | collective-permute-start | bytes 491528 | tf_op jit(solution)/shard_map/ppermute | solution.py:239
  16.8 0.0 copy-start.1
  16.8 0.0 copy-start.2
  16.8 0.0 copy-start.3
  16.8 4.7 %collective-permute-done.4.refs_1_ = bf16[320,256]{1,0:T(8,128)(2,1)S(1)} collective-permute-done((bf16[320,256]{1,0:T(8,128)(2,1)S(1)}, bf16[320,256]{1,0:T(8,128)(2,1)S(1)}, u32[]{:S(2)}, u32[]{:S(2)}) %collective-permute-start.4) | collective-permute-done | bytes 163872 | tf_op jit(solution)/shard_map/ppermute | solution.py:239
  21.5 3.3 %collective-permute-start.6 = (bf16[320,256]{1,0:T(8,128)(2,1)S(1)}, bf16[320,256]{1,0:T(8,128)(2,1)S(1)}, u32[]{:S(2)}, u32[]{:S(2)}) collective-permute-start(bf16[320,256]{1,0:T(8,128)(2,1)S(1)} %collective-permute-done.4.refs_1_), channel_id=1, source_target_pairs={{2,0},{4,2},{6,4},{8,6},{10,8},{12,10},{14,12},{0,14},{3,1},{5,3},... | collective-permute-start | bytes 491528 | tf_op jit(solution)/shard_map/ppermute | solution.py:239
  24.8 0.0 collective-permute-done.14
  24.8 0.1 pad_maximum_fusion
  24.9 0.8 collective-permute-start.15
  25.6 0.0 collective-permute-done.5.refs_2_
  25.6 0.0 collective-permute-start.7
  25.6 2.5 %collective-permute-done.6.refs_3_ = bf16[320,256]{1,0:T(8,128)(2,1)S(1)} collective-permute-done((bf16[320,256]{1,0:T(8,128)(2,1)S(1)}, bf16[320,256]{1,0:T(8,128)(2,1)S(1)}, u32[]{:S(2)}, u32[]{:S(2)}) %collective-permute-start.6) | collective-permute-done | bytes 163872 | tf_op jit(solution)/shard_map/ppermute | solution.py:239
  28.1 3.7 %collective-permute-start.8 = (bf16[320,256]{1,0:T(8,128)(2,1)S(1)}, bf16[320,256]{1,0:T(8,128)(2,1)S(1)}, u32[]{:S(2)}, u32[]{:S(2)}) collective-permute-start(bf16[320,256]{1,0:T(8,128)(2,1)S(1)} %collective-permute-done.6.refs_3_), channel_id=1, source_target_pairs={{2,0},{4,2},{6,4},{8,6},{10,8},{12,10},{14,12},{0,14},{3,1},{5,3},... | collective-permute-start | bytes 491528 | tf_op jit(solution)/shard_map/ppermute | solution.py:239
  31.8 1.0 collective-permute-done.7.refs_4_
  32.8 2.9 %collective-permute-start.11 = (bf16[320,256]{1,0:T(8,128)(2,1)S(1)}, bf16[320,256]{1,0:T(8,128)(2,1)S(1)}, u32[]{:S(2)}, u32[]{:S(2)}) collective-permute-start(bf16[320,256]{1,0:T(8,128)(2,1)S(1)} %slice_dynamic-update-slice_fusion.refs_0_), channel_id=1, source_target_pairs={{32,0},{64,32},{96,64},{0,96},{33,1},{65,33},{97,65},{1,97},{34,2}... | collective-permute-start | bytes 491528 | tf_op jit(solution)/shard_map/ppermute | solution.py:239
  35.7 0.8 collective-permute-start.12
  36.5 0.9 collective-permute-start.13
  37.4 1.8 %collective-permute-done.9.refs_6_ = bf16[320,256]{1,0:T(8,128)(2,1)S(1)} collective-permute-done((bf16[320,256]{1,0:T(8,128)(2,1)S(1)}, bf16[320,256]{1,0:T(8,128)(2,1)S(1)}, u32[]{:S(2)}, u32[]{:S(2)}) %collective-permute-start.9) | collective-permute-done | bytes 163872 | tf_op jit(solution)/shard_map/ppermute | solution.py:239
  39.1 3.2 %collective-permute-start.10 = (bf16[320,256]{1,0:T(8,128)(2,1)S(1)}, bf16[320,256]{1,0:T(8,128)(2,1)S(1)}, u32[]{:S(2)}, u32[]{:S(2)}) collective-permute-start(bf16[320,256]{1,0:T(8,128)(2,1)S(1)} %collective-permute-done.8.refs_5_), channel_id=1, source_target_pairs={{2,0},{4,2},{6,4},{8,6},{10,8},{12,10},{14,12},{0,14},{3,1},{5,3},... | collective-permute-start | bytes 491528 | tf_op jit(solution)/shard_map/ppermute | solution.py:239
  42.4 2.8 %collective-permute-done.10.refs_7_ = bf16[320,256]{1,0:T(8,128)(2,1)S(1)} collective-permute-done((bf16[320,256]{1,0:T(8,128)(2,1)S(1)}, bf16[320,256]{1,0:T(8,128)(2,1)S(1)}, u32[]{:S(2)}, u32[]{:S(2)}) %collective-permute-start.10) | collective-permute-done | bytes 163872 | tf_op jit(solution)/shard_map/ppermute | solution.py:239
  45.2 0.0 collective-permute-done.12.refs_4_
  45.2 0.0 collective-permute-done.13.refs_6_
  45.3 2.9 %collective-permute-start.17 = (bf16[192,256]{1,0:T(8,128)(2,1)S(1)}, bf16[192,256]{1,0:T(8,128)(2,1)S(1)}, u32[]{:S(2)}, u32[]{:S(2)}) collective-permute-start(bf16[192,256]{1,0:T(8,128)(2,1)S(1)} %pad_maximum_fusion.1.refs_1_), channel_id=1, source_target_pairs={{32,0},{64,32},{96,64},{0,96},{33,1},{65,33},{97,65},{1,97},{34,2}... | collective-permute-start | bytes 294920 | tf_op jit(solution)/shard_map/ppermute | solution.py:239
  48.1 0.8 collective-permute-start.18
  48.9 0.9 collective-permute-start.19
  49.8 3.8 %attend.1 = (bf16[128,512]{1,0:T(8,128)(2,1)}, bf16[128,256]{1,0:T(8,128)(2,1)S(1)}, bf16[128,256]{1,0:T(8,128)(2,1)S(1)}) custom-call(s32[5]{0:T(128)S(1)} %stack.23.refs_0_.where_ref, s32[1,16]{1,0:T(1,128)S(1)} %copy-done.2, s32[1,4]{1,0:T(1,128)S(1)} %copy-done.3, bf16[128,512]{1,0:T(8,128)(2,1)S(1)} %copy-done.1, bf16[320,256]{1,0:T(8,128)(2,1)S(1)} %pack.1.refs_0_, ...), custom_call_target="tpu_custom_call" | custom-call | tf_op jit(solution)/shard_map/attend/pallas_call | solution.py:170
  53.6 1.4 %collective-permute-start.16 = (bf16[128,256]{1,0:T(8,128)(2,1)S(1)}, bf16[128,256]{1,0:T(8,128)(2,1)S(1)}, u32[]{:S(2)}, u32[]{:S(2)}) collective-permute-start(bf16[128,256]{1,0:T(8,128)(2,1)S(1)} %get-tuple-element.52), channel_id=1, source_target_pairs={{0,128},{128,0},{1,129},{129,1},{2,130},{130,2},{3,131},{131,3},{4... | collective-permute-start | bytes 196616 | tf_op jit(solution)/shard_map/ppermute | solution.py:234
  54.9 0.1 constant_dynamic-update-slice_fusion.2.n_ref
  55.0 2.8 %collective-permute-done.16.got_ref = bf16[128,256]{1,0:T(8,128)(2,1)S(1)} collective-permute-done((bf16[128,256]{1,0:T(8,128)(2,1)S(1)}, bf16[128,256]{1,0:T(8,128)(2,1)S(1)}, u32[]{:S(2)}, u32[]{:S(2)}) %collective-permute-start.16) | collective-permute-done | bytes 65568 | tf_op jit(solution)/shard_map/ppermute | solution.py:234
  57.8 0.0 collective-permute-done.17.refs_3_
  57.8 0.0 collective-permute-done.18.refs_5_
  57.8 0.0 collective-permute-done.19.refs_7_
  57.8 1.5 %project.1 = (f32[512,256]{1,0:T(8,128)S(1)}, bf16[512,256]{1,0:T(8,128)(2,1)S(1)}) custom-call(s32[5]{0:T(128)S(1)} %stack.23.refs_0_.where_ref, bf16[512,2048]{1,0:T(8,128)(2,1)S(1)} %constant_dynamic-update-slice_fusion.2.n_ref, bf16[128,256]{1,0:T(8,128)(2,1)S(1)} %get-tuple-element.51.mine_ref, bf16[128,256]{1,0:T(8,128)(2,1)S(1)} %collective-permute-done.16.got_ref, ...), custom_call_target="tpu_custom_call" | custom-call | tf_op jit(solution)/shard_map/project/pallas_call | solution.py:213
  59.3 0.1 collective-permute-start.20
  59.5 1.5 %collective-permute-done.20 = bf16[512,256]{1,0:T(8,128)(2,1)S(1)} collective-permute-done((bf16[512,256]{1,0:T(8,128)(2,1)S(1)}, bf16[512,256]{1,0:T(8,128)(2,1)S(1)}, u32[]{:S(2)}, u32[]{:S(2)}) %collective-permute-start.20) | collective-permute-done | bytes 262176 | tf_op jit(solution)/shard_map/ppermute | solution.py:234
  60.9 0.8 convolution_convert_fusion
  61.7 0.7 copy.15
  62.5 1.8 %constant_dynamic-slice_fusion.2 = (bf16[1,448,256]{2,0,1:T(2,128)(2,1)S(1)}, bf16[1,448,256]{2,0,1:T(2,128)(2,1)S(1)}, bf16[1,448,256]{2,0,1:T(2,128)(2,1)S(1)}, f32[1,448,256]{2,0,1:T(1,128)S(1)}) fusion(bf16[4,448,256]{2,0,1:T(4,128)(2,1)S(1)} %bitcast.33, s32[]{:T(128)S(6)} %select_n.45, s32[]{:T(128)S(6)} %select_n.49, s32[]{:T(128)S(6)} %select_n.47, ...), kind=kLoop, calls=%fused_computation.31 | loop fusion | flops 114688 | bytes 2064400 | tf_op jit(solution)/shard_map/jit(dynamic_index_in_dim)/dynamic_slice | solution.py:299
  64.3 2.4 %collective-permute-start.21 = (bf16[448,256]{1,0:T(8,128)(2,1)S(1)}, bf16[448,256]{1,0:T(8,128)(2,1)S(1)}, u32[]{:S(2)}, u32[]{:S(2)}) collective-permute-start(bf16[448,256]{1,0:T(8,128)(2,1)S(1)} %bitcast.35), channel_id=1, source_target_pairs={{32,0},{64,32},{96,64},{0,96},{33,1},{65,33},{97,65},{1,97},{34,2}... | collective-permute-start | bytes 688136 | tf_op jit(solution)/shard_map/ppermute | solution.py:239
  66.7 1.6 %collective-permute-start.22 = (bf16[448,256]{1,0:T(8,128)(2,1)S(1)}, bf16[448,256]{1,0:T(8,128)(2,1)S(1)}, u32[]{:S(2)}, u32[]{:S(2)}) collective-permute-start(bf16[448,256]{1,0:T(8,128)(2,1)S(1)} %bitcast.36), channel_id=1, source_target_pairs={{64,0},{96,32},{0,64},{32,96},{65,1},{97,33},{1,65},{33,97},{66,2}... | collective-permute-start | bytes 688136 | tf_op jit(solution)/shard_map/ppermute | solution.py:239
  68.4 0.1 collective-permute-start.23
  68.5 8.3 %collective-permute-done.21 = bf16[448,256]{1,0:T(8,128)(2,1)S(1)} collective-permute-done((bf16[448,256]{1,0:T(8,128)(2,1)S(1)}, bf16[448,256]{1,0:T(8,128)(2,1)S(1)}, u32[]{:S(2)}, u32[]{:S(2)}) %collective-permute-start.21) | collective-permute-done | bytes 229408 | tf_op jit(solution)/shard_map/ppermute | solution.py:239
  76.8 0.0 collective-permute-done.22
  76.9 3.8 %collective-permute-done.23 = bf16[448,256]{1,0:T(8,128)(2,1)S(1)} collective-permute-done((bf16[448,256]{1,0:T(8,128)(2,1)S(1)}, bf16[448,256]{1,0:T(8,128)(2,1)S(1)}, u32[]{:S(2)}, u32[]{:S(2)}) %collective-permute-start.23) | collective-permute-done | bytes 229408 | tf_op jit(solution)/shard_map/ppermute | solution.py:239
  80.6 0.1 fusion.2
  80.7 0.1 reshape.20
  80.9 20.2 %all_to_all.5 = bf16[32,16,256]{2,1,0:T(8,128)(2,1)S(1)} all-to-all(bf16[32,16,256]{2,1,0:T(8,128)(2,1)S(1)} %pad.4), channel_id=1, replica_groups=mesh['ylo'=2,'x'=4,'core'=2,'z'=8,'yhi'=2] {'ylo','z','yhi'}, dimensions={0} | all-to-all | bytes 524288 | tf_op jit(solution)/shard_map/all_to_all | solution.py:303
  101.1 0.6 pad_maximum_fusion.2
  (26 shorter events, 0.3 us)
Async XLA Ops:
  2.2 12.3 %collective-permute-start = (bf16[128,256]{1,0:T(8,128)(2,1)S(1)}, bf16[128,256]{1,0:T(8,128)(2,1)S(1)}, u32[]{:S(2)}, u32[]{:S(2)}) collective-permute-start(bf16[128,256]{1,0:T(8,128)(2,1)S(1)} %constant_dynamic-update-slice_fusion.kv_ref), channel_id=1, source_target_pairs={{0,1},{1,0},{2,3},{3,2},{4,5},{5,4},{6,7},{7,6},{8,9},{9,8},{10,11... | collective-permute-start | bytes 196616 | tf_op jit(solution)/shard_map/ppermute | solution.py:234
  6.2 8.3 %collective-permute-start.2 = (bf16[14,256]{1,0:T(8,128)(2,1)S(1)}, bf16[14,256]{1,0:T(8,128)(2,1)S(1)}, u32[]{:S(2)}, u32[]{:S(2)}) collective-permute-start(bf16[14,256]{1,0:T(8,128)(2,1)S(1)} %get-tuple-element.34.refs_0_), channel_id=1, source_target_pairs={{0,1},{1,0},{2,3},{3,2},{4,5},{5,4},{6,7},{7,6},{8,9},{9,8},{10,11... | collective-permute-start | bytes 21512 | tf_op jit(solution)/shard_map/ppermute | solution.py:234
  6.5 8.0 %collective-permute-start.1 = (bf16[14,256]{1,0:T(8,128)(2,1)S(1)}, bf16[14,256]{1,0:T(8,128)(2,1)S(1)}, u32[]{:S(2)}, u32[]{:S(2)}) collective-permute-start(bf16[14,256]{1,0:T(8,128)(2,1)S(1)} %get-tuple-element.64), channel_id=1, source_target_pairs={{0,128},{128,0},{1,129},{129,1},{2,130},{130,2},{3,131},{131,3},{4... | collective-permute-start | bytes 21512 | tf_op jit(solution)/shard_map/ppermute | solution.py:234
  8.1 6.4 %collective-permute-start.3 = (bf16[14,256]{1,0:T(8,128)(2,1)S(1)}, bf16[14,256]{1,0:T(8,128)(2,1)S(1)}, u32[]{:S(2)}, u32[]{:S(2)}) collective-permute-start(bf16[14,256]{1,0:T(8,128)(2,1)S(1)} %get-tuple-element.64), channel_id=1, source_target_pairs={{0,129},{1,128},{128,1},{129,0},{2,131},{3,130},{130,3},{131,2},{4... | collective-permute-start | bytes 21512 | tf_op jit(solution)/shard_map/ppermute | solution.py:255
  10.3 1.2 %copy-start = (bf16[128,3584]{1,0:T(8,128)(2,1)S(1)}, bf16[128,3584]{1,0:T(8,128)(2,1)}, u32[]{:S(2)}) copy-start(bf16[128,3584]{1,0:T(8,128)(2,1)} %refs_1_) | copy-start | bytes 2752516
  14.5 10.3 %collective-permute-start.14 = (bf16[128,2048]{1,0:T(8,128)(2,1)S(1)}, bf16[128,2048]{1,0:T(8,128)(2,1)S(1)}, u32[]{:S(2)}, u32[]{:S(2)}) collective-permute-start(bf16[128,2048]{1,0:T(8,128)(2,1)S(1)} %get-tuple-element.49), channel_id=1, source_target_pairs={{0,16},{16,0},{1,17},{17,1},{2,18},{18,2},{3,19},{19,3},{4,20},{20... | collective-permute-start | bytes 1572872 | tf_op jit(solution)/shard_map/ppermute | solution.py:234
  14.6 6.9 %collective-permute-start.4 = (bf16[320,256]{1,0:T(8,128)(2,1)S(1)}, bf16[320,256]{1,0:T(8,128)(2,1)S(1)}, u32[]{:S(2)}, u32[]{:S(2)}) collective-permute-start(bf16[320,256]{1,0:T(8,128)(2,1)S(1)} %pack.1.refs_0_), channel_id=1, source_target_pairs={{2,0},{4,2},{6,4},{8,6},{10,8},{12,10},{14,12},{0,14},{3,1},{5,3},... | collective-permute-start | bytes 491528 | tf_op jit(solution)/shard_map/ppermute | solution.py:239
  14.8 10.8 %collective-permute-start.5 = (bf16[320,256]{1,0:T(8,128)(2,1)S(1)}, bf16[320,256]{1,0:T(8,128)(2,1)S(1)}, u32[]{:S(2)}, u32[]{:S(2)}) collective-permute-start(bf16[320,256]{1,0:T(8,128)(2,1)S(1)} %pack.1.refs_0_), channel_id=1, source_target_pairs={{14,0},{0,2},{2,4},{4,6},{6,8},{8,10},{10,12},{12,14},{15,1},{1,3}... | collective-permute-start | bytes 491528 | tf_op jit(solution)/shard_map/ppermute | solution.py:239
  16.8 33.0 %copy-start.1 = (bf16[128,512]{1,0:T(8,128)(2,1)S(1)}, bf16[128,512]{1,0:T(8,128)(2,1)}, u32[]{:S(2)}) copy-start(bf16[128,512]{1,0:T(8,128)(2,1)} %q_ref.1) | copy-start | bytes 393220
  16.8 33.0 %copy-start.2 = (s32[1,16]{1,0:T(1,128)S(1)}, s32[1,16]{1,0:T(1,128)}, u32[]{:S(2)}) copy-start(s32[1,16]{1,0:T(1,128)} %assign_ref.1) | copy-start | bytes 196
  16.8 33.0 %copy-start.3 = (s32[1,4]{1,0:T(1,128)S(1)}, s32[1,4]{1,0:T(1,128)}, u32[]{:S(2)}) copy-start(s32[1,4]{1,0:T(1,128)} %length_ref.1) | copy-start | bytes 52
  21.5 6.6 %collective-permute-start.6 = (bf16[320,256]{1,0:T(8,128)(2,1)S(1)}, bf16[320,256]{1,0:T(8,128)(2,1)S(1)}, u32[]{:S(2)}, u32[]{:S(2)}) collective-permute-start(bf16[320,256]{1,0:T(8,128)(2,1)S(1)} %collective-permute-done.4.refs_1_), channel_id=1, source_target_pairs={{2,0},{4,2},{6,4},{8,6},{10,8},{12,10},{14,12},{0,14},{3,1},{5,3},... | collective-permute-start | bytes 491528 | tf_op jit(solution)/shard_map/ppermute | solution.py:239
  24.9 30.1 %collective-permute-start.15 = (bf16[256,2048]{1,0:T(8,128)(2,1)S(1)}, bf16[256,2048]{1,0:T(8,128)(2,1)S(1)}, u32[]{:S(2)}, u32[]{:S(2)}) collective-permute-start(bf16[256,2048]{1,0:T(8,128)(2,1)S(1)} %pad_maximum_fusion), channel_id=1, source_target_pairs={{0,128},{128,0},{1,129},{129,1},{2,130},{130,2},{3,131},{131,3},{4... | collective-permute-start | bytes 3145736 | tf_op jit(solution)/shard_map/ppermute | solution.py:234
  25.6 7.2 %collective-permute-start.7 = (bf16[320,256]{1,0:T(8,128)(2,1)S(1)}, bf16[320,256]{1,0:T(8,128)(2,1)S(1)}, u32[]{:S(2)}, u32[]{:S(2)}) collective-permute-start(bf16[320,256]{1,0:T(8,128)(2,1)S(1)} %collective-permute-done.5.refs_2_), channel_id=1, source_target_pairs={{14,0},{0,2},{2,4},{4,6},{6,8},{8,10},{10,12},{12,14},{15,1},{1,3}... | collective-permute-start | bytes 491528 | tf_op jit(solution)/shard_map/ppermute | solution.py:239
  28.1 8.4 %collective-permute-start.8 = (bf16[320,256]{1,0:T(8,128)(2,1)S(1)}, bf16[320,256]{1,0:T(8,128)(2,1)S(1)}, u32[]{:S(2)}, u32[]{:S(2)}) collective-permute-start(bf16[320,256]{1,0:T(8,128)(2,1)S(1)} %collective-permute-done.6.refs_3_), channel_id=1, source_target_pairs={{2,0},{4,2},{6,4},{8,6},{10,8},{12,10},{14,12},{0,14},{3,1},{5,3},... | collective-permute-start | bytes 491528 | tf_op jit(solution)/shard_map/ppermute | solution.py:239
  32.8 6.3 %collective-permute-start.9 = (bf16[320,256]{1,0:T(8,128)(2,1)S(1)}, bf16[320,256]{1,0:T(8,128)(2,1)S(1)}, u32[]{:S(2)}, u32[]{:S(2)}) collective-permute-start(bf16[320,256]{1,0:T(8,128)(2,1)S(1)} %collective-permute-done.7.refs_4_), channel_id=1, source_target_pairs={{14,0},{0,2},{2,4},{4,6},{6,8},{8,10},{10,12},{12,14},{15,1},{1,3}... | collective-permute-start | bytes 491528 | tf_op jit(solution)/shard_map/ppermute | solution.py:239
  32.8 12.4 %collective-permute-start.11 = (bf16[320,256]{1,0:T(8,128)(2,1)S(1)}, bf16[320,256]{1,0:T(8,128)(2,1)S(1)}, u32[]{:S(2)}, u32[]{:S(2)}) collective-permute-start(bf16[320,256]{1,0:T(8,128)(2,1)S(1)} %slice_dynamic-update-slice_fusion.refs_0_), channel_id=1, source_target_pairs={{32,0},{64,32},{96,64},{0,96},{33,1},{65,33},{97,65},{1,97},{34,2}... | collective-permute-start | bytes 491528 | tf_op jit(solution)/shard_map/ppermute | solution.py:239
  35.7 9.6 %collective-permute-start.12 = (bf16[320,256]{1,0:T(8,128)(2,1)S(1)}, bf16[320,256]{1,0:T(8,128)(2,1)S(1)}, u32[]{:S(2)}, u32[]{:S(2)}) collective-permute-start(bf16[320,256]{1,0:T(8,128)(2,1)S(1)} %slice_dynamic-update-slice_fusion.refs_0_), channel_id=1, source_target_pairs={{64,0},{96,32},{0,64},{32,96},{65,1},{97,33},{1,65},{33,97},{66,2}... | collective-permute-start | bytes 491528 | tf_op jit(solution)/shard_map/ppermute | solution.py:239
  36.5 8.8 %collective-permute-start.13 = (bf16[320,256]{1,0:T(8,128)(2,1)S(1)}, bf16[320,256]{1,0:T(8,128)(2,1)S(1)}, u32[]{:S(2)}, u32[]{:S(2)}) collective-permute-start(bf16[320,256]{1,0:T(8,128)(2,1)S(1)} %slice_dynamic-update-slice_fusion.refs_0_), channel_id=1, source_target_pairs={{96,0},{0,32},{32,64},{64,96},{97,1},{1,33},{33,65},{65,97},{98,2}... | collective-permute-start | bytes 491528 | tf_op jit(solution)/shard_map/ppermute | solution.py:239
  39.1 6.1 %collective-permute-start.10 = (bf16[320,256]{1,0:T(8,128)(2,1)S(1)}, bf16[320,256]{1,0:T(8,128)(2,1)S(1)}, u32[]{:S(2)}, u32[]{:S(2)}) collective-permute-start(bf16[320,256]{1,0:T(8,128)(2,1)S(1)} %collective-permute-done.8.refs_5_), channel_id=1, source_target_pairs={{2,0},{4,2},{6,4},{8,6},{10,8},{12,10},{14,12},{0,14},{3,1},{5,3},... | collective-permute-start | bytes 491528 | tf_op jit(solution)/shard_map/ppermute | solution.py:239
  45.3 12.6 %collective-permute-start.17 = (bf16[192,256]{1,0:T(8,128)(2,1)S(1)}, bf16[192,256]{1,0:T(8,128)(2,1)S(1)}, u32[]{:S(2)}, u32[]{:S(2)}) collective-permute-start(bf16[192,256]{1,0:T(8,128)(2,1)S(1)} %pad_maximum_fusion.1.refs_1_), channel_id=1, source_target_pairs={{32,0},{64,32},{96,64},{0,96},{33,1},{65,33},{97,65},{1,97},{34,2}... | collective-permute-start | bytes 294920 | tf_op jit(solution)/shard_map/ppermute | solution.py:239
  48.1 9.7 %collective-permute-start.18 = (bf16[192,256]{1,0:T(8,128)(2,1)S(1)}, bf16[192,256]{1,0:T(8,128)(2,1)S(1)}, u32[]{:S(2)}, u32[]{:S(2)}) collective-permute-start(bf16[192,256]{1,0:T(8,128)(2,1)S(1)} %pad_maximum_fusion.1.refs_1_), channel_id=1, source_target_pairs={{64,0},{96,32},{0,64},{32,96},{65,1},{97,33},{1,65},{33,97},{66,2}... | collective-permute-start | bytes 294920 | tf_op jit(solution)/shard_map/ppermute | solution.py:239
  48.9 8.9 %collective-permute-start.19 = (bf16[192,256]{1,0:T(8,128)(2,1)S(1)}, bf16[192,256]{1,0:T(8,128)(2,1)S(1)}, u32[]{:S(2)}, u32[]{:S(2)}) collective-permute-start(bf16[192,256]{1,0:T(8,128)(2,1)S(1)} %pad_maximum_fusion.1.refs_1_), channel_id=1, source_target_pairs={{96,0},{0,32},{32,64},{64,96},{97,1},{1,33},{33,65},{65,97},{98,2}... | collective-permute-start | bytes 294920 | tf_op jit(solution)/shard_map/ppermute | solution.py:239
  53.6 4.3 %collective-permute-start.16 = (bf16[128,256]{1,0:T(8,128)(2,1)S(1)}, bf16[128,256]{1,0:T(8,128)(2,1)S(1)}, u32[]{:S(2)}, u32[]{:S(2)}) collective-permute-start(bf16[128,256]{1,0:T(8,128)(2,1)S(1)} %get-tuple-element.52), channel_id=1, source_target_pairs={{0,128},{128,0},{1,129},{129,1},{2,130},{130,2},{3,131},{131,3},{4... | collective-permute-start | bytes 196616 | tf_op jit(solution)/shard_map/ppermute | solution.py:234
  59.3 1.6 %collective-permute-start.20 = (bf16[512,256]{1,0:T(8,128)(2,1)S(1)}, bf16[512,256]{1,0:T(8,128)(2,1)S(1)}, u32[]{:S(2)}, u32[]{:S(2)}) collective-permute-start(bf16[512,256]{1,0:T(8,128)(2,1)S(1)} %get-tuple-element.57), channel_id=1, source_target_pairs={{0,16},{16,0},{1,17},{17,1},{2,18},{18,2},{3,19},{19,3},{4,20},{20... | collective-permute-start | bytes 786440 | tf_op jit(solution)/shard_map/ppermute | solution.py:234
  64.3 12.5 %collective-permute-start.21 = (bf16[448,256]{1,0:T(8,128)(2,1)S(1)}, bf16[448,256]{1,0:T(8,128)(2,1)S(1)}, u32[]{:S(2)}, u32[]{:S(2)}) collective-permute-start(bf16[448,256]{1,0:T(8,128)(2,1)S(1)} %bitcast.35), channel_id=1, source_target_pairs={{32,0},{64,32},{96,64},{0,96},{33,1},{65,33},{97,65},{1,97},{34,2}... | collective-permute-start | bytes 688136 | tf_op jit(solution)/shard_map/ppermute | solution.py:239
  66.7 10.1 %collective-permute-start.22 = (bf16[448,256]{1,0:T(8,128)(2,1)S(1)}, bf16[448,256]{1,0:T(8,128)(2,1)S(1)}, u32[]{:S(2)}, u32[]{:S(2)}) collective-permute-start(bf16[448,256]{1,0:T(8,128)(2,1)S(1)} %bitcast.36), channel_id=1, source_target_pairs={{64,0},{96,32},{0,64},{32,96},{65,1},{97,33},{1,65},{33,97},{66,2}... | collective-permute-start | bytes 688136 | tf_op jit(solution)/shard_map/ppermute | solution.py:239
  68.4 12.2 %collective-permute-start.23 = (bf16[448,256]{1,0:T(8,128)(2,1)S(1)}, bf16[448,256]{1,0:T(8,128)(2,1)S(1)}, u32[]{:S(2)}, u32[]{:S(2)}) collective-permute-start(bf16[448,256]{1,0:T(8,128)(2,1)S(1)} %bitcast.37), channel_id=1, source_target_pairs={{96,0},{0,32},{32,64},{64,96},{97,1},{1,33},{33,65},{65,97},{98,2}... | collective-permute-start | bytes 688136 | tf_op jit(solution)/shard_map/ppermute | solution.py:239

commit v7 on v6

--- a/solution.py
+++ b/solution.py
@@ -30,29 +30,35 @@
 VMEM = pl.BlockSpec(memory_space=pltpu.VMEM)
 
 
-def normalise_kernel(where_ref, student_ref, keep_ref, send_ref, spread_ref, *, wrows):
-    core = where_ref[2]
-    rows, features = student_ref.shape
-    chunk, wide = spread_ref.shape
+def spread_tile(first, last, wide, wrows):
     target = lax.broadcasted_iota(jnp.int32, (1, wide), 1)
     inside = lax.rem(target, PADDED)
     target = jnp.where(inside < wrows, target // PADDED * wrows + inside, -1)
-    source = lax.broadcasted_iota(jnp.int32, (chunk, 1), 0)
-    spread_ref[...] = jnp.where(source == target, 1.0, 0.0).astype(jnp.bfloat16)
+    source = lax.broadcasted_iota(jnp.int32, (last - first, 1), 0) + first
+    return jnp.where(source == target, 1.0, 0.0).astype(jnp.bfloat16)
+
+
+def normalise_kernel(where_ref, student_ref, keep_ref, send_ref, *, wrows):
+    core = where_ref[2]
+    rows, features = student_ref.shape
+    group = 16 * PADDED
+    taken = 16 * wrows
+    chunk = features // 4
     as_float = student_ref[...].astype(jnp.float32)
     scale = lax.rsqrt(jnp.mean(as_float * as_float, axis=1, keepdims=True) + EPSILON)
     normed = (as_float * scale).astype(jnp.bfloat16)
-    group = 16 * PADDED
-    for k in range(features // chunk):
+    stacked = jnp.concatenate([normed[:, k * chunk : (k + 1) * chunk] for k in range(4)], axis=0)
+    for q in range(chunk // taken):
+        first = q * taken // 128 * 128
+        last = min(chunk, -(-(q + 1) * taken // 128) * 128)
+        tile = spread_tile(first - q * taken, last - q * taken, group, wrows)
         apart = jnp.dot(
-            normed[:, k * chunk : (k + 1) * chunk],
-            spread_ref[...],
-            preferred_element_type=jnp.float32,
+            stacked[:, first:last], tile, preferred_element_type=jnp.float32
         ).astype(jnp.bfloat16)
-        for q in range(wide // group):
-            g = k * (wide // group) + q
+        for k in range(4):
+            g = k * (chunk // taken) + q
             at = (g // 2 % 4 * 2 + g // 8) * group
-            piece = apart[:, q * group : (q + 1) * group]
+            piece = apart[k * rows : (k + 1) * rows]
 
             @pl.when(core == g % 2)
             def _():
@@ -66,7 +72,6 @@
 def normalise(here, student_in, wrows):
     rows, features = student_in.shape
     shape = jax.ShapeDtypeStruct((rows, features // wrows * PADDED // 2), jnp.bfloat16)
-    chunk = features // 4
 
     def body(*refs):
         normalise_kernel(*refs, wrows=wrows)
@@ -76,7 +81,6 @@
         out_shape=(shape, shape),
         in_specs=[SMEM, VMEM],
         out_specs=(VMEM, VMEM),
-        scratch_shapes=[pltpu.VMEM((chunk, chunk // wrows * PADDED), jnp.bfloat16)],
         compiler_params=pltpu.CompilerParams(vmem_limit_bytes=16 << 20),
         name="normalise",
     )(here, student_in)
@@ -230,6 +234,45 @@
     return jnp.where(which == 0, low, high), jnp.where(which == 0, high, low)
 
 
+def gradient_kernel(where_ref, n_ref, own_ref, back_ref, *out_refs):
+    x = where_ref[4]
+    columns = n_ref.shape[1] // 4
+    taken = out_refs[0].shape[0]
+    wrows = taken * PADDED // columns
+    diff = own_ref[...] + back_ref[...].astype(jnp.float32)
+    scaled = (diff * TOKENS_ALL ** (-0.5)).astype(jnp.bfloat16)
+    step = 128 // PADDED * wrows
+    target = lax.broadcasted_iota(jnp.int32, (1, 128), 1)
+    inside = lax.rem(target, PADDED)
+    target = jnp.where(inside < wrows, target // PADDED * wrows + inside, -1)
+    row = lax.broadcasted_iota(jnp.int32, (step, 1), 0)
+    cut = jnp.where(row == target, 1.0, 0.0).astype(jnp.bfloat16)
+    for d, out_ref in enumerate(out_refs):
+        at = pl.multiple_of(lax.rem(x + 4 - d, 4) * columns, columns)
+        part = lax.dot_general(
+            n_ref[:, pl.ds(at, columns)],
+            scaled,
+            (((0,), (0,)), ((), ())),
+            preferred_element_type=jnp.float32,
+        ).astype(jnp.bfloat16)
+        for j in range(columns // 128):
+            out_ref[j * step : (j + 1) * step, :] = jnp.dot(
+                cut, part[j * 128 : (j + 1) * 128], preferred_element_type=jnp.float32
+            ).astype(jnp.bfloat16)
+
+
+def gradient(here, n_all, own, back, wrows):
+    shape = jax.ShapeDtypeStruct((n_all.shape[1] // 4 // PADDED * wrows, HALF), jnp.bfloat16)
+    return pl.pallas_call(
+        gradient_kernel,
+        out_shape=(shape,) * 4,
+        in_specs=[SMEM, VMEM, VMEM, VMEM],
+        out_specs=(VMEM,) * 4,
+        compiler_params=pltpu.CompilerParams(vmem_limit_bytes=16 << 20),
+        name="gradient",
+    )(here, n_all, own, back)
+
+
 def partner(x, axis):
     return lax.ppermute(x, axis, [(0, 1), (1, 0)])
 
@@ -242,38 +285,34 @@
 def local(student_in, weight, queries, keys, values, lengths, assignment):
     names = ("z", "yhi", "core", "ylo", "x")
     here = jnp.stack([lax.axis_index(a) for a in names]).astype(jnp.int32)
-    ylo, x = here[3], here[4]
     wrows = weight.shape[0]
 
-    kv = jnp.concatenate([keys, values], axis=1)
+    lane = lax.broadcasted_iota(jnp.int32, (keys.shape[0], 2 * HD), 1)
+    kv = jnp.where(
+        lane < HD, jnp.pad(keys, ((0, 0), (0, HD))), jnp.pad(values, ((0, 0), (HD, 0)))
+    )
+    w_mine, w_other = halves(weight, here[3])
     kv_other = partner(kv, "yhi")
-    w_mine, w_other = halves(weight, ylo)
     w_parts = [
         w_mine,
         partner(w_other, "ylo"),
         partner(w_mine, "yhi"),
         lax.ppermute(w_other, ("ylo", "yhi"), [(i, 3 - i) for i in range(4)]),
     ]
-
-    student_in, _ = lax.optimization_barrier((student_in, (kv, w_mine)))
+    packed = pack(kv, kv_other, w_parts)
+
+    student_in, _ = lax.optimization_barrier((student_in, packed))
     n_keep, n_send = normalise(here, student_in, wrows)
-    n_keep, n_send, kv_other, w_parts = lax.optimization_barrier(
-        (n_keep, n_send, kv_other, w_parts)
-    )
-    packed = pack(kv, kv_other, w_parts)
-    n_got = partner(n_send, "core")
-    n_got, _ = lax.optimization_barrier((n_got, packed))
-    n_pair = jnp.concatenate([n_keep, n_got], axis=0)
+    up, down = from_next(packed, "z", 1), from_next(packed, "z", -1)
+    up, down, n_keep, n_send = lax.optimization_barrier((up, down, n_keep, n_send))
+    n_pair = jnp.concatenate([n_keep, partner(n_send, "core")], axis=0)
     n_all = jnp.concatenate([n_pair, partner(n_pair, "ylo")], axis=0)
 
-    up = down = packed
-    held = {0: packed}
-    for d in range(1, 5):
-        up = from_next(up, "z", 1)
-        held[d] = up
+    held = {0: packed, 1: up, -1: down}
+    for d in range(2, 5):
+        held[d] = from_next(held[d - 1], "z", 1)
         if d < 4:
-            down = from_next(down, "z", -1)
-            held[-d] = down
+            held[-d] = from_next(held[1 - d], "z", -1)
     near_rows = jnp.concatenate([held[d][2 * BLK :] for d in NEAR], axis=0)
     far_rows = jnp.concatenate([held[d][2 * BLK :] for d in FAR], axis=0)
     near_got = [from_next(near_rows, "x", d) for d in range(1, 4)]
@@ -288,16 +327,10 @@
     attention, a_mine, a_other = attend(here, queries, parts, lengths, assignment)
 
     own, send = project(here, n_all, a_mine, partner(a_other, "ylo"), w_all)
-    diff = own + partner(send, "core").astype(jnp.float32)
-    scaled = (diff * TOKENS_ALL ** (-0.5)).astype(jnp.bfloat16)
-    part = lax.dot_general(
-        n_all, scaled, (((0,), (0,)), ((), ())), preferred_element_type=jnp.float32
-    ).astype(jnp.bfloat16)
-    part = part.reshape(4, 32, PADDED, HALF)[:, :, :wrows].reshape(4, 32 * wrows, HALF)
-    near = lax.dynamic_index_in_dim(part, x, 0, keepdims=False).astype(jnp.float32)
+    near, *away = gradient(here, n_all, own, partner(send, "core"), wrows)
+    near = near.astype(jnp.float32)
     for d in range(1, 4):
-        away = lax.dynamic_index_in_dim(part, (x - d) % 4, 0, keepdims=False)
-        near = near + from_next(away, "x", d).astype(jnp.float32)
+        near = near + from_next(away[d - 1], "x", d).astype(jnp.float32)
     near = near.astype(jnp.bfloat16).reshape(-1, wrows, HALF)
     near = jnp.pad(near, ((0, 0), (0, PADDED - wrows), (0, 0)))
     last = lax.all_to_all(near, ("ylo", *SEQ), split_axis=0, concat_axis=0, tiled=True)

time: 102 us -> 99.5 us (0.975)
  starting transfers between devices: 35.2 us -> 31.3 us
  waiting for transfers between devices: 29.1 us -> 32.4 us
  local copies, waits for them, and re-layouts: 3.92 us -> 1.59 us
  Pallas kernels: 8.18 us -> 9.84 us
    ppermute x7, waiting for transfers between devices: 4.26 us -> 6.76 us  [partner(): return lax.ppermute(x, axis, [(0, 1), (1, 0)])]
    ppermute x16, starting transfers between devices: 25.5 us -> 23.1 us  [from_next(): lax.ppermute(x, axis, [((i + distance) % size, i) for i in range(size)])]
    pallas_call x0 -> x1, Pallas kernels: none -> 2.26 us  [gradient(): pl.pallas_call(gradient_kernel, out_shape=(shape,) * 4, in_specs=[SMEM, V...]
    dynamic_slice x1 -> x0, other arithmetic: 1.78 us -> none  [local(): away = lax.dynamic_index_in_dim(part, (x - d) % 4, 0, keepdims=False)]
    unnamed x19 -> x14, local copies, waits for them, and re-layouts: 2.85 us -> 1.29 us
    ppermute x1, waiting for transfers between devices: 0.01 us -> 1.55 us  [local(): lax.ppermute(w_other, ('ylo', 'yhi'), [(i, 3 - i) for i in range(4)])]
    ppermute x7, starting transfers between devices: 7.48 us -> 5.99 us  [partner(): return lax.ppermute(x, axis, [(0, 1), (1, 0)])]
  transfers between devices with their start and end apart: 24 -> 24, of which waited for: 9 -> 12; matrix products, arithmetic and copies ran while one was open for 1% -> 1% of each run, Pallas kernels for 7% -> 6%
where the time goes in v7:
time: 99.5 us; the launch traced here: 99.2 us
  waiting for transfers between devices  32.4 us (33%)
  starting transfers between devices  31.3 us (31%)
  blocking collectives  20.9 us (21%)
  Pallas kernels  9.84 us (10%)
  other arithmetic  2.39 us (2%)
  local copies, waits for them, and re-layouts  1.59 us (2%)
    ppermute x16, waiting for transfers between devices, from_next(): lax.ppermute(x, axis, [((i + distance) % size, i) for i in range(size)])  24.1 us
    ppermute x16, starting transfers between devices, from_next(): lax.ppermute(x, axis, [((i + distance) % size, i) for i in range(size)])  23.1 us
    all_to_all x1, blocking collectives, local(): lax.all_to_all(near, ('ylo', *SEQ), split_axis=0, concat_axis=0, tiled=True)  20.9 us
    ppermute x7, waiting for transfers between devices, partner(): return lax.ppermute(x, axis, [(0, 1), (1, 0)])  6.76 us
    ppermute x7, starting transfers between devices, partner(): return lax.ppermute(x, axis, [(0, 1), (1, 0)])  5.99 us
    pallas_call x1, Pallas kernels, attend(): pl.pallas_call(attend_kernel, out_shape=(jax.ShapeDtypeStruct((rows, COLS...  3.76 us
    pallas_call x1, Pallas kernels, normalise(): pl.pallas_call(body, out_shape=(shape, shape), in_specs=[SMEM, VMEM], out...  2.32 us
    pallas_call x1, Pallas kernels, gradient(): pl.pallas_call(gradient_kernel, out_shape=(shape,) * 4, in_specs=[SMEM, V...  2.26 us
  transfers between devices with their start and end apart: 24, of which 12 were waited for; matrix products, arithmetic and copies ran while one was open for 1% of the time, Pallas kernels for 6%

profile of v7, /device:TPU:32, one launch (start us, length us, event | category | flops | bytes accessed | tf_op | source)
XLA Modules:
  0.0 99.2 jit_solution(4981739809621608250)
XLA Ops:
  0.6 0.8 pad_select_fusion.kv_ref
  1.4 3.3 %collective-permute-start = (bf16[128,256]{1,0:T(8,128)(2,1)S(1)}, bf16[128,256]{1,0:T(8,128)(2,1)S(1)}, u32[]{:S(2)}, u32[]{:S(2)}) collective-permute-start(bf16[128,256]{1,0:T(8,128)(2,1)S(1)} %pad_select_fusion.kv_ref), channel_id=1, source_target_pairs={{0,1},{1,0},{2,3},{3,2},{4,5},{5,4},{6,7},{7,6},{8,9},{9,8},{10,11... | collective-permute-start | bytes 196616 | tf_op jit(solution)/shard_map/ppermute | solution.py:277
  4.7 0.7 broadcast_select_fusion
  5.4 0.7 collective-permute-start.1
  6.1 1.8 %collective-permute-start.2 = (bf16[14,256]{1,0:T(8,128)(2,1)S(1)}, bf16[14,256]{1,0:T(8,128)(2,1)S(1)}, u32[]{:S(2)}, u32[]{:S(2)}) collective-permute-start(bf16[14,256]{1,0:T(8,128)(2,1)S(1)} %get-tuple-element.61.refs_0_), channel_id=1, source_target_pairs={{0,1},{1,0},{2,3},{3,2},{4,5},{5,4},{6,7},{7,6},{8,9},{9,8},{10,11... | collective-permute-start | bytes 21512 | tf_op jit(solution)/shard_map/ppermute | solution.py:277
  8.0 2.2 %collective-permute-start.3 = (bf16[14,256]{1,0:T(8,128)(2,1)S(1)}, bf16[14,256]{1,0:T(8,128)(2,1)S(1)}, u32[]{:S(2)}, u32[]{:S(2)}) collective-permute-start(bf16[14,256]{1,0:T(8,128)(2,1)S(1)} %get-tuple-element.60), channel_id=1, source_target_pairs={{0,129},{1,128},{128,1},{129,0},{2,131},{3,130},{130,3},{131,2},{4... | collective-permute-start | bytes 21512 | tf_op jit(solution)/shard_map/ppermute | solution.py:300
  10.1 0.0 collective-permute-done.1.refs_1_
  10.1 1.1 %collective-permute-done.2.refs_2_ = bf16[14,256]{1,0:T(8,128)(2,1)S(1)} collective-permute-done((bf16[14,256]{1,0:T(8,128)(2,1)S(1)}, bf16[14,256]{1,0:T(8,128)(2,1)S(1)}, u32[]{:S(2)}, u32[]{:S(2)}) %collective-permute-start.2) | collective-permute-done | bytes 7200 | tf_op jit(solution)/shard_map/ppermute | solution.py:277
  11.3 1.5 %collective-permute-done.3.refs_3_ = bf16[14,256]{1,0:T(8,128)(2,1)S(1)} collective-permute-done((bf16[14,256]{1,0:T(8,128)(2,1)S(1)}, bf16[14,256]{1,0:T(8,128)(2,1)S(1)}, u32[]{:S(2)}, u32[]{:S(2)}) %collective-permute-start.3) | collective-permute-done | bytes 7200 | tf_op jit(solution)/shard_map/ppermute | solution.py:300
  12.8 0.0 collective-permute-done.kv_other_ref
  12.8 0.2 collective-permute-start.4
  13.0 1.9 %collective-permute-start.5 = (bf16[320,256]{1,0:T(8,128)(2,1)S(1)}, bf16[320,256]{1,0:T(8,128)(2,1)S(1)}, u32[]{:S(2)}, u32[]{:S(2)}) collective-permute-start(bf16[320,256]{1,0:T(8,128)(2,1)S(1)} %pack.1.refs_0_), channel_id=1, source_target_pairs={{14,0},{0,2},{2,4},{4,6},{6,8},{8,10},{10,12},{12,14},{15,1},{1,3}... | collective-permute-start | bytes 491528 | tf_op jit(solution)/shard_map/ppermute | solution.py:282
  14.9 0.1 stack.23.refs_0_.where_ref
  15.0 1.2 %copy-done = bf16[128,3584]{1,0:T(8,128)(2,1)S(1)} copy-done((bf16[128,3584]{1,0:T(8,128)(2,1)S(1)}, bf16[128,3584]{1,0:T(8,128)(2,1)}, u32[]{:S(2)}) %copy-start) | copy-done | bytes 917528
  16.2 2.3 %normalise.1 = (bf16[128,2048]{1,0:T(8,128)(2,1)S(1)}, bf16[128,2048]{1,0:T(8,128)(2,1)S(1)}) custom-call(s32[5]{0:T(128)S(1)} %stack.23.refs_0_.where_ref, bf16[128,3584]{1,0:T(8,128)(2,1)S(1)} %copy-done), custom_call_target="tpu_custom_call" | custom-call | tf_op jit(solution)/shard_map/normalise/pallas_call | solution.py:79
  18.5 0.0 copy-start.1
  18.5 0.0 copy-start.2
  18.6 0.0 copy-start.3
  18.6 0.0 collective-permute-done.4.refs_1_
  18.6 3.6 %collective-permute-done.5.refs_2_ = bf16[320,256]{1,0:T(8,128)(2,1)S(1)} collective-permute-done((bf16[320,256]{1,0:T(8,128)(2,1)S(1)}, bf16[320,256]{1,0:T(8,128)(2,1)S(1)}, u32[]{:S(2)}, u32[]{:S(2)}) %collective-permute-start.5) | collective-permute-done | bytes 163872 | tf_op jit(solution)/shard_map/ppermute | solution.py:282
  22.2 0.0 collective-permute-start.14
  22.2 3.2 %collective-permute-start.6 = (bf16[320,256]{1,0:T(8,128)(2,1)S(1)}, bf16[320,256]{1,0:T(8,128)(2,1)S(1)}, u32[]{:S(2)}, u32[]{:S(2)}) collective-permute-start(bf16[320,256]{1,0:T(8,128)(2,1)S(1)} %collective-permute-done.4.refs_1_), channel_id=1, source_target_pairs={{2,0},{4,2},{6,4},{8,6},{10,8},{12,10},{14,12},{0,14},{3,1},{5,3},... | collective-permute-start | bytes 491528 | tf_op jit(solution)/shard_map/ppermute | solution.py:282
  25.4 0.0 collective-permute-start.7
  25.4 0.0 collective-permute-done.14
  25.4 0.1 pad_maximum_fusion
  25.5 0.1 collective-permute-start.15
  25.6 3.9 %collective-permute-done.6.refs_3_ = bf16[320,256]{1,0:T(8,128)(2,1)S(1)} collective-permute-done((bf16[320,256]{1,0:T(8,128)(2,1)S(1)}, bf16[320,256]{1,0:T(8,128)(2,1)S(1)}, u32[]{:S(2)}, u32[]{:S(2)}) %collective-permute-start.6) | collective-permute-done | bytes 163872 | tf_op jit(solution)/shard_map/ppermute | solution.py:282
  29.5 2.5 %collective-permute-start.8 = (bf16[320,256]{1,0:T(8,128)(2,1)S(1)}, bf16[320,256]{1,0:T(8,128)(2,1)S(1)}, u32[]{:S(2)}, u32[]{:S(2)}) collective-permute-start(bf16[320,256]{1,0:T(8,128)(2,1)S(1)} %collective-permute-done.6.refs_3_), channel_id=1, source_target_pairs={{2,0},{4,2},{6,4},{8,6},{10,8},{12,10},{14,12},{0,14},{3,1},{5,3},... | collective-permute-start | bytes 491528 | tf_op jit(solution)/shard_map/ppermute | solution.py:282
  32.0 0.0 collective-permute-done.7.refs_4_
  32.0 0.0 collective-permute-start.9
  32.1 2.8 %collective-permute-start.11 = (bf16[320,256]{1,0:T(8,128)(2,1)S(1)}, bf16[320,256]{1,0:T(8,128)(2,1)S(1)}, u32[]{:S(2)}, u32[]{:S(2)}) collective-permute-start(bf16[320,256]{1,0:T(8,128)(2,1)S(1)} %slice_dynamic-update-slice_fusion.refs_0_), channel_id=1, source_target_pairs={{32,0},{64,32},{96,64},{0,96},{33,1},{65,33},{97,65},{1,97},{34,2}... | collective-permute-start | bytes 491528 | tf_op jit(solution)/shard_map/ppermute | solution.py:282
  34.9 0.8 collective-permute-start.12
  35.7 0.0 collective-permute-done.8.refs_5_
  35.7 1.2 %collective-permute-start.13 = (bf16[320,256]{1,0:T(8,128)(2,1)S(1)}, bf16[320,256]{1,0:T(8,128)(2,1)S(1)}, u32[]{:S(2)}, u32[]{:S(2)}) collective-permute-start(bf16[320,256]{1,0:T(8,128)(2,1)S(1)} %slice_dynamic-update-slice_fusion.refs_0_), channel_id=1, source_target_pairs={{96,0},{0,32},{32,64},{64,96},{97,1},{1,33},{33,65},{65,97},{98,2}... | collective-permute-start | bytes 491528 | tf_op jit(solution)/shard_map/ppermute | solution.py:282
  36.9 0.7 collective-permute-done.9.refs_6_
  37.6 2.8 %collective-permute-start.10 = (bf16[320,256]{1,0:T(8,128)(2,1)S(1)}, bf16[320,256]{1,0:T(8,128)(2,1)S(1)}, u32[]{:S(2)}, u32[]{:S(2)}) collective-permute-start(bf16[320,256]{1,0:T(8,128)(2,1)S(1)} %collective-permute-done.8.refs_5_), channel_id=1, source_target_pairs={{2,0},{4,2},{6,4},{8,6},{10,8},{12,10},{14,12},{0,14},{3,1},{5,3},... | collective-permute-start | bytes 491528 | tf_op jit(solution)/shard_map/ppermute | solution.py:282
  40.4 2.8 %collective-permute-done.10.refs_7_ = bf16[320,256]{1,0:T(8,128)(2,1)S(1)} collective-permute-done((bf16[320,256]{1,0:T(8,128)(2,1)S(1)}, bf16[320,256]{1,0:T(8,128)(2,1)S(1)}, u32[]{:S(2)}, u32[]{:S(2)}) %collective-permute-start.10) | collective-permute-done | bytes 163872 | tf_op jit(solution)/shard_map/ppermute | solution.py:282
  43.2 0.2 collective-permute-done.12.refs_4_
  43.4 1.7 %collective-permute-done.13.refs_6_ = bf16[320,256]{1,0:T(8,128)(2,1)S(1)} collective-permute-done((bf16[320,256]{1,0:T(8,128)(2,1)S(1)}, bf16[320,256]{1,0:T(8,128)(2,1)S(1)}, u32[]{:S(2)}, u32[]{:S(2)}) %collective-permute-start.13) | collective-permute-done | bytes 163872 | tf_op jit(solution)/shard_map/ppermute | solution.py:282
  45.2 0.9 collective-permute-start.17
  46.1 0.8 collective-permute-start.18
  46.9 0.9 collective-permute-start.19
  47.8 3.8 %attend.1 = (bf16[128,512]{1,0:T(8,128)(2,1)}, bf16[128,256]{1,0:T(8,128)(2,1)S(1)}, bf16[128,256]{1,0:T(8,128)(2,1)S(1)}) custom-call(s32[5]{0:T(128)S(1)} %stack.23.refs_0_.where_ref, s32[1,16]{1,0:T(1,128)S(1)} %copy-done.2, s32[1,4]{1,0:T(1,128)S(1)} %copy-done.3, bf16[128,512]{1,0:T(8,128)(2,1)S(1)} %copy-done.1, bf16[320,256]{1,0:T(8,128)(2,1)S(1)} %pack.1.refs_0_, ...), custom_call_target="tpu_custom_call" | custom-call | tf_op jit(solution)/shard_map/attend/pallas_call | solution.py:174
  51.6 0.0 collective-permute-start.16
  51.6 0.0 collective-permute-done.15
  51.6 0.1 constant_dynamic-update-slice_fusion.n_ref
  51.7 4.1 %collective-permute-done.16.got_ref = bf16[128,256]{1,0:T(8,128)(2,1)S(1)} collective-permute-done((bf16[128,256]{1,0:T(8,128)(2,1)S(1)}, bf16[128,256]{1,0:T(8,128)(2,1)S(1)}, u32[]{:S(2)}, u32[]{:S(2)}) %collective-permute-start.16) | collective-permute-done | bytes 65568 | tf_op jit(solution)/shard_map/ppermute | solution.py:277
  55.8 0.0 collective-permute-done.17.refs_3_
  55.8 0.0 collective-permute-done.18.refs_5_
  55.8 0.0 collective-permute-done.19.refs_7_
  55.8 1.5 %project.1 = (f32[512,256]{1,0:T(8,128)S(1)}, bf16[512,256]{1,0:T(8,128)(2,1)S(1)}) custom-call(s32[5]{0:T(128)S(1)} %stack.23.refs_0_.where_ref, bf16[512,2048]{1,0:T(8,128)(2,1)S(1)} %constant_dynamic-update-slice_fusion.n_ref, bf16[128,256]{1,0:T(8,128)(2,1)S(1)} %get-tuple-element.47.mine_ref, bf16[128,256]{1,0:T(8,128)(2,1)S(1)} %collective-permute-done.16.got_ref, ...), custom_call_target="tpu_custom_call" | custom-call | tf_op jit(solution)/shard_map/project/pallas_call | solution.py:217
  57.3 0.1 collective-permute-start.20
  57.4 1.5 %collective-permute-done.20.back_ref = bf16[512,256]{1,0:T(8,128)(2,1)S(1)} collective-permute-done((bf16[512,256]{1,0:T(8,128)(2,1)S(1)}, bf16[512,256]{1,0:T(8,128)(2,1)S(1)}, u32[]{:S(2)}, u32[]{:S(2)}) %collective-permute-start.20) | collective-permute-done | bytes 262176 | tf_op jit(solution)/shard_map/ppermute | solution.py:277
  59.0 2.3 %gradient.1 = (bf16[448,256]{1,0:T(8,128)(2,1)S(1)}, bf16[448,256]{1,0:T(8,128)(2,1)S(1)}, bf16[448,256]{1,0:T(8,128)(2,1)S(1)}, bf16[448,256]{1,0:T(8,128)(2,1)S(1)}) custom-call(s32[5]{0:T(128)S(1)} %stack.23.refs_0_.where_ref, bf16[512,2048]{1,0:T(8,128)(2,1)S(1)} %constant_dynamic-update-slice_fusion.n_ref, f32[512,256]{1,0:T(8,128)S(1)} %get-tuple-element.52.own_ref, ...), custom_call_target="tpu_custom_call" | custom-call | tf_op jit(solution)/shard_map/gradient/pallas_call | solution.py:266
  61.2 2.4 %collective-permute-start.21 = (bf16[448,256]{1,0:T(8,128)(2,1)S(1)}, bf16[448,256]{1,0:T(8,128)(2,1)S(1)}, u32[]{:S(2)}, u32[]{:S(2)}) collective-permute-start(bf16[448,256]{1,0:T(8,128)(2,1)S(1)} %get-tuple-element.55), channel_id=1, source_target_pairs={{32,0},{64,32},{96,64},{0,96},{33,1},{65,33},{97,65},{1,97},{34,2}... | collective-permute-start | bytes 688136 | tf_op jit(solution)/shard_map/ppermute | solution.py:282
  63.6 1.5 %collective-permute-start.22 = (bf16[448,256]{1,0:T(8,128)(2,1)S(1)}, bf16[448,256]{1,0:T(8,128)(2,1)S(1)}, u32[]{:S(2)}, u32[]{:S(2)}) collective-permute-start(bf16[448,256]{1,0:T(8,128)(2,1)S(1)} %get-tuple-element.56), channel_id=1, source_target_pairs={{64,0},{96,32},{0,64},{32,96},{65,1},{97,33},{1,65},{33,97},{66,2}... | collective-permute-start | bytes 688136 | tf_op jit(solution)/shard_map/ppermute | solution.py:282
  65.2 1.1 %collective-permute-start.23 = (bf16[448,256]{1,0:T(8,128)(2,1)S(1)}, bf16[448,256]{1,0:T(8,128)(2,1)S(1)}, u32[]{:S(2)}, u32[]{:S(2)}) collective-permute-start(bf16[448,256]{1,0:T(8,128)(2,1)S(1)} %get-tuple-element.57), channel_id=1, source_target_pairs={{96,0},{0,32},{32,64},{64,96},{97,1},{1,33},{33,65},{65,97},{98,2}... | collective-permute-start | bytes 688136 | tf_op jit(solution)/shard_map/ppermute | solution.py:282
  66.3 7.5 %collective-permute-done.21 = bf16[448,256]{1,0:T(8,128)(2,1)S(1)} collective-permute-done((bf16[448,256]{1,0:T(8,128)(2,1)S(1)}, bf16[448,256]{1,0:T(8,128)(2,1)S(1)}, u32[]{:S(2)}, u32[]{:S(2)}) %collective-permute-start.21) | collective-permute-done | bytes 229408 | tf_op jit(solution)/shard_map/ppermute | solution.py:282
  73.8 0.0 collective-permute-done.22
  73.8 3.7 %collective-permute-done.23 = bf16[448,256]{1,0:T(8,128)(2,1)S(1)} collective-permute-done((bf16[448,256]{1,0:T(8,128)(2,1)S(1)}, bf16[448,256]{1,0:T(8,128)(2,1)S(1)}, u32[]{:S(2)}, u32[]{:S(2)}) %collective-permute-start.23) | collective-permute-done | bytes 229408 | tf_op jit(solution)/shard_map/ppermute | solution.py:282
  77.4 0.1 add_convert_fusion
  77.5 0.1 reshape.10
  77.7 20.9 %all_to_all.5 = bf16[32,16,256]{2,1,0:T(8,128)(2,1)S(1)} all-to-all(bf16[32,16,256]{2,1,0:T(8,128)(2,1)S(1)} %pad.14), channel_id=1, replica_groups=mesh['ylo'=2,'x'=4,'core'=2,'z'=8,'yhi'=2] {'ylo','z','yhi'}, dimensions={0} | all-to-all | bytes 524288 | tf_op jit(solution)/shard_map/all_to_all | solution.py:336
  98.6 0.6 pad_maximum_fusion.2
  (21 shorter events, 0.2 us)
Async XLA Ops:
  1.4 11.4 %collective-permute-start = (bf16[128,256]{1,0:T(8,128)(2,1)S(1)}, bf16[128,256]{1,0:T(8,128)(2,1)S(1)}, u32[]{:S(2)}, u32[]{:S(2)}) collective-permute-start(bf16[128,256]{1,0:T(8,128)(2,1)S(1)} %pad_select_fusion.kv_ref), channel_id=1, source_target_pairs={{0,1},{1,0},{2,3},{3,2},{4,5},{5,4},{6,7},{7,6},{8,9},{9,8},{10,11... | collective-permute-start | bytes 196616 | tf_op jit(solution)/shard_map/ppermute | solution.py:277
  5.4 4.7 %collective-permute-start.1 = (bf16[14,256]{1,0:T(8,128)(2,1)S(1)}, bf16[14,256]{1,0:T(8,128)(2,1)S(1)}, u32[]{:S(2)}, u32[]{:S(2)}) collective-permute-start(bf16[14,256]{1,0:T(8,128)(2,1)S(1)} %get-tuple-element.60), channel_id=1, source_target_pairs={{0,128},{128,0},{1,129},{129,1},{2,130},{130,2},{3,131},{131,3},{4... | collective-permute-start | bytes 21512 | tf_op jit(solution)/shard_map/ppermute | solution.py:277
  6.1 5.2 %collective-permute-start.2 = (bf16[14,256]{1,0:T(8,128)(2,1)S(1)}, bf16[14,256]{1,0:T(8,128)(2,1)S(1)}, u32[]{:S(2)}, u32[]{:S(2)}) collective-permute-start(bf16[14,256]{1,0:T(8,128)(2,1)S(1)} %get-tuple-element.61.refs_0_), channel_id=1, source_target_pairs={{0,1},{1,0},{2,3},{3,2},{4,5},{5,4},{6,7},{7,6},{8,9},{9,8},{10,11... | collective-permute-start | bytes 21512 | tf_op jit(solution)/shard_map/ppermute | solution.py:277
  8.0 4.9 %collective-permute-start.3 = (bf16[14,256]{1,0:T(8,128)(2,1)S(1)}, bf16[14,256]{1,0:T(8,128)(2,1)S(1)}, u32[]{:S(2)}, u32[]{:S(2)}) collective-permute-start(bf16[14,256]{1,0:T(8,128)(2,1)S(1)} %get-tuple-element.60), channel_id=1, source_target_pairs={{0,129},{1,128},{128,1},{129,0},{2,131},{3,130},{130,3},{131,2},{4... | collective-permute-start | bytes 21512 | tf_op jit(solution)/shard_map/ppermute | solution.py:300
  12.8 5.7 %collective-permute-start.4 = (bf16[320,256]{1,0:T(8,128)(2,1)S(1)}, bf16[320,256]{1,0:T(8,128)(2,1)S(1)}, u32[]{:S(2)}, u32[]{:S(2)}) collective-permute-start(bf16[320,256]{1,0:T(8,128)(2,1)S(1)} %pack.1.refs_0_), channel_id=1, source_target_pairs={{2,0},{4,2},{6,4},{8,6},{10,8},{12,10},{14,12},{0,14},{3,1},{5,3},... | collective-permute-start | bytes 491528 | tf_op jit(solution)/shard_map/ppermute | solution.py:282
  13.0 9.2 %collective-permute-start.5 = (bf16[320,256]{1,0:T(8,128)(2,1)S(1)}, bf16[320,256]{1,0:T(8,128)(2,1)S(1)}, u32[]{:S(2)}, u32[]{:S(2)}) collective-permute-start(bf16[320,256]{1,0:T(8,128)(2,1)S(1)} %pack.1.refs_0_), channel_id=1, source_target_pairs={{14,0},{0,2},{2,4},{4,6},{6,8},{8,10},{10,12},{12,14},{15,1},{1,3}... | collective-permute-start | bytes 491528 | tf_op jit(solution)/shard_map/ppermute | solution.py:282
  15.0 1.2 %copy-start = (bf16[128,3584]{1,0:T(8,128)(2,1)S(1)}, bf16[128,3584]{1,0:T(8,128)(2,1)}, u32[]{:S(2)}) copy-start(bf16[128,3584]{1,0:T(8,128)(2,1)} %refs_1_) | copy-start | bytes 2752516
  18.5 29.3 %copy-start.1 = (bf16[128,512]{1,0:T(8,128)(2,1)S(1)}, bf16[128,512]{1,0:T(8,128)(2,1)}, u32[]{:S(2)}) copy-start(bf16[128,512]{1,0:T(8,128)(2,1)} %q_ref.1) | copy-start | bytes 393220
  18.5 29.2 %copy-start.2 = (s32[1,16]{1,0:T(1,128)S(1)}, s32[1,16]{1,0:T(1,128)}, u32[]{:S(2)}) copy-start(s32[1,16]{1,0:T(1,128)} %assign_ref.1) | copy-start | bytes 196
  18.6 29.2 %copy-start.3 = (s32[1,4]{1,0:T(1,128)S(1)}, s32[1,4]{1,0:T(1,128)}, u32[]{:S(2)}) copy-start(s32[1,4]{1,0:T(1,128)} %length_ref.1) | copy-start | bytes 52
  22.2 3.3 %collective-permute-start.14 = (bf16[128,2048]{1,0:T(8,128)(2,1)S(1)}, bf16[128,2048]{1,0:T(8,128)(2,1)S(1)}, u32[]{:S(2)}, u32[]{:S(2)}) collective-permute-start(bf16[128,2048]{1,0:T(8,128)(2,1)S(1)} %get-tuple-element.46), channel_id=1, source_target_pairs={{0,16},{16,0},{1,17},{17,1},{2,18},{18,2},{3,19},{19,3},{4,20},{20... | collective-permute-start | bytes 1572872 | tf_op jit(solution)/shard_map/ppermute | solution.py:277
  22.2 7.4 %collective-permute-start.6 = (bf16[320,256]{1,0:T(8,128)(2,1)S(1)}, bf16[320,256]{1,0:T(8,128)(2,1)S(1)}, u32[]{:S(2)}, u32[]{:S(2)}) collective-permute-start(bf16[320,256]{1,0:T(8,128)(2,1)S(1)} %collective-permute-done.4.refs_1_), channel_id=1, source_target_pairs={{2,0},{4,2},{6,4},{8,6},{10,8},{12,10},{14,12},{0,14},{3,1},{5,3},... | collective-permute-start | bytes 491528 | tf_op jit(solution)/shard_map/ppermute | solution.py:282
  25.4 6.6 %collective-permute-start.7 = (bf16[320,256]{1,0:T(8,128)(2,1)S(1)}, bf16[320,256]{1,0:T(8,128)(2,1)S(1)}, u32[]{:S(2)}, u32[]{:S(2)}) collective-permute-start(bf16[320,256]{1,0:T(8,128)(2,1)S(1)} %collective-permute-done.5.refs_2_), channel_id=1, source_target_pairs={{14,0},{0,2},{2,4},{4,6},{6,8},{8,10},{10,12},{12,14},{15,1},{1,3}... | collective-permute-start | bytes 491528 | tf_op jit(solution)/shard_map/ppermute | solution.py:282
  25.5 26.1 %collective-permute-start.15 = (bf16[256,2048]{1,0:T(8,128)(2,1)S(1)}, bf16[256,2048]{1,0:T(8,128)(2,1)S(1)}, u32[]{:S(2)}, u32[]{:S(2)}) collective-permute-start(bf16[256,2048]{1,0:T(8,128)(2,1)S(1)} %pad_maximum_fusion), channel_id=1, source_target_pairs={{0,128},{128,0},{1,129},{129,1},{2,130},{130,2},{3,131},{131,3},{4... | collective-permute-start | bytes 3145736 | tf_op jit(solution)/shard_map/ppermute | solution.py:277
  29.5 6.1 %collective-permute-start.8 = (bf16[320,256]{1,0:T(8,128)(2,1)S(1)}, bf16[320,256]{1,0:T(8,128)(2,1)S(1)}, u32[]{:S(2)}, u32[]{:S(2)}) collective-permute-start(bf16[320,256]{1,0:T(8,128)(2,1)S(1)} %collective-permute-done.6.refs_3_), channel_id=1, source_target_pairs={{2,0},{4,2},{6,4},{8,6},{10,8},{12,10},{14,12},{0,14},{3,1},{5,3},... | collective-permute-start | bytes 491528 | tf_op jit(solution)/shard_map/ppermute | solution.py:282
  32.0 5.6 %collective-permute-start.9 = (bf16[320,256]{1,0:T(8,128)(2,1)S(1)}, bf16[320,256]{1,0:T(8,128)(2,1)S(1)}, u32[]{:S(2)}, u32[]{:S(2)}) collective-permute-start(bf16[320,256]{1,0:T(8,128)(2,1)S(1)} %collective-permute-done.7.refs_4_), channel_id=1, source_target_pairs={{14,0},{0,2},{2,4},{4,6},{6,8},{8,10},{10,12},{12,14},{15,1},{1,3}... | collective-permute-start | bytes 491528 | tf_op jit(solution)/shard_map/ppermute | solution.py:282
  32.1 11.2 %collective-permute-start.11 = (bf16[320,256]{1,0:T(8,128)(2,1)S(1)}, bf16[320,256]{1,0:T(8,128)(2,1)S(1)}, u32[]{:S(2)}, u32[]{:S(2)}) collective-permute-start(bf16[320,256]{1,0:T(8,128)(2,1)S(1)} %slice_dynamic-update-slice_fusion.refs_0_), channel_id=1, source_target_pairs={{32,0},{64,32},{96,64},{0,96},{33,1},{65,33},{97,65},{1,97},{34,2}... | collective-permute-start | bytes 491528 | tf_op jit(solution)/shard_map/ppermute | solution.py:282
  34.9 8.5 %collective-permute-start.12 = (bf16[320,256]{1,0:T(8,128)(2,1)S(1)}, bf16[320,256]{1,0:T(8,128)(2,1)S(1)}, u32[]{:S(2)}, u32[]{:S(2)}) collective-permute-start(bf16[320,256]{1,0:T(8,128)(2,1)S(1)} %slice_dynamic-update-slice_fusion.refs_0_), channel_id=1, source_target_pairs={{64,0},{96,32},{0,64},{32,96},{65,1},{97,33},{1,65},{33,97},{66,2}... | collective-permute-start | bytes 491528 | tf_op jit(solution)/shard_map/ppermute | solution.py:282
  35.7 9.5 %collective-permute-start.13 = (bf16[320,256]{1,0:T(8,128)(2,1)S(1)}, bf16[320,256]{1,0:T(8,128)(2,1)S(1)}, u32[]{:S(2)}, u32[]{:S(2)}) collective-permute-start(bf16[320,256]{1,0:T(8,128)(2,1)S(1)} %slice_dynamic-update-slice_fusion.refs_0_), channel_id=1, source_target_pairs={{96,0},{0,32},{32,64},{64,96},{97,1},{1,33},{33,65},{65,97},{98,2}... | collective-permute-start | bytes 491528 | tf_op jit(solution)/shard_map/ppermute | solution.py:282
  37.6 5.6 %collective-permute-start.10 = (bf16[320,256]{1,0:T(8,128)(2,1)S(1)}, bf16[320,256]{1,0:T(8,128)(2,1)S(1)}, u32[]{:S(2)}, u32[]{:S(2)}) collective-permute-start(bf16[320,256]{1,0:T(8,128)(2,1)S(1)} %collective-permute-done.8.refs_5_), channel_id=1, source_target_pairs={{2,0},{4,2},{6,4},{8,6},{10,8},{12,10},{14,12},{0,14},{3,1},{5,3},... | collective-permute-start | bytes 491528 | tf_op jit(solution)/shard_map/ppermute | solution.py:282
  45.2 10.6 %collective-permute-start.17 = (bf16[192,256]{1,0:T(8,128)(2,1)S(1)}, bf16[192,256]{1,0:T(8,128)(2,1)S(1)}, u32[]{:S(2)}, u32[]{:S(2)}) collective-permute-start(bf16[192,256]{1,0:T(8,128)(2,1)S(1)} %pad_maximum_fusion.1.refs_1_), channel_id=1, source_target_pairs={{32,0},{64,32},{96,64},{0,96},{33,1},{65,33},{97,65},{1,97},{34,2}... | collective-permute-start | bytes 294920 | tf_op jit(solution)/shard_map/ppermute | solution.py:282
  46.1 9.7 %collective-permute-start.18 = (bf16[192,256]{1,0:T(8,128)(2,1)S(1)}, bf16[192,256]{1,0:T(8,128)(2,1)S(1)}, u32[]{:S(2)}, u32[]{:S(2)}) collective-permute-start(bf16[192,256]{1,0:T(8,128)(2,1)S(1)} %pad_maximum_fusion.1.refs_1_), channel_id=1, source_target_pairs={{64,0},{96,32},{0,64},{32,96},{65,1},{97,33},{1,65},{33,97},{66,2}... | collective-permute-start | bytes 294920 | tf_op jit(solution)/shard_map/ppermute | solution.py:282
  46.9 8.9 %collective-permute-start.19 = (bf16[192,256]{1,0:T(8,128)(2,1)S(1)}, bf16[192,256]{1,0:T(8,128)(2,1)S(1)}, u32[]{:S(2)}, u32[]{:S(2)}) collective-permute-start(bf16[192,256]{1,0:T(8,128)(2,1)S(1)} %pad_maximum_fusion.1.refs_1_), channel_id=1, source_target_pairs={{96,0},{0,32},{32,64},{64,96},{97,1},{1,33},{33,65},{65,97},{98,2}... | collective-permute-start | bytes 294920 | tf_op jit(solution)/shard_map/ppermute | solution.py:282
  51.6 4.3 %collective-permute-start.16 = (bf16[128,256]{1,0:T(8,128)(2,1)S(1)}, bf16[128,256]{1,0:T(8,128)(2,1)S(1)}, u32[]{:S(2)}, u32[]{:S(2)}) collective-permute-start(bf16[128,256]{1,0:T(8,128)(2,1)S(1)} %get-tuple-element.48), channel_id=1, source_target_pairs={{0,128},{128,0},{1,129},{129,1},{2,130},{130,2},{3,131},{131,3},{4... | collective-permute-start | bytes 196616 | tf_op jit(solution)/shard_map/ppermute | solution.py:277
  57.3 1.6 %collective-permute-start.20 = (bf16[512,256]{1,0:T(8,128)(2,1)S(1)}, bf16[512,256]{1,0:T(8,128)(2,1)S(1)}, u32[]{:S(2)}, u32[]{:S(2)}) collective-permute-start(bf16[512,256]{1,0:T(8,128)(2,1)S(1)} %get-tuple-element.53), channel_id=1, source_target_pairs={{0,16},{16,0},{1,17},{17,1},{2,18},{18,2},{3,19},{19,3},{4,20},{20... | collective-permute-start | bytes 786440 | tf_op jit(solution)/shard_map/ppermute | solution.py:277
  61.2 12.5 %collective-permute-start.21 = (bf16[448,256]{1,0:T(8,128)(2,1)S(1)}, bf16[448,256]{1,0:T(8,128)(2,1)S(1)}, u32[]{:S(2)}, u32[]{:S(2)}) collective-permute-start(bf16[448,256]{1,0:T(8,128)(2,1)S(1)} %get-tuple-element.55), channel_id=1, source_target_pairs={{32,0},{64,32},{96,64},{0,96},{33,1},{65,33},{97,65},{1,97},{34,2}... | collective-permute-start | bytes 688136 | tf_op jit(solution)/shard_map/ppermute | solution.py:282
  63.6 10.1 %collective-permute-start.22 = (bf16[448,256]{1,0:T(8,128)(2,1)S(1)}, bf16[448,256]{1,0:T(8,128)(2,1)S(1)}, u32[]{:S(2)}, u32[]{:S(2)}) collective-permute-start(bf16[448,256]{1,0:T(8,128)(2,1)S(1)} %get-tuple-element.56), channel_id=1, source_target_pairs={{64,0},{96,32},{0,64},{32,96},{65,1},{97,33},{1,65},{33,97},{66,2}... | collective-permute-start | bytes 688136 | tf_op jit(solution)/shard_map/ppermute | solution.py:282
  65.2 12.3 %collective-permute-start.23 = (bf16[448,256]{1,0:T(8,128)(2,1)S(1)}, bf16[448,256]{1,0:T(8,128)(2,1)S(1)}, u32[]{:S(2)}, u32[]{:S(2)}) collective-permute-start(bf16[448,256]{1,0:T(8,128)(2,1)S(1)} %get-tuple-element.57), channel_id=1, source_target_pairs={{96,0},{0,32},{32,64},{64,96},{97,1},{1,33},{33,65},{65,97},{98,2}... | collective-permute-start | bytes 688136 | tf_op jit(solution)/shard_map/ppermute | solution.py:282

commit v8 on v7

--- a/solution.py
+++ b/solution.py
@@ -23,8 +23,7 @@
 SIZES = (2, 4, 2, 8, 2)
 SEQ = ("z", "yhi")
 
-NEAR = (0, 1, -1, 2, -2)
-FAR = (3, -3, 4)
+RING = (0, 1, -1, 2, -2, 3, -3, 4)
 
 SMEM = pl.BlockSpec(memory_space=pltpu.SMEM)
 VMEM = pl.BlockSpec(memory_space=pltpu.VMEM)
@@ -129,7 +128,7 @@
     lane = lax.broadcasted_iota(jnp.int32, (1, BLK), 1)
     chunk = 2 * BLK
     top = None
-    for c, (distance, kv_ref) in enumerate(zip(NEAR + FAR, kv_refs)):
+    for c, (distance, kv_ref) in enumerate(zip(RING, kv_refs)):
         pair = lax.rem(z + distance + 8, 8) * 2
         k_pos = [assign_ref[0, pair + yhi] * BLK + lane, assign_ref[0, pair + 1 - yhi] * BLK + lane]
         k_pos = jnp.concatenate(k_pos, axis=1)
@@ -188,18 +187,17 @@
     group = 16 * PADDED
     for d in range(4):
         at_x = lax.rem(x + d, 4) * 2
-        for batch, w_ref in zip((NEAR, FAR), w_refs[2 * d : 2 * d + 2]):
-            for k, distance in enumerate(batch):
-                pair = lax.rem(z + distance + 8, 8) * 2
-                for t in range(2):
-                    slot = pair + (yhi if t == 0 else 1 - yhi)
-                    for i in range(2):
-                        side = ylo if i == 0 else 1 - ylo
-                        at = (at_x + side) * group + slot * PADDED
-                        first = (k * 4 + t * 2 + i) * PADDED
-                        w_all[pl.ds(pl.multiple_of(at, PADDED), PADDED), :] = w_ref[
-                            first : first + PADDED, :
-                        ]
+        for k, distance in enumerate(RING):
+            pair = lax.rem(z + distance + 8, 8) * 2
+            for t in range(2):
+                slot = pair + (yhi if t == 0 else 1 - yhi)
+                for i in range(2):
+                    side = ylo if i == 0 else 1 - ylo
+                    at = (at_x + side) * group + slot * PADDED
+                    first = (k * 4 + t * 2 + i) * PADDED
+                    w_all[pl.ds(pl.multiple_of(at, PADDED), PADDED), :] = w_refs[d][
+                        first : first + PADDED, :
+                    ]
     rows = n_ref.shape[0] // 4
     for b in range(4):
         part = jnp.dot(
@@ -306,24 +304,19 @@
     up, down = from_next(packed, "z", 1), from_next(packed, "z", -1)
     up, down, n_keep, n_send = lax.optimization_barrier((up, down, n_keep, n_send))
     n_pair = jnp.concatenate([n_keep, partner(n_send, "core")], axis=0)
-    n_all = jnp.concatenate([n_pair, partner(n_pair, "ylo")], axis=0)
-
     held = {0: packed, 1: up, -1: down}
     for d in range(2, 5):
         held[d] = from_next(held[d - 1], "z", 1)
         if d < 4:
             held[-d] = from_next(held[1 - d], "z", -1)
-    near_rows = jnp.concatenate([held[d][2 * BLK :] for d in NEAR], axis=0)
-    far_rows = jnp.concatenate([held[d][2 * BLK :] for d in FAR], axis=0)
-    near_got = [from_next(near_rows, "x", d) for d in range(1, 4)]
-    far_rows, near_got = lax.optimization_barrier((far_rows, near_got))
-    far_got = [from_next(far_rows, "x", d) for d in range(1, 4)]
-    w_all = [near_rows, far_rows]
-    for pair in zip(near_got, far_got):
-        w_all += pair
-
-    parts = [held[d] for d in NEAR + FAR]
-    parts, _ = lax.optimization_barrier((parts, far_rows))
+        if d == 2:
+            held[2], held[-2], n_pair = lax.optimization_barrier((held[2], held[-2], n_pair))
+    n_all = jnp.concatenate([n_pair, partner(n_pair, "ylo")], axis=0)
+    parts = [held[d] for d in RING]
+    w_rows = jnp.concatenate([part[2 * BLK :] for part in parts], axis=0)
+    w_all = [w_rows] + [from_next(w_rows, "x", d) for d in range(1, 4)]
+
+    parts, _ = lax.optimization_barrier((parts, w_rows))
     attention, a_mine, a_other = attend(here, queries, parts, lengths, assignment)
 
     own, send = project(here, n_all, a_mine, partner(a_other, "ylo"), w_all)

time: 99.5 us -> 99.4 us (level)
  waiting for transfers between devices: 32.4 us -> 38.4 us
  starting transfers between devices: 31.3 us -> 27.2 us
  blocking collectives: 20.9 us -> 18.1 us
    ppermute x16 -> x13, starting transfers between devices: 23.1 us -> 19.1 us  [from_next(): lax.ppermute(x, axis, [((i + distance) % size, i) for i in range(size)])]
    ppermute x7, waiting for transfers between devices: 6.76 us -> 10.7 us  [partner(): return lax.ppermute(x, axis, [(0, 1), (1, 0)])]
    all_to_all x1, blocking collectives: 20.9 us -> 18.1 us  [local(): lax.all_to_all(near, ('ylo', *SEQ), split_axis=0, concat_axis=0, tiled=True)]
    ppermute x16 -> x13, waiting for transfers between devices: 24.1 us -> 26.1 us  [from_next(): lax.ppermute(x, axis, [((i + distance) % size, i) for i in range(size)])]
  transfers between devices with their start and end apart: 24 -> 21, of which waited for: 12 -> 12; matrix products, arithmetic and copies ran while one was open for 1% -> 1% of each run, Pallas kernels for 6% -> 6%
where the time goes in v8:
time: 99.4 us; the launch traced here: 98.3 us
  waiting for transfers between devices  38.4 us (39%)
  starting transfers between devices  27.2 us (27%)
  blocking collectives  18.1 us (18%)
  Pallas kernels  9.84 us (10%)
  other arithmetic  2.39 us (2%)
  local copies, waits for them, and re-layouts  1.61 us (2%)
    ppermute x13, waiting for transfers between devices, from_next(): lax.ppermute(x, axis, [((i + distance) % size, i) for i in range(size)])  26.1 us
    ppermute x13, starting transfers between devices, from_next(): lax.ppermute(x, axis, [((i + distance) % size, i) for i in range(size)])  19.1 us
    all_to_all x1, blocking collectives, local(): lax.all_to_all(near, ('ylo', *SEQ), split_axis=0, concat_axis=0, tiled=True)  18.1 us
    ppermute x7, waiting for transfers between devices, partner(): return lax.ppermute(x, axis, [(0, 1), (1, 0)])  10.7 us
    ppermute x7, starting transfers between devices, partner(): return lax.ppermute(x, axis, [(0, 1), (1, 0)])  5.9 us
    pallas_call x1, Pallas kernels, attend(): pl.pallas_call(attend_kernel, out_shape=(jax.ShapeDtypeStruct((rows, COLS...  3.76 us
    pallas_call x1, Pallas kernels, normalise(): pl.pallas_call(body, out_shape=(shape, shape), in_specs=[SMEM, VMEM], out...  2.32 us
    pallas_call x1, Pallas kernels, gradient(): pl.pallas_call(gradient_kernel, out_shape=(shape,) * 4, in_specs=[SMEM, V...  2.26 us
  transfers between devices with their start and end apart: 21, of which 12 were waited for; matrix products, arithmetic and copies ran while one was open for 1% of the time, Pallas kernels for 6%

profile of v8, /device:TPU:32, one launch (start us, length us, event | category | flops | bytes accessed | tf_op | source)
XLA Modules:
  0.0 98.3 jit_solution(7004487162399540821)
XLA Ops:
  0.6 0.8 pad_select_fusion.kv_ref
  1.4 3.3 %collective-permute-start = (bf16[128,256]{1,0:T(8,128)(2,1)S(1)}, bf16[128,256]{1,0:T(8,128)(2,1)S(1)}, u32[]{:S(2)}, u32[]{:S(2)}) collective-permute-start(bf16[128,256]{1,0:T(8,128)(2,1)S(1)} %pad_select_fusion.kv_ref), channel_id=1, source_target_pairs={{0,1},{1,0},{2,3},{3,2},{4,5},{5,4},{6,7},{7,6},{8,9},{9,8},{10,11... | collective-permute-start | bytes 196616 | tf_op jit(solution)/shard_map/ppermute | solution.py:275
  4.7 0.7 broadcast_select_fusion
  5.4 0.7 collective-permute-start.1
  6.1 1.8 %collective-permute-start.2 = (bf16[14,256]{1,0:T(8,128)(2,1)S(1)}, bf16[14,256]{1,0:T(8,128)(2,1)S(1)}, u32[]{:S(2)}, u32[]{:S(2)}) collective-permute-start(bf16[14,256]{1,0:T(8,128)(2,1)S(1)} %get-tuple-element.59.refs_0_), channel_id=1, source_target_pairs={{0,1},{1,0},{2,3},{3,2},{4,5},{5,4},{6,7},{7,6},{8,9},{9,8},{10,11... | collective-permute-start | bytes 21512 | tf_op jit(solution)/shard_map/ppermute | solution.py:275
  8.0 2.2 %collective-permute-start.3 = (bf16[14,256]{1,0:T(8,128)(2,1)S(1)}, bf16[14,256]{1,0:T(8,128)(2,1)S(1)}, u32[]{:S(2)}, u32[]{:S(2)}) collective-permute-start(bf16[14,256]{1,0:T(8,128)(2,1)S(1)} %get-tuple-element.58), channel_id=1, source_target_pairs={{0,129},{1,128},{128,1},{129,0},{2,131},{3,130},{130,3},{131,2},{4... | collective-permute-start | bytes 21512 | tf_op jit(solution)/shard_map/ppermute | solution.py:298
  10.1 0.0 collective-permute-done.1.refs_1_
  10.1 1.1 %collective-permute-done.2.refs_2_ = bf16[14,256]{1,0:T(8,128)(2,1)S(1)} collective-permute-done((bf16[14,256]{1,0:T(8,128)(2,1)S(1)}, bf16[14,256]{1,0:T(8,128)(2,1)S(1)}, u32[]{:S(2)}, u32[]{:S(2)}) %collective-permute-start.2) | collective-permute-done | bytes 7200 | tf_op jit(solution)/shard_map/ppermute | solution.py:275
  11.3 1.5 %collective-permute-done.3.refs_3_ = bf16[14,256]{1,0:T(8,128)(2,1)S(1)} collective-permute-done((bf16[14,256]{1,0:T(8,128)(2,1)S(1)}, bf16[14,256]{1,0:T(8,128)(2,1)S(1)}, u32[]{:S(2)}, u32[]{:S(2)}) %collective-permute-start.3) | collective-permute-done | bytes 7200 | tf_op jit(solution)/shard_map/ppermute | solution.py:298
  12.8 0.0 collective-permute-done.kv_other_ref
  12.8 0.2 collective-permute-start.4
  13.0 1.9 %collective-permute-start.5 = (bf16[320,256]{1,0:T(8,128)(2,1)S(1)}, bf16[320,256]{1,0:T(8,128)(2,1)S(1)}, u32[]{:S(2)}, u32[]{:S(2)}) collective-permute-start(bf16[320,256]{1,0:T(8,128)(2,1)S(1)} %pack.1.refs_0_), channel_id=1, source_target_pairs={{14,0},{0,2},{2,4},{4,6},{6,8},{8,10},{10,12},{12,14},{15,1},{1,3}... | collective-permute-start | bytes 491528 | tf_op jit(solution)/shard_map/ppermute | solution.py:280
  14.9 0.1 stack.23.refs_0_.where_ref
  15.0 0.0 copy-start
  15.0 1.2 %copy-done = bf16[128,3584]{1,0:T(8,128)(2,1)S(1)} copy-done((bf16[128,3584]{1,0:T(8,128)(2,1)S(1)}, bf16[128,3584]{1,0:T(8,128)(2,1)}, u32[]{:S(2)}) %copy-start) | copy-done | bytes 917528
  16.2 2.3 %normalise.1 = (bf16[128,2048]{1,0:T(8,128)(2,1)S(1)}, bf16[128,2048]{1,0:T(8,128)(2,1)S(1)}) custom-call(s32[5]{0:T(128)S(1)} %stack.23.refs_0_.where_ref, bf16[128,3584]{1,0:T(8,128)(2,1)S(1)} %copy-done), custom_call_target="tpu_custom_call" | custom-call | tf_op jit(solution)/shard_map/normalise/pallas_call | solution.py:78
  18.5 0.0 collective-permute-done.4.refs_1_
  18.5 3.6 %collective-permute-done.5.refs_2_ = bf16[320,256]{1,0:T(8,128)(2,1)S(1)} collective-permute-done((bf16[320,256]{1,0:T(8,128)(2,1)S(1)}, bf16[320,256]{1,0:T(8,128)(2,1)S(1)}, u32[]{:S(2)}, u32[]{:S(2)}) %collective-permute-start.5) | collective-permute-done | bytes 163872 | tf_op jit(solution)/shard_map/ppermute | solution.py:280
  22.2 0.0 collective-permute-start.8
  22.2 3.2 %collective-permute-start.6 = (bf16[320,256]{1,0:T(8,128)(2,1)S(1)}, bf16[320,256]{1,0:T(8,128)(2,1)S(1)}, u32[]{:S(2)}, u32[]{:S(2)}) collective-permute-start(bf16[320,256]{1,0:T(8,128)(2,1)S(1)} %collective-permute-done.4.refs_1_), channel_id=1, source_target_pairs={{2,0},{4,2},{6,4},{8,6},{10,8},{12,10},{14,12},{0,14},{3,1},{5,3},... | collective-permute-start | bytes 491528 | tf_op jit(solution)/shard_map/ppermute | solution.py:280
  25.4 0.0 collective-permute-start.7
  25.4 0.0 copy-start.1
  25.4 0.0 copy-start.2
  25.5 0.0 copy-start.3
  25.5 0.0 collective-permute-done.8
  25.5 0.1 pad_maximum_fusion
  25.6 4.0 %collective-permute-done.6.refs_3_ = bf16[320,256]{1,0:T(8,128)(2,1)S(1)} collective-permute-done((bf16[320,256]{1,0:T(8,128)(2,1)S(1)}, bf16[320,256]{1,0:T(8,128)(2,1)S(1)}, u32[]{:S(2)}, u32[]{:S(2)}) %collective-permute-start.6) | collective-permute-done | bytes 163872 | tf_op jit(solution)/shard_map/ppermute | solution.py:280
  29.5 2.2 %collective-permute-done.7.refs_4_ = bf16[320,256]{1,0:T(8,128)(2,1)S(1)} collective-permute-done((bf16[320,256]{1,0:T(8,128)(2,1)S(1)}, bf16[320,256]{1,0:T(8,128)(2,1)S(1)}, u32[]{:S(2)}, u32[]{:S(2)}) %collective-permute-start.7) | collective-permute-done | bytes 163872 | tf_op jit(solution)/shard_map/ppermute | solution.py:280
  31.8 1.6 %collective-permute-start.9 = (bf16[320,256]{1,0:T(8,128)(2,1)S(1)}, bf16[320,256]{1,0:T(8,128)(2,1)S(1)}, u32[]{:S(2)}, u32[]{:S(2)}) collective-permute-start(bf16[320,256]{1,0:T(8,128)(2,1)S(1)} %collective-permute-done.6.refs_3_), channel_id=1, source_target_pairs={{2,0},{4,2},{6,4},{8,6},{10,8},{12,10},{14,12},{0,14},{3,1},{5,3},... | collective-permute-start | bytes 491528 | tf_op jit(solution)/shard_map/ppermute | solution.py:280
  33.4 0.4 collective-permute-start.10
  33.8 0.0 collective-permute-start.12
  33.8 3.5 %collective-permute-done.9.refs_5_ = bf16[320,256]{1,0:T(8,128)(2,1)S(1)} collective-permute-done((bf16[320,256]{1,0:T(8,128)(2,1)S(1)}, bf16[320,256]{1,0:T(8,128)(2,1)S(1)}, u32[]{:S(2)}, u32[]{:S(2)}) %collective-permute-start.9) | collective-permute-done | bytes 163872 | tf_op jit(solution)/shard_map/ppermute | solution.py:280
  37.3 1.5 %collective-permute-start.11 = (bf16[320,256]{1,0:T(8,128)(2,1)S(1)}, bf16[320,256]{1,0:T(8,128)(2,1)S(1)}, u32[]{:S(2)}, u32[]{:S(2)}) collective-permute-start(bf16[320,256]{1,0:T(8,128)(2,1)S(1)} %collective-permute-done.9.refs_5_), channel_id=1, source_target_pairs={{2,0},{4,2},{6,4},{8,6},{10,8},{12,10},{14,12},{0,14},{3,1},{5,3},... | collective-permute-start | bytes 491528 | tf_op jit(solution)/shard_map/ppermute | solution.py:280
  38.8 0.0 collective-permute-done.10.refs_6_
  38.8 3.8 %collective-permute-done.11.refs_7_ = bf16[320,256]{1,0:T(8,128)(2,1)S(1)} collective-permute-done((bf16[320,256]{1,0:T(8,128)(2,1)S(1)}, bf16[320,256]{1,0:T(8,128)(2,1)S(1)}, u32[]{:S(2)}, u32[]{:S(2)}) %collective-permute-start.11) | collective-permute-done | bytes 163872 | tf_op jit(solution)/shard_map/ppermute | solution.py:280
  42.6 2.8 %collective-permute-start.14 = (bf16[512,256]{1,0:T(8,128)(2,1)S(1)}, bf16[512,256]{1,0:T(8,128)(2,1)S(1)}, u32[]{:S(2)}, u32[]{:S(2)}) collective-permute-start(bf16[512,256]{1,0:T(8,128)(2,1)S(1)} %slice_dynamic-update-slice_fusion.refs_0_), channel_id=1, source_target_pairs={{32,0},{64,32},{96,64},{0,96},{33,1},{65,33},{97,65},{1,97},{34,2}... | collective-permute-start | bytes 786440 | tf_op jit(solution)/shard_map/ppermute | solution.py:280
  45.3 0.8 collective-permute-start.15
  46.1 0.9 collective-permute-start.16
  47.0 0.1 constant_dynamic-update-slice_fusion.1
  47.1 0.0 copy-done.1
  47.1 0.0 copy-done.2
  47.2 0.0 copy-done.3
  47.2 3.8 %attend.1 = (bf16[128,512]{1,0:T(8,128)(2,1)}, bf16[128,256]{1,0:T(8,128)(2,1)S(1)}, bf16[128,256]{1,0:T(8,128)(2,1)S(1)}) custom-call(s32[5]{0:T(128)S(1)} %stack.23.refs_0_.where_ref, s32[1,16]{1,0:T(1,128)S(1)} %copy-done.2, s32[1,4]{1,0:T(1,128)S(1)} %copy-done.3, bf16[128,512]{1,0:T(8,128)(2,1)S(1)} %copy-done.1, bf16[320,256]{1,0:T(8,128)(2,1)S(1)} %pack.1.refs_0_, ...), custom_call_target="tpu_custom_call" | custom-call | tf_op jit(solution)/shard_map/attend/pallas_call | solution.py:173
  50.9 0.0 collective-permute-start.13
  50.9 7.5 %collective-permute-done.12 = bf16[256,2048]{1,0:T(8,128)(2,1)S(1)} collective-permute-done((bf16[256,2048]{1,0:T(8,128)(2,1)S(1)}, bf16[256,2048]{1,0:T(8,128)(2,1)S(1)}, u32[]{:S(2)}, u32[]{:S(2)}) %collective-permute-start.12) | collective-permute-done | bytes 1048608 | tf_op jit(solution)/shard_map/ppermute | solution.py:275
  58.4 0.1 constant_dynamic-update-slice_fusion.n_ref
  58.5 0.6 collective-permute-done.13.got_ref
  59.1 0.0 collective-permute-done.14.refs_1_
  59.1 0.0 collective-permute-done.15.refs_2_
  59.1 0.0 collective-permute-done.16.refs_3_
  59.1 1.5 %project.1 = (f32[512,256]{1,0:T(8,128)S(1)}, bf16[512,256]{1,0:T(8,128)(2,1)S(1)}) custom-call(s32[5]{0:T(128)S(1)} %stack.23.refs_0_.where_ref, bf16[512,2048]{1,0:T(8,128)(2,1)S(1)} %constant_dynamic-update-slice_fusion.n_ref, bf16[128,256]{1,0:T(8,128)(2,1)S(1)} %get-tuple-element.48.mine_ref, bf16[128,256]{1,0:T(8,128)(2,1)S(1)} %collective-permute-done.13.got_ref, ...), custom_call_target="tpu_custom_call" | custom-call | tf_op jit(solution)/shard_map/project/pallas_call | solution.py:215
  60.6 0.1 collective-permute-start.17
  60.7 1.5 %collective-permute-done.17.back_ref = bf16[512,256]{1,0:T(8,128)(2,1)S(1)} collective-permute-done((bf16[512,256]{1,0:T(8,128)(2,1)S(1)}, bf16[512,256]{1,0:T(8,128)(2,1)S(1)}, u32[]{:S(2)}, u32[]{:S(2)}) %collective-permute-start.17) | collective-permute-done | bytes 262176 | tf_op jit(solution)/shard_map/ppermute | solution.py:275
  62.2 2.3 %gradient.1 = (bf16[448,256]{1,0:T(8,128)(2,1)S(1)}, bf16[448,256]{1,0:T(8,128)(2,1)S(1)}, bf16[448,256]{1,0:T(8,128)(2,1)S(1)}, bf16[448,256]{1,0:T(8,128)(2,1)S(1)}) custom-call(s32[5]{0:T(128)S(1)} %stack.23.refs_0_.where_ref, bf16[512,2048]{1,0:T(8,128)(2,1)S(1)} %constant_dynamic-update-slice_fusion.n_ref, f32[512,256]{1,0:T(8,128)S(1)} %get-tuple-element.50.own_ref, ...), custom_call_target="tpu_custom_call" | custom-call | tf_op jit(solution)/shard_map/gradient/pallas_call | solution.py:264
  64.5 1.6 %collective-permute-start.20 = (bf16[448,256]{1,0:T(8,128)(2,1)S(1)}, bf16[448,256]{1,0:T(8,128)(2,1)S(1)}, u32[]{:S(2)}, u32[]{:S(2)}) collective-permute-start(bf16[448,256]{1,0:T(8,128)(2,1)S(1)} %get-tuple-element.55), channel_id=1, source_target_pairs={{96,0},{0,32},{32,64},{64,96},{97,1},{1,33},{33,65},{65,97},{98,2}... | collective-permute-start | bytes 688136 | tf_op jit(solution)/shard_map/ppermute | solution.py:280
  66.1 2.7 %collective-permute-start.19 = (bf16[448,256]{1,0:T(8,128)(2,1)S(1)}, bf16[448,256]{1,0:T(8,128)(2,1)S(1)}, u32[]{:S(2)}, u32[]{:S(2)}) collective-permute-start(bf16[448,256]{1,0:T(8,128)(2,1)S(1)} %get-tuple-element.54), channel_id=1, source_target_pairs={{64,0},{96,32},{0,64},{32,96},{65,1},{97,33},{1,65},{33,97},{66,2}... | collective-permute-start | bytes 688136 | tf_op jit(solution)/shard_map/ppermute | solution.py:280
  68.8 1.4 %collective-permute-start.18 = (bf16[448,256]{1,0:T(8,128)(2,1)S(1)}, bf16[448,256]{1,0:T(8,128)(2,1)S(1)}, u32[]{:S(2)}, u32[]{:S(2)}) collective-permute-start(bf16[448,256]{1,0:T(8,128)(2,1)S(1)} %get-tuple-element.53), channel_id=1, source_target_pairs={{32,0},{64,32},{96,64},{0,96},{33,1},{65,33},{97,65},{1,97},{34,2}... | collective-permute-start | bytes 688136 | tf_op jit(solution)/shard_map/ppermute | solution.py:280
  70.2 3.2 %collective-permute-done.20 = bf16[448,256]{1,0:T(8,128)(2,1)S(1)} collective-permute-done((bf16[448,256]{1,0:T(8,128)(2,1)S(1)}, bf16[448,256]{1,0:T(8,128)(2,1)S(1)}, u32[]{:S(2)}, u32[]{:S(2)}) %collective-permute-start.20) | collective-permute-done | bytes 229408 | tf_op jit(solution)/shard_map/ppermute | solution.py:280
  73.4 5.9 %collective-permute-done.19 = bf16[448,256]{1,0:T(8,128)(2,1)S(1)} collective-permute-done((bf16[448,256]{1,0:T(8,128)(2,1)S(1)}, bf16[448,256]{1,0:T(8,128)(2,1)S(1)}, u32[]{:S(2)}, u32[]{:S(2)}) %collective-permute-start.19) | collective-permute-done | bytes 229408 | tf_op jit(solution)/shard_map/ppermute | solution.py:280
  79.3 0.0 collective-permute-done.18
  79.3 0.1 add_convert_fusion
  79.4 0.1 reshape.10
  79.6 18.1 %all_to_all.5 = bf16[32,16,256]{2,1,0:T(8,128)(2,1)S(1)} all-to-all(bf16[32,16,256]{2,1,0:T(8,128)(2,1)S(1)} %pad.14), channel_id=1, replica_groups=mesh['ylo'=2,'x'=4,'core'=2,'z'=8,'yhi'=2] {'ylo','z','yhi'}, dimensions={0} | all-to-all | bytes 524288 | tf_op jit(solution)/shard_map/all_to_all | solution.py:329
  97.7 0.6 pad_maximum_fusion.1
  (13 shorter events, 0.1 us)
Async XLA Ops:
  1.4 11.4 %collective-permute-start = (bf16[128,256]{1,0:T(8,128)(2,1)S(1)}, bf16[128,256]{1,0:T(8,128)(2,1)S(1)}, u32[]{:S(2)}, u32[]{:S(2)}) collective-permute-start(bf16[128,256]{1,0:T(8,128)(2,1)S(1)} %pad_select_fusion.kv_ref), channel_id=1, source_target_pairs={{0,1},{1,0},{2,3},{3,2},{4,5},{5,4},{6,7},{7,6},{8,9},{9,8},{10,11... | collective-permute-start | bytes 196616 | tf_op jit(solution)/shard_map/ppermute | solution.py:275
  5.4 4.7 %collective-permute-start.1 = (bf16[14,256]{1,0:T(8,128)(2,1)S(1)}, bf16[14,256]{1,0:T(8,128)(2,1)S(1)}, u32[]{:S(2)}, u32[]{:S(2)}) collective-permute-start(bf16[14,256]{1,0:T(8,128)(2,1)S(1)} %get-tuple-element.58), channel_id=1, source_target_pairs={{0,128},{128,0},{1,129},{129,1},{2,130},{130,2},{3,131},{131,3},{4... | collective-permute-start | bytes 21512 | tf_op jit(solution)/shard_map/ppermute | solution.py:275
  6.1 5.2 %collective-permute-start.2 = (bf16[14,256]{1,0:T(8,128)(2,1)S(1)}, bf16[14,256]{1,0:T(8,128)(2,1)S(1)}, u32[]{:S(2)}, u32[]{:S(2)}) collective-permute-start(bf16[14,256]{1,0:T(8,128)(2,1)S(1)} %get-tuple-element.59.refs_0_), channel_id=1, source_target_pairs={{0,1},{1,0},{2,3},{3,2},{4,5},{5,4},{6,7},{7,6},{8,9},{9,8},{10,11... | collective-permute-start | bytes 21512 | tf_op jit(solution)/shard_map/ppermute | solution.py:275
  8.0 4.9 %collective-permute-start.3 = (bf16[14,256]{1,0:T(8,128)(2,1)S(1)}, bf16[14,256]{1,0:T(8,128)(2,1)S(1)}, u32[]{:S(2)}, u32[]{:S(2)}) collective-permute-start(bf16[14,256]{1,0:T(8,128)(2,1)S(1)} %get-tuple-element.58), channel_id=1, source_target_pairs={{0,129},{1,128},{128,1},{129,0},{2,131},{3,130},{130,3},{131,2},{4... | collective-permute-start | bytes 21512 | tf_op jit(solution)/shard_map/ppermute | solution.py:298
  12.8 5.7 %collective-permute-start.4 = (bf16[320,256]{1,0:T(8,128)(2,1)S(1)}, bf16[320,256]{1,0:T(8,128)(2,1)S(1)}, u32[]{:S(2)}, u32[]{:S(2)}) collective-permute-start(bf16[320,256]{1,0:T(8,128)(2,1)S(1)} %pack.1.refs_0_), channel_id=1, source_target_pairs={{2,0},{4,2},{6,4},{8,6},{10,8},{12,10},{14,12},{0,14},{3,1},{5,3},... | collective-permute-start | bytes 491528 | tf_op jit(solution)/shard_map/ppermute | solution.py:280
  13.0 9.2 %collective-permute-start.5 = (bf16[320,256]{1,0:T(8,128)(2,1)S(1)}, bf16[320,256]{1,0:T(8,128)(2,1)S(1)}, u32[]{:S(2)}, u32[]{:S(2)}) collective-permute-start(bf16[320,256]{1,0:T(8,128)(2,1)S(1)} %pack.1.refs_0_), channel_id=1, source_target_pairs={{14,0},{0,2},{2,4},{4,6},{6,8},{8,10},{10,12},{12,14},{15,1},{1,3}... | collective-permute-start | bytes 491528 | tf_op jit(solution)/shard_map/ppermute | solution.py:280
  15.0 1.2 %copy-start = (bf16[128,3584]{1,0:T(8,128)(2,1)S(1)}, bf16[128,3584]{1,0:T(8,128)(2,1)}, u32[]{:S(2)}) copy-start(bf16[128,3584]{1,0:T(8,128)(2,1)} %refs_1_) | copy-start | bytes 2752516
  22.2 3.3 %collective-permute-start.8 = (bf16[128,2048]{1,0:T(8,128)(2,1)S(1)}, bf16[128,2048]{1,0:T(8,128)(2,1)S(1)}, u32[]{:S(2)}, u32[]{:S(2)}) collective-permute-start(bf16[128,2048]{1,0:T(8,128)(2,1)S(1)} %get-tuple-element.35), channel_id=1, source_target_pairs={{0,16},{16,0},{1,17},{17,1},{2,18},{18,2},{3,19},{19,3},{4,20},{20... | collective-permute-start | bytes 1572872 | tf_op jit(solution)/shard_map/ppermute | solution.py:275
  22.2 7.4 %collective-permute-start.6 = (bf16[320,256]{1,0:T(8,128)(2,1)S(1)}, bf16[320,256]{1,0:T(8,128)(2,1)S(1)}, u32[]{:S(2)}, u32[]{:S(2)}) collective-permute-start(bf16[320,256]{1,0:T(8,128)(2,1)S(1)} %collective-permute-done.4.refs_1_), channel_id=1, source_target_pairs={{2,0},{4,2},{6,4},{8,6},{10,8},{12,10},{14,12},{0,14},{3,1},{5,3},... | collective-permute-start | bytes 491528 | tf_op jit(solution)/shard_map/ppermute | solution.py:280
  25.4 6.3 %collective-permute-start.7 = (bf16[320,256]{1,0:T(8,128)(2,1)S(1)}, bf16[320,256]{1,0:T(8,128)(2,1)S(1)}, u32[]{:S(2)}, u32[]{:S(2)}) collective-permute-start(bf16[320,256]{1,0:T(8,128)(2,1)S(1)} %collective-permute-done.5.refs_2_), channel_id=1, source_target_pairs={{14,0},{0,2},{2,4},{4,6},{6,8},{8,10},{10,12},{12,14},{15,1},{1,3}... | collective-permute-start | bytes 491528 | tf_op jit(solution)/shard_map/ppermute | solution.py:280
  25.4 21.7 %copy-start.1 = (bf16[128,512]{1,0:T(8,128)(2,1)S(1)}, bf16[128,512]{1,0:T(8,128)(2,1)}, u32[]{:S(2)}) copy-start(bf16[128,512]{1,0:T(8,128)(2,1)} %q_ref.1) | copy-start | bytes 393220
  25.4 21.7 %copy-start.2 = (s32[1,16]{1,0:T(1,128)S(1)}, s32[1,16]{1,0:T(1,128)}, u32[]{:S(2)}) copy-start(s32[1,16]{1,0:T(1,128)} %assign_ref.1) | copy-start | bytes 196
  25.5 21.7 %copy-start.3 = (s32[1,4]{1,0:T(1,128)S(1)}, s32[1,4]{1,0:T(1,128)}, u32[]{:S(2)}) copy-start(s32[1,4]{1,0:T(1,128)} %length_ref.1) | copy-start | bytes 52
  31.8 5.5 %collective-permute-start.9 = (bf16[320,256]{1,0:T(8,128)(2,1)S(1)}, bf16[320,256]{1,0:T(8,128)(2,1)S(1)}, u32[]{:S(2)}, u32[]{:S(2)}) collective-permute-start(bf16[320,256]{1,0:T(8,128)(2,1)S(1)} %collective-permute-done.6.refs_3_), channel_id=1, source_target_pairs={{2,0},{4,2},{6,4},{8,6},{10,8},{12,10},{14,12},{0,14},{3,1},{5,3},... | collective-permute-start | bytes 491528 | tf_op jit(solution)/shard_map/ppermute | solution.py:280
  33.4 5.4 %collective-permute-start.10 = (bf16[320,256]{1,0:T(8,128)(2,1)S(1)}, bf16[320,256]{1,0:T(8,128)(2,1)S(1)}, u32[]{:S(2)}, u32[]{:S(2)}) collective-permute-start(bf16[320,256]{1,0:T(8,128)(2,1)S(1)} %collective-permute-done.7.refs_4_), channel_id=1, source_target_pairs={{14,0},{0,2},{2,4},{4,6},{6,8},{8,10},{10,12},{12,14},{15,1},{1,3}... | collective-permute-start | bytes 491528 | tf_op jit(solution)/shard_map/ppermute | solution.py:280
  33.8 24.6 %collective-permute-start.12 = (bf16[256,2048]{1,0:T(8,128)(2,1)S(1)}, bf16[256,2048]{1,0:T(8,128)(2,1)S(1)}, u32[]{:S(2)}, u32[]{:S(2)}) collective-permute-start(bf16[256,2048]{1,0:T(8,128)(2,1)S(1)} %pad_maximum_fusion), channel_id=1, source_target_pairs={{0,128},{128,0},{1,129},{129,1},{2,130},{130,2},{3,131},{131,3},{4... | collective-permute-start | bytes 3145736 | tf_op jit(solution)/shard_map/ppermute | solution.py:275
  37.3 5.3 %collective-permute-start.11 = (bf16[320,256]{1,0:T(8,128)(2,1)S(1)}, bf16[320,256]{1,0:T(8,128)(2,1)S(1)}, u32[]{:S(2)}, u32[]{:S(2)}) collective-permute-start(bf16[320,256]{1,0:T(8,128)(2,1)S(1)} %collective-permute-done.9.refs_5_), channel_id=1, source_target_pairs={{2,0},{4,2},{6,4},{8,6},{10,8},{12,10},{14,12},{0,14},{3,1},{5,3},... | collective-permute-start | bytes 491528 | tf_op jit(solution)/shard_map/ppermute | solution.py:280
  42.6 16.5 %collective-permute-start.14 = (bf16[512,256]{1,0:T(8,128)(2,1)S(1)}, bf16[512,256]{1,0:T(8,128)(2,1)S(1)}, u32[]{:S(2)}, u32[]{:S(2)}) collective-permute-start(bf16[512,256]{1,0:T(8,128)(2,1)S(1)} %slice_dynamic-update-slice_fusion.refs_0_), channel_id=1, source_target_pairs={{32,0},{64,32},{96,64},{0,96},{33,1},{65,33},{97,65},{1,97},{34,2}... | collective-permute-start | bytes 786440 | tf_op jit(solution)/shard_map/ppermute | solution.py:280
  45.3 13.8 %collective-permute-start.15 = (bf16[512,256]{1,0:T(8,128)(2,1)S(1)}, bf16[512,256]{1,0:T(8,128)(2,1)S(1)}, u32[]{:S(2)}, u32[]{:S(2)}) collective-permute-start(bf16[512,256]{1,0:T(8,128)(2,1)S(1)} %slice_dynamic-update-slice_fusion.refs_0_), channel_id=1, source_target_pairs={{64,0},{96,32},{0,64},{32,96},{65,1},{97,33},{1,65},{33,97},{66,2}... | collective-permute-start | bytes 786440 | tf_op jit(solution)/shard_map/ppermute | solution.py:280
  46.1 13.0 %collective-permute-start.16 = (bf16[512,256]{1,0:T(8,128)(2,1)S(1)}, bf16[512,256]{1,0:T(8,128)(2,1)S(1)}, u32[]{:S(2)}, u32[]{:S(2)}) collective-permute-start(bf16[512,256]{1,0:T(8,128)(2,1)S(1)} %slice_dynamic-update-slice_fusion.refs_0_), channel_id=1, source_target_pairs={{96,0},{0,32},{32,64},{64,96},{97,1},{1,33},{33,65},{65,97},{98,2}... | collective-permute-start | bytes 786440 | tf_op jit(solution)/shard_map/ppermute | solution.py:280
  50.9 8.2 %collective-permute-start.13 = (bf16[128,256]{1,0:T(8,128)(2,1)S(1)}, bf16[128,256]{1,0:T(8,128)(2,1)S(1)}, u32[]{:S(2)}, u32[]{:S(2)}) collective-permute-start(bf16[128,256]{1,0:T(8,128)(2,1)S(1)} %get-tuple-element.49), channel_id=1, source_target_pairs={{0,128},{128,0},{1,129},{129,1},{2,130},{130,2},{3,131},{131,3},{4... | collective-permute-start | bytes 196616 | tf_op jit(solution)/shard_map/ppermute | solution.py:275
  60.6 1.6 %collective-permute-start.17 = (bf16[512,256]{1,0:T(8,128)(2,1)S(1)}, bf16[512,256]{1,0:T(8,128)(2,1)S(1)}, u32[]{:S(2)}, u32[]{:S(2)}) collective-permute-start(bf16[512,256]{1,0:T(8,128)(2,1)S(1)} %get-tuple-element.51), channel_id=1, source_target_pairs={{0,16},{16,0},{1,17},{17,1},{2,18},{18,2},{3,19},{19,3},{4,20},{20... | collective-permute-start | bytes 786440 | tf_op jit(solution)/shard_map/ppermute | solution.py:275
  64.5 8.9 %collective-permute-start.20 = (bf16[448,256]{1,0:T(8,128)(2,1)S(1)}, bf16[448,256]{1,0:T(8,128)(2,1)S(1)}, u32[]{:S(2)}, u32[]{:S(2)}) collective-permute-start(bf16[448,256]{1,0:T(8,128)(2,1)S(1)} %get-tuple-element.55), channel_id=1, source_target_pairs={{96,0},{0,32},{32,64},{64,96},{97,1},{1,33},{33,65},{65,97},{98,2}... | collective-permute-start | bytes 688136 | tf_op jit(solution)/shard_map/ppermute | solution.py:280
  66.1 13.3 %collective-permute-start.19 = (bf16[448,256]{1,0:T(8,128)(2,1)S(1)}, bf16[448,256]{1,0:T(8,128)(2,1)S(1)}, u32[]{:S(2)}, u32[]{:S(2)}) collective-permute-start(bf16[448,256]{1,0:T(8,128)(2,1)S(1)} %get-tuple-element.54), channel_id=1, source_target_pairs={{64,0},{96,32},{0,64},{32,96},{65,1},{97,33},{1,65},{33,97},{66,2}... | collective-permute-start | bytes 688136 | tf_op jit(solution)/shard_map/ppermute | solution.py:280
  68.8 10.5 %collective-permute-start.18 = (bf16[448,256]{1,0:T(8,128)(2,1)S(1)}, bf16[448,256]{1,0:T(8,128)(2,1)S(1)}, u32[]{:S(2)}, u32[]{:S(2)}) collective-permute-start(bf16[448,256]{1,0:T(8,128)(2,1)S(1)} %get-tuple-element.53), channel_id=1, source_target_pairs={{32,0},{64,32},{96,64},{0,96},{33,1},{65,33},{97,65},{1,97},{34,2}... | collective-permute-start | bytes 688136 | tf_op jit(solution)/shard_map/ppermute | solution.py:280

commit v9 on v8

--- a/solution.py
+++ b/solution.py
@@ -303,15 +303,18 @@
     n_keep, n_send = normalise(here, student_in, wrows)
     up, down = from_next(packed, "z", 1), from_next(packed, "z", -1)
     up, down, n_keep, n_send = lax.optimization_barrier((up, down, n_keep, n_send))
-    n_pair = jnp.concatenate([n_keep, partner(n_send, "core")], axis=0)
+    n_got, n_across = partner(n_send, "core"), partner(n_keep, "ylo")
+
     held = {0: packed, 1: up, -1: down}
     for d in range(2, 5):
         held[d] = from_next(held[d - 1], "z", 1)
         if d < 4:
             held[-d] = from_next(held[1 - d], "z", -1)
         if d == 2:
-            held[2], held[-2], n_pair = lax.optimization_barrier((held[2], held[-2], n_pair))
-    n_all = jnp.concatenate([n_pair, partner(n_pair, "ylo")], axis=0)
+            held[2], held[-2], n_got = lax.optimization_barrier((held[2], held[-2], n_got))
+        if d == 3:
+            held[3], held[-3], n_across = lax.optimization_barrier((held[3], held[-3], n_across))
+    n_all = jnp.concatenate([n_keep, n_got, n_across, partner(n_got, "ylo")], axis=0)
     parts = [held[d] for d in RING]
     w_rows = jnp.concatenate([part[2 * BLK :] for part in parts], axis=0)
     w_all = [w_rows] + [from_next(w_rows, "x", d) for d in range(1, 4)]

time: 99.4 us -> 103 us (1.036)
  waiting for transfers between devices: 38.4 us -> 42.1 us
  blocking collectives: 18.1 us -> 19.5 us
  starting transfers between devices: 27.2 us -> 25.9 us
    ppermute x7 -> x8, waiting for transfers between devices: 10.7 us -> 13.6 us  [partner(): return lax.ppermute(x, axis, [(0, 1), (1, 0)])]
    ppermute x13, starting transfers between devices: 19.1 us -> 17.3 us  [from_next(): lax.ppermute(x, axis, [((i + distance) % size, i) for i in range(size)])]
    all_to_all x1, blocking collectives: 18.1 us -> 19.5 us  [local(): lax.all_to_all(near, ('ylo', *SEQ), split_axis=0, concat_axis=0, tiled=True)]
    ppermute x7 -> x8, starting transfers between devices: 5.9 us -> 6.39 us  [partner(): return lax.ppermute(x, axis, [(0, 1), (1, 0)])]
  transfers between devices with their start and end apart: 21 -> 22, of which waited for: 12 -> 13; matrix products, arithmetic and copies ran while one was open for 1% -> 1% of each run, Pallas kernels for 6% -> 6%
where the time goes in v9:
time: 103 us; the launch traced here: 102 us
  waiting for transfers between devices  42.1 us (41%)
  starting transfers between devices  25.9 us (25%)
  blocking collectives  19.5 us (19%)
  Pallas kernels  9.84 us (10%)
  other arithmetic  2.29 us (2%)
  local copies, waits for them, and re-layouts  1.56 us (2%)
    ppermute x13, waiting for transfers between devices, from_next(): lax.ppermute(x, axis, [((i + distance) % size, i) for i in range(size)])  27 us
    all_to_all x1, blocking collectives, local(): lax.all_to_all(near, ('ylo', *SEQ), split_axis=0, concat_axis=0, tiled=True)  19.5 us
    ppermute x13, starting transfers between devices, from_next(): lax.ppermute(x, axis, [((i + distance) % size, i) for i in range(size)])  17.3 us
    ppermute x8, waiting for transfers between devices, partner(): return lax.ppermute(x, axis, [(0, 1), (1, 0)])  13.6 us
    ppermute x8, starting transfers between devices, partner(): return lax.ppermute(x, axis, [(0, 1), (1, 0)])  6.39 us
    pallas_call x1, Pallas kernels, attend(): pl.pallas_call(attend_kernel, out_shape=(jax.ShapeDtypeStruct((rows, COLS...  3.77 us
    pallas_call x1, Pallas kernels, normalise(): pl.pallas_call(body, out_shape=(shape, shape), in_specs=[SMEM, VMEM], out...  2.32 us
    pallas_call x1, Pallas kernels, gradient(): pl.pallas_call(gradient_kernel, out_shape=(shape,) * 4, in_specs=[SMEM, V...  2.26 us
  transfers between devices with their start and end apart: 22, of which 13 were waited for; matrix products, arithmetic and copies ran while one was open for 1% of the time, Pallas kernels for 6%

profile of v9, /device:TPU:32, one launch (start us, length us, event | category | flops | bytes accessed | tf_op | source)
XLA Modules:
  0.0 102.1 jit_solution(4037563693683413101)
XLA Ops:
  0.6 0.8 pad_select_fusion.kv_ref
  1.4 3.3 %collective-permute-start = (bf16[128,256]{1,0:T(8,128)(2,1)S(1)}, bf16[128,256]{1,0:T(8,128)(2,1)S(1)}, u32[]{:S(2)}, u32[]{:S(2)}) collective-permute-start(bf16[128,256]{1,0:T(8,128)(2,1)S(1)} %pad_select_fusion.kv_ref), channel_id=1, source_target_pairs={{0,1},{1,0},{2,3},{3,2},{4,5},{5,4},{6,7},{7,6},{8,9},{9,8},{10,11... | collective-permute-start | bytes 196616 | tf_op jit(solution)/shard_map/ppermute | solution.py:275
  4.7 0.7 broadcast_select_fusion
  5.4 0.7 collective-permute-start.1
  6.1 1.8 %collective-permute-start.2 = (bf16[14,256]{1,0:T(8,128)(2,1)S(1)}, bf16[14,256]{1,0:T(8,128)(2,1)S(1)}, u32[]{:S(2)}, u32[]{:S(2)}) collective-permute-start(bf16[14,256]{1,0:T(8,128)(2,1)S(1)} %get-tuple-element.65.refs_0_), channel_id=1, source_target_pairs={{0,1},{1,0},{2,3},{3,2},{4,5},{5,4},{6,7},{7,6},{8,9},{9,8},{10,11... | collective-permute-start | bytes 21512 | tf_op jit(solution)/shard_map/ppermute | solution.py:275
  8.0 2.2 %collective-permute-start.3 = (bf16[14,256]{1,0:T(8,128)(2,1)S(1)}, bf16[14,256]{1,0:T(8,128)(2,1)S(1)}, u32[]{:S(2)}, u32[]{:S(2)}) collective-permute-start(bf16[14,256]{1,0:T(8,128)(2,1)S(1)} %get-tuple-element.64), channel_id=1, source_target_pairs={{0,129},{1,128},{128,1},{129,0},{2,131},{3,130},{130,3},{131,2},{4... | collective-permute-start | bytes 21512 | tf_op jit(solution)/shard_map/ppermute | solution.py:298
  10.1 0.1 stack.23.refs_0_.where_ref
  10.2 0.0 collective-permute-done.1.refs_1_
  10.2 1.0 %collective-permute-done.2.refs_2_ = bf16[14,256]{1,0:T(8,128)(2,1)S(1)} collective-permute-done((bf16[14,256]{1,0:T(8,128)(2,1)S(1)}, bf16[14,256]{1,0:T(8,128)(2,1)S(1)}, u32[]{:S(2)}, u32[]{:S(2)}) %collective-permute-start.2) | collective-permute-done | bytes 7200 | tf_op jit(solution)/shard_map/ppermute | solution.py:275
  11.3 1.5 %collective-permute-done.3.refs_3_ = bf16[14,256]{1,0:T(8,128)(2,1)S(1)} collective-permute-done((bf16[14,256]{1,0:T(8,128)(2,1)S(1)}, bf16[14,256]{1,0:T(8,128)(2,1)S(1)}, u32[]{:S(2)}, u32[]{:S(2)}) %collective-permute-start.3) | collective-permute-done | bytes 7200 | tf_op jit(solution)/shard_map/ppermute | solution.py:298
  12.8 0.0 collective-permute-done.kv_other_ref
  12.8 0.0 copy-start.1
  12.8 0.0 copy-start.2
  12.8 0.0 copy-start.3
  12.9 0.2 collective-permute-start.4
  13.0 1.9 %collective-permute-start.5 = (bf16[320,256]{1,0:T(8,128)(2,1)S(1)}, bf16[320,256]{1,0:T(8,128)(2,1)S(1)}, u32[]{:S(2)}, u32[]{:S(2)}) collective-permute-start(bf16[320,256]{1,0:T(8,128)(2,1)S(1)} %pack.1.refs_0_), channel_id=1, source_target_pairs={{14,0},{0,2},{2,4},{4,6},{6,8},{8,10},{10,12},{12,14},{15,1},{1,3}... | collective-permute-start | bytes 491528 | tf_op jit(solution)/shard_map/ppermute | solution.py:280
  15.0 0.0 copy-start
  15.0 1.2 %copy-done = bf16[128,3584]{1,0:T(8,128)(2,1)S(1)} copy-done((bf16[128,3584]{1,0:T(8,128)(2,1)S(1)}, bf16[128,3584]{1,0:T(8,128)(2,1)}, u32[]{:S(2)}) %copy-start) | copy-done | bytes 917528
  16.1 2.3 %normalise.1 = (bf16[128,2048]{1,0:T(8,128)(2,1)S(1)}, bf16[128,2048]{1,0:T(8,128)(2,1)S(1)}) custom-call(s32[5]{0:T(128)S(1)} %stack.23.refs_0_.where_ref, bf16[128,3584]{1,0:T(8,128)(2,1)S(1)} %copy-done), custom_call_target="tpu_custom_call" | custom-call | tf_op jit(solution)/shard_map/normalise/pallas_call | solution.py:78
  18.5 0.0 collective-permute-done.4.refs_1_
  18.5 3.7 %collective-permute-done.5.refs_2_ = bf16[320,256]{1,0:T(8,128)(2,1)S(1)} collective-permute-done((bf16[320,256]{1,0:T(8,128)(2,1)S(1)}, bf16[320,256]{1,0:T(8,128)(2,1)S(1)}, u32[]{:S(2)}, u32[]{:S(2)}) %collective-permute-start.5) | collective-permute-done | bytes 163872 | tf_op jit(solution)/shard_map/ppermute | solution.py:280
  22.2 3.2 %collective-permute-start.6 = (bf16[320,256]{1,0:T(8,128)(2,1)S(1)}, bf16[320,256]{1,0:T(8,128)(2,1)S(1)}, u32[]{:S(2)}, u32[]{:S(2)}) collective-permute-start(bf16[320,256]{1,0:T(8,128)(2,1)S(1)} %collective-permute-done.4.refs_1_), channel_id=1, source_target_pairs={{2,0},{4,2},{6,4},{8,6},{10,8},{12,10},{14,12},{0,14},{3,1},{5,3},... | collective-permute-start | bytes 491528 | tf_op jit(solution)/shard_map/ppermute | solution.py:280
  25.4 0.0 collective-permute-start.7
  25.4 0.0 collective-permute-start.8
  25.4 0.0 collective-permute-start.11
  25.5 2.8 %collective-permute-done.6.refs_3_ = bf16[320,256]{1,0:T(8,128)(2,1)S(1)} collective-permute-done((bf16[320,256]{1,0:T(8,128)(2,1)S(1)}, bf16[320,256]{1,0:T(8,128)(2,1)S(1)}, u32[]{:S(2)}, u32[]{:S(2)}) %collective-permute-start.6) | collective-permute-done | bytes 163872 | tf_op jit(solution)/shard_map/ppermute | solution.py:280
  28.3 2.5 %collective-permute-done.7.refs_4_ = bf16[320,256]{1,0:T(8,128)(2,1)S(1)} collective-permute-done((bf16[320,256]{1,0:T(8,128)(2,1)S(1)}, bf16[320,256]{1,0:T(8,128)(2,1)S(1)}, u32[]{:S(2)}, u32[]{:S(2)}) %collective-permute-start.7) | collective-permute-done | bytes 163872 | tf_op jit(solution)/shard_map/ppermute | solution.py:280
  30.7 0.0 collective-permute-done.8
  30.8 1.5 %collective-permute-start.9 = (bf16[320,256]{1,0:T(8,128)(2,1)S(1)}, bf16[320,256]{1,0:T(8,128)(2,1)S(1)}, u32[]{:S(2)}, u32[]{:S(2)}) collective-permute-start(bf16[320,256]{1,0:T(8,128)(2,1)S(1)} %collective-permute-done.6.refs_3_), channel_id=1, source_target_pairs={{2,0},{4,2},{6,4},{8,6},{10,8},{12,10},{14,12},{0,14},{3,1},{5,3},... | collective-permute-start | bytes 491528 | tf_op jit(solution)/shard_map/ppermute | solution.py:280
  32.3 0.5 collective-permute-start.10
  32.8 0.0 collective-permute-start.13
  32.8 7.3 %collective-permute-done.11 = bf16[128,2048]{1,0:T(8,128)(2,1)S(1)} collective-permute-done((bf16[128,2048]{1,0:T(8,128)(2,1)S(1)}, bf16[128,2048]{1,0:T(8,128)(2,1)S(1)}, u32[]{:S(2)}, u32[]{:S(2)}) %collective-permute-start.11) | collective-permute-done | bytes 524320 | tf_op jit(solution)/shard_map/ppermute | solution.py:275
  40.2 0.0 collective-permute-done.9.refs_5_
  40.2 0.0 collective-permute-done.10.refs_6_
  40.2 2.0 %collective-permute-start.12 = (bf16[320,256]{1,0:T(8,128)(2,1)S(1)}, bf16[320,256]{1,0:T(8,128)(2,1)S(1)}, u32[]{:S(2)}, u32[]{:S(2)}) collective-permute-start(bf16[320,256]{1,0:T(8,128)(2,1)S(1)} %collective-permute-done.9.refs_5_), channel_id=1, source_target_pairs={{2,0},{4,2},{6,4},{8,6},{10,8},{12,10},{14,12},{0,14},{3,1},{5,3},... | collective-permute-start | bytes 491528 | tf_op jit(solution)/shard_map/ppermute | solution.py:280
  42.2 3.4 %collective-permute-done.12.refs_7_ = bf16[320,256]{1,0:T(8,128)(2,1)S(1)} collective-permute-done((bf16[320,256]{1,0:T(8,128)(2,1)S(1)}, bf16[320,256]{1,0:T(8,128)(2,1)S(1)}, u32[]{:S(2)}, u32[]{:S(2)}) %collective-permute-start.12) | collective-permute-done | bytes 163872 | tf_op jit(solution)/shard_map/ppermute | solution.py:280
  45.6 2.8 %collective-permute-start.15 = (bf16[512,256]{1,0:T(8,128)(2,1)S(1)}, bf16[512,256]{1,0:T(8,128)(2,1)S(1)}, u32[]{:S(2)}, u32[]{:S(2)}) collective-permute-start(bf16[512,256]{1,0:T(8,128)(2,1)S(1)} %slice_dynamic-update-slice_fusion.refs_0_), channel_id=1, source_target_pairs={{32,0},{64,32},{96,64},{0,96},{33,1},{65,33},{97,65},{1,97},{34,2}... | collective-permute-start | bytes 786440 | tf_op jit(solution)/shard_map/ppermute | solution.py:280
  48.4 0.8 collective-permute-start.16
  49.2 0.9 collective-permute-start.17
  50.1 0.0 copy-done.1
  50.1 0.0 copy-done.2
  50.1 0.0 copy-done.3
  50.1 3.8 %attend.1 = (bf16[128,512]{1,0:T(8,128)(2,1)}, bf16[128,256]{1,0:T(8,128)(2,1)S(1)}, bf16[128,256]{1,0:T(8,128)(2,1)S(1)}) custom-call(s32[5]{0:T(128)S(1)} %stack.23.refs_0_.where_ref, s32[1,16]{1,0:T(1,128)S(1)} %copy-done.2, s32[1,4]{1,0:T(1,128)S(1)} %copy-done.3, bf16[128,512]{1,0:T(8,128)(2,1)S(1)} %copy-done.1, bf16[320,256]{1,0:T(8,128)(2,1)S(1)} %pack.1.refs_0_, ...), custom_call_target="tpu_custom_call" | custom-call | tf_op jit(solution)/shard_map/attend/pallas_call | solution.py:173
  53.9 0.5 collective-permute-start.14
  54.4 0.0 collective-permute-done.13
  54.4 3.7 %collective-permute-done.14.got_ref = bf16[128,256]{1,0:T(8,128)(2,1)S(1)} collective-permute-done((bf16[128,256]{1,0:T(8,128)(2,1)S(1)}, bf16[128,256]{1,0:T(8,128)(2,1)S(1)}, u32[]{:S(2)}, u32[]{:S(2)}) %collective-permute-start.14) | collective-permute-done | bytes 65568 | tf_op jit(solution)/shard_map/ppermute | solution.py:275
  58.2 0.0 collective-permute-done.15.refs_1_
  58.2 0.9 collective-permute-done.16.refs_2_
  59.1 2.8 %collective-permute-done.17.refs_3_ = bf16[512,256]{1,0:T(8,128)(2,1)S(1)} collective-permute-done((bf16[512,256]{1,0:T(8,128)(2,1)S(1)}, bf16[512,256]{1,0:T(8,128)(2,1)S(1)}, u32[]{:S(2)}, u32[]{:S(2)}) %collective-permute-start.17) | collective-permute-done | bytes 262176 | tf_op jit(solution)/shard_map/ppermute | solution.py:280
  61.8 1.5 %project.1 = (f32[512,256]{1,0:T(8,128)S(1)}, bf16[512,256]{1,0:T(8,128)(2,1)S(1)}) custom-call(s32[5]{0:T(128)S(1)} %stack.23.refs_0_.where_ref, bf16[512,2048]{1,0:T(8,128)(2,1)S(1)} %constant_dynamic-update-slice_fusion.n_ref, bf16[128,256]{1,0:T(8,128)(2,1)S(1)} %get-tuple-element.54.mine_ref, bf16[128,256]{1,0:T(8,128)(2,1)S(1)} %collective-permute-done.14.got_ref, ...), custom_call_target="tpu_custom_call" | custom-call | tf_op jit(solution)/shard_map/project/pallas_call | solution.py:215
  63.3 0.1 collective-permute-start.18
  63.4 1.5 %collective-permute-done.18.back_ref = bf16[512,256]{1,0:T(8,128)(2,1)S(1)} collective-permute-done((bf16[512,256]{1,0:T(8,128)(2,1)S(1)}, bf16[512,256]{1,0:T(8,128)(2,1)S(1)}, u32[]{:S(2)}, u32[]{:S(2)}) %collective-permute-start.18) | collective-permute-done | bytes 262176 | tf_op jit(solution)/shard_map/ppermute | solution.py:275
  65.0 2.3 %gradient.1 = (bf16[448,256]{1,0:T(8,128)(2,1)S(1)}, bf16[448,256]{1,0:T(8,128)(2,1)S(1)}, bf16[448,256]{1,0:T(8,128)(2,1)S(1)}, bf16[448,256]{1,0:T(8,128)(2,1)S(1)}) custom-call(s32[5]{0:T(128)S(1)} %stack.23.refs_0_.where_ref, bf16[512,2048]{1,0:T(8,128)(2,1)S(1)} %constant_dynamic-update-slice_fusion.n_ref, f32[512,256]{1,0:T(8,128)S(1)} %get-tuple-element.56.own_ref, ...), custom_call_target="tpu_custom_call" | custom-call | tf_op jit(solution)/shard_map/gradient/pallas_call | solution.py:264
  67.2 0.1 collective-permute-start.21
  67.3 2.1 %collective-permute-start.20 = (bf16[448,256]{1,0:T(8,128)(2,1)S(1)}, bf16[448,256]{1,0:T(8,128)(2,1)S(1)}, u32[]{:S(2)}, u32[]{:S(2)}) collective-permute-start(bf16[448,256]{1,0:T(8,128)(2,1)S(1)} %get-tuple-element.60), channel_id=1, source_target_pairs={{64,0},{96,32},{0,64},{32,96},{65,1},{97,33},{1,65},{33,97},{66,2}... | collective-permute-start | bytes 688136 | tf_op jit(solution)/shard_map/ppermute | solution.py:280
  69.4 1.4 %collective-permute-start.19 = (bf16[448,256]{1,0:T(8,128)(2,1)S(1)}, bf16[448,256]{1,0:T(8,128)(2,1)S(1)}, u32[]{:S(2)}, u32[]{:S(2)}) collective-permute-start(bf16[448,256]{1,0:T(8,128)(2,1)S(1)} %get-tuple-element.59), channel_id=1, source_target_pairs={{32,0},{64,32},{96,64},{0,96},{33,1},{65,33},{97,65},{1,97},{34,2}... | collective-permute-start | bytes 688136 | tf_op jit(solution)/shard_map/ppermute | solution.py:280
  70.7 10.3 %collective-permute-done.21 = bf16[448,256]{1,0:T(8,128)(2,1)S(1)} collective-permute-done((bf16[448,256]{1,0:T(8,128)(2,1)S(1)}, bf16[448,256]{1,0:T(8,128)(2,1)S(1)}, u32[]{:S(2)}, u32[]{:S(2)}) %collective-permute-start.21) | collective-permute-done | bytes 229408 | tf_op jit(solution)/shard_map/ppermute | solution.py:280
  81.1 0.0 collective-permute-done.20
  81.1 0.6 collective-permute-done.19
  81.7 0.1 add_convert_fusion
  81.8 0.1 reshape.10
  81.9 19.5 %all_to_all.5 = bf16[32,16,256]{2,1,0:T(8,128)(2,1)S(1)} all-to-all(bf16[32,16,256]{2,1,0:T(8,128)(2,1)S(1)} %pad.14), channel_id=1, replica_groups=mesh['ylo'=2,'x'=4,'core'=2,'z'=8,'yhi'=2] {'ylo','z','yhi'}, dimensions={0} | all-to-all | bytes 524288 | tf_op jit(solution)/shard_map/all_to_all | solution.py:332
  101.5 0.6 pad_maximum_fusion
  (17 shorter events, 0.3 us)
Async XLA Ops:
  1.4 11.4 %collective-permute-start = (bf16[128,256]{1,0:T(8,128)(2,1)S(1)}, bf16[128,256]{1,0:T(8,128)(2,1)S(1)}, u32[]{:S(2)}, u32[]{:S(2)}) collective-permute-start(bf16[128,256]{1,0:T(8,128)(2,1)S(1)} %pad_select_fusion.kv_ref), channel_id=1, source_target_pairs={{0,1},{1,0},{2,3},{3,2},{4,5},{5,4},{6,7},{7,6},{8,9},{9,8},{10,11... | collective-permute-start | bytes 196616 | tf_op jit(solution)/shard_map/ppermute | solution.py:275
  5.4 4.8 %collective-permute-start.1 = (bf16[14,256]{1,0:T(8,128)(2,1)S(1)}, bf16[14,256]{1,0:T(8,128)(2,1)S(1)}, u32[]{:S(2)}, u32[]{:S(2)}) collective-permute-start(bf16[14,256]{1,0:T(8,128)(2,1)S(1)} %get-tuple-element.64), channel_id=1, source_target_pairs={{0,128},{128,0},{1,129},{129,1},{2,130},{130,2},{3,131},{131,3},{4... | collective-permute-start | bytes 21512 | tf_op jit(solution)/shard_map/ppermute | solution.py:275
  6.1 5.2 %collective-permute-start.2 = (bf16[14,256]{1,0:T(8,128)(2,1)S(1)}, bf16[14,256]{1,0:T(8,128)(2,1)S(1)}, u32[]{:S(2)}, u32[]{:S(2)}) collective-permute-start(bf16[14,256]{1,0:T(8,128)(2,1)S(1)} %get-tuple-element.65.refs_0_), channel_id=1, source_target_pairs={{0,1},{1,0},{2,3},{3,2},{4,5},{5,4},{6,7},{7,6},{8,9},{9,8},{10,11... | collective-permute-start | bytes 21512 | tf_op jit(solution)/shard_map/ppermute | solution.py:275
  8.0 4.9 %collective-permute-start.3 = (bf16[14,256]{1,0:T(8,128)(2,1)S(1)}, bf16[14,256]{1,0:T(8,128)(2,1)S(1)}, u32[]{:S(2)}, u32[]{:S(2)}) collective-permute-start(bf16[14,256]{1,0:T(8,128)(2,1)S(1)} %get-tuple-element.64), channel_id=1, source_target_pairs={{0,129},{1,128},{128,1},{129,0},{2,131},{3,130},{130,3},{131,2},{4... | collective-permute-start | bytes 21512 | tf_op jit(solution)/shard_map/ppermute | solution.py:298
  12.8 37.3 %copy-start.1 = (bf16[128,512]{1,0:T(8,128)(2,1)S(1)}, bf16[128,512]{1,0:T(8,128)(2,1)}, u32[]{:S(2)}) copy-start(bf16[128,512]{1,0:T(8,128)(2,1)} %q_ref.1) | copy-start | bytes 393220
  12.8 37.3 %copy-start.2 = (s32[1,16]{1,0:T(1,128)S(1)}, s32[1,16]{1,0:T(1,128)}, u32[]{:S(2)}) copy-start(s32[1,16]{1,0:T(1,128)} %assign_ref.1) | copy-start | bytes 196
  12.8 37.3 %copy-start.3 = (s32[1,4]{1,0:T(1,128)S(1)}, s32[1,4]{1,0:T(1,128)}, u32[]{:S(2)}) copy-start(s32[1,4]{1,0:T(1,128)} %length_ref.1) | copy-start | bytes 52
  12.9 5.6 %collective-permute-start.4 = (bf16[320,256]{1,0:T(8,128)(2,1)S(1)}, bf16[320,256]{1,0:T(8,128)(2,1)S(1)}, u32[]{:S(2)}, u32[]{:S(2)}) collective-permute-start(bf16[320,256]{1,0:T(8,128)(2,1)S(1)} %pack.1.refs_0_), channel_id=1, source_target_pairs={{2,0},{4,2},{6,4},{8,6},{10,8},{12,10},{14,12},{0,14},{3,1},{5,3},... | collective-permute-start | bytes 491528 | tf_op jit(solution)/shard_map/ppermute | solution.py:280
  13.0 9.2 %collective-permute-start.5 = (bf16[320,256]{1,0:T(8,128)(2,1)S(1)}, bf16[320,256]{1,0:T(8,128)(2,1)S(1)}, u32[]{:S(2)}, u32[]{:S(2)}) collective-permute-start(bf16[320,256]{1,0:T(8,128)(2,1)S(1)} %pack.1.refs_0_), channel_id=1, source_target_pairs={{14,0},{0,2},{2,4},{4,6},{6,8},{8,10},{10,12},{12,14},{15,1},{1,3}... | collective-permute-start | bytes 491528 | tf_op jit(solution)/shard_map/ppermute | solution.py:280
  15.0 1.2 %copy-start = (bf16[128,3584]{1,0:T(8,128)(2,1)S(1)}, bf16[128,3584]{1,0:T(8,128)(2,1)}, u32[]{:S(2)}) copy-start(bf16[128,3584]{1,0:T(8,128)(2,1)} %refs_1_) | copy-start | bytes 2752516
  22.2 6.1 %collective-permute-start.6 = (bf16[320,256]{1,0:T(8,128)(2,1)S(1)}, bf16[320,256]{1,0:T(8,128)(2,1)S(1)}, u32[]{:S(2)}, u32[]{:S(2)}) collective-permute-start(bf16[320,256]{1,0:T(8,128)(2,1)S(1)} %collective-permute-done.4.refs_1_), channel_id=1, source_target_pairs={{2,0},{4,2},{6,4},{8,6},{10,8},{12,10},{14,12},{0,14},{3,1},{5,3},... | collective-permute-start | bytes 491528 | tf_op jit(solution)/shard_map/ppermute | solution.py:280
  25.4 5.3 %collective-permute-start.7 = (bf16[320,256]{1,0:T(8,128)(2,1)S(1)}, bf16[320,256]{1,0:T(8,128)(2,1)S(1)}, u32[]{:S(2)}, u32[]{:S(2)}) collective-permute-start(bf16[320,256]{1,0:T(8,128)(2,1)S(1)} %collective-permute-done.5.refs_2_), channel_id=1, source_target_pairs={{14,0},{0,2},{2,4},{4,6},{6,8},{8,10},{10,12},{12,14},{15,1},{1,3}... | collective-permute-start | bytes 491528 | tf_op jit(solution)/shard_map/ppermute | solution.py:280
  25.4 5.3 %collective-permute-start.8 = (bf16[128,2048]{1,0:T(8,128)(2,1)S(1)}, bf16[128,2048]{1,0:T(8,128)(2,1)S(1)}, u32[]{:S(2)}, u32[]{:S(2)}) collective-permute-start(bf16[128,2048]{1,0:T(8,128)(2,1)S(1)} %get-tuple-element.37), channel_id=1, source_target_pairs={{0,16},{16,0},{1,17},{17,1},{2,18},{18,2},{3,19},{19,3},{4,20},{20... | collective-permute-start | bytes 1572872 | tf_op jit(solution)/shard_map/ppermute | solution.py:275
  25.4 14.7 %collective-permute-start.11 = (bf16[128,2048]{1,0:T(8,128)(2,1)S(1)}, bf16[128,2048]{1,0:T(8,128)(2,1)S(1)}, u32[]{:S(2)}, u32[]{:S(2)}) collective-permute-start(bf16[128,2048]{1,0:T(8,128)(2,1)S(1)} %get-tuple-element.40), channel_id=1, source_target_pairs={{0,128},{128,0},{1,129},{129,1},{2,130},{130,2},{3,131},{131,3},{4... | collective-permute-start | bytes 1572872 | tf_op jit(solution)/shard_map/ppermute | solution.py:275
  30.8 9.4 %collective-permute-start.9 = (bf16[320,256]{1,0:T(8,128)(2,1)S(1)}, bf16[320,256]{1,0:T(8,128)(2,1)S(1)}, u32[]{:S(2)}, u32[]{:S(2)}) collective-permute-start(bf16[320,256]{1,0:T(8,128)(2,1)S(1)} %collective-permute-done.6.refs_3_), channel_id=1, source_target_pairs={{2,0},{4,2},{6,4},{8,6},{10,8},{12,10},{14,12},{0,14},{3,1},{5,3},... | collective-permute-start | bytes 491528 | tf_op jit(solution)/shard_map/ppermute | solution.py:280
  32.3 7.9 %collective-permute-start.10 = (bf16[320,256]{1,0:T(8,128)(2,1)S(1)}, bf16[320,256]{1,0:T(8,128)(2,1)S(1)}, u32[]{:S(2)}, u32[]{:S(2)}) collective-permute-start(bf16[320,256]{1,0:T(8,128)(2,1)S(1)} %collective-permute-done.7.refs_4_), channel_id=1, source_target_pairs={{14,0},{0,2},{2,4},{4,6},{6,8},{8,10},{10,12},{12,14},{15,1},{1,3}... | collective-permute-start | bytes 491528 | tf_op jit(solution)/shard_map/ppermute | solution.py:280
  32.8 21.6 %collective-permute-start.13 = (bf16[128,2048]{1,0:T(8,128)(2,1)S(1)}, bf16[128,2048]{1,0:T(8,128)(2,1)S(1)}, u32[]{:S(2)}, u32[]{:S(2)}) collective-permute-start(bf16[128,2048]{1,0:T(8,128)(2,1)S(1)} %collective-permute-done.8), channel_id=1, source_target_pairs={{0,128},{128,0},{1,129},{129,1},{2,130},{130,2},{3,131},{131,3},{4... | collective-permute-start | bytes 1572872 | tf_op jit(solution)/shard_map/ppermute | solution.py:275
  40.2 5.4 %collective-permute-start.12 = (bf16[320,256]{1,0:T(8,128)(2,1)S(1)}, bf16[320,256]{1,0:T(8,128)(2,1)S(1)}, u32[]{:S(2)}, u32[]{:S(2)}) collective-permute-start(bf16[320,256]{1,0:T(8,128)(2,1)S(1)} %collective-permute-done.9.refs_5_), channel_id=1, source_target_pairs={{2,0},{4,2},{6,4},{8,6},{10,8},{12,10},{14,12},{0,14},{3,1},{5,3},... | collective-permute-start | bytes 491528 | tf_op jit(solution)/shard_map/ppermute | solution.py:280
  45.6 12.6 %collective-permute-start.15 = (bf16[512,256]{1,0:T(8,128)(2,1)S(1)}, bf16[512,256]{1,0:T(8,128)(2,1)S(1)}, u32[]{:S(2)}, u32[]{:S(2)}) collective-permute-start(bf16[512,256]{1,0:T(8,128)(2,1)S(1)} %slice_dynamic-update-slice_fusion.refs_0_), channel_id=1, source_target_pairs={{32,0},{64,32},{96,64},{0,96},{33,1},{65,33},{97,65},{1,97},{34,2}... | collective-permute-start | bytes 786440 | tf_op jit(solution)/shard_map/ppermute | solution.py:280
  48.4 10.7 %collective-permute-start.16 = (bf16[512,256]{1,0:T(8,128)(2,1)S(1)}, bf16[512,256]{1,0:T(8,128)(2,1)S(1)}, u32[]{:S(2)}, u32[]{:S(2)}) collective-permute-start(bf16[512,256]{1,0:T(8,128)(2,1)S(1)} %slice_dynamic-update-slice_fusion.refs_0_), channel_id=1, source_target_pairs={{64,0},{96,32},{0,64},{32,96},{65,1},{97,33},{1,65},{33,97},{66,2}... | collective-permute-start | bytes 786440 | tf_op jit(solution)/shard_map/ppermute | solution.py:280
  49.2 12.7 %collective-permute-start.17 = (bf16[512,256]{1,0:T(8,128)(2,1)S(1)}, bf16[512,256]{1,0:T(8,128)(2,1)S(1)}, u32[]{:S(2)}, u32[]{:S(2)}) collective-permute-start(bf16[512,256]{1,0:T(8,128)(2,1)S(1)} %slice_dynamic-update-slice_fusion.refs_0_), channel_id=1, source_target_pairs={{96,0},{0,32},{32,64},{64,96},{97,1},{1,33},{33,65},{65,97},{98,2}... | collective-permute-start | bytes 786440 | tf_op jit(solution)/shard_map/ppermute | solution.py:280
  53.9 4.3 %collective-permute-start.14 = (bf16[128,256]{1,0:T(8,128)(2,1)S(1)}, bf16[128,256]{1,0:T(8,128)(2,1)S(1)}, u32[]{:S(2)}, u32[]{:S(2)}) collective-permute-start(bf16[128,256]{1,0:T(8,128)(2,1)S(1)} %get-tuple-element.55), channel_id=1, source_target_pairs={{0,128},{128,0},{1,129},{129,1},{2,130},{130,2},{3,131},{131,3},{4... | collective-permute-start | bytes 196616 | tf_op jit(solution)/shard_map/ppermute | solution.py:275
  63.3 1.6 %collective-permute-start.18 = (bf16[512,256]{1,0:T(8,128)(2,1)S(1)}, bf16[512,256]{1,0:T(8,128)(2,1)S(1)}, u32[]{:S(2)}, u32[]{:S(2)}) collective-permute-start(bf16[512,256]{1,0:T(8,128)(2,1)S(1)} %get-tuple-element.57), channel_id=1, source_target_pairs={{0,16},{16,0},{1,17},{17,1},{2,18},{18,2},{3,19},{19,3},{4,20},{20... | collective-permute-start | bytes 786440 | tf_op jit(solution)/shard_map/ppermute | solution.py:275
  67.2 13.8 %collective-permute-start.21 = (bf16[448,256]{1,0:T(8,128)(2,1)S(1)}, bf16[448,256]{1,0:T(8,128)(2,1)S(1)}, u32[]{:S(2)}, u32[]{:S(2)}) collective-permute-start(bf16[448,256]{1,0:T(8,128)(2,1)S(1)} %get-tuple-element.61), channel_id=1, source_target_pairs={{96,0},{0,32},{32,64},{64,96},{97,1},{1,33},{33,65},{65,97},{98,2}... | collective-permute-start | bytes 688136 | tf_op jit(solution)/shard_map/ppermute | solution.py:280
  67.3 13.8 %collective-permute-start.20 = (bf16[448,256]{1,0:T(8,128)(2,1)S(1)}, bf16[448,256]{1,0:T(8,128)(2,1)S(1)}, u32[]{:S(2)}, u32[]{:S(2)}) collective-permute-start(bf16[448,256]{1,0:T(8,128)(2,1)S(1)} %get-tuple-element.60), channel_id=1, source_target_pairs={{64,0},{96,32},{0,64},{32,96},{65,1},{97,33},{1,65},{33,97},{66,2}... | collective-permute-start | bytes 688136 | tf_op jit(solution)/shard_map/ppermute | solution.py:280
  69.4 12.3 %collective-permute-start.19 = (bf16[448,256]{1,0:T(8,128)(2,1)S(1)}, bf16[448,256]{1,0:T(8,128)(2,1)S(1)}, u32[]{:S(2)}, u32[]{:S(2)}) collective-permute-start(bf16[448,256]{1,0:T(8,128)(2,1)S(1)} %get-tuple-element.59), channel_id=1, source_target_pairs={{32,0},{64,32},{96,64},{0,96},{33,1},{65,33},{97,65},{1,97},{34,2}... | collective-permute-start | bytes 688136 | tf_op jit(solution)/shard_map/ppermute | solution.py:280

commit v10 on v9

--- a/solution.py
+++ b/solution.py
@@ -312,14 +312,12 @@
             held[-d] = from_next(held[1 - d], "z", -1)
         if d == 2:
             held[2], held[-2], n_got = lax.optimization_barrier((held[2], held[-2], n_got))
-        if d == 3:
-            held[3], held[-3], n_across = lax.optimization_barrier((held[3], held[-3], n_across))
     n_all = jnp.concatenate([n_keep, n_got, n_across, partner(n_got, "ylo")], axis=0)
     parts = [held[d] for d in RING]
     w_rows = jnp.concatenate([part[2 * BLK :] for part in parts], axis=0)
     w_all = [w_rows] + [from_next(w_rows, "x", d) for d in range(1, 4)]
 
-    parts, _ = lax.optimization_barrier((parts, w_rows))
+    parts, _ = lax.optimization_barrier((parts, (w_rows, n_across)))
     attention, a_mine, a_other = attend(here, queries, parts, lengths, assignment)
 
     own, send = project(here, n_all, a_mine, partner(a_other, "ylo"), w_all)

time: 103 us -> 97.6 us (0.948)
  waiting for transfers between devices: 42.1 us -> 37.7 us
    ppermute x8, waiting for transfers between devices: 13.6 us -> 6.79 us  [partner(): return lax.ppermute(x, axis, [(0, 1), (1, 0)])]
    ppermute x13, waiting for transfers between devices: 27 us -> 29.4 us  [from_next(): lax.ppermute(x, axis, [((i + distance) % size, i) for i in range(size)])]
where the time goes in v10:
time: 97.6 us; the launch traced here: 96.3 us
  waiting for transfers between devices  37.7 us (39%)
  starting transfers between devices  24.9 us (26%)
  blocking collectives  19.2 us (20%)
  Pallas kernels  9.84 us (10%)
  other arithmetic  2.29 us (2%)
  local copies, waits for them, and re-layouts  1.56 us (2%)
    ppermute x13, waiting for transfers between devices, from_next(): lax.ppermute(x, axis, [((i + distance) % size, i) for i in range(size)])  29.4 us
    all_to_all x1, blocking collectives, local(): lax.all_to_all(near, ('ylo', *SEQ), split_axis=0, concat_axis=0, tiled=True)  19.2 us
    ppermute x13, starting transfers between devices, from_next(): lax.ppermute(x, axis, [((i + distance) % size, i) for i in range(size)])  16.7 us
    ppermute x8, waiting for transfers between devices, partner(): return lax.ppermute(x, axis, [(0, 1), (1, 0)])  6.79 us
    ppermute x8, starting transfers between devices, partner(): return lax.ppermute(x, axis, [(0, 1), (1, 0)])  5.99 us
    pallas_call x1, Pallas kernels, attend(): pl.pallas_call(attend_kernel, out_shape=(jax.ShapeDtypeStruct((rows, COLS...  3.77 us
    pallas_call x1, Pallas kernels, normalise(): pl.pallas_call(body, out_shape=(shape, shape), in_specs=[SMEM, VMEM], out...  2.32 us
    pallas_call x1, Pallas kernels, gradient(): pl.pallas_call(gradient_kernel, out_shape=(shape,) * 4, in_specs=[SMEM, V...  2.26 us
  transfers between devices with their start and end apart: 22, of which 13 were waited for; matrix products, arithmetic and copies ran while one was open for 1% of the time, Pallas kernels for 6%

profile of v10, /device:TPU:32, one launch (start us, length us, event | category | flops | bytes accessed | tf_op | source)
XLA Modules:
  0.0 96.3 jit_solution(6037204234464745875)
XLA Ops:
  0.6 0.8 pad_select_fusion.kv_ref
  1.4 3.3 %collective-permute-start = (bf16[128,256]{1,0:T(8,128)(2,1)S(1)}, bf16[128,256]{1,0:T(8,128)(2,1)S(1)}, u32[]{:S(2)}, u32[]{:S(2)}) collective-permute-start(bf16[128,256]{1,0:T(8,128)(2,1)S(1)} %pad_select_fusion.kv_ref), channel_id=1, source_target_pairs={{0,1},{1,0},{2,3},{3,2},{4,5},{5,4},{6,7},{7,6},{8,9},{9,8},{10,11... | collective-permute-start | bytes 196616 | tf_op jit(solution)/shard_map/ppermute | solution.py:275
  4.7 0.7 broadcast_select_fusion
  5.4 0.7 collective-permute-start.1
  6.1 1.8 %collective-permute-start.2 = (bf16[14,256]{1,0:T(8,128)(2,1)S(1)}, bf16[14,256]{1,0:T(8,128)(2,1)S(1)}, u32[]{:S(2)}, u32[]{:S(2)}) collective-permute-start(bf16[14,256]{1,0:T(8,128)(2,1)S(1)} %get-tuple-element.59.refs_0_), channel_id=1, source_target_pairs={{0,1},{1,0},{2,3},{3,2},{4,5},{5,4},{6,7},{7,6},{8,9},{9,8},{10,11... | collective-permute-start | bytes 21512 | tf_op jit(solution)/shard_map/ppermute | solution.py:275
  8.0 2.2 %collective-permute-start.3 = (bf16[14,256]{1,0:T(8,128)(2,1)S(1)}, bf16[14,256]{1,0:T(8,128)(2,1)S(1)}, u32[]{:S(2)}, u32[]{:S(2)}) collective-permute-start(bf16[14,256]{1,0:T(8,128)(2,1)S(1)} %get-tuple-element.58), channel_id=1, source_target_pairs={{0,129},{1,128},{128,1},{129,0},{2,131},{3,130},{130,3},{131,2},{4... | collective-permute-start | bytes 21512 | tf_op jit(solution)/shard_map/ppermute | solution.py:298
  10.1 0.1 stack.23.refs_0_.where_ref
  10.2 0.0 collective-permute-done.1.refs_1_
  10.2 1.0 %collective-permute-done.2.refs_2_ = bf16[14,256]{1,0:T(8,128)(2,1)S(1)} collective-permute-done((bf16[14,256]{1,0:T(8,128)(2,1)S(1)}, bf16[14,256]{1,0:T(8,128)(2,1)S(1)}, u32[]{:S(2)}, u32[]{:S(2)}) %collective-permute-start.2) | collective-permute-done | bytes 7200 | tf_op jit(solution)/shard_map/ppermute | solution.py:275
  11.3 1.5 %collective-permute-done.3.refs_3_ = bf16[14,256]{1,0:T(8,128)(2,1)S(1)} collective-permute-done((bf16[14,256]{1,0:T(8,128)(2,1)S(1)}, bf16[14,256]{1,0:T(8,128)(2,1)S(1)}, u32[]{:S(2)}, u32[]{:S(2)}) %collective-permute-start.3) | collective-permute-done | bytes 7200 | tf_op jit(solution)/shard_map/ppermute | solution.py:298
  12.8 0.0 collective-permute-done.kv_other_ref
  12.8 0.0 copy-start.1
  12.8 0.0 copy-start.2
  12.8 0.0 copy-start.3
  12.9 0.2 collective-permute-start.4
  13.0 1.9 %collective-permute-start.5 = (bf16[320,256]{1,0:T(8,128)(2,1)S(1)}, bf16[320,256]{1,0:T(8,128)(2,1)S(1)}, u32[]{:S(2)}, u32[]{:S(2)}) collective-permute-start(bf16[320,256]{1,0:T(8,128)(2,1)S(1)} %pack.1.refs_0_), channel_id=1, source_target_pairs={{14,0},{0,2},{2,4},{4,6},{6,8},{8,10},{10,12},{12,14},{15,1},{1,3}... | collective-permute-start | bytes 491528 | tf_op jit(solution)/shard_map/ppermute | solution.py:280
  15.0 0.0 copy-start
  15.0 1.2 %copy-done = bf16[128,3584]{1,0:T(8,128)(2,1)S(1)} copy-done((bf16[128,3584]{1,0:T(8,128)(2,1)S(1)}, bf16[128,3584]{1,0:T(8,128)(2,1)}, u32[]{:S(2)}) %copy-start) | copy-done | bytes 917528
  16.1 2.3 %normalise.1 = (bf16[128,2048]{1,0:T(8,128)(2,1)S(1)}, bf16[128,2048]{1,0:T(8,128)(2,1)S(1)}) custom-call(s32[5]{0:T(128)S(1)} %stack.23.refs_0_.where_ref, bf16[128,3584]{1,0:T(8,128)(2,1)S(1)} %copy-done), custom_call_target="tpu_custom_call" | custom-call | tf_op jit(solution)/shard_map/normalise/pallas_call | solution.py:78
  18.5 0.0 collective-permute-done.4.refs_1_
  18.5 3.7 %collective-permute-done.5.refs_2_ = bf16[320,256]{1,0:T(8,128)(2,1)S(1)} collective-permute-done((bf16[320,256]{1,0:T(8,128)(2,1)S(1)}, bf16[320,256]{1,0:T(8,128)(2,1)S(1)}, u32[]{:S(2)}, u32[]{:S(2)}) %collective-permute-start.5) | collective-permute-done | bytes 163872 | tf_op jit(solution)/shard_map/ppermute | solution.py:280
  22.2 3.2 %collective-permute-start.6 = (bf16[320,256]{1,0:T(8,128)(2,1)S(1)}, bf16[320,256]{1,0:T(8,128)(2,1)S(1)}, u32[]{:S(2)}, u32[]{:S(2)}) collective-permute-start(bf16[320,256]{1,0:T(8,128)(2,1)S(1)} %collective-permute-done.4.refs_1_), channel_id=1, source_target_pairs={{2,0},{4,2},{6,4},{8,6},{10,8},{12,10},{14,12},{0,14},{3,1},{5,3},... | collective-permute-start | bytes 491528 | tf_op jit(solution)/shard_map/ppermute | solution.py:280
  25.4 0.0 collective-permute-start.7
  25.4 0.0 collective-permute-start.8
  25.4 0.1 collective-permute-start.12
  25.6 2.7 %collective-permute-done.6.refs_3_ = bf16[320,256]{1,0:T(8,128)(2,1)S(1)} collective-permute-done((bf16[320,256]{1,0:T(8,128)(2,1)S(1)}, bf16[320,256]{1,0:T(8,128)(2,1)S(1)}, u32[]{:S(2)}, u32[]{:S(2)}) %collective-permute-start.6) | collective-permute-done | bytes 163872 | tf_op jit(solution)/shard_map/ppermute | solution.py:280
  28.3 2.5 %collective-permute-done.7.refs_4_ = bf16[320,256]{1,0:T(8,128)(2,1)S(1)} collective-permute-done((bf16[320,256]{1,0:T(8,128)(2,1)S(1)}, bf16[320,256]{1,0:T(8,128)(2,1)S(1)}, u32[]{:S(2)}, u32[]{:S(2)}) %collective-permute-start.7) | collective-permute-done | bytes 163872 | tf_op jit(solution)/shard_map/ppermute | solution.py:280
  30.7 0.0 collective-permute-done.8
  30.8 1.5 %collective-permute-start.9 = (bf16[320,256]{1,0:T(8,128)(2,1)S(1)}, bf16[320,256]{1,0:T(8,128)(2,1)S(1)}, u32[]{:S(2)}, u32[]{:S(2)}) collective-permute-start(bf16[320,256]{1,0:T(8,128)(2,1)S(1)} %collective-permute-done.6.refs_3_), channel_id=1, source_target_pairs={{2,0},{4,2},{6,4},{8,6},{10,8},{12,10},{14,12},{0,14},{3,1},{5,3},... | collective-permute-start | bytes 491528 | tf_op jit(solution)/shard_map/ppermute | solution.py:280
  32.3 0.5 collective-permute-start.10
  32.8 0.0 collective-permute-start.13
  32.8 4.8 %collective-permute-done.9.refs_5_ = bf16[320,256]{1,0:T(8,128)(2,1)S(1)} collective-permute-done((bf16[320,256]{1,0:T(8,128)(2,1)S(1)}, bf16[320,256]{1,0:T(8,128)(2,1)S(1)}, u32[]{:S(2)}, u32[]{:S(2)}) %collective-permute-start.9) | collective-permute-done | bytes 163872 | tf_op jit(solution)/shard_map/ppermute | solution.py:280
  37.6 1.1 %collective-permute-start.11 = (bf16[320,256]{1,0:T(8,128)(2,1)S(1)}, bf16[320,256]{1,0:T(8,128)(2,1)S(1)}, u32[]{:S(2)}, u32[]{:S(2)}) collective-permute-start(bf16[320,256]{1,0:T(8,128)(2,1)S(1)} %collective-permute-done.9.refs_5_), channel_id=1, source_target_pairs={{2,0},{4,2},{6,4},{8,6},{10,8},{12,10},{14,12},{0,14},{3,1},{5,3},... | collective-permute-start | bytes 491528 | tf_op jit(solution)/shard_map/ppermute | solution.py:280
  38.7 0.0 collective-permute-done.10.refs_6_
  38.7 4.2 %collective-permute-done.11.refs_7_ = bf16[320,256]{1,0:T(8,128)(2,1)S(1)} collective-permute-done((bf16[320,256]{1,0:T(8,128)(2,1)S(1)}, bf16[320,256]{1,0:T(8,128)(2,1)S(1)}, u32[]{:S(2)}, u32[]{:S(2)}) %collective-permute-start.11) | collective-permute-done | bytes 163872 | tf_op jit(solution)/shard_map/ppermute | solution.py:280
  42.9 2.8 %collective-permute-start.15 = (bf16[512,256]{1,0:T(8,128)(2,1)S(1)}, bf16[512,256]{1,0:T(8,128)(2,1)S(1)}, u32[]{:S(2)}, u32[]{:S(2)}) collective-permute-start(bf16[512,256]{1,0:T(8,128)(2,1)S(1)} %slice_dynamic-update-slice_fusion.refs_0_), channel_id=1, source_target_pairs={{32,0},{64,32},{96,64},{0,96},{33,1},{65,33},{97,65},{1,97},{34,2}... | collective-permute-start | bytes 786440 | tf_op jit(solution)/shard_map/ppermute | solution.py:280
  45.7 0.8 collective-permute-start.16
  46.5 0.9 collective-permute-start.17
  47.4 0.0 collective-permute-done.12
  47.4 0.0 copy-done.1
  47.4 0.0 copy-done.2
  47.4 0.0 copy-done.3
  47.4 3.8 %attend.1 = (bf16[128,512]{1,0:T(8,128)(2,1)}, bf16[128,256]{1,0:T(8,128)(2,1)S(1)}, bf16[128,256]{1,0:T(8,128)(2,1)S(1)}) custom-call(s32[5]{0:T(128)S(1)} %stack.23.refs_0_.where_ref, s32[1,16]{1,0:T(1,128)S(1)} %copy-done.2, s32[1,4]{1,0:T(1,128)S(1)} %copy-done.3, bf16[128,512]{1,0:T(8,128)(2,1)S(1)} %copy-done.1, bf16[320,256]{1,0:T(8,128)(2,1)S(1)} %pack.1.refs_0_, ...), custom_call_target="tpu_custom_call" | custom-call | tf_op jit(solution)/shard_map/attend/pallas_call | solution.py:173
  51.2 0.0 collective-permute-start.14
  51.2 0.3 collective-permute-done.13
  51.5 3.9 %collective-permute-done.14.got_ref = bf16[128,256]{1,0:T(8,128)(2,1)S(1)} collective-permute-done((bf16[128,256]{1,0:T(8,128)(2,1)S(1)}, bf16[128,256]{1,0:T(8,128)(2,1)S(1)}, u32[]{:S(2)}, u32[]{:S(2)}) %collective-permute-start.14) | collective-permute-done | bytes 65568 | tf_op jit(solution)/shard_map/ppermute | solution.py:275
  55.5 0.0 collective-permute-done.15.refs_1_
  55.5 0.0 collective-permute-done.16.refs_2_
  55.5 0.9 collective-permute-done.17.refs_3_
  56.4 1.5 %project.1 = (f32[512,256]{1,0:T(8,128)S(1)}, bf16[512,256]{1,0:T(8,128)(2,1)S(1)}) custom-call(s32[5]{0:T(128)S(1)} %stack.23.refs_0_.where_ref, bf16[512,2048]{1,0:T(8,128)(2,1)S(1)} %constant_dynamic-update-slice_fusion.n_ref, bf16[128,256]{1,0:T(8,128)(2,1)S(1)} %get-tuple-element.48.mine_ref, bf16[128,256]{1,0:T(8,128)(2,1)S(1)} %collective-permute-done.14.got_ref, ...), custom_call_target="tpu_custom_call" | custom-call | tf_op jit(solution)/shard_map/project/pallas_call | solution.py:215
  57.8 0.1 collective-permute-start.18
  58.0 1.5 %collective-permute-done.18.back_ref = bf16[512,256]{1,0:T(8,128)(2,1)S(1)} collective-permute-done((bf16[512,256]{1,0:T(8,128)(2,1)S(1)}, bf16[512,256]{1,0:T(8,128)(2,1)S(1)}, u32[]{:S(2)}, u32[]{:S(2)}) %collective-permute-start.18) | collective-permute-done | bytes 262176 | tf_op jit(solution)/shard_map/ppermute | solution.py:275
  59.5 2.3 %gradient.1 = (bf16[448,256]{1,0:T(8,128)(2,1)S(1)}, bf16[448,256]{1,0:T(8,128)(2,1)S(1)}, bf16[448,256]{1,0:T(8,128)(2,1)S(1)}, bf16[448,256]{1,0:T(8,128)(2,1)S(1)}) custom-call(s32[5]{0:T(128)S(1)} %stack.23.refs_0_.where_ref, bf16[512,2048]{1,0:T(8,128)(2,1)S(1)} %constant_dynamic-update-slice_fusion.n_ref, f32[512,256]{1,0:T(8,128)S(1)} %get-tuple-element.50.own_ref, ...), custom_call_target="tpu_custom_call" | custom-call | tf_op jit(solution)/shard_map/gradient/pallas_call | solution.py:264
  61.7 1.0 %collective-permute-start.21 = (bf16[448,256]{1,0:T(8,128)(2,1)S(1)}, bf16[448,256]{1,0:T(8,128)(2,1)S(1)}, u32[]{:S(2)}, u32[]{:S(2)}) collective-permute-start(bf16[448,256]{1,0:T(8,128)(2,1)S(1)} %get-tuple-element.55), channel_id=1, source_target_pairs={{96,0},{0,32},{32,64},{64,96},{97,1},{1,33},{33,65},{65,97},{98,2}... | collective-permute-start | bytes 688136 | tf_op jit(solution)/shard_map/ppermute | solution.py:280
  62.8 2.0 %collective-permute-start.20 = (bf16[448,256]{1,0:T(8,128)(2,1)S(1)}, bf16[448,256]{1,0:T(8,128)(2,1)S(1)}, u32[]{:S(2)}, u32[]{:S(2)}) collective-permute-start(bf16[448,256]{1,0:T(8,128)(2,1)S(1)} %get-tuple-element.54), channel_id=1, source_target_pairs={{64,0},{96,32},{0,64},{32,96},{65,1},{97,33},{1,65},{33,97},{66,2}... | collective-permute-start | bytes 688136 | tf_op jit(solution)/shard_map/ppermute | solution.py:280
  64.8 0.8 collective-permute-start.19
  65.5 10.1 %collective-permute-done.21 = bf16[448,256]{1,0:T(8,128)(2,1)S(1)} collective-permute-done((bf16[448,256]{1,0:T(8,128)(2,1)S(1)}, bf16[448,256]{1,0:T(8,128)(2,1)S(1)}, u32[]{:S(2)}, u32[]{:S(2)}) %collective-permute-start.21) | collective-permute-done | bytes 229408 | tf_op jit(solution)/shard_map/ppermute | solution.py:280
  75.6 0.0 collective-permute-done.20
  75.6 0.6 collective-permute-done.19
  76.2 0.1 add_convert_fusion
  76.3 0.1 reshape.10
  76.4 19.2 %all_to_all.5 = bf16[32,16,256]{2,1,0:T(8,128)(2,1)S(1)} all-to-all(bf16[32,16,256]{2,1,0:T(8,128)(2,1)S(1)} %pad.14), channel_id=1, replica_groups=mesh['ylo'=2,'x'=4,'core'=2,'z'=8,'yhi'=2] {'ylo','z','yhi'}, dimensions={0} | all-to-all | bytes 524288 | tf_op jit(solution)/shard_map/all_to_all | solution.py:330
  95.7 0.6 pad_maximum_fusion
  (17 shorter events, 0.3 us)
Async XLA Ops:
  1.4 11.4 %collective-permute-start = (bf16[128,256]{1,0:T(8,128)(2,1)S(1)}, bf16[128,256]{1,0:T(8,128)(2,1)S(1)}, u32[]{:S(2)}, u32[]{:S(2)}) collective-permute-start(bf16[128,256]{1,0:T(8,128)(2,1)S(1)} %pad_select_fusion.kv_ref), channel_id=1, source_target_pairs={{0,1},{1,0},{2,3},{3,2},{4,5},{5,4},{6,7},{7,6},{8,9},{9,8},{10,11... | collective-permute-start | bytes 196616 | tf_op jit(solution)/shard_map/ppermute | solution.py:275
  5.4 4.8 %collective-permute-start.1 = (bf16[14,256]{1,0:T(8,128)(2,1)S(1)}, bf16[14,256]{1,0:T(8,128)(2,1)S(1)}, u32[]{:S(2)}, u32[]{:S(2)}) collective-permute-start(bf16[14,256]{1,0:T(8,128)(2,1)S(1)} %get-tuple-element.58), channel_id=1, source_target_pairs={{0,128},{128,0},{1,129},{129,1},{2,130},{130,2},{3,131},{131,3},{4... | collective-permute-start | bytes 21512 | tf_op jit(solution)/shard_map/ppermute | solution.py:275
  6.1 5.2 %collective-permute-start.2 = (bf16[14,256]{1,0:T(8,128)(2,1)S(1)}, bf16[14,256]{1,0:T(8,128)(2,1)S(1)}, u32[]{:S(2)}, u32[]{:S(2)}) collective-permute-start(bf16[14,256]{1,0:T(8,128)(2,1)S(1)} %get-tuple-element.59.refs_0_), channel_id=1, source_target_pairs={{0,1},{1,0},{2,3},{3,2},{4,5},{5,4},{6,7},{7,6},{8,9},{9,8},{10,11... | collective-permute-start | bytes 21512 | tf_op jit(solution)/shard_map/ppermute | solution.py:275
  8.0 4.9 %collective-permute-start.3 = (bf16[14,256]{1,0:T(8,128)(2,1)S(1)}, bf16[14,256]{1,0:T(8,128)(2,1)S(1)}, u32[]{:S(2)}, u32[]{:S(2)}) collective-permute-start(bf16[14,256]{1,0:T(8,128)(2,1)S(1)} %get-tuple-element.58), channel_id=1, source_target_pairs={{0,129},{1,128},{128,1},{129,0},{2,131},{3,130},{130,3},{131,2},{4... | collective-permute-start | bytes 21512 | tf_op jit(solution)/shard_map/ppermute | solution.py:298
  12.8 34.6 %copy-start.1 = (bf16[128,512]{1,0:T(8,128)(2,1)S(1)}, bf16[128,512]{1,0:T(8,128)(2,1)}, u32[]{:S(2)}) copy-start(bf16[128,512]{1,0:T(8,128)(2,1)} %q_ref.1) | copy-start | bytes 393220
  12.8 34.6 %copy-start.2 = (s32[1,16]{1,0:T(1,128)S(1)}, s32[1,16]{1,0:T(1,128)}, u32[]{:S(2)}) copy-start(s32[1,16]{1,0:T(1,128)} %assign_ref.1) | copy-start | bytes 196
  12.8 34.6 %copy-start.3 = (s32[1,4]{1,0:T(1,128)S(1)}, s32[1,4]{1,0:T(1,128)}, u32[]{:S(2)}) copy-start(s32[1,4]{1,0:T(1,128)} %length_ref.1) | copy-start | bytes 52
  12.9 5.6 %collective-permute-start.4 = (bf16[320,256]{1,0:T(8,128)(2,1)S(1)}, bf16[320,256]{1,0:T(8,128)(2,1)S(1)}, u32[]{:S(2)}, u32[]{:S(2)}) collective-permute-start(bf16[320,256]{1,0:T(8,128)(2,1)S(1)} %pack.1.refs_0_), channel_id=1, source_target_pairs={{2,0},{4,2},{6,4},{8,6},{10,8},{12,10},{14,12},{0,14},{3,1},{5,3},... | collective-permute-start | bytes 491528 | tf_op jit(solution)/shard_map/ppermute | solution.py:280
  13.0 9.2 %collective-permute-start.5 = (bf16[320,256]{1,0:T(8,128)(2,1)S(1)}, bf16[320,256]{1,0:T(8,128)(2,1)S(1)}, u32[]{:S(2)}, u32[]{:S(2)}) collective-permute-start(bf16[320,256]{1,0:T(8,128)(2,1)S(1)} %pack.1.refs_0_), channel_id=1, source_target_pairs={{14,0},{0,2},{2,4},{4,6},{6,8},{8,10},{10,12},{12,14},{15,1},{1,3}... | collective-permute-start | bytes 491528 | tf_op jit(solution)/shard_map/ppermute | solution.py:280
  15.0 1.2 %copy-start = (bf16[128,3584]{1,0:T(8,128)(2,1)S(1)}, bf16[128,3584]{1,0:T(8,128)(2,1)}, u32[]{:S(2)}) copy-start(bf16[128,3584]{1,0:T(8,128)(2,1)} %refs_1_) | copy-start | bytes 2752516
  22.2 6.1 %collective-permute-start.6 = (bf16[320,256]{1,0:T(8,128)(2,1)S(1)}, bf16[320,256]{1,0:T(8,128)(2,1)S(1)}, u32[]{:S(2)}, u32[]{:S(2)}) collective-permute-start(bf16[320,256]{1,0:T(8,128)(2,1)S(1)} %collective-permute-done.4.refs_1_), channel_id=1, source_target_pairs={{2,0},{4,2},{6,4},{8,6},{10,8},{12,10},{14,12},{0,14},{3,1},{5,3},... | collective-permute-start | bytes 491528 | tf_op jit(solution)/shard_map/ppermute | solution.py:280
  25.4 5.3 %collective-permute-start.7 = (bf16[320,256]{1,0:T(8,128)(2,1)S(1)}, bf16[320,256]{1,0:T(8,128)(2,1)S(1)}, u32[]{:S(2)}, u32[]{:S(2)}) collective-permute-start(bf16[320,256]{1,0:T(8,128)(2,1)S(1)} %collective-permute-done.5.refs_2_), channel_id=1, source_target_pairs={{14,0},{0,2},{2,4},{4,6},{6,8},{8,10},{10,12},{12,14},{15,1},{1,3}... | collective-permute-start | bytes 491528 | tf_op jit(solution)/shard_map/ppermute | solution.py:280
  25.4 5.3 %collective-permute-start.8 = (bf16[128,2048]{1,0:T(8,128)(2,1)S(1)}, bf16[128,2048]{1,0:T(8,128)(2,1)S(1)}, u32[]{:S(2)}, u32[]{:S(2)}) collective-permute-start(bf16[128,2048]{1,0:T(8,128)(2,1)S(1)} %get-tuple-element.34), channel_id=1, source_target_pairs={{0,16},{16,0},{1,17},{17,1},{2,18},{18,2},{3,19},{19,3},{4,20},{20... | collective-permute-start | bytes 1572872 | tf_op jit(solution)/shard_map/ppermute | solution.py:275
  25.4 21.9 %collective-permute-start.12 = (bf16[128,2048]{1,0:T(8,128)(2,1)S(1)}, bf16[128,2048]{1,0:T(8,128)(2,1)S(1)}, u32[]{:S(2)}, u32[]{:S(2)}) collective-permute-start(bf16[128,2048]{1,0:T(8,128)(2,1)S(1)} %get-tuple-element.37), channel_id=1, source_target_pairs={{0,128},{128,0},{1,129},{129,1},{2,130},{130,2},{3,131},{131,3},{4... | collective-permute-start | bytes 1572872 | tf_op jit(solution)/shard_map/ppermute | solution.py:275
  30.8 6.9 %collective-permute-start.9 = (bf16[320,256]{1,0:T(8,128)(2,1)S(1)}, bf16[320,256]{1,0:T(8,128)(2,1)S(1)}, u32[]{:S(2)}, u32[]{:S(2)}) collective-permute-start(bf16[320,256]{1,0:T(8,128)(2,1)S(1)} %collective-permute-done.6.refs_3_), channel_id=1, source_target_pairs={{2,0},{4,2},{6,4},{8,6},{10,8},{12,10},{14,12},{0,14},{3,1},{5,3},... | collective-permute-start | bytes 491528 | tf_op jit(solution)/shard_map/ppermute | solution.py:280
  32.3 6.4 %collective-permute-start.10 = (bf16[320,256]{1,0:T(8,128)(2,1)S(1)}, bf16[320,256]{1,0:T(8,128)(2,1)S(1)}, u32[]{:S(2)}, u32[]{:S(2)}) collective-permute-start(bf16[320,256]{1,0:T(8,128)(2,1)S(1)} %collective-permute-done.7.refs_4_), channel_id=1, source_target_pairs={{14,0},{0,2},{2,4},{4,6},{6,8},{8,10},{10,12},{12,14},{15,1},{1,3}... | collective-permute-start | bytes 491528 | tf_op jit(solution)/shard_map/ppermute | solution.py:280
  32.8 18.7 %collective-permute-start.13 = (bf16[128,2048]{1,0:T(8,128)(2,1)S(1)}, bf16[128,2048]{1,0:T(8,128)(2,1)S(1)}, u32[]{:S(2)}, u32[]{:S(2)}) collective-permute-start(bf16[128,2048]{1,0:T(8,128)(2,1)S(1)} %collective-permute-done.8), channel_id=1, source_target_pairs={{0,128},{128,0},{1,129},{129,1},{2,130},{130,2},{3,131},{131,3},{4... | collective-permute-start | bytes 1572872 | tf_op jit(solution)/shard_map/ppermute | solution.py:275
  37.6 5.3 %collective-permute-start.11 = (bf16[320,256]{1,0:T(8,128)(2,1)S(1)}, bf16[320,256]{1,0:T(8,128)(2,1)S(1)}, u32[]{:S(2)}, u32[]{:S(2)}) collective-permute-start(bf16[320,256]{1,0:T(8,128)(2,1)S(1)} %collective-permute-done.9.refs_5_), channel_id=1, source_target_pairs={{2,0},{4,2},{6,4},{8,6},{10,8},{12,10},{14,12},{0,14},{3,1},{5,3},... | collective-permute-start | bytes 491528 | tf_op jit(solution)/shard_map/ppermute | solution.py:280
  42.9 12.6 %collective-permute-start.15 = (bf16[512,256]{1,0:T(8,128)(2,1)S(1)}, bf16[512,256]{1,0:T(8,128)(2,1)S(1)}, u32[]{:S(2)}, u32[]{:S(2)}) collective-permute-start(bf16[512,256]{1,0:T(8,128)(2,1)S(1)} %slice_dynamic-update-slice_fusion.refs_0_), channel_id=1, source_target_pairs={{32,0},{64,32},{96,64},{0,96},{33,1},{65,33},{97,65},{1,97},{34,2}... | collective-permute-start | bytes 786440 | tf_op jit(solution)/shard_map/ppermute | solution.py:280
  45.7 9.8 %collective-permute-start.16 = (bf16[512,256]{1,0:T(8,128)(2,1)S(1)}, bf16[512,256]{1,0:T(8,128)(2,1)S(1)}, u32[]{:S(2)}, u32[]{:S(2)}) collective-permute-start(bf16[512,256]{1,0:T(8,128)(2,1)S(1)} %slice_dynamic-update-slice_fusion.refs_0_), channel_id=1, source_target_pairs={{64,0},{96,32},{0,64},{32,96},{65,1},{97,33},{1,65},{33,97},{66,2}... | collective-permute-start | bytes 786440 | tf_op jit(solution)/shard_map/ppermute | solution.py:280
  46.5 9.9 %collective-permute-start.17 = (bf16[512,256]{1,0:T(8,128)(2,1)S(1)}, bf16[512,256]{1,0:T(8,128)(2,1)S(1)}, u32[]{:S(2)}, u32[]{:S(2)}) collective-permute-start(bf16[512,256]{1,0:T(8,128)(2,1)S(1)} %slice_dynamic-update-slice_fusion.refs_0_), channel_id=1, source_target_pairs={{96,0},{0,32},{32,64},{64,96},{97,1},{1,33},{33,65},{65,97},{98,2}... | collective-permute-start | bytes 786440 | tf_op jit(solution)/shard_map/ppermute | solution.py:280
  51.2 4.3 %collective-permute-start.14 = (bf16[128,256]{1,0:T(8,128)(2,1)S(1)}, bf16[128,256]{1,0:T(8,128)(2,1)S(1)}, u32[]{:S(2)}, u32[]{:S(2)}) collective-permute-start(bf16[128,256]{1,0:T(8,128)(2,1)S(1)} %get-tuple-element.49), channel_id=1, source_target_pairs={{0,128},{128,0},{1,129},{129,1},{2,130},{130,2},{3,131},{131,3},{4... | collective-permute-start | bytes 196616 | tf_op jit(solution)/shard_map/ppermute | solution.py:275
  57.8 1.6 %collective-permute-start.18 = (bf16[512,256]{1,0:T(8,128)(2,1)S(1)}, bf16[512,256]{1,0:T(8,128)(2,1)S(1)}, u32[]{:S(2)}, u32[]{:S(2)}) collective-permute-start(bf16[512,256]{1,0:T(8,128)(2,1)S(1)} %get-tuple-element.51), channel_id=1, source_target_pairs={{0,16},{16,0},{1,17},{17,1},{2,18},{18,2},{3,19},{19,3},{4,20},{20... | collective-permute-start | bytes 786440 | tf_op jit(solution)/shard_map/ppermute | solution.py:275
  61.7 13.8 %collective-permute-start.21 = (bf16[448,256]{1,0:T(8,128)(2,1)S(1)}, bf16[448,256]{1,0:T(8,128)(2,1)S(1)}, u32[]{:S(2)}, u32[]{:S(2)}) collective-permute-start(bf16[448,256]{1,0:T(8,128)(2,1)S(1)} %get-tuple-element.55), channel_id=1, source_target_pairs={{96,0},{0,32},{32,64},{64,96},{97,1},{1,33},{33,65},{65,97},{98,2}... | collective-permute-start | bytes 688136 | tf_op jit(solution)/shard_map/ppermute | solution.py:280
  62.8 12.8 %collective-permute-start.20 = (bf16[448,256]{1,0:T(8,128)(2,1)S(1)}, bf16[448,256]{1,0:T(8,128)(2,1)S(1)}, u32[]{:S(2)}, u32[]{:S(2)}) collective-permute-start(bf16[448,256]{1,0:T(8,128)(2,1)S(1)} %get-tuple-element.54), channel_id=1, source_target_pairs={{64,0},{96,32},{0,64},{32,96},{65,1},{97,33},{1,65},{33,97},{66,2}... | collective-permute-start | bytes 688136 | tf_op jit(solution)/shard_map/ppermute | solution.py:280
  64.8 11.4 %collective-permute-start.19 = (bf16[448,256]{1,0:T(8,128)(2,1)S(1)}, bf16[448,256]{1,0:T(8,128)(2,1)S(1)}, u32[]{:S(2)}, u32[]{:S(2)}) collective-permute-start(bf16[448,256]{1,0:T(8,128)(2,1)S(1)} %get-tuple-element.53), channel_id=1, source_target_pairs={{32,0},{64,32},{96,64},{0,96},{33,1},{65,33},{97,65},{1,97},{34,2}... | collective-permute-start | bytes 688136 | tf_op jit(solution)/shard_map/ppermute | solution.py:280

commit v11 on v10

--- a/solution.py
+++ b/solution.py
@@ -232,7 +232,7 @@
     return jnp.where(which == 0, low, high), jnp.where(which == 0, high, low)
 
 
-def gradient_kernel(where_ref, n_ref, own_ref, back_ref, *out_refs):
+def gradient_kernel(where_ref, n_ref, own_ref, back_ref, *out_refs, steps):
     x = where_ref[4]
     columns = n_ref.shape[1] // 4
     taken = out_refs[0].shape[0]
@@ -245,7 +245,7 @@
     target = jnp.where(inside < wrows, target // PADDED * wrows + inside, -1)
     row = lax.broadcasted_iota(jnp.int32, (step, 1), 0)
     cut = jnp.where(row == target, 1.0, 0.0).astype(jnp.bfloat16)
-    for d, out_ref in enumerate(out_refs):
+    for d, out_ref in zip(steps, out_refs):
         at = pl.multiple_of(lax.rem(x + 4 - d, 4) * columns, columns)
         part = lax.dot_general(
             n_ref[:, pl.ds(at, columns)],
@@ -259,13 +259,17 @@
             ).astype(jnp.bfloat16)
 
 
-def gradient(here, n_all, own, back, wrows):
+def gradient(here, n_all, own, back, wrows, steps):
     shape = jax.ShapeDtypeStruct((n_all.shape[1] // 4 // PADDED * wrows, HALF), jnp.bfloat16)
-    return pl.pallas_call(
-        gradient_kernel,
-        out_shape=(shape,) * 4,
+
+    def body(*refs):
+        gradient_kernel(*refs, steps=steps)
+
+    return pl.pallas_call(
+        body,
+        out_shape=(shape,) * len(steps),
         in_specs=[SMEM, VMEM, VMEM, VMEM],
-        out_specs=(VMEM,) * 4,
+        out_specs=(VMEM,) * len(steps),
         compiler_params=pltpu.CompilerParams(vmem_limit_bytes=16 << 20),
         name="gradient",
     )(here, n_all, own, back)
@@ -315,16 +319,22 @@
     n_all = jnp.concatenate([n_keep, n_got, n_across, partner(n_got, "ylo")], axis=0)
     parts = [held[d] for d in RING]
     w_rows = jnp.concatenate([part[2 * BLK :] for part in parts], axis=0)
-    w_all = [w_rows] + [from_next(w_rows, "x", d) for d in range(1, 4)]
+    w_sent = {d: from_next(w_rows, "x", d) for d in (2, 1, 3)}
+    w_all = [w_rows] + [w_sent[d] for d in range(1, 4)]
 
     parts, _ = lax.optimization_barrier((parts, (w_rows, n_across)))
     attention, a_mine, a_other = attend(here, queries, parts, lengths, assignment)
 
     own, send = project(here, n_all, a_mine, partner(a_other, "ylo"), w_all)
-    near, *away = gradient(here, n_all, own, partner(send, "core"), wrows)
+    back = partner(send, "core")
+    far, left = gradient(here, n_all, own, back, wrows, (2, 3))
+    arrived = [from_next(left, "x", 3), from_next(far, "x", 2)]
+    back, _ = lax.optimization_barrier((back, far))
+    near, right = gradient(here, n_all, own, back, wrows, (0, 1))
+    arrived.append(from_next(right, "x", 1))
     near = near.astype(jnp.float32)
-    for d in range(1, 4):
-        near = near + from_next(away[d - 1], "x", d).astype(jnp.float32)
+    for block in arrived:
+        near = near + block.astype(jnp.float32)
     near = near.astype(jnp.bfloat16).reshape(-1, wrows, HALF)
     near = jnp.pad(near, ((0, 0), (0, PADDED - wrows), (0, 0)))
     last = lax.all_to_all(near, ("ylo", *SEQ), split_axis=0, concat_axis=0, tiled=True)

time: 97.6 us -> 96.6 us (0.990); the launches traced: 96.3 us -> 96.3 us
  waiting for transfers between devices: 37.7 us -> 36 us
    ppermute x13, waiting for transfers between devices: 29.4 us -> 27.7 us  [from_next(): lax.ppermute(x, axis, [((i + distance) % size, i) for i in range(size)])]
    pallas_call x1 -> x2, Pallas kernels: 2.26 us -> 3.12 us  [gradient(): pl.pallas_call(body, out_shape=(shape,) * len(steps), in_specs=[SMEM, VME...]
  transfers between devices with their start and end apart: 22 -> 22, of which waited for: 13 -> 13; matrix products, arithmetic and copies ran while one was open for 1% -> 1% of each run, Pallas kernels for 6% -> 8%
where the time goes in v11:
time: 96.6 us; the launch traced here: 96.3 us
  waiting for transfers between devices  36 us (37%)
  starting transfers between devices  24.8 us (26%)
  blocking collectives  20 us (21%)
  Pallas kernels  10.7 us (11%)
  other arithmetic  2.29 us (2%)
  local copies, waits for them, and re-layouts  1.56 us (2%)
    ppermute x13, waiting for transfers between devices, from_next(): lax.ppermute(x, axis, [((i + distance) % size, i) for i in range(size)])  27.7 us
    all_to_all x1, blocking collectives, local(): lax.all_to_all(near, ('ylo', *SEQ), split_axis=0, concat_axis=0, tiled=True)  20 us
    ppermute x13, starting transfers between devices, from_next(): lax.ppermute(x, axis, [((i + distance) % size, i) for i in range(size)])  16.7 us
    ppermute x8, waiting for transfers between devices, partner(): return lax.ppermute(x, axis, [(0, 1), (1, 0)])  6.79 us
    ppermute x8, starting transfers between devices, partner(): return lax.ppermute(x, axis, [(0, 1), (1, 0)])  5.99 us
    pallas_call x1, Pallas kernels, attend(): pl.pallas_call(attend_kernel, out_shape=(jax.ShapeDtypeStruct((rows, COLS...  3.77 us
    pallas_call x2, Pallas kernels, gradient(): pl.pallas_call(body, out_shape=(shape,) * len(steps), in_specs=[SMEM, VME...  3.12 us
    pallas_call x1, Pallas kernels, normalise(): pl.pallas_call(body, out_shape=(shape, shape), in_specs=[SMEM, VMEM], out...  2.32 us
  transfers between devices with their start and end apart: 22, of which 13 were waited for; matrix products, arithmetic and copies ran while one was open for 1% of the time, Pallas kernels for 8%

profile of v11, /device:TPU:32, one launch (start us, length us, event | category | flops | bytes accessed | tf_op | source)
XLA Modules:
  0.0 96.3 jit_solution(682675181012032530)
XLA Ops:
  0.6 0.8 pad_select_fusion.kv_ref
  1.4 3.3 %collective-permute-start = (bf16[128,256]{1,0:T(8,128)(2,1)S(1)}, bf16[128,256]{1,0:T(8,128)(2,1)S(1)}, u32[]{:S(2)}, u32[]{:S(2)}) collective-permute-start(bf16[128,256]{1,0:T(8,128)(2,1)S(1)} %pad_select_fusion.kv_ref), channel_id=1, source_target_pairs={{0,1},{1,0},{2,3},{3,2},{4,5},{5,4},{6,7},{7,6},{8,9},{9,8},{10,11... | collective-permute-start | bytes 196616 | tf_op jit(solution)/shard_map/ppermute | solution.py:279
  4.7 0.7 broadcast_select_fusion
  5.4 0.7 collective-permute-start.1
  6.1 1.8 %collective-permute-start.2 = (bf16[14,256]{1,0:T(8,128)(2,1)S(1)}, bf16[14,256]{1,0:T(8,128)(2,1)S(1)}, u32[]{:S(2)}, u32[]{:S(2)}) collective-permute-start(bf16[14,256]{1,0:T(8,128)(2,1)S(1)} %get-tuple-element.61.refs_0_), channel_id=1, source_target_pairs={{0,1},{1,0},{2,3},{3,2},{4,5},{5,4},{6,7},{7,6},{8,9},{9,8},{10,11... | collective-permute-start | bytes 21512 | tf_op jit(solution)/shard_map/ppermute | solution.py:279
  8.0 2.2 %collective-permute-start.3 = (bf16[14,256]{1,0:T(8,128)(2,1)S(1)}, bf16[14,256]{1,0:T(8,128)(2,1)S(1)}, u32[]{:S(2)}, u32[]{:S(2)}) collective-permute-start(bf16[14,256]{1,0:T(8,128)(2,1)S(1)} %get-tuple-element.60), channel_id=1, source_target_pairs={{0,129},{1,128},{128,1},{129,0},{2,131},{3,130},{130,3},{131,2},{4... | collective-permute-start | bytes 21512 | tf_op jit(solution)/shard_map/ppermute | solution.py:302
  10.1 0.1 stack.23.refs_0_.where_ref
  10.2 0.0 collective-permute-done.1.refs_1_
  10.2 1.0 %collective-permute-done.2.refs_2_ = bf16[14,256]{1,0:T(8,128)(2,1)S(1)} collective-permute-done((bf16[14,256]{1,0:T(8,128)(2,1)S(1)}, bf16[14,256]{1,0:T(8,128)(2,1)S(1)}, u32[]{:S(2)}, u32[]{:S(2)}) %collective-permute-start.2) | collective-permute-done | bytes 7200 | tf_op jit(solution)/shard_map/ppermute | solution.py:279
  11.3 1.5 %collective-permute-done.3.refs_3_ = bf16[14,256]{1,0:T(8,128)(2,1)S(1)} collective-permute-done((bf16[14,256]{1,0:T(8,128)(2,1)S(1)}, bf16[14,256]{1,0:T(8,128)(2,1)S(1)}, u32[]{:S(2)}, u32[]{:S(2)}) %collective-permute-start.3) | collective-permute-done | bytes 7200 | tf_op jit(solution)/shard_map/ppermute | solution.py:302
  12.8 0.0 collective-permute-done.kv_other_ref
  12.8 0.0 copy-start.1
  12.8 0.0 copy-start.2
  12.8 0.0 copy-start.3
  12.9 0.2 collective-permute-start.4
  13.0 1.9 %collective-permute-start.5 = (bf16[320,256]{1,0:T(8,128)(2,1)S(1)}, bf16[320,256]{1,0:T(8,128)(2,1)S(1)}, u32[]{:S(2)}, u32[]{:S(2)}) collective-permute-start(bf16[320,256]{1,0:T(8,128)(2,1)S(1)} %pack.1.refs_0_), channel_id=1, source_target_pairs={{14,0},{0,2},{2,4},{4,6},{6,8},{8,10},{10,12},{12,14},{15,1},{1,3}... | collective-permute-start | bytes 491528 | tf_op jit(solution)/shard_map/ppermute | solution.py:284
  15.0 0.0 copy-start
  15.0 1.2 %copy-done = bf16[128,3584]{1,0:T(8,128)(2,1)S(1)} copy-done((bf16[128,3584]{1,0:T(8,128)(2,1)S(1)}, bf16[128,3584]{1,0:T(8,128)(2,1)}, u32[]{:S(2)}) %copy-start) | copy-done | bytes 917528
  16.1 2.3 %normalise.1 = (bf16[128,2048]{1,0:T(8,128)(2,1)S(1)}, bf16[128,2048]{1,0:T(8,128)(2,1)S(1)}) custom-call(s32[5]{0:T(128)S(1)} %stack.23.refs_0_.where_ref, bf16[128,3584]{1,0:T(8,128)(2,1)S(1)} %copy-done), custom_call_target="tpu_custom_call" | custom-call | tf_op jit(solution)/shard_map/normalise/pallas_call | solution.py:78
  18.5 0.0 collective-permute-done.4.refs_1_
  18.5 3.7 %collective-permute-done.5.refs_2_ = bf16[320,256]{1,0:T(8,128)(2,1)S(1)} collective-permute-done((bf16[320,256]{1,0:T(8,128)(2,1)S(1)}, bf16[320,256]{1,0:T(8,128)(2,1)S(1)}, u32[]{:S(2)}, u32[]{:S(2)}) %collective-permute-start.5) | collective-permute-done | bytes 163872 | tf_op jit(solution)/shard_map/ppermute | solution.py:284
  22.2 3.2 %collective-permute-start.6 = (bf16[320,256]{1,0:T(8,128)(2,1)S(1)}, bf16[320,256]{1,0:T(8,128)(2,1)S(1)}, u32[]{:S(2)}, u32[]{:S(2)}) collective-permute-start(bf16[320,256]{1,0:T(8,128)(2,1)S(1)} %collective-permute-done.4.refs_1_), channel_id=1, source_target_pairs={{2,0},{4,2},{6,4},{8,6},{10,8},{12,10},{14,12},{0,14},{3,1},{5,3},... | collective-permute-start | bytes 491528 | tf_op jit(solution)/shard_map/ppermute | solution.py:284
  25.4 0.0 collective-permute-start.7
  25.4 0.0 collective-permute-start.8
  25.4 0.1 collective-permute-start.12
  25.6 2.7 %collective-permute-done.6.refs_3_ = bf16[320,256]{1,0:T(8,128)(2,1)S(1)} collective-permute-done((bf16[320,256]{1,0:T(8,128)(2,1)S(1)}, bf16[320,256]{1,0:T(8,128)(2,1)S(1)}, u32[]{:S(2)}, u32[]{:S(2)}) %collective-permute-start.6) | collective-permute-done | bytes 163872 | tf_op jit(solution)/shard_map/ppermute | solution.py:284
  28.3 2.5 %collective-permute-done.7.refs_4_ = bf16[320,256]{1,0:T(8,128)(2,1)S(1)} collective-permute-done((bf16[320,256]{1,0:T(8,128)(2,1)S(1)}, bf16[320,256]{1,0:T(8,128)(2,1)S(1)}, u32[]{:S(2)}, u32[]{:S(2)}) %collective-permute-start.7) | collective-permute-done | bytes 163872 | tf_op jit(solution)/shard_map/ppermute | solution.py:284
  30.7 0.0 collective-permute-done.8
  30.8 1.5 %collective-permute-start.9 = (bf16[320,256]{1,0:T(8,128)(2,1)S(1)}, bf16[320,256]{1,0:T(8,128)(2,1)S(1)}, u32[]{:S(2)}, u32[]{:S(2)}) collective-permute-start(bf16[320,256]{1,0:T(8,128)(2,1)S(1)} %collective-permute-done.6.refs_3_), channel_id=1, source_target_pairs={{2,0},{4,2},{6,4},{8,6},{10,8},{12,10},{14,12},{0,14},{3,1},{5,3},... | collective-permute-start | bytes 491528 | tf_op jit(solution)/shard_map/ppermute | solution.py:284
  32.3 0.5 collective-permute-start.10
  32.8 0.0 collective-permute-start.13
  32.8 4.8 %collective-permute-done.9.refs_5_ = bf16[320,256]{1,0:T(8,128)(2,1)S(1)} collective-permute-done((bf16[320,256]{1,0:T(8,128)(2,1)S(1)}, bf16[320,256]{1,0:T(8,128)(2,1)S(1)}, u32[]{:S(2)}, u32[]{:S(2)}) %collective-permute-start.9) | collective-permute-done | bytes 163872 | tf_op jit(solution)/shard_map/ppermute | solution.py:284
  37.6 1.1 %collective-permute-start.11 = (bf16[320,256]{1,0:T(8,128)(2,1)S(1)}, bf16[320,256]{1,0:T(8,128)(2,1)S(1)}, u32[]{:S(2)}, u32[]{:S(2)}) collective-permute-start(bf16[320,256]{1,0:T(8,128)(2,1)S(1)} %collective-permute-done.9.refs_5_), channel_id=1, source_target_pairs={{2,0},{4,2},{6,4},{8,6},{10,8},{12,10},{14,12},{0,14},{3,1},{5,3},... | collective-permute-start | bytes 491528 | tf_op jit(solution)/shard_map/ppermute | solution.py:284
  38.7 0.0 collective-permute-done.10.refs_6_
  38.7 4.2 %collective-permute-done.11.refs_7_ = bf16[320,256]{1,0:T(8,128)(2,1)S(1)} collective-permute-done((bf16[320,256]{1,0:T(8,128)(2,1)S(1)}, bf16[320,256]{1,0:T(8,128)(2,1)S(1)}, u32[]{:S(2)}, u32[]{:S(2)}) %collective-permute-start.11) | collective-permute-done | bytes 163872 | tf_op jit(solution)/shard_map/ppermute | solution.py:284
  42.9 2.8 %collective-permute-start.15 = (bf16[512,256]{1,0:T(8,128)(2,1)S(1)}, bf16[512,256]{1,0:T(8,128)(2,1)S(1)}, u32[]{:S(2)}, u32[]{:S(2)}) collective-permute-start(bf16[512,256]{1,0:T(8,128)(2,1)S(1)} %slice_dynamic-update-slice_fusion.refs_0_), channel_id=1, source_target_pairs={{32,0},{64,32},{96,64},{0,96},{33,1},{65,33},{97,65},{1,97},{34,2}... | collective-permute-start | bytes 786440 | tf_op jit(solution)/shard_map/ppermute | solution.py:284
  45.7 0.8 collective-permute-start.16
  46.5 0.9 collective-permute-start.17
  47.4 0.0 collective-permute-done.12
  47.4 0.0 copy-done.1
  47.4 0.0 copy-done.2
  47.4 0.0 copy-done.3
  47.4 3.8 %attend.1 = (bf16[128,512]{1,0:T(8,128)(2,1)}, bf16[128,256]{1,0:T(8,128)(2,1)S(1)}, bf16[128,256]{1,0:T(8,128)(2,1)S(1)}) custom-call(s32[5]{0:T(128)S(1)} %stack.23.refs_0_.where_ref, s32[1,16]{1,0:T(1,128)S(1)} %copy-done.2, s32[1,4]{1,0:T(1,128)S(1)} %copy-done.3, bf16[128,512]{1,0:T(8,128)(2,1)S(1)} %copy-done.1, bf16[320,256]{1,0:T(8,128)(2,1)S(1)} %pack.1.refs_0_, ...), custom_call_target="tpu_custom_call" | custom-call | tf_op jit(solution)/shard_map/attend/pallas_call | solution.py:173
  51.2 0.0 collective-permute-start.14
  51.2 0.3 collective-permute-done.13
  51.5 3.9 %collective-permute-done.14.got_ref = bf16[128,256]{1,0:T(8,128)(2,1)S(1)} collective-permute-done((bf16[128,256]{1,0:T(8,128)(2,1)S(1)}, bf16[128,256]{1,0:T(8,128)(2,1)S(1)}, u32[]{:S(2)}, u32[]{:S(2)}) %collective-permute-start.14) | collective-permute-done | bytes 65568 | tf_op jit(solution)/shard_map/ppermute | solution.py:279
  55.5 0.0 collective-permute-done.15.refs_1_
  55.5 0.0 collective-permute-done.16.refs_2_
  55.5 0.9 collective-permute-done.17.refs_3_
  56.4 1.5 %project.1 = (f32[512,256]{1,0:T(8,128)S(1)}, bf16[512,256]{1,0:T(8,128)(2,1)S(1)}) custom-call(s32[5]{0:T(128)S(1)} %stack.23.refs_0_.where_ref, bf16[512,2048]{1,0:T(8,128)(2,1)S(1)} %constant_dynamic-update-slice_fusion.n_ref.refs_1_, bf16[128,256]{1,0:T(8,128)(2,1)S(1)} %get-tuple-element.49.mine_ref, ...), custom_call_target="tpu_custom_call" | custom-call | tf_op jit(solution)/shard_map/project/pallas_call | solution.py:215
  57.8 0.1 collective-permute-start.18
  57.9 1.5 %collective-permute-done.18.refs_3_ = bf16[512,256]{1,0:T(8,128)(2,1)S(1)} collective-permute-done((bf16[512,256]{1,0:T(8,128)(2,1)S(1)}, bf16[512,256]{1,0:T(8,128)(2,1)S(1)}, u32[]{:S(2)}, u32[]{:S(2)}) %collective-permute-start.18) | collective-permute-done | bytes 262176 | tf_op jit(solution)/shard_map/ppermute | solution.py:279
  59.5 1.6 %gradient.2 = (bf16[448,256]{1,0:T(8,128)(2,1)S(1)}, bf16[448,256]{1,0:T(8,128)(2,1)S(1)}) custom-call(s32[5]{0:T(128)S(1)} %stack.23.refs_0_.where_ref, bf16[512,2048]{1,0:T(8,128)(2,1)S(1)} %constant_dynamic-update-slice_fusion.n_ref.refs_1_, f32[512,256]{1,0:T(8,128)S(1)} %get-tuple-element.51.refs_2_, bf16[512,256]{1,0:T(8,128)(2,1)S(1)} %collective-permute-done.18.refs_3_), custom_call_target="tpu_custom_call" | custom-call | tf_op jit(solution)/shard_map/gradient/pallas_call | solution.py:268
  61.0 1.1 %collective-permute-start.20 = (bf16[448,256]{1,0:T(8,128)(2,1)S(1)}, bf16[448,256]{1,0:T(8,128)(2,1)S(1)}, u32[]{:S(2)}, u32[]{:S(2)}) collective-permute-start(bf16[448,256]{1,0:T(8,128)(2,1)S(1)} %get-tuple-element.53), channel_id=1, source_target_pairs={{64,0},{96,32},{0,64},{32,96},{65,1},{97,33},{1,65},{33,97},{66,2}... | collective-permute-start | bytes 688136 | tf_op jit(solution)/shard_map/ppermute | solution.py:284
  62.1 1.6 %gradient.3 = (bf16[448,256]{1,0:T(8,128)(2,1)S(1)}, bf16[448,256]{1,0:T(8,128)(2,1)S(1)}) custom-call(s32[5]{0:T(128)S(1)} %stack.23.refs_0_.where_ref, bf16[512,2048]{1,0:T(8,128)(2,1)S(1)} %constant_dynamic-update-slice_fusion.n_ref.refs_1_, f32[512,256]{1,0:T(8,128)S(1)} %get-tuple-element.51.refs_2_, bf16[512,256]{1,0:T(8,128)(2,1)S(1)} %collective-permute-done.18.refs_3_), custom_call_target="tpu_custom_call" | custom-call | tf_op jit(solution)/shard_map/gradient/pallas_call | solution.py:268
  63.7 2.7 %collective-permute-start.21 = (bf16[448,256]{1,0:T(8,128)(2,1)S(1)}, bf16[448,256]{1,0:T(8,128)(2,1)S(1)}, u32[]{:S(2)}, u32[]{:S(2)}) collective-permute-start(bf16[448,256]{1,0:T(8,128)(2,1)S(1)} %get-tuple-element.57), channel_id=1, source_target_pairs={{32,0},{64,32},{96,64},{0,96},{33,1},{65,33},{97,65},{1,97},{34,2}... | collective-permute-start | bytes 688136 | tf_op jit(solution)/shard_map/ppermute | solution.py:284
  66.4 0.0 collective-permute-start.19
  66.4 7.6 %collective-permute-done.21 = bf16[448,256]{1,0:T(8,128)(2,1)S(1)} collective-permute-done((bf16[448,256]{1,0:T(8,128)(2,1)S(1)}, bf16[448,256]{1,0:T(8,128)(2,1)S(1)}, u32[]{:S(2)}, u32[]{:S(2)}) %collective-permute-start.21) | collective-permute-done | bytes 229408 | tf_op jit(solution)/shard_map/ppermute | solution.py:284
  74.0 0.0 collective-permute-done.20
  74.0 1.3 %collective-permute-done.19 = bf16[448,256]{1,0:T(8,128)(2,1)S(1)} collective-permute-done((bf16[448,256]{1,0:T(8,128)(2,1)S(1)}, bf16[448,256]{1,0:T(8,128)(2,1)S(1)}, u32[]{:S(2)}, u32[]{:S(2)}) %collective-permute-start.19) | collective-permute-done | bytes 229408 | tf_op jit(solution)/shard_map/ppermute | solution.py:284
  75.3 0.1 add_convert_fusion
  75.5 0.1 reshape.10
  75.6 20.0 %all_to_all.5 = bf16[32,16,256]{2,1,0:T(8,128)(2,1)S(1)} all-to-all(bf16[32,16,256]{2,1,0:T(8,128)(2,1)S(1)} %pad.14), channel_id=1, replica_groups=mesh['ylo'=2,'x'=4,'core'=2,'z'=8,'yhi'=2] {'ylo','z','yhi'}, dimensions={0} | all-to-all | bytes 524288 | tf_op jit(solution)/shard_map/all_to_all | solution.py:340
  95.7 0.6 pad_maximum_fusion
  (17 shorter events, 0.3 us)
Async XLA Ops:
  1.4 11.4 %collective-permute-start = (bf16[128,256]{1,0:T(8,128)(2,1)S(1)}, bf16[128,256]{1,0:T(8,128)(2,1)S(1)}, u32[]{:S(2)}, u32[]{:S(2)}) collective-permute-start(bf16[128,256]{1,0:T(8,128)(2,1)S(1)} %pad_select_fusion.kv_ref), channel_id=1, source_target_pairs={{0,1},{1,0},{2,3},{3,2},{4,5},{5,4},{6,7},{7,6},{8,9},{9,8},{10,11... | collective-permute-start | bytes 196616 | tf_op jit(solution)/shard_map/ppermute | solution.py:279
  5.4 4.8 %collective-permute-start.1 = (bf16[14,256]{1,0:T(8,128)(2,1)S(1)}, bf16[14,256]{1,0:T(8,128)(2,1)S(1)}, u32[]{:S(2)}, u32[]{:S(2)}) collective-permute-start(bf16[14,256]{1,0:T(8,128)(2,1)S(1)} %get-tuple-element.60), channel_id=1, source_target_pairs={{0,128},{128,0},{1,129},{129,1},{2,130},{130,2},{3,131},{131,3},{4... | collective-permute-start | bytes 21512 | tf_op jit(solution)/shard_map/ppermute | solution.py:279
  6.1 5.2 %collective-permute-start.2 = (bf16[14,256]{1,0:T(8,128)(2,1)S(1)}, bf16[14,256]{1,0:T(8,128)(2,1)S(1)}, u32[]{:S(2)}, u32[]{:S(2)}) collective-permute-start(bf16[14,256]{1,0:T(8,128)(2,1)S(1)} %get-tuple-element.61.refs_0_), channel_id=1, source_target_pairs={{0,1},{1,0},{2,3},{3,2},{4,5},{5,4},{6,7},{7,6},{8,9},{9,8},{10,11... | collective-permute-start | bytes 21512 | tf_op jit(solution)/shard_map/ppermute | solution.py:279
  8.0 4.9 %collective-permute-start.3 = (bf16[14,256]{1,0:T(8,128)(2,1)S(1)}, bf16[14,256]{1,0:T(8,128)(2,1)S(1)}, u32[]{:S(2)}, u32[]{:S(2)}) collective-permute-start(bf16[14,256]{1,0:T(8,128)(2,1)S(1)} %get-tuple-element.60), channel_id=1, source_target_pairs={{0,129},{1,128},{128,1},{129,0},{2,131},{3,130},{130,3},{131,2},{4... | collective-permute-start | bytes 21512 | tf_op jit(solution)/shard_map/ppermute | solution.py:302
  12.8 34.6 %copy-start.1 = (bf16[128,512]{1,0:T(8,128)(2,1)S(1)}, bf16[128,512]{1,0:T(8,128)(2,1)}, u32[]{:S(2)}) copy-start(bf16[128,512]{1,0:T(8,128)(2,1)} %q_ref.1) | copy-start | bytes 393220
  12.8 34.6 %copy-start.2 = (s32[1,16]{1,0:T(1,128)S(1)}, s32[1,16]{1,0:T(1,128)}, u32[]{:S(2)}) copy-start(s32[1,16]{1,0:T(1,128)} %assign_ref.1) | copy-start | bytes 196
  12.8 34.6 %copy-start.3 = (s32[1,4]{1,0:T(1,128)S(1)}, s32[1,4]{1,0:T(1,128)}, u32[]{:S(2)}) copy-start(s32[1,4]{1,0:T(1,128)} %length_ref.1) | copy-start | bytes 52
  12.9 5.6 %collective-permute-start.4 = (bf16[320,256]{1,0:T(8,128)(2,1)S(1)}, bf16[320,256]{1,0:T(8,128)(2,1)S(1)}, u32[]{:S(2)}, u32[]{:S(2)}) collective-permute-start(bf16[320,256]{1,0:T(8,128)(2,1)S(1)} %pack.1.refs_0_), channel_id=1, source_target_pairs={{2,0},{4,2},{6,4},{8,6},{10,8},{12,10},{14,12},{0,14},{3,1},{5,3},... | collective-permute-start | bytes 491528 | tf_op jit(solution)/shard_map/ppermute | solution.py:284
  13.0 9.2 %collective-permute-start.5 = (bf16[320,256]{1,0:T(8,128)(2,1)S(1)}, bf16[320,256]{1,0:T(8,128)(2,1)S(1)}, u32[]{:S(2)}, u32[]{:S(2)}) collective-permute-start(bf16[320,256]{1,0:T(8,128)(2,1)S(1)} %pack.1.refs_0_), channel_id=1, source_target_pairs={{14,0},{0,2},{2,4},{4,6},{6,8},{8,10},{10,12},{12,14},{15,1},{1,3}... | collective-permute-start | bytes 491528 | tf_op jit(solution)/shard_map/ppermute | solution.py:284
  15.0 1.2 %copy-start = (bf16[128,3584]{1,0:T(8,128)(2,1)S(1)}, bf16[128,3584]{1,0:T(8,128)(2,1)}, u32[]{:S(2)}) copy-start(bf16[128,3584]{1,0:T(8,128)(2,1)} %refs_1_) | copy-start | bytes 2752516
  22.2 6.1 %collective-permute-start.6 = (bf16[320,256]{1,0:T(8,128)(2,1)S(1)}, bf16[320,256]{1,0:T(8,128)(2,1)S(1)}, u32[]{:S(2)}, u32[]{:S(2)}) collective-permute-start(bf16[320,256]{1,0:T(8,128)(2,1)S(1)} %collective-permute-done.4.refs_1_), channel_id=1, source_target_pairs={{2,0},{4,2},{6,4},{8,6},{10,8},{12,10},{14,12},{0,14},{3,1},{5,3},... | collective-permute-start | bytes 491528 | tf_op jit(solution)/shard_map/ppermute | solution.py:284
  25.4 5.3 %collective-permute-start.7 = (bf16[320,256]{1,0:T(8,128)(2,1)S(1)}, bf16[320,256]{1,0:T(8,128)(2,1)S(1)}, u32[]{:S(2)}, u32[]{:S(2)}) collective-permute-start(bf16[320,256]{1,0:T(8,128)(2,1)S(1)} %collective-permute-done.5.refs_2_), channel_id=1, source_target_pairs={{14,0},{0,2},{2,4},{4,6},{6,8},{8,10},{10,12},{12,14},{15,1},{1,3}... | collective-permute-start | bytes 491528 | tf_op jit(solution)/shard_map/ppermute | solution.py:284
  25.4 5.3 %collective-permute-start.8 = (bf16[128,2048]{1,0:T(8,128)(2,1)S(1)}, bf16[128,2048]{1,0:T(8,128)(2,1)S(1)}, u32[]{:S(2)}, u32[]{:S(2)}) collective-permute-start(bf16[128,2048]{1,0:T(8,128)(2,1)S(1)} %get-tuple-element.35), channel_id=1, source_target_pairs={{0,16},{16,0},{1,17},{17,1},{2,18},{18,2},{3,19},{19,3},{4,20},{20... | collective-permute-start | bytes 1572872 | tf_op jit(solution)/shard_map/ppermute | solution.py:279
  25.4 21.9 %collective-permute-start.12 = (bf16[128,2048]{1,0:T(8,128)(2,1)S(1)}, bf16[128,2048]{1,0:T(8,128)(2,1)S(1)}, u32[]{:S(2)}, u32[]{:S(2)}) collective-permute-start(bf16[128,2048]{1,0:T(8,128)(2,1)S(1)} %get-tuple-element.38), channel_id=1, source_target_pairs={{0,128},{128,0},{1,129},{129,1},{2,130},{130,2},{3,131},{131,3},{4... | collective-permute-start | bytes 1572872 | tf_op jit(solution)/shard_map/ppermute | solution.py:279
  30.8 6.9 %collective-permute-start.9 = (bf16[320,256]{1,0:T(8,128)(2,1)S(1)}, bf16[320,256]{1,0:T(8,128)(2,1)S(1)}, u32[]{:S(2)}, u32[]{:S(2)}) collective-permute-start(bf16[320,256]{1,0:T(8,128)(2,1)S(1)} %collective-permute-done.6.refs_3_), channel_id=1, source_target_pairs={{2,0},{4,2},{6,4},{8,6},{10,8},{12,10},{14,12},{0,14},{3,1},{5,3},... | collective-permute-start | bytes 491528 | tf_op jit(solution)/shard_map/ppermute | solution.py:284
  32.3 6.4 %collective-permute-start.10 = (bf16[320,256]{1,0:T(8,128)(2,1)S(1)}, bf16[320,256]{1,0:T(8,128)(2,1)S(1)}, u32[]{:S(2)}, u32[]{:S(2)}) collective-permute-start(bf16[320,256]{1,0:T(8,128)(2,1)S(1)} %collective-permute-done.7.refs_4_), channel_id=1, source_target_pairs={{14,0},{0,2},{2,4},{4,6},{6,8},{8,10},{10,12},{12,14},{15,1},{1,3}... | collective-permute-start | bytes 491528 | tf_op jit(solution)/shard_map/ppermute | solution.py:284
  32.8 18.7 %collective-permute-start.13 = (bf16[128,2048]{1,0:T(8,128)(2,1)S(1)}, bf16[128,2048]{1,0:T(8,128)(2,1)S(1)}, u32[]{:S(2)}, u32[]{:S(2)}) collective-permute-start(bf16[128,2048]{1,0:T(8,128)(2,1)S(1)} %collective-permute-done.8), channel_id=1, source_target_pairs={{0,128},{128,0},{1,129},{129,1},{2,130},{130,2},{3,131},{131,3},{4... | collective-permute-start | bytes 1572872 | tf_op jit(solution)/shard_map/ppermute | solution.py:279
  37.6 5.3 %collective-permute-start.11 = (bf16[320,256]{1,0:T(8,128)(2,1)S(1)}, bf16[320,256]{1,0:T(8,128)(2,1)S(1)}, u32[]{:S(2)}, u32[]{:S(2)}) collective-permute-start(bf16[320,256]{1,0:T(8,128)(2,1)S(1)} %collective-permute-done.9.refs_5_), channel_id=1, source_target_pairs={{2,0},{4,2},{6,4},{8,6},{10,8},{12,10},{14,12},{0,14},{3,1},{5,3},... | collective-permute-start | bytes 491528 | tf_op jit(solution)/shard_map/ppermute | solution.py:284
  42.9 12.6 %collective-permute-start.15 = (bf16[512,256]{1,0:T(8,128)(2,1)S(1)}, bf16[512,256]{1,0:T(8,128)(2,1)S(1)}, u32[]{:S(2)}, u32[]{:S(2)}) collective-permute-start(bf16[512,256]{1,0:T(8,128)(2,1)S(1)} %slice_dynamic-update-slice_fusion.refs_0_), channel_id=1, source_target_pairs={{32,0},{64,32},{96,64},{0,96},{33,1},{65,33},{97,65},{1,97},{34,2}... | collective-permute-start | bytes 786440 | tf_op jit(solution)/shard_map/ppermute | solution.py:284
  45.7 9.8 %collective-permute-start.16 = (bf16[512,256]{1,0:T(8,128)(2,1)S(1)}, bf16[512,256]{1,0:T(8,128)(2,1)S(1)}, u32[]{:S(2)}, u32[]{:S(2)}) collective-permute-start(bf16[512,256]{1,0:T(8,128)(2,1)S(1)} %slice_dynamic-update-slice_fusion.refs_0_), channel_id=1, source_target_pairs={{64,0},{96,32},{0,64},{32,96},{65,1},{97,33},{1,65},{33,97},{66,2}... | collective-permute-start | bytes 786440 | tf_op jit(solution)/shard_map/ppermute | solution.py:284
  46.5 9.9 %collective-permute-start.17 = (bf16[512,256]{1,0:T(8,128)(2,1)S(1)}, bf16[512,256]{1,0:T(8,128)(2,1)S(1)}, u32[]{:S(2)}, u32[]{:S(2)}) collective-permute-start(bf16[512,256]{1,0:T(8,128)(2,1)S(1)} %slice_dynamic-update-slice_fusion.refs_0_), channel_id=1, source_target_pairs={{96,0},{0,32},{32,64},{64,96},{97,1},{1,33},{33,65},{65,97},{98,2}... | collective-permute-start | bytes 786440 | tf_op jit(solution)/shard_map/ppermute | solution.py:284
  51.2 4.3 %collective-permute-start.14 = (bf16[128,256]{1,0:T(8,128)(2,1)S(1)}, bf16[128,256]{1,0:T(8,128)(2,1)S(1)}, u32[]{:S(2)}, u32[]{:S(2)}) collective-permute-start(bf16[128,256]{1,0:T(8,128)(2,1)S(1)} %get-tuple-element.50), channel_id=1, source_target_pairs={{0,128},{128,0},{1,129},{129,1},{2,130},{130,2},{3,131},{131,3},{4... | collective-permute-start | bytes 196616 | tf_op jit(solution)/shard_map/ppermute | solution.py:279
  57.8 1.6 %collective-permute-start.18 = (bf16[512,256]{1,0:T(8,128)(2,1)S(1)}, bf16[512,256]{1,0:T(8,128)(2,1)S(1)}, u32[]{:S(2)}, u32[]{:S(2)}) collective-permute-start(bf16[512,256]{1,0:T(8,128)(2,1)S(1)} %get-tuple-element.52), channel_id=1, source_target_pairs={{0,16},{16,0},{1,17},{17,1},{2,18},{18,2},{3,19},{19,3},{4,20},{20... | collective-permute-start | bytes 786440 | tf_op jit(solution)/shard_map/ppermute | solution.py:279
  61.0 13.0 %collective-permute-start.20 = (bf16[448,256]{1,0:T(8,128)(2,1)S(1)}, bf16[448,256]{1,0:T(8,128)(2,1)S(1)}, u32[]{:S(2)}, u32[]{:S(2)}) collective-permute-start(bf16[448,256]{1,0:T(8,128)(2,1)S(1)} %get-tuple-element.53), channel_id=1, source_target_pairs={{64,0},{96,32},{0,64},{32,96},{65,1},{97,33},{1,65},{33,97},{66,2}... | collective-permute-start | bytes 688136 | tf_op jit(solution)/shard_map/ppermute | solution.py:284
  63.7 10.3 %collective-permute-start.21 = (bf16[448,256]{1,0:T(8,128)(2,1)S(1)}, bf16[448,256]{1,0:T(8,128)(2,1)S(1)}, u32[]{:S(2)}, u32[]{:S(2)}) collective-permute-start(bf16[448,256]{1,0:T(8,128)(2,1)S(1)} %get-tuple-element.57), channel_id=1, source_target_pairs={{32,0},{64,32},{96,64},{0,96},{33,1},{65,33},{97,65},{1,97},{34,2}... | collective-permute-start | bytes 688136 | tf_op jit(solution)/shard_map/ppermute | solution.py:284
  66.4 9.0 %collective-permute-start.19 = (bf16[448,256]{1,0:T(8,128)(2,1)S(1)}, bf16[448,256]{1,0:T(8,128)(2,1)S(1)}, u32[]{:S(2)}, u32[]{:S(2)}) collective-permute-start(bf16[448,256]{1,0:T(8,128)(2,1)S(1)} %get-tuple-element.56), channel_id=1, source_target_pairs={{96,0},{0,32},{32,64},{64,96},{97,1},{1,33},{33,65},{65,97},{98,2}... | collective-permute-start | bytes 688136 | tf_op jit(solution)/shard_map/ppermute | solution.py:284

commit v12 on v11

--- a/solution.py
+++ b/solution.py
@@ -314,8 +314,8 @@
         held[d] = from_next(held[d - 1], "z", 1)
         if d < 4:
             held[-d] = from_next(held[1 - d], "z", -1)
-        if d == 2:
-            held[2], held[-2], n_got = lax.optimization_barrier((held[2], held[-2], n_got))
+        if d == 3:
+            held[3], n_got = lax.optimization_barrier((held[3], n_got))
     n_all = jnp.concatenate([n_keep, n_got, n_across, partner(n_got, "ylo")], axis=0)
     parts = [held[d] for d in RING]
     w_rows = jnp.concatenate([part[2 * BLK :] for part in parts], axis=0)

time: 96.6 us -> 95.7 us (level)
  waiting for transfers between devices: 36 us -> 27.2 us
  starting transfers between devices: 24.8 us -> 30.7 us
  blocking collectives: 20 us -> 21.6 us
    ppermute x13, waiting for transfers between devices: 27.7 us -> 20.9 us  [from_next(): lax.ppermute(x, axis, [((i + distance) % size, i) for i in range(size)])]
    ppermute x8, starting transfers between devices: 5.99 us -> 9.95 us  [partner(): return lax.ppermute(x, axis, [(0, 1), (1, 0)])]
    ppermute x8, waiting for transfers between devices: 6.79 us -> 4.77 us  [partner(): return lax.ppermute(x, axis, [(0, 1), (1, 0)])]
    ppermute x13, starting transfers between devices: 16.7 us -> 18.6 us  [from_next(): lax.ppermute(x, axis, [((i + distance) % size, i) for i in range(size)])]
    all_to_all x1, blocking collectives: 20 us -> 21.6 us  [local(): lax.all_to_all(near, ('ylo', *SEQ), split_axis=0, concat_axis=0, tiled=True)]
  transfers between devices with their start and end apart: 22 -> 22, of which waited for: 13 -> 12; matrix products, arithmetic and copies ran while one was open for 1% -> 1% of each run, Pallas kernels for 8% -> 8%
where the time goes in v12:
time: 95.7 us; the launch traced here: 95 us
  starting transfers between devices  30.7 us (32%)
  waiting for transfers between devices  27.2 us (28%)
  blocking collectives  21.6 us (23%)
  Pallas kernels  10.7 us (11%)
  other arithmetic  2.29 us (2%)
  local copies, waits for them, and re-layouts  1.56 us (2%)
    all_to_all x1, blocking collectives, local(): lax.all_to_all(near, ('ylo', *SEQ), split_axis=0, concat_axis=0, tiled=True)  21.6 us
    ppermute x13, waiting for transfers between devices, from_next(): lax.ppermute(x, axis, [((i + distance) % size, i) for i in range(size)])  20.9 us
    ppermute x13, starting transfers between devices, from_next(): lax.ppermute(x, axis, [((i + distance) % size, i) for i in range(size)])  18.6 us
    ppermute x8, starting transfers between devices, partner(): return lax.ppermute(x, axis, [(0, 1), (1, 0)])  9.95 us
    ppermute x8, waiting for transfers between devices, partner(): return lax.ppermute(x, axis, [(0, 1), (1, 0)])  4.77 us
    pallas_call x1, Pallas kernels, attend(): pl.pallas_call(attend_kernel, out_shape=(jax.ShapeDtypeStruct((rows, COLS...  3.77 us
    pallas_call x2, Pallas kernels, gradient(): pl.pallas_call(body, out_shape=(shape,) * len(steps), in_specs=[SMEM, VME...  3.12 us
    pallas_call x1, Pallas kernels, normalise(): pl.pallas_call(body, out_shape=(shape, shape), in_specs=[SMEM, VMEM], out...  2.32 us
  transfers between devices with their start and end apart: 22, of which 12 were waited for; matrix products, arithmetic and copies ran while one was open for 1% of the time, Pallas kernels for 8%

profile of v12, /device:TPU:32, one launch (start us, length us, event | category | flops | bytes accessed | tf_op | source)
XLA Modules:
  0.0 95.0 jit_solution(17154619796517139489)
XLA Ops:
  0.6 0.8 pad_select_fusion.kv_ref
  1.4 3.3 %collective-permute-start = (bf16[128,256]{1,0:T(8,128)(2,1)S(1)}, bf16[128,256]{1,0:T(8,128)(2,1)S(1)}, u32[]{:S(2)}, u32[]{:S(2)}) collective-permute-start(bf16[128,256]{1,0:T(8,128)(2,1)S(1)} %pad_select_fusion.kv_ref), channel_id=1, source_target_pairs={{0,1},{1,0},{2,3},{3,2},{4,5},{5,4},{6,7},{7,6},{8,9},{9,8},{10,11... | collective-permute-start | bytes 196616 | tf_op jit(solution)/shard_map/ppermute | solution.py:279
  4.7 0.7 broadcast_select_fusion
  5.4 0.7 collective-permute-start.1
  6.1 1.8 %collective-permute-start.2 = (bf16[14,256]{1,0:T(8,128)(2,1)S(1)}, bf16[14,256]{1,0:T(8,128)(2,1)S(1)}, u32[]{:S(2)}, u32[]{:S(2)}) collective-permute-start(bf16[14,256]{1,0:T(8,128)(2,1)S(1)} %get-tuple-element.59.refs_0_), channel_id=1, source_target_pairs={{0,1},{1,0},{2,3},{3,2},{4,5},{5,4},{6,7},{7,6},{8,9},{9,8},{10,11... | collective-permute-start | bytes 21512 | tf_op jit(solution)/shard_map/ppermute | solution.py:279
  8.0 2.2 %collective-permute-start.3 = (bf16[14,256]{1,0:T(8,128)(2,1)S(1)}, bf16[14,256]{1,0:T(8,128)(2,1)S(1)}, u32[]{:S(2)}, u32[]{:S(2)}) collective-permute-start(bf16[14,256]{1,0:T(8,128)(2,1)S(1)} %get-tuple-element.58), channel_id=1, source_target_pairs={{0,129},{1,128},{128,1},{129,0},{2,131},{3,130},{130,3},{131,2},{4... | collective-permute-start | bytes 21512 | tf_op jit(solution)/shard_map/ppermute | solution.py:302
  10.1 0.1 stack.23.refs_0_.where_ref
  10.2 0.0 collective-permute-done.1.refs_1_
  10.2 1.0 %collective-permute-done.2.refs_2_ = bf16[14,256]{1,0:T(8,128)(2,1)S(1)} collective-permute-done((bf16[14,256]{1,0:T(8,128)(2,1)S(1)}, bf16[14,256]{1,0:T(8,128)(2,1)S(1)}, u32[]{:S(2)}, u32[]{:S(2)}) %collective-permute-start.2) | collective-permute-done | bytes 7200 | tf_op jit(solution)/shard_map/ppermute | solution.py:279
  11.3 1.5 %collective-permute-done.3.refs_3_ = bf16[14,256]{1,0:T(8,128)(2,1)S(1)} collective-permute-done((bf16[14,256]{1,0:T(8,128)(2,1)S(1)}, bf16[14,256]{1,0:T(8,128)(2,1)S(1)}, u32[]{:S(2)}, u32[]{:S(2)}) %collective-permute-start.3) | collective-permute-done | bytes 7200 | tf_op jit(solution)/shard_map/ppermute | solution.py:302
  12.8 0.0 collective-permute-done.kv_other_ref
  12.8 0.0 copy-start.1
  12.8 0.0 copy-start.2
  12.8 0.0 copy-start.3
  12.9 0.2 collective-permute-start.4
  13.0 1.9 %collective-permute-start.5 = (bf16[320,256]{1,0:T(8,128)(2,1)S(1)}, bf16[320,256]{1,0:T(8,128)(2,1)S(1)}, u32[]{:S(2)}, u32[]{:S(2)}) collective-permute-start(bf16[320,256]{1,0:T(8,128)(2,1)S(1)} %pack.1.refs_0_), channel_id=1, source_target_pairs={{14,0},{0,2},{2,4},{4,6},{6,8},{8,10},{10,12},{12,14},{15,1},{1,3}... | collective-permute-start | bytes 491528 | tf_op jit(solution)/shard_map/ppermute | solution.py:284
  15.0 0.0 copy-start
  15.0 1.2 %copy-done = bf16[128,3584]{1,0:T(8,128)(2,1)S(1)} copy-done((bf16[128,3584]{1,0:T(8,128)(2,1)S(1)}, bf16[128,3584]{1,0:T(8,128)(2,1)}, u32[]{:S(2)}) %copy-start) | copy-done | bytes 917528
  16.1 2.3 %normalise.1 = (bf16[128,2048]{1,0:T(8,128)(2,1)S(1)}, bf16[128,2048]{1,0:T(8,128)(2,1)S(1)}) custom-call(s32[5]{0:T(128)S(1)} %stack.23.refs_0_.where_ref, bf16[128,3584]{1,0:T(8,128)(2,1)S(1)} %copy-done), custom_call_target="tpu_custom_call" | custom-call | tf_op jit(solution)/shard_map/normalise/pallas_call | solution.py:78
  18.5 0.0 collective-permute-done.4.refs_1_
  18.5 3.7 %collective-permute-done.5.refs_2_ = bf16[320,256]{1,0:T(8,128)(2,1)S(1)} collective-permute-done((bf16[320,256]{1,0:T(8,128)(2,1)S(1)}, bf16[320,256]{1,0:T(8,128)(2,1)S(1)}, u32[]{:S(2)}, u32[]{:S(2)}) %collective-permute-start.5) | collective-permute-done | bytes 163872 | tf_op jit(solution)/shard_map/ppermute | solution.py:284
  22.2 0.0 collective-permute-start.12
  22.2 3.3 %collective-permute-start.6 = (bf16[320,256]{1,0:T(8,128)(2,1)S(1)}, bf16[320,256]{1,0:T(8,128)(2,1)S(1)}, u32[]{:S(2)}, u32[]{:S(2)}) collective-permute-start(bf16[320,256]{1,0:T(8,128)(2,1)S(1)} %collective-permute-done.4.refs_1_), channel_id=1, source_target_pairs={{2,0},{4,2},{6,4},{8,6},{10,8},{12,10},{14,12},{0,14},{3,1},{5,3},... | collective-permute-start | bytes 491528 | tf_op jit(solution)/shard_map/ppermute | solution.py:284
  25.6 0.0 collective-permute-start.7
  25.6 0.0 collective-permute-start.9
  25.6 2.8 %collective-permute-done.6.refs_3_ = bf16[320,256]{1,0:T(8,128)(2,1)S(1)} collective-permute-done((bf16[320,256]{1,0:T(8,128)(2,1)S(1)}, bf16[320,256]{1,0:T(8,128)(2,1)S(1)}, u32[]{:S(2)}, u32[]{:S(2)}) %collective-permute-start.6) | collective-permute-done | bytes 163872 | tf_op jit(solution)/shard_map/ppermute | solution.py:284
  28.4 2.5 %collective-permute-start.8 = (bf16[320,256]{1,0:T(8,128)(2,1)S(1)}, bf16[320,256]{1,0:T(8,128)(2,1)S(1)}, u32[]{:S(2)}, u32[]{:S(2)}) collective-permute-start(bf16[320,256]{1,0:T(8,128)(2,1)S(1)} %collective-permute-done.6.refs_3_), channel_id=1, source_target_pairs={{2,0},{4,2},{6,4},{8,6},{10,8},{12,10},{14,12},{0,14},{3,1},{5,3},... | collective-permute-start | bytes 491528 | tf_op jit(solution)/shard_map/ppermute | solution.py:284
  30.9 0.3 collective-permute-done.7.refs_4_
  31.2 0.0 collective-permute-start.10
  31.2 3.4 %collective-permute-done.8.refs_5_ = bf16[320,256]{1,0:T(8,128)(2,1)S(1)} collective-permute-done((bf16[320,256]{1,0:T(8,128)(2,1)S(1)}, bf16[320,256]{1,0:T(8,128)(2,1)S(1)}, u32[]{:S(2)}, u32[]{:S(2)}) %collective-permute-start.8) | collective-permute-done | bytes 163872 | tf_op jit(solution)/shard_map/ppermute | solution.py:284
  34.6 0.0 collective-permute-done.9
  34.6 2.5 %collective-permute-start.11 = (bf16[320,256]{1,0:T(8,128)(2,1)S(1)}, bf16[320,256]{1,0:T(8,128)(2,1)S(1)}, u32[]{:S(2)}, u32[]{:S(2)}) collective-permute-start(bf16[320,256]{1,0:T(8,128)(2,1)S(1)} %collective-permute-done.8.refs_5_), channel_id=1, source_target_pairs={{2,0},{4,2},{6,4},{8,6},{10,8},{12,10},{14,12},{0,14},{3,1},{5,3},... | collective-permute-start | bytes 491528 | tf_op jit(solution)/shard_map/ppermute | solution.py:284
  37.1 2.0 %collective-permute-start.13 = (bf16[128,2048]{1,0:T(8,128)(2,1)S(1)}, bf16[128,2048]{1,0:T(8,128)(2,1)S(1)}, u32[]{:S(2)}, u32[]{:S(2)}) collective-permute-start(bf16[128,2048]{1,0:T(8,128)(2,1)S(1)} %collective-permute-done.9), channel_id=1, source_target_pairs={{0,128},{128,0},{1,129},{129,1},{2,130},{130,2},{3,131},{131,3},{4... | collective-permute-start | bytes 1572872 | tf_op jit(solution)/shard_map/ppermute | solution.py:279
  39.2 0.0 collective-permute-done.10.refs_6_
  39.2 0.7 collective-permute-done.11.refs_7_
  40.0 2.8 %collective-permute-start.15 = (bf16[512,256]{1,0:T(8,128)(2,1)S(1)}, bf16[512,256]{1,0:T(8,128)(2,1)S(1)}, u32[]{:S(2)}, u32[]{:S(2)}) collective-permute-start(bf16[512,256]{1,0:T(8,128)(2,1)S(1)} %slice_dynamic-update-slice_fusion.refs_0_), channel_id=1, source_target_pairs={{32,0},{64,32},{96,64},{0,96},{33,1},{65,33},{97,65},{1,97},{34,2}... | collective-permute-start | bytes 786440 | tf_op jit(solution)/shard_map/ppermute | solution.py:284
  42.7 0.8 collective-permute-start.16
  43.5 0.9 collective-permute-start.17
  44.4 0.0 collective-permute-done.12
  44.4 0.0 copy-done.1
  44.5 0.0 copy-done.2
  44.5 0.0 copy-done.3
  44.5 3.8 %attend.1 = (bf16[128,512]{1,0:T(8,128)(2,1)}, bf16[128,256]{1,0:T(8,128)(2,1)S(1)}, bf16[128,256]{1,0:T(8,128)(2,1)S(1)}) custom-call(s32[5]{0:T(128)S(1)} %stack.23.refs_0_.where_ref, s32[1,16]{1,0:T(1,128)S(1)} %copy-done.2, s32[1,4]{1,0:T(1,128)S(1)} %copy-done.3, bf16[128,512]{1,0:T(8,128)(2,1)S(1)} %copy-done.1, bf16[320,256]{1,0:T(8,128)(2,1)S(1)} %pack.1.refs_0_, ...), custom_call_target="tpu_custom_call" | custom-call | tf_op jit(solution)/shard_map/attend/pallas_call | solution.py:173
  48.2 2.0 %collective-permute-start.14 = (bf16[128,256]{1,0:T(8,128)(2,1)S(1)}, bf16[128,256]{1,0:T(8,128)(2,1)S(1)}, u32[]{:S(2)}, u32[]{:S(2)}) collective-permute-start(bf16[128,256]{1,0:T(8,128)(2,1)S(1)} %get-tuple-element.48), channel_id=1, source_target_pairs={{0,128},{128,0},{1,129},{129,1},{2,130},{130,2},{3,131},{131,3},{4... | collective-permute-start | bytes 196616 | tf_op jit(solution)/shard_map/ppermute | solution.py:279
  50.3 0.0 collective-permute-done.13
  50.3 2.2 %collective-permute-done.14.got_ref = bf16[128,256]{1,0:T(8,128)(2,1)S(1)} collective-permute-done((bf16[128,256]{1,0:T(8,128)(2,1)S(1)}, bf16[128,256]{1,0:T(8,128)(2,1)S(1)}, u32[]{:S(2)}, u32[]{:S(2)}) %collective-permute-start.14) | collective-permute-done | bytes 65568 | tf_op jit(solution)/shard_map/ppermute | solution.py:279
  52.5 0.0 collective-permute-done.15.refs_1_
  52.5 0.0 collective-permute-done.16.refs_2_
  52.5 0.9 collective-permute-done.17.refs_3_
  53.5 1.5 %project.1 = (f32[512,256]{1,0:T(8,128)S(1)}, bf16[512,256]{1,0:T(8,128)(2,1)S(1)}) custom-call(s32[5]{0:T(128)S(1)} %stack.23.refs_0_.where_ref, bf16[512,2048]{1,0:T(8,128)(2,1)S(1)} %constant_dynamic-update-slice_fusion.n_ref.refs_1_, bf16[128,256]{1,0:T(8,128)(2,1)S(1)} %get-tuple-element.47.mine_ref, ...), custom_call_target="tpu_custom_call" | custom-call | tf_op jit(solution)/shard_map/project/pallas_call | solution.py:215
  55.0 0.1 collective-permute-start.18
  55.1 1.5 %collective-permute-done.18.refs_3_ = bf16[512,256]{1,0:T(8,128)(2,1)S(1)} collective-permute-done((bf16[512,256]{1,0:T(8,128)(2,1)S(1)}, bf16[512,256]{1,0:T(8,128)(2,1)S(1)}, u32[]{:S(2)}, u32[]{:S(2)}) %collective-permute-start.18) | collective-permute-done | bytes 262176 | tf_op jit(solution)/shard_map/ppermute | solution.py:279
  56.6 1.6 %gradient.2 = (bf16[448,256]{1,0:T(8,128)(2,1)S(1)}, bf16[448,256]{1,0:T(8,128)(2,1)S(1)}) custom-call(s32[5]{0:T(128)S(1)} %stack.23.refs_0_.where_ref, bf16[512,2048]{1,0:T(8,128)(2,1)S(1)} %constant_dynamic-update-slice_fusion.n_ref.refs_1_, f32[512,256]{1,0:T(8,128)S(1)} %get-tuple-element.49.refs_2_, bf16[512,256]{1,0:T(8,128)(2,1)S(1)} %collective-permute-done.18.refs_3_), custom_call_target="tpu_custom_call" | custom-call | tf_op jit(solution)/shard_map/gradient/pallas_call | solution.py:268
  58.1 1.0 %collective-permute-start.20 = (bf16[448,256]{1,0:T(8,128)(2,1)S(1)}, bf16[448,256]{1,0:T(8,128)(2,1)S(1)}, u32[]{:S(2)}, u32[]{:S(2)}) collective-permute-start(bf16[448,256]{1,0:T(8,128)(2,1)S(1)} %get-tuple-element.51), channel_id=1, source_target_pairs={{64,0},{96,32},{0,64},{32,96},{65,1},{97,33},{1,65},{33,97},{66,2}... | collective-permute-start | bytes 688136 | tf_op jit(solution)/shard_map/ppermute | solution.py:284
  59.1 1.6 %gradient.3 = (bf16[448,256]{1,0:T(8,128)(2,1)S(1)}, bf16[448,256]{1,0:T(8,128)(2,1)S(1)}) custom-call(s32[5]{0:T(128)S(1)} %stack.23.refs_0_.where_ref, bf16[512,2048]{1,0:T(8,128)(2,1)S(1)} %constant_dynamic-update-slice_fusion.n_ref.refs_1_, f32[512,256]{1,0:T(8,128)S(1)} %get-tuple-element.49.refs_2_, bf16[512,256]{1,0:T(8,128)(2,1)S(1)} %collective-permute-done.18.refs_3_), custom_call_target="tpu_custom_call" | custom-call | tf_op jit(solution)/shard_map/gradient/pallas_call | solution.py:268
  60.7 2.7 %collective-permute-start.21 = (bf16[448,256]{1,0:T(8,128)(2,1)S(1)}, bf16[448,256]{1,0:T(8,128)(2,1)S(1)}, u32[]{:S(2)}, u32[]{:S(2)}) collective-permute-start(bf16[448,256]{1,0:T(8,128)(2,1)S(1)} %get-tuple-element.55), channel_id=1, source_target_pairs={{32,0},{64,32},{96,64},{0,96},{33,1},{65,33},{97,65},{1,97},{34,2}... | collective-permute-start | bytes 688136 | tf_op jit(solution)/shard_map/ppermute | solution.py:284
  63.4 0.0 collective-permute-start.19
  63.4 7.6 %collective-permute-done.21 = bf16[448,256]{1,0:T(8,128)(2,1)S(1)} collective-permute-done((bf16[448,256]{1,0:T(8,128)(2,1)S(1)}, bf16[448,256]{1,0:T(8,128)(2,1)S(1)}, u32[]{:S(2)}, u32[]{:S(2)}) %collective-permute-start.21) | collective-permute-done | bytes 229408 | tf_op jit(solution)/shard_map/ppermute | solution.py:284
  71.0 0.0 collective-permute-done.20
  71.0 1.4 %collective-permute-done.19 = bf16[448,256]{1,0:T(8,128)(2,1)S(1)} collective-permute-done((bf16[448,256]{1,0:T(8,128)(2,1)S(1)}, bf16[448,256]{1,0:T(8,128)(2,1)S(1)}, u32[]{:S(2)}, u32[]{:S(2)}) %collective-permute-start.19) | collective-permute-done | bytes 229408 | tf_op jit(solution)/shard_map/ppermute | solution.py:284
  72.4 0.1 add_convert_fusion
  72.5 0.1 reshape.10
  72.6 21.6 %all_to_all.5 = bf16[32,16,256]{2,1,0:T(8,128)(2,1)S(1)} all-to-all(bf16[32,16,256]{2,1,0:T(8,128)(2,1)S(1)} %pad.14), channel_id=1, replica_groups=mesh['ylo'=2,'x'=4,'core'=2,'z'=8,'yhi'=2] {'ylo','z','yhi'}, dimensions={0} | all-to-all | bytes 524288 | tf_op jit(solution)/shard_map/all_to_all | solution.py:340
  94.3 0.6 pad_maximum_fusion
  (17 shorter events, 0.3 us)
Async XLA Ops:
  1.4 11.4 %collective-permute-start = (bf16[128,256]{1,0:T(8,128)(2,1)S(1)}, bf16[128,256]{1,0:T(8,128)(2,1)S(1)}, u32[]{:S(2)}, u32[]{:S(2)}) collective-permute-start(bf16[128,256]{1,0:T(8,128)(2,1)S(1)} %pad_select_fusion.kv_ref), channel_id=1, source_target_pairs={{0,1},{1,0},{2,3},{3,2},{4,5},{5,4},{6,7},{7,6},{8,9},{9,8},{10,11... | collective-permute-start | bytes 196616 | tf_op jit(solution)/shard_map/ppermute | solution.py:279
  5.4 4.8 %collective-permute-start.1 = (bf16[14,256]{1,0:T(8,128)(2,1)S(1)}, bf16[14,256]{1,0:T(8,128)(2,1)S(1)}, u32[]{:S(2)}, u32[]{:S(2)}) collective-permute-start(bf16[14,256]{1,0:T(8,128)(2,1)S(1)} %get-tuple-element.58), channel_id=1, source_target_pairs={{0,128},{128,0},{1,129},{129,1},{2,130},{130,2},{3,131},{131,3},{4... | collective-permute-start | bytes 21512 | tf_op jit(solution)/shard_map/ppermute | solution.py:279
  6.1 5.2 %collective-permute-start.2 = (bf16[14,256]{1,0:T(8,128)(2,1)S(1)}, bf16[14,256]{1,0:T(8,128)(2,1)S(1)}, u32[]{:S(2)}, u32[]{:S(2)}) collective-permute-start(bf16[14,256]{1,0:T(8,128)(2,1)S(1)} %get-tuple-element.59.refs_0_), channel_id=1, source_target_pairs={{0,1},{1,0},{2,3},{3,2},{4,5},{5,4},{6,7},{7,6},{8,9},{9,8},{10,11... | collective-permute-start | bytes 21512 | tf_op jit(solution)/shard_map/ppermute | solution.py:279
  8.0 4.9 %collective-permute-start.3 = (bf16[14,256]{1,0:T(8,128)(2,1)S(1)}, bf16[14,256]{1,0:T(8,128)(2,1)S(1)}, u32[]{:S(2)}, u32[]{:S(2)}) collective-permute-start(bf16[14,256]{1,0:T(8,128)(2,1)S(1)} %get-tuple-element.58), channel_id=1, source_target_pairs={{0,129},{1,128},{128,1},{129,0},{2,131},{3,130},{130,3},{131,2},{4... | collective-permute-start | bytes 21512 | tf_op jit(solution)/shard_map/ppermute | solution.py:302
  12.8 31.6 %copy-start.1 = (bf16[128,512]{1,0:T(8,128)(2,1)S(1)}, bf16[128,512]{1,0:T(8,128)(2,1)}, u32[]{:S(2)}) copy-start(bf16[128,512]{1,0:T(8,128)(2,1)} %q_ref.1) | copy-start | bytes 393220
  12.8 31.6 %copy-start.2 = (s32[1,16]{1,0:T(1,128)S(1)}, s32[1,16]{1,0:T(1,128)}, u32[]{:S(2)}) copy-start(s32[1,16]{1,0:T(1,128)} %assign_ref.1) | copy-start | bytes 196
  12.8 31.6 %copy-start.3 = (s32[1,4]{1,0:T(1,128)S(1)}, s32[1,4]{1,0:T(1,128)}, u32[]{:S(2)}) copy-start(s32[1,4]{1,0:T(1,128)} %length_ref.1) | copy-start | bytes 52
  12.9 5.6 %collective-permute-start.4 = (bf16[320,256]{1,0:T(8,128)(2,1)S(1)}, bf16[320,256]{1,0:T(8,128)(2,1)S(1)}, u32[]{:S(2)}, u32[]{:S(2)}) collective-permute-start(bf16[320,256]{1,0:T(8,128)(2,1)S(1)} %pack.1.refs_0_), channel_id=1, source_target_pairs={{2,0},{4,2},{6,4},{8,6},{10,8},{12,10},{14,12},{0,14},{3,1},{5,3},... | collective-permute-start | bytes 491528 | tf_op jit(solution)/shard_map/ppermute | solution.py:284
  13.0 9.2 %collective-permute-start.5 = (bf16[320,256]{1,0:T(8,128)(2,1)S(1)}, bf16[320,256]{1,0:T(8,128)(2,1)S(1)}, u32[]{:S(2)}, u32[]{:S(2)}) collective-permute-start(bf16[320,256]{1,0:T(8,128)(2,1)S(1)} %pack.1.refs_0_), channel_id=1, source_target_pairs={{14,0},{0,2},{2,4},{4,6},{6,8},{8,10},{10,12},{12,14},{15,1},{1,3}... | collective-permute-start | bytes 491528 | tf_op jit(solution)/shard_map/ppermute | solution.py:284
  15.0 1.2 %copy-start = (bf16[128,3584]{1,0:T(8,128)(2,1)S(1)}, bf16[128,3584]{1,0:T(8,128)(2,1)}, u32[]{:S(2)}) copy-start(bf16[128,3584]{1,0:T(8,128)(2,1)} %refs_1_) | copy-start | bytes 2752516
  22.2 22.2 %collective-permute-start.12 = (bf16[128,2048]{1,0:T(8,128)(2,1)S(1)}, bf16[128,2048]{1,0:T(8,128)(2,1)S(1)}, u32[]{:S(2)}, u32[]{:S(2)}) collective-permute-start(bf16[128,2048]{1,0:T(8,128)(2,1)S(1)} %get-tuple-element.36), channel_id=1, source_target_pairs={{0,128},{128,0},{1,129},{129,1},{2,130},{130,2},{3,131},{131,3},{4... | collective-permute-start | bytes 1572872 | tf_op jit(solution)/shard_map/ppermute | solution.py:279
  22.2 6.1 %collective-permute-start.6 = (bf16[320,256]{1,0:T(8,128)(2,1)S(1)}, bf16[320,256]{1,0:T(8,128)(2,1)S(1)}, u32[]{:S(2)}, u32[]{:S(2)}) collective-permute-start(bf16[320,256]{1,0:T(8,128)(2,1)S(1)} %collective-permute-done.4.refs_1_), channel_id=1, source_target_pairs={{2,0},{4,2},{6,4},{8,6},{10,8},{12,10},{14,12},{0,14},{3,1},{5,3},... | collective-permute-start | bytes 491528 | tf_op jit(solution)/shard_map/ppermute | solution.py:284
  25.6 5.6 %collective-permute-start.7 = (bf16[320,256]{1,0:T(8,128)(2,1)S(1)}, bf16[320,256]{1,0:T(8,128)(2,1)S(1)}, u32[]{:S(2)}, u32[]{:S(2)}) collective-permute-start(bf16[320,256]{1,0:T(8,128)(2,1)S(1)} %collective-permute-done.5.refs_2_), channel_id=1, source_target_pairs={{14,0},{0,2},{2,4},{4,6},{6,8},{8,10},{10,12},{12,14},{15,1},{1,3}... | collective-permute-start | bytes 491528 | tf_op jit(solution)/shard_map/ppermute | solution.py:284
  25.6 9.1 %collective-permute-start.9 = (bf16[128,2048]{1,0:T(8,128)(2,1)S(1)}, bf16[128,2048]{1,0:T(8,128)(2,1)S(1)}, u32[]{:S(2)}, u32[]{:S(2)}) collective-permute-start(bf16[128,2048]{1,0:T(8,128)(2,1)S(1)} %get-tuple-element.34), channel_id=1, source_target_pairs={{0,16},{16,0},{1,17},{17,1},{2,18},{18,2},{3,19},{19,3},{4,20},{20... | collective-permute-start | bytes 1572872 | tf_op jit(solution)/shard_map/ppermute | solution.py:279
  28.4 6.2 %collective-permute-start.8 = (bf16[320,256]{1,0:T(8,128)(2,1)S(1)}, bf16[320,256]{1,0:T(8,128)(2,1)S(1)}, u32[]{:S(2)}, u32[]{:S(2)}) collective-permute-start(bf16[320,256]{1,0:T(8,128)(2,1)S(1)} %collective-permute-done.6.refs_3_), channel_id=1, source_target_pairs={{2,0},{4,2},{6,4},{8,6},{10,8},{12,10},{14,12},{0,14},{3,1},{5,3},... | collective-permute-start | bytes 491528 | tf_op jit(solution)/shard_map/ppermute | solution.py:284
  31.2 8.0 %collective-permute-start.10 = (bf16[320,256]{1,0:T(8,128)(2,1)S(1)}, bf16[320,256]{1,0:T(8,128)(2,1)S(1)}, u32[]{:S(2)}, u32[]{:S(2)}) collective-permute-start(bf16[320,256]{1,0:T(8,128)(2,1)S(1)} %collective-permute-done.7.refs_4_), channel_id=1, source_target_pairs={{14,0},{0,2},{2,4},{4,6},{6,8},{8,10},{10,12},{12,14},{15,1},{1,3}... | collective-permute-start | bytes 491528 | tf_op jit(solution)/shard_map/ppermute | solution.py:284
  34.6 5.3 %collective-permute-start.11 = (bf16[320,256]{1,0:T(8,128)(2,1)S(1)}, bf16[320,256]{1,0:T(8,128)(2,1)S(1)}, u32[]{:S(2)}, u32[]{:S(2)}) collective-permute-start(bf16[320,256]{1,0:T(8,128)(2,1)S(1)} %collective-permute-done.8.refs_5_), channel_id=1, source_target_pairs={{2,0},{4,2},{6,4},{8,6},{10,8},{12,10},{14,12},{0,14},{3,1},{5,3},... | collective-permute-start | bytes 491528 | tf_op jit(solution)/shard_map/ppermute | solution.py:284
  37.1 13.2 %collective-permute-start.13 = (bf16[128,2048]{1,0:T(8,128)(2,1)S(1)}, bf16[128,2048]{1,0:T(8,128)(2,1)S(1)}, u32[]{:S(2)}, u32[]{:S(2)}) collective-permute-start(bf16[128,2048]{1,0:T(8,128)(2,1)S(1)} %collective-permute-done.9), channel_id=1, source_target_pairs={{0,128},{128,0},{1,129},{129,1},{2,130},{130,2},{3,131},{131,3},{4... | collective-permute-start | bytes 1572872 | tf_op jit(solution)/shard_map/ppermute | solution.py:279
  40.0 12.6 %collective-permute-start.15 = (bf16[512,256]{1,0:T(8,128)(2,1)S(1)}, bf16[512,256]{1,0:T(8,128)(2,1)S(1)}, u32[]{:S(2)}, u32[]{:S(2)}) collective-permute-start(bf16[512,256]{1,0:T(8,128)(2,1)S(1)} %slice_dynamic-update-slice_fusion.refs_0_), channel_id=1, source_target_pairs={{32,0},{64,32},{96,64},{0,96},{33,1},{65,33},{97,65},{1,97},{34,2}... | collective-permute-start | bytes 786440 | tf_op jit(solution)/shard_map/ppermute | solution.py:284
  42.7 9.8 %collective-permute-start.16 = (bf16[512,256]{1,0:T(8,128)(2,1)S(1)}, bf16[512,256]{1,0:T(8,128)(2,1)S(1)}, u32[]{:S(2)}, u32[]{:S(2)}) collective-permute-start(bf16[512,256]{1,0:T(8,128)(2,1)S(1)} %slice_dynamic-update-slice_fusion.refs_0_), channel_id=1, source_target_pairs={{64,0},{96,32},{0,64},{32,96},{65,1},{97,33},{1,65},{33,97},{66,2}... | collective-permute-start | bytes 786440 | tf_op jit(solution)/shard_map/ppermute | solution.py:284
  43.5 9.9 %collective-permute-start.17 = (bf16[512,256]{1,0:T(8,128)(2,1)S(1)}, bf16[512,256]{1,0:T(8,128)(2,1)S(1)}, u32[]{:S(2)}, u32[]{:S(2)}) collective-permute-start(bf16[512,256]{1,0:T(8,128)(2,1)S(1)} %slice_dynamic-update-slice_fusion.refs_0_), channel_id=1, source_target_pairs={{96,0},{0,32},{32,64},{64,96},{97,1},{1,33},{33,65},{65,97},{98,2}... | collective-permute-start | bytes 786440 | tf_op jit(solution)/shard_map/ppermute | solution.py:284
  48.2 4.3 %collective-permute-start.14 = (bf16[128,256]{1,0:T(8,128)(2,1)S(1)}, bf16[128,256]{1,0:T(8,128)(2,1)S(1)}, u32[]{:S(2)}, u32[]{:S(2)}) collective-permute-start(bf16[128,256]{1,0:T(8,128)(2,1)S(1)} %get-tuple-element.48), channel_id=1, source_target_pairs={{0,128},{128,0},{1,129},{129,1},{2,130},{130,2},{3,131},{131,3},{4... | collective-permute-start | bytes 196616 | tf_op jit(solution)/shard_map/ppermute | solution.py:279
  55.0 1.6 %collective-permute-start.18 = (bf16[512,256]{1,0:T(8,128)(2,1)S(1)}, bf16[512,256]{1,0:T(8,128)(2,1)S(1)}, u32[]{:S(2)}, u32[]{:S(2)}) collective-permute-start(bf16[512,256]{1,0:T(8,128)(2,1)S(1)} %get-tuple-element.50), channel_id=1, source_target_pairs={{0,16},{16,0},{1,17},{17,1},{2,18},{18,2},{3,19},{19,3},{4,20},{20... | collective-permute-start | bytes 786440 | tf_op jit(solution)/shard_map/ppermute | solution.py:279
  58.1 12.9 %collective-permute-start.20 = (bf16[448,256]{1,0:T(8,128)(2,1)S(1)}, bf16[448,256]{1,0:T(8,128)(2,1)S(1)}, u32[]{:S(2)}, u32[]{:S(2)}) collective-permute-start(bf16[448,256]{1,0:T(8,128)(2,1)S(1)} %get-tuple-element.51), channel_id=1, source_target_pairs={{64,0},{96,32},{0,64},{32,96},{65,1},{97,33},{1,65},{33,97},{66,2}... | collective-permute-start | bytes 688136 | tf_op jit(solution)/shard_map/ppermute | solution.py:284
  60.7 10.3 %collective-permute-start.21 = (bf16[448,256]{1,0:T(8,128)(2,1)S(1)}, bf16[448,256]{1,0:T(8,128)(2,1)S(1)}, u32[]{:S(2)}, u32[]{:S(2)}) collective-permute-start(bf16[448,256]{1,0:T(8,128)(2,1)S(1)} %get-tuple-element.55), channel_id=1, source_target_pairs={{32,0},{64,32},{96,64},{0,96},{33,1},{65,33},{97,65},{1,97},{34,2}... | collective-permute-start | bytes 688136 | tf_op jit(solution)/shard_map/ppermute | solution.py:284
  63.4 9.0 %collective-permute-start.19 = (bf16[448,256]{1,0:T(8,128)(2,1)S(1)}, bf16[448,256]{1,0:T(8,128)(2,1)S(1)}, u32[]{:S(2)}, u32[]{:S(2)}) collective-permute-start(bf16[448,256]{1,0:T(8,128)(2,1)S(1)} %get-tuple-element.54), channel_id=1, source_target_pairs={{96,0},{0,32},{32,64},{64,96},{97,1},{1,33},{33,65},{65,97},{98,2}... | collective-permute-start | bytes 688136 | tf_op jit(solution)/shard_map/ppermute | solution.py:284

commit v13 on v11

--- a/solution.py
+++ b/solution.py
@@ -307,7 +307,7 @@
     n_keep, n_send = normalise(here, student_in, wrows)
     up, down = from_next(packed, "z", 1), from_next(packed, "z", -1)
     up, down, n_keep, n_send = lax.optimization_barrier((up, down, n_keep, n_send))
-    n_got, n_across = partner(n_send, "core"), partner(n_keep, "ylo")
+    n_across = partner(n_keep, "ylo")
 
     held = {0: packed, 1: up, -1: down}
     for d in range(2, 5):
@@ -315,8 +315,11 @@
         if d < 4:
             held[-d] = from_next(held[1 - d], "z", -1)
         if d == 2:
-            held[2], held[-2], n_got = lax.optimization_barrier((held[2], held[-2], n_got))
-    n_all = jnp.concatenate([n_keep, n_got, n_across, partner(n_got, "ylo")], axis=0)
+            n_sent, _ = lax.optimization_barrier((n_send, held[2]))
+            n_diag = lax.ppermute(n_sent, ("ylo", "core"), [(i, 3 - i) for i in range(4)])
+    n_late, _ = lax.optimization_barrier((n_send, held[4]))
+    n_got = partner(n_late, "core")
+    n_all = jnp.concatenate([n_keep, n_got, n_across, n_diag], axis=0)
     parts = [held[d] for d in RING]
     w_rows = jnp.concatenate([part[2 * BLK :] for part in parts], axis=0)
     w_sent = {d: from_next(w_rows, "x", d) for d in (2, 1, 3)}

time: 96.6 us -> 102 us (1.056)
  blocking collectives: 20 us -> 22.3 us
  starting transfers between devices: 24.8 us -> 27 us
    all_to_all x1, blocking collectives: 20 us -> 22.3 us  [local(): lax.all_to_all(near, ('ylo', *SEQ), split_axis=0, concat_axis=0, tiled=True)]
    ppermute x13, waiting for transfers between devices: 27.7 us -> 29.1 us  [from_next(): lax.ppermute(x, axis, [((i + distance) % size, i) for i in range(size)])]
    ppermute x13, starting transfers between devices: 16.7 us -> 17.9 us  [from_next(): lax.ppermute(x, axis, [((i + distance) % size, i) for i in range(size)])]
    ppermute x8 -> x7, starting transfers between devices: 5.99 us -> 6.93 us  [partner(): return lax.ppermute(x, axis, [(0, 1), (1, 0)])]
    ppermute x8 -> x7, waiting for transfers between devices: 6.79 us -> 6.11 us  [partner(): return lax.ppermute(x, axis, [(0, 1), (1, 0)])]
  transfers between devices with their start and end apart: 22 -> 22, of which waited for: 13 -> 12; matrix products, arithmetic and copies ran while one was open for 1% -> 1% of each run, Pallas kernels for 8% -> 8%
where the time goes in v13:
time: 102 us
  waiting for transfers between devices  36.8 us (36%)
  starting transfers between devices  27 us (26%)
  blocking collectives  22.3 us (22%)
  Pallas kernels  10.7 us (10%)
  other arithmetic  2.34 us (2%)
  local copies, waits for them, and re-layouts  1.57 us (2%)
    ppermute x13, waiting for transfers between devices, from_next(): lax.ppermute(x, axis, [((i + distance) % size, i) for i in range(size)])  29.1 us
    all_to_all x1, blocking collectives, local(): lax.all_to_all(near, ('ylo', *SEQ), split_axis=0, concat_axis=0, tiled=True)  22.3 us
    ppermute x13, starting transfers between devices, from_next(): lax.ppermute(x, axis, [((i + distance) % size, i) for i in range(size)])  17.9 us
    ppermute x7, starting transfers between devices, partner(): return lax.ppermute(x, axis, [(0, 1), (1, 0)])  6.93 us
    ppermute x7, waiting for transfers between devices, partner(): return lax.ppermute(x, axis, [(0, 1), (1, 0)])  6.11 us
    pallas_call x1, Pallas kernels, attend(): pl.pallas_call(attend_kernel, out_shape=(jax.ShapeDtypeStruct((rows, COLS...  3.76 us
    pallas_call x2, Pallas kernels, gradient(): pl.pallas_call(body, out_shape=(shape,) * len(steps), in_specs=[SMEM, VME...  3.12 us
    pallas_call x1, Pallas kernels, normalise(): pl.pallas_call(body, out_shape=(shape, shape), in_specs=[SMEM, VMEM], out...  2.32 us
  transfers between devices with their start and end apart: 22, of which 12 were waited for; matrix products, arithmetic and copies ran while one was open for 1% of the time, Pallas kernels for 8%

profile of v13, /device:TPU:32, one launch (start us, length us, event | category | flops | bytes accessed | tf_op | source)
XLA Modules:
  0.0 101.5 jit_solution(4456296251877363903)
XLA Ops:
  0.6 0.0 copy-start.2
  0.6 0.0 copy-start.3
  0.7 0.0 copy-start.1
  0.7 0.8 pad_select_fusion.kv_ref
  1.5 3.3 %collective-permute-start = (bf16[128,256]{1,0:T(8,128)(2,1)S(1)}, bf16[128,256]{1,0:T(8,128)(2,1)S(1)}, u32[]{:S(2)}, u32[]{:S(2)}) collective-permute-start(bf16[128,256]{1,0:T(8,128)(2,1)S(1)} %pad_select_fusion.kv_ref), channel_id=1, source_target_pairs={{0,1},{1,0},{2,3},{3,2},{4,5},{5,4},{6,7},{7,6},{8,9},{9,8},{10,11... | collective-permute-start | bytes 196616 | tf_op jit(solution)/shard_map/ppermute | solution.py:279
  4.8 0.7 broadcast_select_fusion
  5.5 0.7 collective-permute-start.1
  6.2 1.8 %collective-permute-start.2 = (bf16[14,256]{1,0:T(8,128)(2,1)S(1)}, bf16[14,256]{1,0:T(8,128)(2,1)S(1)}, u32[]{:S(2)}, u32[]{:S(2)}) collective-permute-start(bf16[14,256]{1,0:T(8,128)(2,1)S(1)} %get-tuple-element.59.refs_0_), channel_id=1, source_target_pairs={{0,1},{1,0},{2,3},{3,2},{4,5},{5,4},{6,7},{7,6},{8,9},{9,8},{10,11... | collective-permute-start | bytes 21512 | tf_op jit(solution)/shard_map/ppermute | solution.py:279
  8.0 2.2 %collective-permute-start.3 = (bf16[14,256]{1,0:T(8,128)(2,1)S(1)}, bf16[14,256]{1,0:T(8,128)(2,1)S(1)}, u32[]{:S(2)}, u32[]{:S(2)}) collective-permute-start(bf16[14,256]{1,0:T(8,128)(2,1)S(1)} %get-tuple-element.58), channel_id=1, source_target_pairs={{0,129},{1,128},{128,1},{129,0},{2,131},{3,130},{130,3},{131,2},{4... | collective-permute-start | bytes 21512 | tf_op jit(solution)/shard_map/ppermute | solution.py:302
  10.2 0.1 stack.23.refs_0_.where_ref
  10.3 0.0 collective-permute-done.1.refs_1_
  10.3 1.0 %collective-permute-done.2.refs_2_ = bf16[14,256]{1,0:T(8,128)(2,1)S(1)} collective-permute-done((bf16[14,256]{1,0:T(8,128)(2,1)S(1)}, bf16[14,256]{1,0:T(8,128)(2,1)S(1)}, u32[]{:S(2)}, u32[]{:S(2)}) %collective-permute-start.2) | collective-permute-done | bytes 7200 | tf_op jit(solution)/shard_map/ppermute | solution.py:279
  11.4 1.5 %collective-permute-done.3.refs_3_ = bf16[14,256]{1,0:T(8,128)(2,1)S(1)} collective-permute-done((bf16[14,256]{1,0:T(8,128)(2,1)S(1)}, bf16[14,256]{1,0:T(8,128)(2,1)S(1)}, u32[]{:S(2)}, u32[]{:S(2)}) %collective-permute-start.3) | collective-permute-done | bytes 7200 | tf_op jit(solution)/shard_map/ppermute | solution.py:302
  12.9 0.0 collective-permute-done.kv_other_ref
  12.9 0.2 collective-permute-start.4
  13.1 1.9 %collective-permute-start.5 = (bf16[320,256]{1,0:T(8,128)(2,1)S(1)}, bf16[320,256]{1,0:T(8,128)(2,1)S(1)}, u32[]{:S(2)}, u32[]{:S(2)}) collective-permute-start(bf16[320,256]{1,0:T(8,128)(2,1)S(1)} %pack.1.refs_0_), channel_id=1, source_target_pairs={{14,0},{0,2},{2,4},{4,6},{6,8},{8,10},{10,12},{12,14},{15,1},{1,3}... | collective-permute-start | bytes 491528 | tf_op jit(solution)/shard_map/ppermute | solution.py:284
  15.0 0.0 copy-start
  15.0 1.2 %copy-done = bf16[128,3584]{1,0:T(8,128)(2,1)S(1)} copy-done((bf16[128,3584]{1,0:T(8,128)(2,1)S(1)}, bf16[128,3584]{1,0:T(8,128)(2,1)}, u32[]{:S(2)}) %copy-start) | copy-done | bytes 917528
  16.2 2.3 %normalise.1 = (bf16[128,2048]{1,0:T(8,128)(2,1)S(1)}, bf16[128,2048]{1,0:T(8,128)(2,1)S(1)}) custom-call(s32[5]{0:T(128)S(1)} %stack.23.refs_0_.where_ref, bf16[128,3584]{1,0:T(8,128)(2,1)S(1)} %copy-done), custom_call_target="tpu_custom_call" | custom-call | tf_op jit(solution)/shard_map/normalise/pallas_call | solution.py:78
  18.5 0.0 collective-permute-done.4.refs_1_
  18.6 3.7 %collective-permute-done.5.refs_2_ = bf16[320,256]{1,0:T(8,128)(2,1)S(1)} collective-permute-done((bf16[320,256]{1,0:T(8,128)(2,1)S(1)}, bf16[320,256]{1,0:T(8,128)(2,1)S(1)}, u32[]{:S(2)}, u32[]{:S(2)}) %collective-permute-start.5) | collective-permute-done | bytes 163872 | tf_op jit(solution)/shard_map/ppermute | solution.py:284
  22.3 0.0 collective-permute-start.11
  22.3 3.3 %collective-permute-start.6 = (bf16[320,256]{1,0:T(8,128)(2,1)S(1)}, bf16[320,256]{1,0:T(8,128)(2,1)S(1)}, u32[]{:S(2)}, u32[]{:S(2)}) collective-permute-start(bf16[320,256]{1,0:T(8,128)(2,1)S(1)} %collective-permute-done.4.refs_1_), channel_id=1, source_target_pairs={{2,0},{4,2},{6,4},{8,6},{10,8},{12,10},{14,12},{0,14},{3,1},{5,3},... | collective-permute-start | bytes 491528 | tf_op jit(solution)/shard_map/ppermute | solution.py:284
  25.6 0.0 collective-permute-start.7
  25.6 2.8 %collective-permute-done.6.refs_3_ = bf16[320,256]{1,0:T(8,128)(2,1)S(1)} collective-permute-done((bf16[320,256]{1,0:T(8,128)(2,1)S(1)}, bf16[320,256]{1,0:T(8,128)(2,1)S(1)}, u32[]{:S(2)}, u32[]{:S(2)}) %collective-permute-start.6) | collective-permute-done | bytes 163872 | tf_op jit(solution)/shard_map/ppermute | solution.py:284
  28.5 0.0 collective-permute-start.13
  28.5 2.5 %collective-permute-start.8 = (bf16[320,256]{1,0:T(8,128)(2,1)S(1)}, bf16[320,256]{1,0:T(8,128)(2,1)S(1)}, u32[]{:S(2)}, u32[]{:S(2)}) collective-permute-start(bf16[320,256]{1,0:T(8,128)(2,1)S(1)} %collective-permute-done.6.refs_3_), channel_id=1, source_target_pairs={{2,0},{4,2},{6,4},{8,6},{10,8},{12,10},{14,12},{0,14},{3,1},{5,3},... | collective-permute-start | bytes 491528 | tf_op jit(solution)/shard_map/ppermute | solution.py:284
  30.9 0.0 collective-permute-done.7.refs_4_
  30.9 0.0 collective-permute-start.9
  30.9 3.4 %collective-permute-done.8.refs_5_ = bf16[320,256]{1,0:T(8,128)(2,1)S(1)} collective-permute-done((bf16[320,256]{1,0:T(8,128)(2,1)S(1)}, bf16[320,256]{1,0:T(8,128)(2,1)S(1)}, u32[]{:S(2)}, u32[]{:S(2)}) %collective-permute-start.8) | collective-permute-done | bytes 163872 | tf_op jit(solution)/shard_map/ppermute | solution.py:284
  34.3 2.5 %collective-permute-start.10 = (bf16[320,256]{1,0:T(8,128)(2,1)S(1)}, bf16[320,256]{1,0:T(8,128)(2,1)S(1)}, u32[]{:S(2)}, u32[]{:S(2)}) collective-permute-start(bf16[320,256]{1,0:T(8,128)(2,1)S(1)} %collective-permute-done.8.refs_5_), channel_id=1, source_target_pairs={{2,0},{4,2},{6,4},{8,6},{10,8},{12,10},{14,12},{0,14},{3,1},{5,3},... | collective-permute-start | bytes 491528 | tf_op jit(solution)/shard_map/ppermute | solution.py:284
  36.8 4.2 %collective-permute-done.10.refs_7_ = bf16[320,256]{1,0:T(8,128)(2,1)S(1)} collective-permute-done((bf16[320,256]{1,0:T(8,128)(2,1)S(1)}, bf16[320,256]{1,0:T(8,128)(2,1)S(1)}, u32[]{:S(2)}, u32[]{:S(2)}) %collective-permute-start.10) | collective-permute-done | bytes 163872 | tf_op jit(solution)/shard_map/ppermute | solution.py:284
  41.1 0.5 collective-permute-start.12
  41.5 0.0 collective-permute-done.9.refs_6_
  41.6 2.8 %collective-permute-start.15 = (bf16[512,256]{1,0:T(8,128)(2,1)S(1)}, bf16[512,256]{1,0:T(8,128)(2,1)S(1)}, u32[]{:S(2)}, u32[]{:S(2)}) collective-permute-start(bf16[512,256]{1,0:T(8,128)(2,1)S(1)} %slice_dynamic-update-slice_fusion.refs_0_), channel_id=1, source_target_pairs={{32,0},{64,32},{96,64},{0,96},{33,1},{65,33},{97,65},{1,97},{34,2}... | collective-permute-start | bytes 786440 | tf_op jit(solution)/shard_map/ppermute | solution.py:284
  44.4 0.8 collective-permute-start.16
  45.2 0.0 collective-permute-done.11
  45.2 0.9 collective-permute-start.17
  46.1 0.0 copy-done.2
  46.1 0.0 copy-done.3
  46.1 0.0 copy-done.1
  46.1 3.8 %attend.1 = (bf16[128,512]{1,0:T(8,128)(2,1)}, bf16[128,256]{1,0:T(8,128)(2,1)S(1)}, bf16[128,256]{1,0:T(8,128)(2,1)S(1)}) custom-call(s32[5]{0:T(128)S(1)} %stack.23.refs_0_.where_ref, s32[1,16]{1,0:T(1,128)S(1)} %copy-done.2, s32[1,4]{1,0:T(1,128)S(1)} %copy-done.3, bf16[128,512]{1,0:T(8,128)(2,1)S(1)} %copy-done.1, bf16[320,256]{1,0:T(8,128)(2,1)S(1)} %pack.1.refs_0_, ...), custom_call_target="tpu_custom_call" | custom-call | tf_op jit(solution)/shard_map/attend/pallas_call | solution.py:173
  49.9 0.0 collective-permute-done.12
  49.9 0.6 collective-permute-start.14
  50.5 0.0 collective-permute-done.13
  50.6 3.5 %collective-permute-done.14.got_ref = bf16[128,256]{1,0:T(8,128)(2,1)S(1)} collective-permute-done((bf16[128,256]{1,0:T(8,128)(2,1)S(1)}, bf16[128,256]{1,0:T(8,128)(2,1)S(1)}, u32[]{:S(2)}, u32[]{:S(2)}) %collective-permute-start.14) | collective-permute-done | bytes 65568 | tf_op jit(solution)/shard_map/ppermute | solution.py:279
  54.1 1.7 %collective-permute-done.15.refs_1_ = bf16[512,256]{1,0:T(8,128)(2,1)S(1)} collective-permute-done((bf16[512,256]{1,0:T(8,128)(2,1)S(1)}, bf16[512,256]{1,0:T(8,128)(2,1)S(1)}, u32[]{:S(2)}, u32[]{:S(2)}) %collective-permute-start.15) | collective-permute-done | bytes 262176 | tf_op jit(solution)/shard_map/ppermute | solution.py:284
  55.8 0.0 collective-permute-done.16.refs_2_
  55.8 3.7 %collective-permute-done.17.refs_3_ = bf16[512,256]{1,0:T(8,128)(2,1)S(1)} collective-permute-done((bf16[512,256]{1,0:T(8,128)(2,1)S(1)}, bf16[512,256]{1,0:T(8,128)(2,1)S(1)}, u32[]{:S(2)}, u32[]{:S(2)}) %collective-permute-start.17) | collective-permute-done | bytes 262176 | tf_op jit(solution)/shard_map/ppermute | solution.py:284
  59.5 1.5 %project.1 = (f32[512,256]{1,0:T(8,128)S(1)}, bf16[512,256]{1,0:T(8,128)(2,1)S(1)}) custom-call(s32[5]{0:T(128)S(1)} %stack.23.refs_0_.where_ref, bf16[512,2048]{1,0:T(8,128)(2,1)S(1)} %constant_dynamic-update-slice_fusion.n_ref.refs_1_, bf16[128,256]{1,0:T(8,128)(2,1)S(1)} %get-tuple-element.47.mine_ref, ...), custom_call_target="tpu_custom_call" | custom-call | tf_op jit(solution)/shard_map/project/pallas_call | solution.py:215
  61.0 0.1 collective-permute-start.18
  61.1 1.5 %collective-permute-done.18.refs_3_ = bf16[512,256]{1,0:T(8,128)(2,1)S(1)} collective-permute-done((bf16[512,256]{1,0:T(8,128)(2,1)S(1)}, bf16[512,256]{1,0:T(8,128)(2,1)S(1)}, u32[]{:S(2)}, u32[]{:S(2)}) %collective-permute-start.18) | collective-permute-done | bytes 262176 | tf_op jit(solution)/shard_map/ppermute | solution.py:279
  62.6 1.6 %gradient.2 = (bf16[448,256]{1,0:T(8,128)(2,1)S(1)}, bf16[448,256]{1,0:T(8,128)(2,1)S(1)}) custom-call(s32[5]{0:T(128)S(1)} %stack.23.refs_0_.where_ref, bf16[512,2048]{1,0:T(8,128)(2,1)S(1)} %constant_dynamic-update-slice_fusion.n_ref.refs_1_, f32[512,256]{1,0:T(8,128)S(1)} %get-tuple-element.49.refs_2_, bf16[512,256]{1,0:T(8,128)(2,1)S(1)} %collective-permute-done.18.refs_3_), custom_call_target="tpu_custom_call" | custom-call | tf_op jit(solution)/shard_map/gradient/pallas_call | solution.py:268
  64.2 0.9 collective-permute-start.20
  65.1 1.6 %gradient.3 = (bf16[448,256]{1,0:T(8,128)(2,1)S(1)}, bf16[448,256]{1,0:T(8,128)(2,1)S(1)}) custom-call(s32[5]{0:T(128)S(1)} %stack.23.refs_0_.where_ref, bf16[512,2048]{1,0:T(8,128)(2,1)S(1)} %constant_dynamic-update-slice_fusion.n_ref.refs_1_, f32[512,256]{1,0:T(8,128)S(1)} %get-tuple-element.49.refs_2_, bf16[512,256]{1,0:T(8,128)(2,1)S(1)} %collective-permute-done.18.refs_3_), custom_call_target="tpu_custom_call" | custom-call | tf_op jit(solution)/shard_map/gradient/pallas_call | solution.py:268
  66.6 1.3 %collective-permute-start.21 = (bf16[448,256]{1,0:T(8,128)(2,1)S(1)}, bf16[448,256]{1,0:T(8,128)(2,1)S(1)}, u32[]{:S(2)}, u32[]{:S(2)}) collective-permute-start(bf16[448,256]{1,0:T(8,128)(2,1)S(1)} %get-tuple-element.55), channel_id=1, source_target_pairs={{32,0},{64,32},{96,64},{0,96},{33,1},{65,33},{97,65},{1,97},{34,2}... | collective-permute-start | bytes 688136 | tf_op jit(solution)/shard_map/ppermute | solution.py:284
  67.9 0.8 collective-permute-start.19
  68.7 7.5 %collective-permute-done.21 = bf16[448,256]{1,0:T(8,128)(2,1)S(1)} collective-permute-done((bf16[448,256]{1,0:T(8,128)(2,1)S(1)}, bf16[448,256]{1,0:T(8,128)(2,1)S(1)}, u32[]{:S(2)}, u32[]{:S(2)}) %collective-permute-start.21) | collective-permute-done | bytes 229408 | tf_op jit(solution)/shard_map/ppermute | solution.py:284
  76.3 0.0 collective-permute-done.20
  76.3 2.1 %collective-permute-done.19 = bf16[448,256]{1,0:T(8,128)(2,1)S(1)} collective-permute-done((bf16[448,256]{1,0:T(8,128)(2,1)S(1)}, bf16[448,256]{1,0:T(8,128)(2,1)S(1)}, u32[]{:S(2)}, u32[]{:S(2)}) %collective-permute-start.19) | collective-permute-done | bytes 229408 | tf_op jit(solution)/shard_map/ppermute | solution.py:284
  78.3 0.1 add_convert_fusion
  78.4 0.1 reshape.10
  78.6 22.3 %all_to_all.5 = bf16[32,16,256]{2,1,0:T(8,128)(2,1)S(1)} all-to-all(bf16[32,16,256]{2,1,0:T(8,128)(2,1)S(1)} %pad.14), channel_id=1, replica_groups=mesh['ylo'=2,'x'=4,'core'=2,'z'=8,'yhi'=2] {'ylo','z','yhi'}, dimensions={0} | all-to-all | bytes 524288 | tf_op jit(solution)/shard_map/all_to_all | solution.py:343
  100.9 0.6 pad_maximum_fusion
  (17 shorter events, 0.3 us)
Async XLA Ops:
  0.6 45.5 %copy-start.2 = (s32[1,16]{1,0:T(1,128)S(1)}, s32[1,16]{1,0:T(1,128)}, u32[]{:S(2)}) copy-start(s32[1,16]{1,0:T(1,128)} %assign_ref.1) | copy-start | bytes 196
  0.6 45.4 %copy-start.3 = (s32[1,4]{1,0:T(1,128)S(1)}, s32[1,4]{1,0:T(1,128)}, u32[]{:S(2)}) copy-start(s32[1,4]{1,0:T(1,128)} %length_ref.1) | copy-start | bytes 52
  0.7 45.4 %copy-start.1 = (bf16[128,512]{1,0:T(8,128)(2,1)S(1)}, bf16[128,512]{1,0:T(8,128)(2,1)}, u32[]{:S(2)}) copy-start(bf16[128,512]{1,0:T(8,128)(2,1)} %q_ref.1) | copy-start | bytes 393220
  1.5 11.4 %collective-permute-start = (bf16[128,256]{1,0:T(8,128)(2,1)S(1)}, bf16[128,256]{1,0:T(8,128)(2,1)S(1)}, u32[]{:S(2)}, u32[]{:S(2)}) collective-permute-start(bf16[128,256]{1,0:T(8,128)(2,1)S(1)} %pad_select_fusion.kv_ref), channel_id=1, source_target_pairs={{0,1},{1,0},{2,3},{3,2},{4,5},{5,4},{6,7},{7,6},{8,9},{9,8},{10,11... | collective-permute-start | bytes 196616 | tf_op jit(solution)/shard_map/ppermute | solution.py:279
  5.5 4.8 %collective-permute-start.1 = (bf16[14,256]{1,0:T(8,128)(2,1)S(1)}, bf16[14,256]{1,0:T(8,128)(2,1)S(1)}, u32[]{:S(2)}, u32[]{:S(2)}) collective-permute-start(bf16[14,256]{1,0:T(8,128)(2,1)S(1)} %get-tuple-element.58), channel_id=1, source_target_pairs={{0,128},{128,0},{1,129},{129,1},{2,130},{130,2},{3,131},{131,3},{4... | collective-permute-start | bytes 21512 | tf_op jit(solution)/shard_map/ppermute | solution.py:279
  6.2 5.2 %collective-permute-start.2 = (bf16[14,256]{1,0:T(8,128)(2,1)S(1)}, bf16[14,256]{1,0:T(8,128)(2,1)S(1)}, u32[]{:S(2)}, u32[]{:S(2)}) collective-permute-start(bf16[14,256]{1,0:T(8,128)(2,1)S(1)} %get-tuple-element.59.refs_0_), channel_id=1, source_target_pairs={{0,1},{1,0},{2,3},{3,2},{4,5},{5,4},{6,7},{7,6},{8,9},{9,8},{10,11... | collective-permute-start | bytes 21512 | tf_op jit(solution)/shard_map/ppermute | solution.py:279
  8.0 4.9 %collective-permute-start.3 = (bf16[14,256]{1,0:T(8,128)(2,1)S(1)}, bf16[14,256]{1,0:T(8,128)(2,1)S(1)}, u32[]{:S(2)}, u32[]{:S(2)}) collective-permute-start(bf16[14,256]{1,0:T(8,128)(2,1)S(1)} %get-tuple-element.58), channel_id=1, source_target_pairs={{0,129},{1,128},{128,1},{129,0},{2,131},{3,130},{130,3},{131,2},{4... | collective-permute-start | bytes 21512 | tf_op jit(solution)/shard_map/ppermute | solution.py:302
  12.9 5.6 %collective-permute-start.4 = (bf16[320,256]{1,0:T(8,128)(2,1)S(1)}, bf16[320,256]{1,0:T(8,128)(2,1)S(1)}, u32[]{:S(2)}, u32[]{:S(2)}) collective-permute-start(bf16[320,256]{1,0:T(8,128)(2,1)S(1)} %pack.1.refs_0_), channel_id=1, source_target_pairs={{2,0},{4,2},{6,4},{8,6},{10,8},{12,10},{14,12},{0,14},{3,1},{5,3},... | collective-permute-start | bytes 491528 | tf_op jit(solution)/shard_map/ppermute | solution.py:284
  13.1 9.2 %collective-permute-start.5 = (bf16[320,256]{1,0:T(8,128)(2,1)S(1)}, bf16[320,256]{1,0:T(8,128)(2,1)S(1)}, u32[]{:S(2)}, u32[]{:S(2)}) collective-permute-start(bf16[320,256]{1,0:T(8,128)(2,1)S(1)} %pack.1.refs_0_), channel_id=1, source_target_pairs={{14,0},{0,2},{2,4},{4,6},{6,8},{8,10},{10,12},{12,14},{15,1},{1,3}... | collective-permute-start | bytes 491528 | tf_op jit(solution)/shard_map/ppermute | solution.py:284
  15.0 1.2 %copy-start = (bf16[128,3584]{1,0:T(8,128)(2,1)S(1)}, bf16[128,3584]{1,0:T(8,128)(2,1)}, u32[]{:S(2)}) copy-start(bf16[128,3584]{1,0:T(8,128)(2,1)} %refs_1_) | copy-start | bytes 2752516
  22.3 22.9 %collective-permute-start.11 = (bf16[128,2048]{1,0:T(8,128)(2,1)S(1)}, bf16[128,2048]{1,0:T(8,128)(2,1)S(1)}, u32[]{:S(2)}, u32[]{:S(2)}) collective-permute-start(bf16[128,2048]{1,0:T(8,128)(2,1)S(1)} %get-tuple-element.34), channel_id=1, source_target_pairs={{0,128},{128,0},{1,129},{129,1},{2,130},{130,2},{3,131},{131,3},{4... | collective-permute-start | bytes 1572872 | tf_op jit(solution)/shard_map/ppermute | solution.py:279
  22.3 6.1 %collective-permute-start.6 = (bf16[320,256]{1,0:T(8,128)(2,1)S(1)}, bf16[320,256]{1,0:T(8,128)(2,1)S(1)}, u32[]{:S(2)}, u32[]{:S(2)}) collective-permute-start(bf16[320,256]{1,0:T(8,128)(2,1)S(1)} %collective-permute-done.4.refs_1_), channel_id=1, source_target_pairs={{2,0},{4,2},{6,4},{8,6},{10,8},{12,10},{14,12},{0,14},{3,1},{5,3},... | collective-permute-start | bytes 491528 | tf_op jit(solution)/shard_map/ppermute | solution.py:284
  25.6 5.3 %collective-permute-start.7 = (bf16[320,256]{1,0:T(8,128)(2,1)S(1)}, bf16[320,256]{1,0:T(8,128)(2,1)S(1)}, u32[]{:S(2)}, u32[]{:S(2)}) collective-permute-start(bf16[320,256]{1,0:T(8,128)(2,1)S(1)} %collective-permute-done.5.refs_2_), channel_id=1, source_target_pairs={{14,0},{0,2},{2,4},{4,6},{6,8},{8,10},{10,12},{12,14},{15,1},{1,3}... | collective-permute-start | bytes 491528 | tf_op jit(solution)/shard_map/ppermute | solution.py:284
  28.5 22.1 %collective-permute-start.13 = (bf16[128,2048]{1,0:T(8,128)(2,1)S(1)}, bf16[128,2048]{1,0:T(8,128)(2,1)S(1)}, u32[]{:S(2)}, u32[]{:S(2)}) collective-permute-start(bf16[128,2048]{1,0:T(8,128)(2,1)S(1)} %get-tuple-element.46), channel_id=1, source_target_pairs={{0,144},{16,128},{128,16},{144,0},{1,145},{17,129},{129,17},{145,1... | collective-permute-start | bytes 1572872 | tf_op jit(solution)/shard_map/ppermute | solution.py:319
  28.5 5.9 %collective-permute-start.8 = (bf16[320,256]{1,0:T(8,128)(2,1)S(1)}, bf16[320,256]{1,0:T(8,128)(2,1)S(1)}, u32[]{:S(2)}, u32[]{:S(2)}) collective-permute-start(bf16[320,256]{1,0:T(8,128)(2,1)S(1)} %collective-permute-done.6.refs_3_), channel_id=1, source_target_pairs={{2,0},{4,2},{6,4},{8,6},{10,8},{12,10},{14,12},{0,14},{3,1},{5,3},... | collective-permute-start | bytes 491528 | tf_op jit(solution)/shard_map/ppermute | solution.py:284
  30.9 10.6 %collective-permute-start.9 = (bf16[320,256]{1,0:T(8,128)(2,1)S(1)}, bf16[320,256]{1,0:T(8,128)(2,1)S(1)}, u32[]{:S(2)}, u32[]{:S(2)}) collective-permute-start(bf16[320,256]{1,0:T(8,128)(2,1)S(1)} %collective-permute-done.7.refs_4_), channel_id=1, source_target_pairs={{14,0},{0,2},{2,4},{4,6},{6,8},{8,10},{10,12},{12,14},{15,1},{1,3}... | collective-permute-start | bytes 491528 | tf_op jit(solution)/shard_map/ppermute | solution.py:284
  34.3 6.7 %collective-permute-start.10 = (bf16[320,256]{1,0:T(8,128)(2,1)S(1)}, bf16[320,256]{1,0:T(8,128)(2,1)S(1)}, u32[]{:S(2)}, u32[]{:S(2)}) collective-permute-start(bf16[320,256]{1,0:T(8,128)(2,1)S(1)} %collective-permute-done.8.refs_5_), channel_id=1, source_target_pairs={{2,0},{4,2},{6,4},{8,6},{10,8},{12,10},{14,12},{0,14},{3,1},{5,3},... | collective-permute-start | bytes 491528 | tf_op jit(solution)/shard_map/ppermute | solution.py:284
  41.1 8.8 %collective-permute-start.12 = (bf16[128,2048]{1,0:T(8,128)(2,1)S(1)}, bf16[128,2048]{1,0:T(8,128)(2,1)S(1)}, u32[]{:S(2)}, u32[]{:S(2)}) collective-permute-start(bf16[128,2048]{1,0:T(8,128)(2,1)S(1)} %get-tuple-element.46), channel_id=1, source_target_pairs={{0,16},{16,0},{1,17},{17,1},{2,18},{18,2},{3,19},{19,3},{4,20},{20... | collective-permute-start | bytes 1572872 | tf_op jit(solution)/shard_map/ppermute | solution.py:279
  41.6 14.3 %collective-permute-start.15 = (bf16[512,256]{1,0:T(8,128)(2,1)S(1)}, bf16[512,256]{1,0:T(8,128)(2,1)S(1)}, u32[]{:S(2)}, u32[]{:S(2)}) collective-permute-start(bf16[512,256]{1,0:T(8,128)(2,1)S(1)} %slice_dynamic-update-slice_fusion.refs_0_), channel_id=1, source_target_pairs={{32,0},{64,32},{96,64},{0,96},{33,1},{65,33},{97,65},{1,97},{34,2}... | collective-permute-start | bytes 786440 | tf_op jit(solution)/shard_map/ppermute | solution.py:284
  44.4 11.4 %collective-permute-start.16 = (bf16[512,256]{1,0:T(8,128)(2,1)S(1)}, bf16[512,256]{1,0:T(8,128)(2,1)S(1)}, u32[]{:S(2)}, u32[]{:S(2)}) collective-permute-start(bf16[512,256]{1,0:T(8,128)(2,1)S(1)} %slice_dynamic-update-slice_fusion.refs_0_), channel_id=1, source_target_pairs={{64,0},{96,32},{0,64},{32,96},{65,1},{97,33},{1,65},{33,97},{66,2}... | collective-permute-start | bytes 786440 | tf_op jit(solution)/shard_map/ppermute | solution.py:284
  45.2 14.3 %collective-permute-start.17 = (bf16[512,256]{1,0:T(8,128)(2,1)S(1)}, bf16[512,256]{1,0:T(8,128)(2,1)S(1)}, u32[]{:S(2)}, u32[]{:S(2)}) collective-permute-start(bf16[512,256]{1,0:T(8,128)(2,1)S(1)} %slice_dynamic-update-slice_fusion.refs_0_), channel_id=1, source_target_pairs={{96,0},{0,32},{32,64},{64,96},{97,1},{1,33},{33,65},{65,97},{98,2}... | collective-permute-start | bytes 786440 | tf_op jit(solution)/shard_map/ppermute | solution.py:284
  49.9 4.3 %collective-permute-start.14 = (bf16[128,256]{1,0:T(8,128)(2,1)S(1)}, bf16[128,256]{1,0:T(8,128)(2,1)S(1)}, u32[]{:S(2)}, u32[]{:S(2)}) collective-permute-start(bf16[128,256]{1,0:T(8,128)(2,1)S(1)} %get-tuple-element.48), channel_id=1, source_target_pairs={{0,128},{128,0},{1,129},{129,1},{2,130},{130,2},{3,131},{131,3},{4... | collective-permute-start | bytes 196616 | tf_op jit(solution)/shard_map/ppermute | solution.py:279
  61.0 1.6 %collective-permute-start.18 = (bf16[512,256]{1,0:T(8,128)(2,1)S(1)}, bf16[512,256]{1,0:T(8,128)(2,1)S(1)}, u32[]{:S(2)}, u32[]{:S(2)}) collective-permute-start(bf16[512,256]{1,0:T(8,128)(2,1)S(1)} %get-tuple-element.50), channel_id=1, source_target_pairs={{0,16},{16,0},{1,17},{17,1},{2,18},{18,2},{3,19},{19,3},{4,20},{20... | collective-permute-start | bytes 786440 | tf_op jit(solution)/shard_map/ppermute | solution.py:279
  64.2 12.1 %collective-permute-start.20 = (bf16[448,256]{1,0:T(8,128)(2,1)S(1)}, bf16[448,256]{1,0:T(8,128)(2,1)S(1)}, u32[]{:S(2)}, u32[]{:S(2)}) collective-permute-start(bf16[448,256]{1,0:T(8,128)(2,1)S(1)} %get-tuple-element.51), channel_id=1, source_target_pairs={{64,0},{96,32},{0,64},{32,96},{65,1},{97,33},{1,65},{33,97},{66,2}... | collective-permute-start | bytes 688136 | tf_op jit(solution)/shard_map/ppermute | solution.py:284
  66.6 9.6 %collective-permute-start.21 = (bf16[448,256]{1,0:T(8,128)(2,1)S(1)}, bf16[448,256]{1,0:T(8,128)(2,1)S(1)}, u32[]{:S(2)}, u32[]{:S(2)}) collective-permute-start(bf16[448,256]{1,0:T(8,128)(2,1)S(1)} %get-tuple-element.55), channel_id=1, source_target_pairs={{32,0},{64,32},{96,64},{0,96},{33,1},{65,33},{97,65},{1,97},{34,2}... | collective-permute-start | bytes 688136 | tf_op jit(solution)/shard_map/ppermute | solution.py:284
  67.9 10.4 %collective-permute-start.19 = (bf16[448,256]{1,0:T(8,128)(2,1)S(1)}, bf16[448,256]{1,0:T(8,128)(2,1)S(1)}, u32[]{:S(2)}, u32[]{:S(2)}) collective-permute-start(bf16[448,256]{1,0:T(8,128)(2,1)S(1)} %get-tuple-element.54), channel_id=1, source_target_pairs={{96,0},{0,32},{32,64},{64,96},{97,1},{1,33},{33,65},{65,97},{98,2}... | collective-permute-start | bytes 688136 | tf_op jit(solution)/shard_map/ppermute | solution.py:284

commit v14 on v12

--- a/solution.py
+++ b/solution.py
@@ -327,11 +327,11 @@
 
     own, send = project(here, n_all, a_mine, partner(a_other, "ylo"), w_all)
     back = partner(send, "core")
-    far, left = gradient(here, n_all, own, back, wrows, (2, 3))
-    arrived = [from_next(left, "x", 3), from_next(far, "x", 2)]
+    (far,) = gradient(here, n_all, own, back, wrows, (2,))
+    arrived = [from_next(far, "x", 2)]
     back, _ = lax.optimization_barrier((back, far))
-    near, right = gradient(here, n_all, own, back, wrows, (0, 1))
-    arrived.append(from_next(right, "x", 1))
+    near, right, left = gradient(here, n_all, own, back, wrows, (0, 1, 3))
+    arrived += [from_next(left, "x", 3), from_next(right, "x", 1)]
     near = near.astype(jnp.float32)
     for block in arrived:
         near = near + block.astype(jnp.float32)

time: 95.7 us -> 97 us (1.014)
  waiting for transfers between devices: 27.2 us -> 30.2 us
    ppermute x13, waiting for transfers between devices: 20.9 us -> 23.9 us  [from_next(): lax.ppermute(x, axis, [((i + distance) % size, i) for i in range(size)])]
  transfers between devices with their start and end apart: 22 -> 22, of which waited for: 12 -> 12; matrix products, arithmetic and copies ran while one was open for 1% -> 1% of each run, Pallas kernels for 8% -> 6%
where the time goes in v14:
time: 97 us; the launch traced here: 96.7 us
  waiting for transfers between devices  30.2 us (31%)
  starting transfers between devices  30 us (31%)
  blocking collectives  21.3 us (22%)
  Pallas kernels  10.4 us (11%)
  other arithmetic  2.29 us (2%)
  local copies, waits for them, and re-layouts  1.56 us (2%)
    ppermute x13, waiting for transfers between devices, from_next(): lax.ppermute(x, axis, [((i + distance) % size, i) for i in range(size)])  23.9 us
    all_to_all x1, blocking collectives, local(): lax.all_to_all(near, ('ylo', *SEQ), split_axis=0, concat_axis=0, tiled=True)  21.3 us
    ppermute x13, starting transfers between devices, from_next(): lax.ppermute(x, axis, [((i + distance) % size, i) for i in range(size)])  17.9 us
    ppermute x8, starting transfers between devices, partner(): return lax.ppermute(x, axis, [(0, 1), (1, 0)])  9.95 us
    ppermute x8, waiting for transfers between devices, partner(): return lax.ppermute(x, axis, [(0, 1), (1, 0)])  4.77 us
    pallas_call x1, Pallas kernels, attend(): pl.pallas_call(attend_kernel, out_shape=(jax.ShapeDtypeStruct((rows, COLS...  3.77 us
    pallas_call x2, Pallas kernels, gradient(): pl.pallas_call(body, out_shape=(shape,) * len(steps), in_specs=[SMEM, VME...  2.86 us
    pallas_call x1, Pallas kernels, normalise(): pl.pallas_call(body, out_shape=(shape, shape), in_specs=[SMEM, VMEM], out...  2.32 us
  transfers between devices with their start and end apart: 22, of which 12 were waited for; matrix products, arithmetic and copies ran while one was open for 1% of the time, Pallas kernels for 6%

profile of v14, /device:TPU:32, one launch (start us, length us, event | category | flops | bytes accessed | tf_op | source)
XLA Modules:
  0.0 96.7 jit_solution(5433944798490106509)
XLA Ops:
  0.6 0.8 pad_select_fusion.kv_ref
  1.4 3.3 %collective-permute-start = (bf16[128,256]{1,0:T(8,128)(2,1)S(1)}, bf16[128,256]{1,0:T(8,128)(2,1)S(1)}, u32[]{:S(2)}, u32[]{:S(2)}) collective-permute-start(bf16[128,256]{1,0:T(8,128)(2,1)S(1)} %pad_select_fusion.kv_ref), channel_id=1, source_target_pairs={{0,1},{1,0},{2,3},{3,2},{4,5},{5,4},{6,7},{7,6},{8,9},{9,8},{10,11... | collective-permute-start | bytes 196616 | tf_op jit(solution)/shard_map/ppermute | solution.py:279
  4.7 0.7 broadcast_select_fusion
  5.4 0.7 collective-permute-start.1
  6.1 1.8 %collective-permute-start.2 = (bf16[14,256]{1,0:T(8,128)(2,1)S(1)}, bf16[14,256]{1,0:T(8,128)(2,1)S(1)}, u32[]{:S(2)}, u32[]{:S(2)}) collective-permute-start(bf16[14,256]{1,0:T(8,128)(2,1)S(1)} %get-tuple-element.57.refs_0_), channel_id=1, source_target_pairs={{0,1},{1,0},{2,3},{3,2},{4,5},{5,4},{6,7},{7,6},{8,9},{9,8},{10,11... | collective-permute-start | bytes 21512 | tf_op jit(solution)/shard_map/ppermute | solution.py:279
  8.0 2.2 %collective-permute-start.3 = (bf16[14,256]{1,0:T(8,128)(2,1)S(1)}, bf16[14,256]{1,0:T(8,128)(2,1)S(1)}, u32[]{:S(2)}, u32[]{:S(2)}) collective-permute-start(bf16[14,256]{1,0:T(8,128)(2,1)S(1)} %get-tuple-element.56), channel_id=1, source_target_pairs={{0,129},{1,128},{128,1},{129,0},{2,131},{3,130},{130,3},{131,2},{4... | collective-permute-start | bytes 21512 | tf_op jit(solution)/shard_map/ppermute | solution.py:302
  10.1 0.1 stack.23.refs_0_.where_ref
  10.2 0.0 collective-permute-done.1.refs_1_
  10.2 1.0 %collective-permute-done.2.refs_2_ = bf16[14,256]{1,0:T(8,128)(2,1)S(1)} collective-permute-done((bf16[14,256]{1,0:T(8,128)(2,1)S(1)}, bf16[14,256]{1,0:T(8,128)(2,1)S(1)}, u32[]{:S(2)}, u32[]{:S(2)}) %collective-permute-start.2) | collective-permute-done | bytes 7200 | tf_op jit(solution)/shard_map/ppermute | solution.py:279
  11.3 1.5 %collective-permute-done.3.refs_3_ = bf16[14,256]{1,0:T(8,128)(2,1)S(1)} collective-permute-done((bf16[14,256]{1,0:T(8,128)(2,1)S(1)}, bf16[14,256]{1,0:T(8,128)(2,1)S(1)}, u32[]{:S(2)}, u32[]{:S(2)}) %collective-permute-start.3) | collective-permute-done | bytes 7200 | tf_op jit(solution)/shard_map/ppermute | solution.py:302
  12.8 0.0 collective-permute-done.kv_other_ref
  12.8 0.0 copy-start.1
  12.8 0.0 copy-start.2
  12.8 0.0 copy-start.3
  12.9 0.2 collective-permute-start.4
  13.0 1.9 %collective-permute-start.5 = (bf16[320,256]{1,0:T(8,128)(2,1)S(1)}, bf16[320,256]{1,0:T(8,128)(2,1)S(1)}, u32[]{:S(2)}, u32[]{:S(2)}) collective-permute-start(bf16[320,256]{1,0:T(8,128)(2,1)S(1)} %pack.1.refs_0_), channel_id=1, source_target_pairs={{14,0},{0,2},{2,4},{4,6},{6,8},{8,10},{10,12},{12,14},{15,1},{1,3}... | collective-permute-start | bytes 491528 | tf_op jit(solution)/shard_map/ppermute | solution.py:284
  15.0 0.0 copy-start
  15.0 1.2 %copy-done = bf16[128,3584]{1,0:T(8,128)(2,1)S(1)} copy-done((bf16[128,3584]{1,0:T(8,128)(2,1)S(1)}, bf16[128,3584]{1,0:T(8,128)(2,1)}, u32[]{:S(2)}) %copy-start) | copy-done | bytes 917528
  16.1 2.3 %normalise.1 = (bf16[128,2048]{1,0:T(8,128)(2,1)S(1)}, bf16[128,2048]{1,0:T(8,128)(2,1)S(1)}) custom-call(s32[5]{0:T(128)S(1)} %stack.23.refs_0_.where_ref, bf16[128,3584]{1,0:T(8,128)(2,1)S(1)} %copy-done), custom_call_target="tpu_custom_call" | custom-call | tf_op jit(solution)/shard_map/normalise/pallas_call | solution.py:78
  18.5 0.0 collective-permute-done.4.refs_1_
  18.5 3.7 %collective-permute-done.5.refs_2_ = bf16[320,256]{1,0:T(8,128)(2,1)S(1)} collective-permute-done((bf16[320,256]{1,0:T(8,128)(2,1)S(1)}, bf16[320,256]{1,0:T(8,128)(2,1)S(1)}, u32[]{:S(2)}, u32[]{:S(2)}) %collective-permute-start.5) | collective-permute-done | bytes 163872 | tf_op jit(solution)/shard_map/ppermute | solution.py:284
  22.2 0.0 collective-permute-start.12
  22.2 3.3 %collective-permute-start.6 = (bf16[320,256]{1,0:T(8,128)(2,1)S(1)}, bf16[320,256]{1,0:T(8,128)(2,1)S(1)}, u32[]{:S(2)}, u32[]{:S(2)}) collective-permute-start(bf16[320,256]{1,0:T(8,128)(2,1)S(1)} %collective-permute-done.4.refs_1_), channel_id=1, source_target_pairs={{2,0},{4,2},{6,4},{8,6},{10,8},{12,10},{14,12},{0,14},{3,1},{5,3},... | collective-permute-start | bytes 491528 | tf_op jit(solution)/shard_map/ppermute | solution.py:284
  25.6 0.0 collective-permute-start.7
  25.6 0.0 collective-permute-start.9
  25.6 2.8 %collective-permute-done.6.refs_3_ = bf16[320,256]{1,0:T(8,128)(2,1)S(1)} collective-permute-done((bf16[320,256]{1,0:T(8,128)(2,1)S(1)}, bf16[320,256]{1,0:T(8,128)(2,1)S(1)}, u32[]{:S(2)}, u32[]{:S(2)}) %collective-permute-start.6) | collective-permute-done | bytes 163872 | tf_op jit(solution)/shard_map/ppermute | solution.py:284
  28.4 2.5 %collective-permute-start.8 = (bf16[320,256]{1,0:T(8,128)(2,1)S(1)}, bf16[320,256]{1,0:T(8,128)(2,1)S(1)}, u32[]{:S(2)}, u32[]{:S(2)}) collective-permute-start(bf16[320,256]{1,0:T(8,128)(2,1)S(1)} %collective-permute-done.6.refs_3_), channel_id=1, source_target_pairs={{2,0},{4,2},{6,4},{8,6},{10,8},{12,10},{14,12},{0,14},{3,1},{5,3},... | collective-permute-start | bytes 491528 | tf_op jit(solution)/shard_map/ppermute | solution.py:284
  30.9 0.3 collective-permute-done.7.refs_4_
  31.2 0.0 collective-permute-start.10
  31.2 3.4 %collective-permute-done.8.refs_5_ = bf16[320,256]{1,0:T(8,128)(2,1)S(1)} collective-permute-done((bf16[320,256]{1,0:T(8,128)(2,1)S(1)}, bf16[320,256]{1,0:T(8,128)(2,1)S(1)}, u32[]{:S(2)}, u32[]{:S(2)}) %collective-permute-start.8) | collective-permute-done | bytes 163872 | tf_op jit(solution)/shard_map/ppermute | solution.py:284
  34.6 0.0 collective-permute-done.9
  34.6 2.5 %collective-permute-start.11 = (bf16[320,256]{1,0:T(8,128)(2,1)S(1)}, bf16[320,256]{1,0:T(8,128)(2,1)S(1)}, u32[]{:S(2)}, u32[]{:S(2)}) collective-permute-start(bf16[320,256]{1,0:T(8,128)(2,1)S(1)} %collective-permute-done.8.refs_5_), channel_id=1, source_target_pairs={{2,0},{4,2},{6,4},{8,6},{10,8},{12,10},{14,12},{0,14},{3,1},{5,3},... | collective-permute-start | bytes 491528 | tf_op jit(solution)/shard_map/ppermute | solution.py:284
  37.1 2.0 %collective-permute-start.13 = (bf16[128,2048]{1,0:T(8,128)(2,1)S(1)}, bf16[128,2048]{1,0:T(8,128)(2,1)S(1)}, u32[]{:S(2)}, u32[]{:S(2)}) collective-permute-start(bf16[128,2048]{1,0:T(8,128)(2,1)S(1)} %collective-permute-done.9), channel_id=1, source_target_pairs={{0,128},{128,0},{1,129},{129,1},{2,130},{130,2},{3,131},{131,3},{4... | collective-permute-start | bytes 1572872 | tf_op jit(solution)/shard_map/ppermute | solution.py:279
  39.2 0.0 collective-permute-done.10.refs_6_
  39.2 0.7 collective-permute-done.11.refs_7_
  40.0 2.8 %collective-permute-start.15 = (bf16[512,256]{1,0:T(8,128)(2,1)S(1)}, bf16[512,256]{1,0:T(8,128)(2,1)S(1)}, u32[]{:S(2)}, u32[]{:S(2)}) collective-permute-start(bf16[512,256]{1,0:T(8,128)(2,1)S(1)} %slice_dynamic-update-slice_fusion.refs_0_), channel_id=1, source_target_pairs={{32,0},{64,32},{96,64},{0,96},{33,1},{65,33},{97,65},{1,97},{34,2}... | collective-permute-start | bytes 786440 | tf_op jit(solution)/shard_map/ppermute | solution.py:284
  42.7 0.8 collective-permute-start.16
  43.5 0.9 collective-permute-start.17
  44.4 0.0 collective-permute-done.12
  44.4 0.0 copy-done.1
  44.5 0.0 copy-done.2
  44.5 0.0 copy-done.3
  44.5 3.8 %attend.1 = (bf16[128,512]{1,0:T(8,128)(2,1)}, bf16[128,256]{1,0:T(8,128)(2,1)S(1)}, bf16[128,256]{1,0:T(8,128)(2,1)S(1)}) custom-call(s32[5]{0:T(128)S(1)} %stack.23.refs_0_.where_ref, s32[1,16]{1,0:T(1,128)S(1)} %copy-done.2, s32[1,4]{1,0:T(1,128)S(1)} %copy-done.3, bf16[128,512]{1,0:T(8,128)(2,1)S(1)} %copy-done.1, bf16[320,256]{1,0:T(8,128)(2,1)S(1)} %pack.1.refs_0_, ...), custom_call_target="tpu_custom_call" | custom-call | tf_op jit(solution)/shard_map/attend/pallas_call | solution.py:173
  48.2 2.0 %collective-permute-start.14 = (bf16[128,256]{1,0:T(8,128)(2,1)S(1)}, bf16[128,256]{1,0:T(8,128)(2,1)S(1)}, u32[]{:S(2)}, u32[]{:S(2)}) collective-permute-start(bf16[128,256]{1,0:T(8,128)(2,1)S(1)} %get-tuple-element.47), channel_id=1, source_target_pairs={{0,128},{128,0},{1,129},{129,1},{2,130},{130,2},{3,131},{131,3},{4... | collective-permute-start | bytes 196616 | tf_op jit(solution)/shard_map/ppermute | solution.py:279
  50.3 0.0 collective-permute-done.13
  50.3 2.2 %collective-permute-done.14.got_ref = bf16[128,256]{1,0:T(8,128)(2,1)S(1)} collective-permute-done((bf16[128,256]{1,0:T(8,128)(2,1)S(1)}, bf16[128,256]{1,0:T(8,128)(2,1)S(1)}, u32[]{:S(2)}, u32[]{:S(2)}) %collective-permute-start.14) | collective-permute-done | bytes 65568 | tf_op jit(solution)/shard_map/ppermute | solution.py:279
  52.5 0.0 collective-permute-done.15.refs_1_
  52.5 0.0 collective-permute-done.16.refs_2_
  52.5 0.9 collective-permute-done.17.refs_3_
  53.5 1.5 %project.1 = (f32[512,256]{1,0:T(8,128)S(1)}, bf16[512,256]{1,0:T(8,128)(2,1)S(1)}) custom-call(s32[5]{0:T(128)S(1)} %stack.23.refs_0_.where_ref, bf16[512,2048]{1,0:T(8,128)(2,1)S(1)} %constant_dynamic-update-slice_fusion.n_ref.refs_1_, bf16[128,256]{1,0:T(8,128)(2,1)S(1)} %get-tuple-element.46.mine_ref, ...), custom_call_target="tpu_custom_call" | custom-call | tf_op jit(solution)/shard_map/project/pallas_call | solution.py:215
  55.0 0.1 collective-permute-start.18
  55.1 1.5 %collective-permute-done.18.refs_3_ = bf16[512,256]{1,0:T(8,128)(2,1)S(1)} collective-permute-done((bf16[512,256]{1,0:T(8,128)(2,1)S(1)}, bf16[512,256]{1,0:T(8,128)(2,1)S(1)}, u32[]{:S(2)}, u32[]{:S(2)}) %collective-permute-start.18) | collective-permute-done | bytes 262176 | tf_op jit(solution)/shard_map/ppermute | solution.py:279
  56.6 1.1 %gradient.2 = bf16[448,256]{1,0:T(8,128)(2,1)S(1)} custom-call(s32[5]{0:T(128)S(1)} %stack.23.refs_0_.where_ref, bf16[512,2048]{1,0:T(8,128)(2,1)S(1)} %constant_dynamic-update-slice_fusion.n_ref.refs_1_, f32[512,256]{1,0:T(8,128)S(1)} %get-tuple-element.48.refs_2_, bf16[512,256]{1,0:T(8,128)(2,1)S(1)} %collective-permute-done.18.refs_3_), custom_call_target="tpu_custom_call" | custom-call | tf_op jit(solution)/shard_map/gradient/pallas_call | solution.py:268
  57.7 1.8 %gradient.3 = (bf16[448,256]{1,0:T(8,128)(2,1)S(1)}, bf16[448,256]{1,0:T(8,128)(2,1)S(1)}, bf16[448,256]{1,0:T(8,128)(2,1)S(1)}) custom-call(s32[5]{0:T(128)S(1)} %stack.23.refs_0_.where_ref, bf16[512,2048]{1,0:T(8,128)(2,1)S(1)} %constant_dynamic-update-slice_fusion.n_ref.refs_1_, f32[512,256]{1,0:T(8,128)S(1)} %get-tuple-element.48.refs_2_, ...), custom_call_target="tpu_custom_call" | custom-call | tf_op jit(solution)/shard_map/gradient/pallas_call | solution.py:268
  59.5 1.5 %collective-permute-start.21 = (bf16[448,256]{1,0:T(8,128)(2,1)S(1)}, bf16[448,256]{1,0:T(8,128)(2,1)S(1)}, u32[]{:S(2)}, u32[]{:S(2)}) collective-permute-start(bf16[448,256]{1,0:T(8,128)(2,1)S(1)} %get-tuple-element.53), channel_id=1, source_target_pairs={{32,0},{64,32},{96,64},{0,96},{33,1},{65,33},{97,65},{1,97},{34,2}... | collective-permute-start | bytes 688136 | tf_op jit(solution)/shard_map/ppermute | solution.py:284
  60.9 0.6 collective-permute-start.20
  61.6 0.9 collective-permute-start.19
  62.5 5.5 %collective-permute-done.21 = bf16[448,256]{1,0:T(8,128)(2,1)S(1)} collective-permute-done((bf16[448,256]{1,0:T(8,128)(2,1)S(1)}, bf16[448,256]{1,0:T(8,128)(2,1)S(1)}, u32[]{:S(2)}, u32[]{:S(2)}) %collective-permute-start.21) | collective-permute-done | bytes 229408 | tf_op jit(solution)/shard_map/ppermute | solution.py:284
  68.0 6.5 %collective-permute-done.20 = bf16[448,256]{1,0:T(8,128)(2,1)S(1)} collective-permute-done((bf16[448,256]{1,0:T(8,128)(2,1)S(1)}, bf16[448,256]{1,0:T(8,128)(2,1)S(1)}, u32[]{:S(2)}, u32[]{:S(2)}) %collective-permute-start.20) | collective-permute-done | bytes 229408 | tf_op jit(solution)/shard_map/ppermute | solution.py:284
  74.4 0.0 collective-permute-done.19
  74.4 0.1 add_convert_fusion
  74.6 0.1 reshape.10
  74.7 21.3 %all_to_all.5 = bf16[32,16,256]{2,1,0:T(8,128)(2,1)S(1)} all-to-all(bf16[32,16,256]{2,1,0:T(8,128)(2,1)S(1)} %pad.14), channel_id=1, replica_groups=mesh['ylo'=2,'x'=4,'core'=2,'z'=8,'yhi'=2] {'ylo','z','yhi'}, dimensions={0} | all-to-all | bytes 524288 | tf_op jit(solution)/shard_map/all_to_all | solution.py:340
  96.1 0.6 pad_maximum_fusion
  (17 shorter events, 0.3 us)
Async XLA Ops:
  1.4 11.4 %collective-permute-start = (bf16[128,256]{1,0:T(8,128)(2,1)S(1)}, bf16[128,256]{1,0:T(8,128)(2,1)S(1)}, u32[]{:S(2)}, u32[]{:S(2)}) collective-permute-start(bf16[128,256]{1,0:T(8,128)(2,1)S(1)} %pad_select_fusion.kv_ref), channel_id=1, source_target_pairs={{0,1},{1,0},{2,3},{3,2},{4,5},{5,4},{6,7},{7,6},{8,9},{9,8},{10,11... | collective-permute-start | bytes 196616 | tf_op jit(solution)/shard_map/ppermute | solution.py:279
  5.4 4.8 %collective-permute-start.1 = (bf16[14,256]{1,0:T(8,128)(2,1)S(1)}, bf16[14,256]{1,0:T(8,128)(2,1)S(1)}, u32[]{:S(2)}, u32[]{:S(2)}) collective-permute-start(bf16[14,256]{1,0:T(8,128)(2,1)S(1)} %get-tuple-element.56), channel_id=1, source_target_pairs={{0,128},{128,0},{1,129},{129,1},{2,130},{130,2},{3,131},{131,3},{4... | collective-permute-start | bytes 21512 | tf_op jit(solution)/shard_map/ppermute | solution.py:279
  6.1 5.2 %collective-permute-start.2 = (bf16[14,256]{1,0:T(8,128)(2,1)S(1)}, bf16[14,256]{1,0:T(8,128)(2,1)S(1)}, u32[]{:S(2)}, u32[]{:S(2)}) collective-permute-start(bf16[14,256]{1,0:T(8,128)(2,1)S(1)} %get-tuple-element.57.refs_0_), channel_id=1, source_target_pairs={{0,1},{1,0},{2,3},{3,2},{4,5},{5,4},{6,7},{7,6},{8,9},{9,8},{10,11... | collective-permute-start | bytes 21512 | tf_op jit(solution)/shard_map/ppermute | solution.py:279
  8.0 4.9 %collective-permute-start.3 = (bf16[14,256]{1,0:T(8,128)(2,1)S(1)}, bf16[14,256]{1,0:T(8,128)(2,1)S(1)}, u32[]{:S(2)}, u32[]{:S(2)}) collective-permute-start(bf16[14,256]{1,0:T(8,128)(2,1)S(1)} %get-tuple-element.56), channel_id=1, source_target_pairs={{0,129},{1,128},{128,1},{129,0},{2,131},{3,130},{130,3},{131,2},{4... | collective-permute-start | bytes 21512 | tf_op jit(solution)/shard_map/ppermute | solution.py:302
  12.8 31.6 %copy-start.1 = (bf16[128,512]{1,0:T(8,128)(2,1)S(1)}, bf16[128,512]{1,0:T(8,128)(2,1)}, u32[]{:S(2)}) copy-start(bf16[128,512]{1,0:T(8,128)(2,1)} %q_ref.1) | copy-start | bytes 393220
  12.8 31.6 %copy-start.2 = (s32[1,16]{1,0:T(1,128)S(1)}, s32[1,16]{1,0:T(1,128)}, u32[]{:S(2)}) copy-start(s32[1,16]{1,0:T(1,128)} %assign_ref.1) | copy-start | bytes 196
  12.8 31.6 %copy-start.3 = (s32[1,4]{1,0:T(1,128)S(1)}, s32[1,4]{1,0:T(1,128)}, u32[]{:S(2)}) copy-start(s32[1,4]{1,0:T(1,128)} %length_ref.1) | copy-start | bytes 52
  12.9 5.6 %collective-permute-start.4 = (bf16[320,256]{1,0:T(8,128)(2,1)S(1)}, bf16[320,256]{1,0:T(8,128)(2,1)S(1)}, u32[]{:S(2)}, u32[]{:S(2)}) collective-permute-start(bf16[320,256]{1,0:T(8,128)(2,1)S(1)} %pack.1.refs_0_), channel_id=1, source_target_pairs={{2,0},{4,2},{6,4},{8,6},{10,8},{12,10},{14,12},{0,14},{3,1},{5,3},... | collective-permute-start | bytes 491528 | tf_op jit(solution)/shard_map/ppermute | solution.py:284
  13.0 9.2 %collective-permute-start.5 = (bf16[320,256]{1,0:T(8,128)(2,1)S(1)}, bf16[320,256]{1,0:T(8,128)(2,1)S(1)}, u32[]{:S(2)}, u32[]{:S(2)}) collective-permute-start(bf16[320,256]{1,0:T(8,128)(2,1)S(1)} %pack.1.refs_0_), channel_id=1, source_target_pairs={{14,0},{0,2},{2,4},{4,6},{6,8},{8,10},{10,12},{12,14},{15,1},{1,3}... | collective-permute-start | bytes 491528 | tf_op jit(solution)/shard_map/ppermute | solution.py:284
  15.0 1.2 %copy-start = (bf16[128,3584]{1,0:T(8,128)(2,1)S(1)}, bf16[128,3584]{1,0:T(8,128)(2,1)}, u32[]{:S(2)}) copy-start(bf16[128,3584]{1,0:T(8,128)(2,1)} %refs_1_) | copy-start | bytes 2752516
  22.2 22.2 %collective-permute-start.12 = (bf16[128,2048]{1,0:T(8,128)(2,1)S(1)}, bf16[128,2048]{1,0:T(8,128)(2,1)S(1)}, u32[]{:S(2)}, u32[]{:S(2)}) collective-permute-start(bf16[128,2048]{1,0:T(8,128)(2,1)S(1)} %get-tuple-element.35), channel_id=1, source_target_pairs={{0,128},{128,0},{1,129},{129,1},{2,130},{130,2},{3,131},{131,3},{4... | collective-permute-start | bytes 1572872 | tf_op jit(solution)/shard_map/ppermute | solution.py:279
  22.2 6.1 %collective-permute-start.6 = (bf16[320,256]{1,0:T(8,128)(2,1)S(1)}, bf16[320,256]{1,0:T(8,128)(2,1)S(1)}, u32[]{:S(2)}, u32[]{:S(2)}) collective-permute-start(bf16[320,256]{1,0:T(8,128)(2,1)S(1)} %collective-permute-done.4.refs_1_), channel_id=1, source_target_pairs={{2,0},{4,2},{6,4},{8,6},{10,8},{12,10},{14,12},{0,14},{3,1},{5,3},... | collective-permute-start | bytes 491528 | tf_op jit(solution)/shard_map/ppermute | solution.py:284
  25.6 5.6 %collective-permute-start.7 = (bf16[320,256]{1,0:T(8,128)(2,1)S(1)}, bf16[320,256]{1,0:T(8,128)(2,1)S(1)}, u32[]{:S(2)}, u32[]{:S(2)}) collective-permute-start(bf16[320,256]{1,0:T(8,128)(2,1)S(1)} %collective-permute-done.5.refs_2_), channel_id=1, source_target_pairs={{14,0},{0,2},{2,4},{4,6},{6,8},{8,10},{10,12},{12,14},{15,1},{1,3}... | collective-permute-start | bytes 491528 | tf_op jit(solution)/shard_map/ppermute | solution.py:284
  25.6 9.1 %collective-permute-start.9 = (bf16[128,2048]{1,0:T(8,128)(2,1)S(1)}, bf16[128,2048]{1,0:T(8,128)(2,1)S(1)}, u32[]{:S(2)}, u32[]{:S(2)}) collective-permute-start(bf16[128,2048]{1,0:T(8,128)(2,1)S(1)} %get-tuple-element.33), channel_id=1, source_target_pairs={{0,16},{16,0},{1,17},{17,1},{2,18},{18,2},{3,19},{19,3},{4,20},{20... | collective-permute-start | bytes 1572872 | tf_op jit(solution)/shard_map/ppermute | solution.py:279
  28.4 6.2 %collective-permute-start.8 = (bf16[320,256]{1,0:T(8,128)(2,1)S(1)}, bf16[320,256]{1,0:T(8,128)(2,1)S(1)}, u32[]{:S(2)}, u32[]{:S(2)}) collective-permute-start(bf16[320,256]{1,0:T(8,128)(2,1)S(1)} %collective-permute-done.6.refs_3_), channel_id=1, source_target_pairs={{2,0},{4,2},{6,4},{8,6},{10,8},{12,10},{14,12},{0,14},{3,1},{5,3},... | collective-permute-start | bytes 491528 | tf_op jit(solution)/shard_map/ppermute | solution.py:284
  31.2 8.0 %collective-permute-start.10 = (bf16[320,256]{1,0:T(8,128)(2,1)S(1)}, bf16[320,256]{1,0:T(8,128)(2,1)S(1)}, u32[]{:S(2)}, u32[]{:S(2)}) collective-permute-start(bf16[320,256]{1,0:T(8,128)(2,1)S(1)} %collective-permute-done.7.refs_4_), channel_id=1, source_target_pairs={{14,0},{0,2},{2,4},{4,6},{6,8},{8,10},{10,12},{12,14},{15,1},{1,3}... | collective-permute-start | bytes 491528 | tf_op jit(solution)/shard_map/ppermute | solution.py:284
  34.6 5.3 %collective-permute-start.11 = (bf16[320,256]{1,0:T(8,128)(2,1)S(1)}, bf16[320,256]{1,0:T(8,128)(2,1)S(1)}, u32[]{:S(2)}, u32[]{:S(2)}) collective-permute-start(bf16[320,256]{1,0:T(8,128)(2,1)S(1)} %collective-permute-done.8.refs_5_), channel_id=1, source_target_pairs={{2,0},{4,2},{6,4},{8,6},{10,8},{12,10},{14,12},{0,14},{3,1},{5,3},... | collective-permute-start | bytes 491528 | tf_op jit(solution)/shard_map/ppermute | solution.py:284
  37.1 13.2 %collective-permute-start.13 = (bf16[128,2048]{1,0:T(8,128)(2,1)S(1)}, bf16[128,2048]{1,0:T(8,128)(2,1)S(1)}, u32[]{:S(2)}, u32[]{:S(2)}) collective-permute-start(bf16[128,2048]{1,0:T(8,128)(2,1)S(1)} %collective-permute-done.9), channel_id=1, source_target_pairs={{0,128},{128,0},{1,129},{129,1},{2,130},{130,2},{3,131},{131,3},{4... | collective-permute-start | bytes 1572872 | tf_op jit(solution)/shard_map/ppermute | solution.py:279
  40.0 12.6 %collective-permute-start.15 = (bf16[512,256]{1,0:T(8,128)(2,1)S(1)}, bf16[512,256]{1,0:T(8,128)(2,1)S(1)}, u32[]{:S(2)}, u32[]{:S(2)}) collective-permute-start(bf16[512,256]{1,0:T(8,128)(2,1)S(1)} %slice_dynamic-update-slice_fusion.refs_0_), channel_id=1, source_target_pairs={{32,0},{64,32},{96,64},{0,96},{33,1},{65,33},{97,65},{1,97},{34,2}... | collective-permute-start | bytes 786440 | tf_op jit(solution)/shard_map/ppermute | solution.py:284
  42.7 9.8 %collective-permute-start.16 = (bf16[512,256]{1,0:T(8,128)(2,1)S(1)}, bf16[512,256]{1,0:T(8,128)(2,1)S(1)}, u32[]{:S(2)}, u32[]{:S(2)}) collective-permute-start(bf16[512,256]{1,0:T(8,128)(2,1)S(1)} %slice_dynamic-update-slice_fusion.refs_0_), channel_id=1, source_target_pairs={{64,0},{96,32},{0,64},{32,96},{65,1},{97,33},{1,65},{33,97},{66,2}... | collective-permute-start | bytes 786440 | tf_op jit(solution)/shard_map/ppermute | solution.py:284
  43.5 9.9 %collective-permute-start.17 = (bf16[512,256]{1,0:T(8,128)(2,1)S(1)}, bf16[512,256]{1,0:T(8,128)(2,1)S(1)}, u32[]{:S(2)}, u32[]{:S(2)}) collective-permute-start(bf16[512,256]{1,0:T(8,128)(2,1)S(1)} %slice_dynamic-update-slice_fusion.refs_0_), channel_id=1, source_target_pairs={{96,0},{0,32},{32,64},{64,96},{97,1},{1,33},{33,65},{65,97},{98,2}... | collective-permute-start | bytes 786440 | tf_op jit(solution)/shard_map/ppermute | solution.py:284
  48.2 4.3 %collective-permute-start.14 = (bf16[128,256]{1,0:T(8,128)(2,1)S(1)}, bf16[128,256]{1,0:T(8,128)(2,1)S(1)}, u32[]{:S(2)}, u32[]{:S(2)}) collective-permute-start(bf16[128,256]{1,0:T(8,128)(2,1)S(1)} %get-tuple-element.47), channel_id=1, source_target_pairs={{0,128},{128,0},{1,129},{129,1},{2,130},{130,2},{3,131},{131,3},{4... | collective-permute-start | bytes 196616 | tf_op jit(solution)/shard_map/ppermute | solution.py:279
  55.0 1.6 %collective-permute-start.18 = (bf16[512,256]{1,0:T(8,128)(2,1)S(1)}, bf16[512,256]{1,0:T(8,128)(2,1)S(1)}, u32[]{:S(2)}, u32[]{:S(2)}) collective-permute-start(bf16[512,256]{1,0:T(8,128)(2,1)S(1)} %get-tuple-element.49), channel_id=1, source_target_pairs={{0,16},{16,0},{1,17},{17,1},{2,18},{18,2},{3,19},{19,3},{4,20},{20... | collective-permute-start | bytes 786440 | tf_op jit(solution)/shard_map/ppermute | solution.py:279
  59.5 8.5 %collective-permute-start.21 = (bf16[448,256]{1,0:T(8,128)(2,1)S(1)}, bf16[448,256]{1,0:T(8,128)(2,1)S(1)}, u32[]{:S(2)}, u32[]{:S(2)}) collective-permute-start(bf16[448,256]{1,0:T(8,128)(2,1)S(1)} %get-tuple-element.53), channel_id=1, source_target_pairs={{32,0},{64,32},{96,64},{0,96},{33,1},{65,33},{97,65},{1,97},{34,2}... | collective-permute-start | bytes 688136 | tf_op jit(solution)/shard_map/ppermute | solution.py:284
  60.9 13.5 %collective-permute-start.20 = (bf16[448,256]{1,0:T(8,128)(2,1)S(1)}, bf16[448,256]{1,0:T(8,128)(2,1)S(1)}, u32[]{:S(2)}, u32[]{:S(2)}) collective-permute-start(bf16[448,256]{1,0:T(8,128)(2,1)S(1)} %get-tuple-element.52), channel_id=1, source_target_pairs={{96,0},{0,32},{32,64},{64,96},{97,1},{1,33},{33,65},{65,97},{98,2}... | collective-permute-start | bytes 688136 | tf_op jit(solution)/shard_map/ppermute | solution.py:284
  61.6 12.9 %collective-permute-start.19 = (bf16[448,256]{1,0:T(8,128)(2,1)S(1)}, bf16[448,256]{1,0:T(8,128)(2,1)S(1)}, u32[]{:S(2)}, u32[]{:S(2)}) collective-permute-start(bf16[448,256]{1,0:T(8,128)(2,1)S(1)} %gradient.2), channel_id=1, source_target_pairs={{64,0},{96,32},{0,64},{32,96},{65,1},{97,33},{1,65},{33,97},{66,2}... | collective-permute-start | bytes 688136 | tf_op jit(solution)/shard_map/ppermute | solution.py:284
